TPU v7x, 32 devices: a whole 2x2x4 slice. The times are simulated.
32 devices in a mesh: gx: 4 (over y, core), gy: 8 (over z, x).
Axes of the slice: x: 2, y: 2, z: 4, core: 2. Of those that a mesh axis runs over, the one named last changes fastest.
Arguments:
- solute_load: bfloat16 [512, 64, 256], P(('gx', 'gy')), may hold values from 0.099609375 to 3
- walker_displacement: float32 [512, 3, 256], P(('gx', 'gy')), may hold values from -4 to 4
- local_kelvin: float32 [512, 256], P(('gx', 'gy')), may hold values from 0.5 to 2
- couple_kinetic_factor: float32 [32], replicated, may hold values from 0.3 to 3
- arrhenius_onset: float32 [32], replicated, may hold values from 0.2 to 1.5
- adjacent_cell_keys: int32 [512, 16], P(('gx', 'gy')), may hold values from 0 to 24, as said below
- downstream_zone: int32 [512, 1], P(('gx', 'gy')), may hold values from 0 to 7; in each aligned block of 16 rows (0 to 15, 16 to 31, ...) at most 2 rows name the same one
Outputs:
- arrived: bfloat16 [512, 64, 256], P(('gx', 'gy'))
Inputs may be any that keep to these rules, and one draw needn't show every extreme that they name: `adjacent_cell_keys`: each row lists 16 different codes; code o stands for the bin o // 5 - 2 rows and o % 5 - 2 columns away, and the first entry is 12, the bin itself. `downstream_zone`: entry t hands the bin to the region with the same index along gx and index t along gy; at most 2 bins of one region name the same t.
All inputs are finite; a program needn't handle non-finite values.
Results may differ from a plain program's by a relative error of at most 0.0035.
Values may be sent and summed in bfloat16 or wider, within the bound.
No kernel may reach another device: no remote copies, remote signals or barrier semaphores. Data moves between devices by JAX's collectives and lax.ppermute only.
A program may use at most 128 MiB of HBM per device.

v0:
```python
import jax
import jax.numpy as jnp
from jax import lax
from jax.sharding import PartitionSpec as P

BX = 4
BY = 4
STEPS = 2
CAP = 2


inverse_width = 4.0


def with_halo(block, sides, width):
    for axis, dim in sides:
        count = lax.axis_size(axis)
        forward = [(i, i + 1) for i in range(count - 1)]
        backward = [(target, source) for source, target in forward]
        low = lax.ppermute(
            lax.slice_in_dim(block, block.shape[dim] - width, None, axis=dim), axis, forward
        )
        high = lax.ppermute(lax.slice_in_dim(block, 0, width, axis=dim), axis, backward)
        block = jnp.concatenate([low, block, high], axis=dim)
    return block


def react(mixture, warming_curve, couple_kinetic_factor, arrhenius_onset):
    halves = mixture.shape[1] // 2
    kind_one = mixture[:, :halves]
    kind_two = mixture[:, halves:]
    speeds = couple_kinetic_factor[None, :, None] * jnp.exp(
        -arrhenius_onset[None, :, None] / warming_curve[:, None, :]
    )
    reacted = speeds * kind_one * kind_two / (1.0 + speeds * (kind_one + kind_two))
    return jnp.concatenate([kind_one - reacted, kind_two - reacted], axis=1).astype(jnp.bfloat16)


def build_weights(ext_pos, centre, neighbour_idx, offsets, inside):
    centre_pos = ext_pos[centre]
    neigh_pos = ext_pos[neighbour_idx]
    shift_along = (offsets // 5 - 2).astype(jnp.float32)
    shift_across = (offsets % 5 - 2).astype(jnp.float32)
    offset_gap = (
        centre_pos[:, None, 0, :, None]
        - neigh_pos[:, :, 0, None, :]
        - shift_along[:, :, None, None]
    )
    squared = offset_gap * offset_gap
    offset_gap = (
        centre_pos[:, None, 1, :, None]
        - neigh_pos[:, :, 1, None, :]
        - shift_across[:, :, None, None]
    )
    squared = squared + offset_gap * offset_gap
    offset_gap = centre_pos[:, None, 2, :, None] - neigh_pos[:, :, 2, None, :]
    squared = squared + offset_gap * offset_gap
    kernel = jnp.exp(-squared * inverse_width) * inside[:, :, None, None]
    row_total = jnp.sum(kernel, axis=(1, 3))
    return (kernel / row_total[:, None, :, None]).astype(jnp.bfloat16)


def apply_weights(
    ext_species, couple_kinetic_factor, arrhenius_onset, neighbour_idx, weights, warming_curve
):
    sources = ext_species[neighbour_idx]
    mixture = jnp.einsum("gksq,gkpq->gsp", sources, weights, preferred_element_type=jnp.float32)
    return react(mixture, warming_curve, couple_kinetic_factor, arrhenius_onset)


def grouped(members):
    return tuple((member.reshape((-1, 4) + member.shape[1:]) for member in members))


def flatten_groups(result):
    return result.reshape((-1,) + result.shape[2:])


def layout(ext_x, ext_y, row_width, offsets, glob_x, glob_y, total_x, total_y):
    shift_along = offsets // 5 - 2
    shift_across = offsets % 5 - 2
    centre = ext_x * row_width + ext_y
    neighbour_idx = (ext_x[:, None] + shift_along) * row_width + ext_y[:, None] + shift_across
    target_x = glob_x[:, None] + shift_along
    target_y = glob_y[:, None] + shift_across
    inside = (
        (target_x >= 0) & (target_x < total_x) & (target_y >= 0) & (target_y < total_y)
    ).astype(jnp.float32)
    return (centre, neighbour_idx, inside)


def body(
    solute_load,
    walker_displacement,
    local_kelvin,
    couple_kinetic_factor,
    arrhenius_onset,
    adjacent_cell_keys,
    downstream_zone,
):
    band_count = lax.axis_size("gx")
    lane_count = lax.axis_size("gy")
    band_index = lax.axis_index("gx")
    lane_index = lax.axis_index("gy")
    bin_count = BX * BY
    species_count = solute_load.shape[1]
    part_count = solute_load.shape[2]
    total_x = band_count * BX
    total_y = lane_count * BY
    local_ids = jnp.arange(bin_count, dtype=jnp.int32)
    local_x = local_ids // BY
    local_y = local_ids % BY
    own_x = band_index * BX + local_x
    own_y = lane_index * BY + local_y
    framed = with_halo(
        walker_displacement.reshape(BX, BY, 3, part_count), (("gx", 0), ("gy", 1)), 2
    ).reshape(-1, 3, part_count)
    centre, neighbour_idx, inside = layout(
        local_x + 2, local_y + 2, BY + 4, adjacent_cell_keys, own_x, own_y, total_x, total_y
    )

    def build_one(packet):
        return build_weights(framed, packet[0], packet[1], packet[2], packet[3])

    weights = lax.map(build_one, grouped((centre, neighbour_idx, adjacent_cell_keys, inside)))
    applied = grouped((neighbour_idx, local_kelvin))
    species = solute_load
    for repeat in range(STEPS):
        ext_species = with_halo(
            species.reshape(BX, BY, species_count, part_count), (("gx", 0), ("gy", 1)), 2
        ).reshape(-1, species_count, part_count)

        def apply_one(packet):
            return apply_weights(
                ext_species, couple_kinetic_factor, arrhenius_onset, packet[0], packet[1], packet[2]
            )

        species = flatten_groups(lax.map(apply_one, (applied[0], weights, applied[1])))
    target = downstream_zone[:, 0]
    slot_count = lane_count * CAP
    chosen = (target[:, None] == jnp.arange(lane_count, dtype=jnp.int32)[None, :]).astype(jnp.int32)
    earlier_count = jnp.cumsum(chosen, axis=0) - chosen
    order_slot = jnp.sum(earlier_count * chosen, axis=1)
    slot_of_bin = target * CAP + order_slot
    select = (jnp.arange(slot_count, dtype=jnp.int32)[:, None] == slot_of_bin[None, :]).astype(
        jnp.bfloat16
    )
    packed = jnp.dot(select, species.reshape(bin_count, -1), preferred_element_type=jnp.float32)
    packed = packed.astype(jnp.bfloat16).reshape(slot_count, species_count, part_count)
    return lax.all_to_all(packed, "gy", split_axis=0, concat_axis=0, tiled=True)


def solution(mesh):
    in_specs = (
        P(("gx", "gy"), None, None),
        P(("gx", "gy"), None, None),
        P(("gx", "gy"), None),
        P(),
        P(),
        P(("gx", "gy"), None),
        P(("gx", "gy"), None),
    )
    out_specs = P(("gx", "gy"), None, None)
    return jax.shard_map(body, mesh=mesh, in_specs=in_specs, out_specs=out_specs, check_vma=False)
```

profile of v0, /device:TPU:1, one launch (start us, length us, event | category | flops | bytes accessed | tf_op | source)
XLA Modules:
  0.0 259.9 jit_solution(4770896948833591391)
XLA Ops:
  0.8 4.5 %collective-permute-start.4 = (f32[2,4,3,256]{3,2,1,0:T(4,128)S(1)}, f32[2,4,3,256]{3,2,1,0:T(4,128)S(1)}, u32[]{:S(2)}, u32[]{:S(2)}) collective-permute-start(f32[2,4,3,256]{3,2,1,0:T(4,128)S(1)} %bitcast.198), channel_id=1, source_target_pairs={{0,8},{8,16},{16,24},{1,9},{9,17},{17,25},{2,10},{10,18},{18,26},{... | collective-permute-start | bytes 73736 | tf_op jit(solution)/shard_map/ppermute | solution.py:20
  32.0 97.0 %while.37 = (s32[]{:T(128)}, bf16[4,4,16,256,256]{4,3,2,1,0:T(8,128)(2,1)}, s32[4,4]{1,0:T(4,128)S(1)}, f32[64,3,256]{2,1,0:T(4,128)S(1)}, s32[4,4,16]{2,1,0:T(4...) while((s32[]{:T(128)}, bf16[4,4,16,256,256]{4,3,2,1,0:T(8,128)(2,1)}, ...), condition=%wide.region_4.5_spmd, body=%wide.region_2.4_spmd.sunk | while | flops 121637072 | bytes 10081189 | solution.py:125
  34.4 10.1 %multiply_reduce_fusion.2 = f32[4,256]{1,0:T(4,128)S(1)} fusion(f32[4,16]{1,0:T(4,128)S(1)} %dynamic-slice_bitcast_fusion.6, f32[4,16,256]{2,1,0:T(8,128)S(1)} %get-tuple-element.538, f32[4,256]{1,0:T(4,128)S(1)} %get-tuple-element.541, f32[4,16]{1,0:T(4,128)S(1)} %get-tuple-element.542, f32[4,16,256]{2,1,0:T(8,128)S(1)} %get-tuple-element.543, ...), kind=kLoop, calls=%fused_computation.5.clone.1 | loop fusion | flops 58719232 | bytes 213760 | tf_op jit(solution)/shard_map/while/body/eval_jaxpr/reduce_sum | solution.py:59
  44.5 11.8 %fusion.72 = bf16[4,4,16,256,256]{4,3,2,1,0:T(8,128)(2,1)} fusion(bf16[4,4,16,256,256]{4,3,2,1,0:T(8,128)(2,1)} %get-tuple-element.577, s32[]{:T(128)} %get-tuple-element.576, f32[4,256]{1,0:T(4,128)S(1)} %multiply_reduce_fusion.2, f32[4,16]{1,0:T(4,128)S(1)} %dynamic-slice_bitcast_fusion.6, f32[4,16,256]{2,1,0:T(8,128)S(1)} %get-tuple-element.538, ...), kind=kLoop, calls=%fused_computation.6.clone.1 | loop fusion | flops 62914560 | bytes 8602880 | tf_op jit(solution)/shard_map/while/body/jit(dynamic_update_index_in_dim)/dynamic_update_slice | solution.py:125
  58.7 10.1 %multiply_reduce_fusion.2 = f32[4,256]{1,0:T(4,128)S(1)} fusion(f32[4,16]{1,0:T(4,128)S(1)} %dynamic-slice_bitcast_fusion.6, f32[4,16,256]{2,1,0:T(8,128)S(1)} %get-tuple-element.538, f32[4,256]{1,0:T(4,128)S(1)} %get-tuple-element.541, f32[4,16]{1,0:T(4,128)S(1)} %get-tuple-element.542, f32[4,16,256]{2,1,0:T(8,128)S(1)} %get-tuple-element.543, ...), kind=kLoop, calls=%fused_computation.5.clone.1 | loop fusion | flops 58719232 | bytes 213760 | tf_op jit(solution)/shard_map/while/body/eval_jaxpr/reduce_sum | solution.py:59
  68.7 11.8 %fusion.72 = bf16[4,4,16,256,256]{4,3,2,1,0:T(8,128)(2,1)} fusion(bf16[4,4,16,256,256]{4,3,2,1,0:T(8,128)(2,1)} %get-tuple-element.577, s32[]{:T(128)} %get-tuple-element.576, f32[4,256]{1,0:T(4,128)S(1)} %multiply_reduce_fusion.2, f32[4,16]{1,0:T(4,128)S(1)} %dynamic-slice_bitcast_fusion.6, f32[4,16,256]{2,1,0:T(8,128)S(1)} %get-tuple-element.538, ...), kind=kLoop, calls=%fused_computation.6.clone.1 | loop fusion | flops 62914560 | bytes 8602880 | tf_op jit(solution)/shard_map/while/body/jit(dynamic_update_index_in_dim)/dynamic_update_slice | solution.py:125
  82.9 10.1 %multiply_reduce_fusion.2 = f32[4,256]{1,0:T(4,128)S(1)} fusion(f32[4,16]{1,0:T(4,128)S(1)} %dynamic-slice_bitcast_fusion.6, f32[4,16,256]{2,1,0:T(8,128)S(1)} %get-tuple-element.538, f32[4,256]{1,0:T(4,128)S(1)} %get-tuple-element.541, f32[4,16]{1,0:T(4,128)S(1)} %get-tuple-element.542, f32[4,16,256]{2,1,0:T(8,128)S(1)} %get-tuple-element.543, ...), kind=kLoop, calls=%fused_computation.5.clone.1 | loop fusion | flops 58719232 | bytes 213760 | tf_op jit(solution)/shard_map/while/body/eval_jaxpr/reduce_sum | solution.py:59
  93.0 11.8 %fusion.72 = bf16[4,4,16,256,256]{4,3,2,1,0:T(8,128)(2,1)} fusion(bf16[4,4,16,256,256]{4,3,2,1,0:T(8,128)(2,1)} %get-tuple-element.577, s32[]{:T(128)} %get-tuple-element.576, f32[4,256]{1,0:T(4,128)S(1)} %multiply_reduce_fusion.2, f32[4,16]{1,0:T(4,128)S(1)} %dynamic-slice_bitcast_fusion.6, f32[4,16,256]{2,1,0:T(8,128)S(1)} %get-tuple-element.538, ...), kind=kLoop, calls=%fused_computation.6.clone.1 | loop fusion | flops 62914560 | bytes 8602880 | tf_op jit(solution)/shard_map/while/body/jit(dynamic_update_index_in_dim)/dynamic_update_slice | solution.py:125
  107.1 10.1 %multiply_reduce_fusion.2 = f32[4,256]{1,0:T(4,128)S(1)} fusion(f32[4,16]{1,0:T(4,128)S(1)} %dynamic-slice_bitcast_fusion.6, f32[4,16,256]{2,1,0:T(8,128)S(1)} %get-tuple-element.538, f32[4,256]{1,0:T(4,128)S(1)} %get-tuple-element.541, f32[4,16]{1,0:T(4,128)S(1)} %get-tuple-element.542, f32[4,16,256]{2,1,0:T(8,128)S(1)} %get-tuple-element.543, ...), kind=kLoop, calls=%fused_computation.5.clone.1 | loop fusion | flops 58719232 | bytes 213760 | tf_op jit(solution)/shard_map/while/body/eval_jaxpr/reduce_sum | solution.py:59
  117.2 11.8 %fusion.72 = bf16[4,4,16,256,256]{4,3,2,1,0:T(8,128)(2,1)} fusion(bf16[4,4,16,256,256]{4,3,2,1,0:T(8,128)(2,1)} %get-tuple-element.577, s32[]{:T(128)} %get-tuple-element.576, f32[4,256]{1,0:T(4,128)S(1)} %multiply_reduce_fusion.2, f32[4,16]{1,0:T(4,128)S(1)} %dynamic-slice_bitcast_fusion.6, f32[4,16,256]{2,1,0:T(8,128)S(1)} %get-tuple-element.538, ...), kind=kLoop, calls=%fused_computation.6.clone.1 | loop fusion | flops 62914560 | bytes 8602880 | tf_op jit(solution)/shard_map/while/body/jit(dynamic_update_index_in_dim)/dynamic_update_slice | solution.py:125
  131.5 34.4 %while.38 = (s32[]{:T(128)}, bf16[4,4,64,256]{3,2,1,0:T(8,128)(2,1)S(1)}, s32[4,4,16]{2,1,0:T(4,128)S(1)}, bf16[64,64,256]{2,1,0:T(8,128)(2,1)}, bf16[4,4,16,256...) while((s32[]{:T(128)}, ...), condition=%wide.region_6.7_spmd, body=%wide.region_5.6_spmd.sunk | while | flops 537527488 | bytes 16009577 | solution.py:138
  133.9 6.0 %fusion.75 = f32[4,64,256]{2,1,0:T(8,128)S(1)} fusion(bf16[4,16,64,256]{3,2,1,0:T(8,128)(2,1)S(1)} %bitcast.173, bf16[4,4,16,256,256]{4,3,2,1,0:T(8,128)(2,1)} %get-tuple-element.614, s32[]{:T(128)} %get-tuple-element.601), kind=kOutput, calls=%fused_computation.36.clone.1 | convolution fusion | flops 536870912 | bytes 10748416 | tf_op jit(solution)/shard_map/while/body/eval_jaxpr/gksq,gkpq->gsp/dot_general | solution.py:67
  142.5 6.0 %fusion.75 = f32[4,64,256]{2,1,0:T(8,128)S(1)} fusion(bf16[4,16,64,256]{3,2,1,0:T(8,128)(2,1)S(1)} %bitcast.173, bf16[4,4,16,256,256]{4,3,2,1,0:T(8,128)(2,1)} %get-tuple-element.614, s32[]{:T(128)} %get-tuple-element.601), kind=kOutput, calls=%fused_computation.36.clone.1 | convolution fusion | flops 536870912 | bytes 10748416 | tf_op jit(solution)/shard_map/while/body/eval_jaxpr/gksq,gkpq->gsp/dot_general | solution.py:67
  151.1 6.0 %fusion.75 = f32[4,64,256]{2,1,0:T(8,128)S(1)} fusion(bf16[4,16,64,256]{3,2,1,0:T(8,128)(2,1)S(1)} %bitcast.173, bf16[4,4,16,256,256]{4,3,2,1,0:T(8,128)(2,1)} %get-tuple-element.614, s32[]{:T(128)} %get-tuple-element.601), kind=kOutput, calls=%fused_computation.36.clone.1 | convolution fusion | flops 536870912 | bytes 10748416 | tf_op jit(solution)/shard_map/while/body/eval_jaxpr/gksq,gkpq->gsp/dot_general | solution.py:67
  159.7 6.0 %fusion.75 = f32[4,64,256]{2,1,0:T(8,128)S(1)} fusion(bf16[4,16,64,256]{3,2,1,0:T(8,128)(2,1)S(1)} %bitcast.173, bf16[4,4,16,256,256]{4,3,2,1,0:T(8,128)(2,1)} %get-tuple-element.614, s32[]{:T(128)} %get-tuple-element.601), kind=kOutput, calls=%fused_computation.36.clone.1 | convolution fusion | flops 536870912 | bytes 10748416 | tf_op jit(solution)/shard_map/while/body/eval_jaxpr/gksq,gkpq->gsp/dot_general | solution.py:67
  166.0 5.3 %collective-permute-start.8 = (bf16[2,4,64,256]{3,2,1,0:T(8,128)(2,1)S(1)}, bf16[2,4,64,256]{3,2,1,0:T(8,128)(2,1)S(1)}, u32[]{:S(2)}, u32[]{:S(2)}) collective-permute-start(bf16[2,4,64,256]{3,2,1,0:T(8,128)(2,1)S(1)} %get-tuple-element.384), channel_id=1, source_target_pairs={{0,8},{8,16},{16,24},{1,9},{9,17},{17,25},{2,10},{10,18},{18,26},{... | collective-permute-start | bytes 786440 | tf_op jit(solution)/shard_map/ppermute | solution.py:20
  174.7 4.3 %collective-permute-done.9 = bf16[2,4,64,256]{3,2,1,0:T(8,128)(2,1)S(1)} collective-permute-done((bf16[2,4,64,256]{3,2,1,0:T(8,128)(2,1)S(1)}, bf16[2,4,64,256]{3,2,1,0:T(8,128)(2,1)S(1)}, u32[]{:S(2)}, u32[]{:S(2)}) %collective-permute-start.9) | collective-permute-done | bytes 262176 | tf_op jit(solution)/shard_map/ppermute | solution.py:23
  185.3 17.3 %collective-permute-done.10 = bf16[8,2,64,256]{3,2,1,0:T(8,128)(2,1)S(1)} collective-permute-done((bf16[8,2,64,256]{3,2,1,0:T(8,128)(2,1)S(1)}, bf16[8,2,64,256]{3,2,1,0:T(8,128)(2,1)S(1)}, u32[]{:S(2)}, u32[]{:S(2)}) %collective-permute-start.10) | collective-permute-done | bytes 524320 | tf_op jit(solution)/shard_map/ppermute | solution.py:20
  204.2 34.4 %while.39 = (s32[]{:T(128)}, bf16[4,4,64,256]{3,2,1,0:T(8,128)(2,1)S(1)}, s32[4,4,16]{2,1,0:T(4,128)S(1)}, bf16[64,64,256]{2,1,0:T(8,128)(2,1)}, bf16[4,4,16,256...) while((s32[]{:T(128)}, ...), condition=%wide.region_8.9_spmd, body=%wide.region_7.8_spmd.sunk | while | flops 537527488 | bytes 16009577 | solution.py:138
  206.6 6.0 %fusion.80 = f32[4,64,256]{2,1,0:T(8,128)S(1)} fusion(bf16[4,16,64,256]{3,2,1,0:T(8,128)(2,1)S(1)} %bitcast.174, bf16[4,4,16,256,256]{4,3,2,1,0:T(8,128)(2,1)} %get-tuple-element.641, s32[]{:T(128)} %get-tuple-element.628), kind=kOutput, calls=%fused_computation.52.clone.1 | convolution fusion | flops 536870912 | bytes 10748416 | tf_op jit(solution)/shard_map/while/body/eval_jaxpr/gksq,gkpq->gsp/dot_general | solution.py:67
  215.2 6.0 %fusion.80 = f32[4,64,256]{2,1,0:T(8,128)S(1)} fusion(bf16[4,16,64,256]{3,2,1,0:T(8,128)(2,1)S(1)} %bitcast.174, bf16[4,4,16,256,256]{4,3,2,1,0:T(8,128)(2,1)} %get-tuple-element.641, s32[]{:T(128)} %get-tuple-element.628), kind=kOutput, calls=%fused_computation.52.clone.1 | convolution fusion | flops 536870912 | bytes 10748416 | tf_op jit(solution)/shard_map/while/body/eval_jaxpr/gksq,gkpq->gsp/dot_general | solution.py:67
  223.8 6.0 %fusion.80 = f32[4,64,256]{2,1,0:T(8,128)S(1)} fusion(bf16[4,16,64,256]{3,2,1,0:T(8,128)(2,1)S(1)} %bitcast.174, bf16[4,4,16,256,256]{4,3,2,1,0:T(8,128)(2,1)} %get-tuple-element.641, s32[]{:T(128)} %get-tuple-element.628), kind=kOutput, calls=%fused_computation.52.clone.1 | convolution fusion | flops 536870912 | bytes 10748416 | tf_op jit(solution)/shard_map/while/body/eval_jaxpr/gksq,gkpq->gsp/dot_general | solution.py:67
  232.4 6.0 %fusion.80 = f32[4,64,256]{2,1,0:T(8,128)S(1)} fusion(bf16[4,16,64,256]{3,2,1,0:T(8,128)(2,1)S(1)} %bitcast.174, bf16[4,4,16,256,256]{4,3,2,1,0:T(8,128)(2,1)} %get-tuple-element.641, s32[]{:T(128)} %get-tuple-element.628), kind=kOutput, calls=%fused_computation.52.clone.1 | convolution fusion | flops 536870912 | bytes 10748416 | tf_op jit(solution)/shard_map/while/body/eval_jaxpr/gksq,gkpq->gsp/dot_general | solution.py:67
  239.4 19.8 %all_to_all.5 = bf16[16,64,256]{2,1,0:T(8,128)(2,1)S(1)} all-to-all(bf16[16,64,256]{2,1,0:T(8,128)(2,1)S(1)} %bitcast.186), channel_id=1, replica_groups=mesh['gx'=4,'gy'=8] {'gy'}, dimensions={0} | all-to-all | bytes 1048576 | tf_op jit(solution)/shard_map/all_to_all | solution.py:150
  (185 shorter events, 71.9 us)
Async XLA Ops:
  0.8 16.2 %collective-permute-start.4 = (f32[2,4,3,256]{3,2,1,0:T(4,128)S(1)}, f32[2,4,3,256]{3,2,1,0:T(4,128)S(1)}, u32[]{:S(2)}, u32[]{:S(2)}) collective-permute-start(f32[2,4,3,256]{3,2,1,0:T(4,128)S(1)} %bitcast.198), channel_id=1, source_target_pairs={{0,8},{8,16},{16,24},{1,9},{9,17},{17,25},{2,10},{10,18},{18,26},{... | collective-permute-start | bytes 73736 | tf_op jit(solution)/shard_map/ppermute | solution.py:20
  5.3 11.7 %collective-permute-start.5 = (f32[2,4,3,256]{3,2,1,0:T(4,128)S(1)}, f32[2,4,3,256]{3,2,1,0:T(4,128)S(1)}, u32[]{:S(2)}, u32[]{:S(2)}) collective-permute-start(f32[2,4,3,256]{3,2,1,0:T(4,128)S(1)} %bitcast.199), channel_id=1, source_target_pairs={{8,0},{16,8},{24,16},{9,1},{17,9},{25,17},{10,2},{18,10},{26,18},{... | collective-permute-start | bytes 73736 | tf_op jit(solution)/shard_map/ppermute | solution.py:23
  8.3 17.0 %collective-permute-start = (bf16[2,4,64,256]{3,2,1,0:T(8,128)(2,1)S(1)}, bf16[2,4,64,256]{3,2,1,0:T(8,128)(2,1)S(1)}, u32[]{:S(2)}, u32[]{:S(2)}) collective-permute-start(bf16[2,4,64,256]{3,2,1,0:T(8,128)(2,1)S(1)} %bitcast.192), channel_id=1, source_target_pairs={{0,8},{8,16},{16,24},{1,9},{9,17},{17,25},{2,10},{10,18},{18,26},{... | collective-permute-start | bytes 786440 | tf_op jit(solution)/shard_map/ppermute | solution.py:20
  12.0 13.3 %collective-permute-start.1 = (bf16[2,4,64,256]{3,2,1,0:T(8,128)(2,1)S(1)}, bf16[2,4,64,256]{3,2,1,0:T(8,128)(2,1)S(1)}, u32[]{:S(2)}, u32[]{:S(2)}) collective-permute-start(bf16[2,4,64,256]{3,2,1,0:T(8,128)(2,1)S(1)} %bitcast.191), channel_id=1, source_target_pairs={{8,0},{16,8},{24,16},{9,1},{17,9},{25,17},{10,2},{18,10},{26,18},{... | collective-permute-start | bytes 786440 | tf_op jit(solution)/shard_map/ppermute | solution.py:23
  17.1 5.2 %collective-permute-start.6 = (f32[8,2,3,256]{3,2,1,0:T(4,128)S(1)}, f32[8,2,3,256]{3,2,1,0:T(4,128)S(1)}, u32[]{:S(2)}, u32[]{:S(2)}) collective-permute-start(f32[8,2,3,256]{3,2,1,0:T(4,128)S(1)} %get-tuple-element.387), channel_id=1, source_target_pairs={{0,1},{1,2},{2,3},{3,4},{4,5},{5,6},{6,7},{8,9},{9,10},{10,11},{11... | collective-permute-start | bytes 147464 | tf_op jit(solution)/shard_map/ppermute | solution.py:20
  20.2 5.0 %collective-permute-start.7 = (f32[8,2,3,256]{3,2,1,0:T(4,128)S(1)}, f32[8,2,3,256]{3,2,1,0:T(4,128)S(1)}, u32[]{:S(2)}, u32[]{:S(2)}) collective-permute-start(f32[8,2,3,256]{3,2,1,0:T(4,128)S(1)} %get-tuple-element.388), channel_id=1, source_target_pairs={{1,0},{2,1},{3,2},{4,3},{5,4},{6,5},{7,6},{9,8},{10,9},{11,10},{12... | collective-permute-start | bytes 147464 | tf_op jit(solution)/shard_map/ppermute | solution.py:23
  26.6 102.4 %collective-permute-start.2 = (bf16[8,2,64,256]{3,2,1,0:T(8,128)(2,1)S(1)}, bf16[8,2,64,256]{3,2,1,0:T(8,128)(2,1)S(1)}, u32[]{:S(2)}, u32[]{:S(2)}) collective-permute-start(bf16[8,2,64,256]{3,2,1,0:T(8,128)(2,1)S(1)} %get-tuple-element.381), channel_id=1, source_target_pairs={{0,1},{1,2},{2,3},{3,4},{4,5},{5,6},{6,7},{8,9},{9,10},{10,11},{11... | collective-permute-start | bytes 1572872 | tf_op jit(solution)/shard_map/ppermute | solution.py:20
  30.7 98.3 %collective-permute-start.3 = (bf16[8,2,64,256]{3,2,1,0:T(8,128)(2,1)S(1)}, bf16[8,2,64,256]{3,2,1,0:T(8,128)(2,1)}, u32[]{:S(2)}, u32[]{:S(2)}) collective-permute-start(bf16[8,2,64,256]{3,2,1,0:T(8,128)(2,1)S(1)} %get-tuple-element.382), channel_id=1, source_target_pairs={{1,0},{2,1},{3,2},{4,3},{5,4},{6,5},{7,6},{9,8},{10,9},{11,10},{12... | collective-permute-start | bytes 1572872 | tf_op jit(solution)/shard_map/ppermute | solution.py:23
  32.0 97.0 %copy-start = (bf16[16,64,256]{2,1,0:T(8,128)(2,1)S(1)}, bf16[16,64,256]{2,1,0:T(8,128)(2,1)}, u32[]{:S(2)}) copy-start(bf16[16,64,256]{2,1,0:T(8,128)(2,1)} %param.13) | copy-start | bytes 1572868
  32.0 99.5 %copy-start.1 = (f32[32]{0:T(128)S(1)}, f32[32]{0:T(128)}, u32[]{:S(2)}) copy-start(f32[32]{0:T(128)} %param.16) | copy-start | bytes 388
  131.5 53.5 %copy-start.2 = (s32[16,1]{0,1:T(1,128)S(1)}, s32[16,1]{0,1:T(1,128)}, u32[]{:S(2)}) copy-start(s32[16,1]{0,1:T(1,128)} %param.19) | copy-start | bytes 196
  166.0 8.7 %collective-permute-start.8 = (bf16[2,4,64,256]{3,2,1,0:T(8,128)(2,1)S(1)}, bf16[2,4,64,256]{3,2,1,0:T(8,128)(2,1)S(1)}, u32[]{:S(2)}, u32[]{:S(2)}) collective-permute-start(bf16[2,4,64,256]{3,2,1,0:T(8,128)(2,1)S(1)} %get-tuple-element.384), channel_id=1, source_target_pairs={{0,8},{8,16},{16,24},{1,9},{9,17},{17,25},{2,10},{10,18},{18,26},{... | collective-permute-start | bytes 786440 | tf_op jit(solution)/shard_map/ppermute | solution.py:20
  171.3 7.7 %collective-permute-start.9 = (bf16[2,4,64,256]{3,2,1,0:T(8,128)(2,1)S(1)}, bf16[2,4,64,256]{3,2,1,0:T(8,128)(2,1)S(1)}, u32[]{:S(2)}, u32[]{:S(2)}) collective-permute-start(bf16[2,4,64,256]{3,2,1,0:T(8,128)(2,1)S(1)} %get-tuple-element.383), channel_id=1, source_target_pairs={{8,0},{16,8},{24,16},{9,1},{17,9},{25,17},{10,2},{18,10},{26,18},{... | collective-permute-start | bytes 786440 | tf_op jit(solution)/shard_map/ppermute | solution.py:23
  179.2 23.4 %collective-permute-start.10 = (bf16[8,2,64,256]{3,2,1,0:T(8,128)(2,1)S(1)}, bf16[8,2,64,256]{3,2,1,0:T(8,128)(2,1)S(1)}, u32[]{:S(2)}, u32[]{:S(2)}) collective-permute-start(bf16[8,2,64,256]{3,2,1,0:T(8,128)(2,1)S(1)} %get-tuple-element.379), channel_id=1, source_target_pairs={{0,1},{1,2},{2,3},{3,4},{4,5},{5,6},{6,7},{8,9},{9,10},{10,11},{11... | collective-permute-start | bytes 1572872 | tf_op jit(solution)/shard_map/ppermute | solution.py:20
  183.5 19.1 %collective-permute-start.11 = (bf16[8,2,64,256]{3,2,1,0:T(8,128)(2,1)S(1)}, bf16[8,2,64,256]{3,2,1,0:T(8,128)(2,1)S(1)}, u32[]{:S(2)}, u32[]{:S(2)}) collective-permute-start(bf16[8,2,64,256]{3,2,1,0:T(8,128)(2,1)S(1)} %get-tuple-element.380), channel_id=1, source_target_pairs={{1,0},{2,1},{3,2},{4,3},{5,4},{6,5},{7,6},{9,8},{10,9},{11,10},{12... | collective-permute-start | bytes 1572872 | tf_op jit(solution)/shard_map/ppermute | solution.py:23
where the time goes:
time: 263 us; the launch traced here: 260 us
  other arithmetic  99.6 us (38%)
  matrix products  48.3 us (18%)
  starting transfers between devices  34.9 us (13%)
  local copies, waits for them, and re-layouts  30.2 us (11%)
  waiting for transfers between devices  26 us (10%)
  blocking collectives  19.8 us (8%)
    dot_general x8, matrix products, apply_weights(): jnp.einsum('gksq,gkpq->gsp', sources, weights, preferred_element_type=jnp...  48 us
    dynamic_update_slice x4, other arithmetic, body(): lax.map(build_one, grouped((centre, neighbour_idx, adjacent_cell_keys, in...  47.2 us
    reduce_sum x4, other arithmetic, build_weights(): row_total = jnp.sum(kernel, axis=(1, 3))  40.3 us
    ppermute x6, starting transfers between devices, with_halo(): lax.ppermute(lax.slice_in_dim(block, block.shape[dim] - width, None, axis...  25 us
    all_to_all x1, blocking collectives, body(): return lax.all_to_all(packed, 'gy', split_axis=0, concat_axis=0, tiled=True)  19.8 us
    ppermute x6, waiting for transfers between devices, with_halo(): lax.ppermute(lax.slice_in_dim(block, block.shape[dim] - width, None, axis...  18.7 us
    gather x8, local copies, waits for them, and re-layouts, apply_weights(): sources = ext_species[neighbour_idx]  18.2 us
    ppermute x6, starting transfers between devices, with_halo(): lax.ppermute(lax.slice_in_dim(block, 0, width, axis=dim), axis, backward)  9.82 us
  transfers between devices with their start and end apart: 12, of which 4 were waited for; matrix products, arithmetic and copies ran while one was open for 39% of the time, Pallas kernels for 0%

commit v1 on v0

v1 whole, which is shorter than its diff:
```python
import functools
import math

import jax
import jax.numpy as jnp
from jax import lax
from jax.experimental import pallas as pl
from jax.experimental.pallas import tpu as pltpu
from jax.sharding import PartitionSpec as P

BX = 4
BY = 4
STEPS = 2
CAP = 2
HALO = 2
WIDTH = 2 * HALO + 1

inverse_width = 4.0
SCALE = math.sqrt(inverse_width * math.log2(math.e))
FAR = -1e30

f32 = jnp.float32
bf16 = jnp.bfloat16

OWN = BX * BY
SIDE = BX * HALO
BAND = HALO * (BY + 2 * HALO)
LEFT = OWN
RIGHT = LEFT + SIDE
UP = RIGHT + SIDE
DOWN = UP + BAND
EXT = DOWN + BAND


def chain(count):
    forward = [(i, i + 1) for i in range(count - 1)]
    return forward, [(b, a) for a, b in forward]


def exchange(block):
    trailing = block.shape[1:]
    grid = block.reshape((BX, BY) + trailing)
    forward, backward = chain(lax.axis_size("gy"))
    left = lax.ppermute(grid[:, BY - HALO :], "gy", forward)
    right = lax.ppermute(grid[:, :HALO], "gy", backward)
    rows = jnp.concatenate([left, grid, right], axis=1)
    forward, backward = chain(lax.axis_size("gx"))
    up = lax.ppermute(rows[BX - HALO :], "gx", forward)
    down = lax.ppermute(rows[:HALO], "gx", backward)
    flat = lambda x: x.reshape((-1,) + trailing)
    return block, flat(left), flat(right), flat(up), flat(down)


PIECES = (OWN, SIDE, SIDE, BAND, BAND)
STARTS = (0, LEFT, RIGHT, UP, DOWN)


def slot_of(ex, ey):
    wide = BY + 2 * HALO
    inner = jnp.where(
        ey < 0,
        LEFT + ex * HALO + ey + HALO,
        jnp.where(ey >= BY, RIGHT + ex * HALO + ey - BY, ex * BY + ey),
    )
    outer = jnp.where(
        ex < 0, UP + (ex + HALO) * wide + ey + HALO, DOWN + (ex - BX) * wide + ey + HALO
    )
    return jnp.where((ex >= 0) & (ex < BX), inner, outer)


def place_of(piece, i):
    wide = BY + 2 * HALO
    if piece == 0:
        return i // BY, i % BY
    if piece == 1:
        return i // HALO, i % HALO - HALO
    if piece == 2:
        return i // HALO, i % HALO + BY
    if piece == 3:
        return i // wide - HALO, i % wide - HALO
    return i // wide + BX, i % wide - HALO


def three_parts(x):
    high = x.astype(bf16).astype(f32)
    rest = x - high
    middle = rest.astype(bf16).astype(f32)
    return high, middle, rest - middle


def coordinates(pos, ex, ey):
    row = lax.broadcasted_iota(jnp.int32, (8, pos.shape[-1]), 0)
    padded = jnp.concatenate([pos, jnp.zeros((5, pos.shape[-1]), f32)], axis=0)
    middle = jnp.where(
        row == 0,
        ex.astype(f32) - (BX - 1) / 2,
        jnp.where(row == 1, ey.astype(f32) - (BY - 1) / 2, 0.0),
    )
    return (padded + middle) * SCALE, row


def features_of_source(pos, ex, ey, inside):
    v, row = coordinates(pos, ex, ey)
    norm = jnp.sum(v * v, axis=0, keepdims=True)
    high, middle, low = three_parts(v)
    nh, nm, nl = three_parts(norm)
    nh = jnp.where(inside, -nh, FAR)
    last = row == 3
    groups = (
        jnp.where(last, nh, high),
        jnp.where(last, -nm, high),
        jnp.where(last, -nl, middle),
        jnp.where(last, 1.0, high),
        jnp.where(last, 1.0, low),
        jnp.where(last, 1.0, middle),
    )
    return jnp.concatenate(groups, axis=0)


def features_of_target(pos, ex, ey):
    u, row = coordinates(pos, ex, ey)
    norm = jnp.sum(u * u, axis=0, keepdims=True)
    high, middle, low = three_parts(u)
    nh, nm, nl = three_parts(norm)
    last = row == 3
    groups = (
        jnp.where(last, 1.0, 2.0 * high),
        jnp.where(last, 1.0, 2.0 * middle),
        jnp.where(last, 1.0, 2.0 * high),
        jnp.where(last, -nh, 2.0 * low),
        jnp.where(last, -nm, 2.0 * high),
        jnp.where(last, -nl, 2.0 * middle),
    )
    return jnp.concatenate(groups, axis=0)


FEATURES = 48


def react(mixture, kelvin, factor, onset):
    half = mixture.shape[0] // 2
    u = mixture[:half]
    v = mixture[half:]
    speed = factor * jnp.exp(-onset / kelvin)
    reacted = speed * u * v / (1.0 + speed * (u + v))
    return jnp.concatenate([u - reacted, v - reacted], axis=0).astype(bf16)


def load_species(refs, buffer, sem):
    copies = [
        pltpu.make_async_copy(ref, buffer.at[pl.ds(start, count)], sem.at[i])
        for i, (ref, start, count) in enumerate(zip(refs, STARTS, PIECES))
    ]
    for copy in copies:
        copy.start()
    return copies


def first_step(
    near_ref,
    meta_ref,
    p0,
    p1,
    p2,
    p3,
    p4,
    s0,
    s1,
    s2,
    s3,
    s4,
    kelvin_ref,
    factor_ref,
    onset_ref,
    out_ref,
    w_ref,
    inv_ref,
    source,
    target,
    species,
    gathered,
    sem,
):
    b = pl.program_id(0)
    neighbours = near_ref.shape[0] // OWN
    parts = source.shape[1]

    @pl.when(b == 0)
    def _():
        copies = load_species((s0, s1, s2, s3, s4), species, sem)
        for piece, ref in enumerate((p0, p1, p2, p3, p4)):

            def one(i, _, piece=piece, ref=ref):
                ex, ey = place_of(piece, i)
                gx = meta_ref[0] + ex
                gy = meta_ref[1] + ey
                inside = (gx >= 0) & (gx < meta_ref[2]) & (gy >= 0) & (gy < meta_ref[3])
                pos = ref[i]
                f = features_of_source(pos, ex, ey, inside)
                source[STARTS[piece] + i] = f.T.astype(bf16)
                if piece == 0:
                    target[i] = features_of_target(pos, ex, ey).astype(bf16)
                return 0

            lax.fori_loop(0, PIECES[piece], one, 0)
        for copy in copies:
            copy.wait()

    f = target[b]
    total = jnp.zeros((8, parts), f32)
    for k in range(neighbours):
        q = near_ref[b * neighbours + k]
        e = jnp.dot(source[q], f, preferred_element_type=f32)
        w = jnp.exp2(e)
        total = total + w.reshape(parts // 8, 8, parts).sum(0)
        w_ref[0, pl.ds(k * parts, parts)] = w.astype(bf16)
        gathered[:, k * parts : (k + 1) * parts] = species[q]
    mixed = jnp.dot(gathered[...], w_ref[0], preferred_element_type=f32)
    inv = 1.0 / jnp.sum(total, axis=0, keepdims=True)
    inv_ref[0] = inv
    out_ref[0] = react(mixed * inv, kelvin_ref[0], factor_ref[...], onset_ref[...])


def last_step(
    near_ref,
    bin_ref,
    used_ref,
    s0,
    s1,
    s2,
    s3,
    s4,
    w_ref,
    inv_ref,
    kelvin_ref,
    factor_ref,
    onset_ref,
    out_ref,
    species,
    gathered,
    sem,
):
    s = pl.program_id(0)
    neighbours = near_ref.shape[0] // OWN
    parts = species.shape[2]

    @pl.when(s == 0)
    def _():
        for copy in load_species((s0, s1, s2, s3, s4), species, sem):
            copy.wait()

    @pl.when(used_ref[s] == 0)
    def _():
        out_ref[...] = jnp.zeros_like(out_ref)

    @pl.when(used_ref[s] != 0)
    def _():
        b = bin_ref[s]
        for k in range(neighbours):
            q = near_ref[b * neighbours + k]
            gathered[:, k * parts : (k + 1) * parts] = species[q]
        mixed = jnp.dot(gathered[...], w_ref[0], preferred_element_type=f32)
        out_ref[0] = react(mixed * inv_ref[0], kelvin_ref[0], factor_ref[...], onset_ref[...])


def body(
    solute_load,
    walker_displacement,
    local_kelvin,
    couple_kinetic_factor,
    arrhenius_onset,
    adjacent_cell_keys,
    downstream_zone,
):
    lane_count = lax.axis_size("gy")
    bins, kinds, parts = solute_load.shape
    neighbours = adjacent_cell_keys.shape[1]
    meta = jnp.stack(
        [
            lax.axis_index("gx") * BX,
            lax.axis_index("gy") * BY,
            jnp.int32(lax.axis_size("gx") * BX),
            jnp.int32(lane_count * BY),
        ]
    ).astype(jnp.int32)
    ids = jnp.arange(bins, dtype=jnp.int32)
    near = slot_of(
        (ids // BY)[:, None] + adjacent_cell_keys // WIDTH - HALO,
        (ids % BY)[:, None] + adjacent_cell_keys % WIDTH - HALO,
    ).reshape(-1)
    kelvin = local_kelvin.reshape(bins, 1, parts)
    factor = couple_kinetic_factor.reshape(-1, 1)
    onset = arrhenius_onset.reshape(-1, 1)

    anywhere = pl.BlockSpec(memory_space=pl.ANY)
    whole = lambda shape: pl.BlockSpec(shape, lambda *_: (0,) * len(shape))
    scratch = [
        pltpu.VMEM((EXT, kinds, parts), bf16),
        pltpu.VMEM((kinds, neighbours * parts), bf16),
        pltpu.SemaphoreType.DMA((5,)),
    ]
    positions = exchange(walker_displacement)
    species = exchange(solute_load)
    moved, weights, inv = pl.pallas_call(
        first_step,
        out_shape=(
            jax.ShapeDtypeStruct((bins, kinds, parts), bf16),
            jax.ShapeDtypeStruct((bins, neighbours * parts, parts), bf16),
            jax.ShapeDtypeStruct((bins, 1, parts), f32),
        ),
        grid_spec=pltpu.PrefetchScalarGridSpec(
            num_scalar_prefetch=2,
            grid=(bins,),
            in_specs=[whole(p.shape) for p in positions]
            + [anywhere] * 5
            + [
                pl.BlockSpec((1, 1, parts), lambda b, *_: (b, 0, 0)),
                whole(factor.shape),
                whole(onset.shape),
            ],
            out_specs=(
                pl.BlockSpec((1, kinds, parts), lambda b, *_: (b, 0, 0)),
                pl.BlockSpec((1, neighbours * parts, parts), lambda b, *_: (b, 0, 0)),
                pl.BlockSpec((1, 1, parts), lambda b, *_: (b, 0, 0)),
            ),
            scratch_shapes=[
                pltpu.VMEM((EXT, parts, FEATURES), bf16),
                pltpu.VMEM((bins, FEATURES, parts), bf16),
            ]
            + scratch,
        ),
        name="first_step",
    )(near, meta, *positions, *species, kelvin, factor, onset)

    target = downstream_zone[:, 0]
    earlier = (target[None, :] == target[:, None]) & (ids[None, :] < ids[:, None])
    slot_of_bin = target * CAP + jnp.sum(earlier.astype(jnp.int32), axis=1)
    slots = lane_count * CAP
    hit = slot_of_bin[None, :] == jnp.arange(slots, dtype=jnp.int32)[:, None]
    bin_of_slot = jnp.sum(jnp.where(hit, ids[None, :], 0), axis=1)
    used = jnp.sum(hit.astype(jnp.int32), axis=1)

    species = exchange(moved)
    by_bin = lambda s, near, bin_of, used: (bin_of[s], 0, 0)
    packed = pl.pallas_call(
        last_step,
        out_shape=jax.ShapeDtypeStruct((slots, kinds, parts), bf16),
        grid_spec=pltpu.PrefetchScalarGridSpec(
            num_scalar_prefetch=3,
            grid=(slots,),
            in_specs=[anywhere] * 5
            + [
                pl.BlockSpec((1, neighbours * parts, parts), by_bin),
                pl.BlockSpec((1, 1, parts), by_bin),
                pl.BlockSpec((1, 1, parts), by_bin),
                whole(factor.shape),
                whole(onset.shape),
            ],
            out_specs=pl.BlockSpec((1, kinds, parts), lambda s, *_: (s, 0, 0)),
            scratch_shapes=scratch,
        ),
        name="last_step",
    )(near, bin_of_slot, used, *species, weights, inv, kelvin, factor, onset)
    return lax.all_to_all(packed, "gy", split_axis=0, concat_axis=0, tiled=True)


def solution(mesh):
    in_specs = (
        P(("gx", "gy"), None, None),
        P(("gx", "gy"), None, None),
        P(("gx", "gy"), None),
        P(),
        P(),
        P(("gx", "gy"), None),
        P(("gx", "gy"), None),
    )
    out_specs = P(("gx", "gy"), None, None)
    return jax.shard_map(body, mesh=mesh, in_specs=in_specs, out_specs=out_specs, check_vma=False)
```

time: 263 us -> 139 us (0.53)
  other arithmetic: 99.6 us -> 6.35 us
  Pallas kernels: 0 us -> 52 us
  matrix products: 48.3 us -> 0 us
  local copies, waits for them, and re-layouts: 30.2 us -> 10.4 us
  waiting for transfers between devices: 26 us -> 16.6 us
  blocking collectives: 19.8 us -> 16.4 us
    pallas_call x0 -> x2, Pallas kernels: none -> 52 us  [the longest x1 30.2 us: body(): pl.pallas_call(first_step, out_shape=(jax.ShapeDtypeStruct((bins, kinds,...]
    dot_general x9 -> x0, matrix products: 48.3 us -> none  [the longest x8 48 us: apply_weights(): jnp.einsum('gksq,gkpq->gsp', sources, weights, preferred_element_type=jnp...]
    dynamic_update_slice x12 -> x0, other arithmetic: 47.3 us -> none  [the longest x4 47.2 us: body(): lax.map(build_one, grouped((centre, neighbour_idx, adjacent_cell_keys, in...]
    reduce_sum x5 -> x2, other arithmetic: 40.5 us -> 1.62 us  [the longest x1 0.91 us: body(): slot_of_bin = target * CAP + jnp.sum(earlier.astype(jnp.int32), axis=1)]
    gather x16 -> x0, local copies, waits for them, and re-layouts: 23.3 us -> none  [the longest x8 18.2 us: apply_weights(): sources = ext_species[neighbour_idx]]
    ppermute x12, waiting for transfers between devices: 26 us -> 16.6 us  [the longest x3 9.02 us: exchange(): left = lax.ppermute(grid[:, BY - HALO:], 'gy', forward)]
    concatenate x21 -> x3, other arithmetic: 6.4 us -> 2.64 us  [exchange(): rows = jnp.concatenate([left, grid, right], axis=1)]
    all_to_all x1, blocking collectives: 19.8 us -> 16.4 us  [body(): return lax.all_to_all(packed, 'gy', split_axis=0, concat_axis=0, tiled=True)]
  transfers between devices with their start and end apart: 12 -> 12, of which waited for: 4 -> 4; matrix products, arithmetic and copies ran while one was open for 39% -> 8% of each run, Pallas kernels for 0% -> 0%
where the time goes in v1:
time: 139 us; the launch traced here: 138 us
  Pallas kernels  52 us (37%)
  starting transfers between devices  36.2 us (26%)
  waiting for transfers between devices  16.6 us (12%)
  blocking collectives  16.4 us (12%)
  local copies, waits for them, and re-layouts  10.4 us (7%)
  other arithmetic  6.35 us (5%)
    pallas_call x1, Pallas kernels, body(): pl.pallas_call(first_step, out_shape=(jax.ShapeDtypeStruct((bins, kinds,...  30.2 us
    pallas_call x1, Pallas kernels, body(): pl.pallas_call(last_step, out_shape=jax.ShapeDtypeStruct((slots, kinds, p...  21.8 us
    all_to_all x1, blocking collectives, body(): return lax.all_to_all(packed, 'gy', split_axis=0, concat_axis=0, tiled=True)  16.4 us
    ppermute x3, starting transfers between devices, exchange(): up = lax.ppermute(rows[BX - HALO:], 'gx', forward)  14.5 us
    ppermute x3, starting transfers between devices, exchange(): left = lax.ppermute(grid[:, BY - HALO:], 'gy', forward)  12 us
    ppermute x3, waiting for transfers between devices, exchange(): left = lax.ppermute(grid[:, BY - HALO:], 'gy', forward)  9.02 us
    ppermute x3, starting transfers between devices, exchange(): down = lax.ppermute(rows[:HALO], 'gx', backward)  5.76 us
    ppermute x3, waiting for transfers between devices, exchange(): down = lax.ppermute(rows[:HALO], 'gx', backward)  4.4 us
  transfers between devices with their start and end apart: 12, of which 4 were waited for; matrix products, arithmetic and copies ran while one was open for 8% of the time, Pallas kernels for 0%

profile of v1, /device:TPU:1, one launch (start us, length us, event | category | flops | bytes accessed | tf_op | source)
XLA Modules:
  0.0 138.3 jit_solution(18431520270445471924)
XLA Ops:
  1.1 3.9 %collective-permute-start.4 = (bf16[4,2,64,256]{3,2,1,0:T(8,128)(2,1)S(1)}, bf16[4,2,64,256]{3,2,1,0:T(8,128)(2,1)S(1)}, u32[]{:S(2)}, u32[]{:S(2)}) collective-permute-start(bf16[4,2,64,256]{3,2,1,0:T(8,128)(2,1)S(1)} %get-tuple-element.20), channel_id=1, source_target_pairs={{0,1},{1,2},{2,3},{3,4},{4,5},{5,6},{6,7},{8,9},{9,10},{10,11},{11... | collective-permute-start | bytes 786440 | tf_op jit(solution)/shard_map/ppermute | solution.py:44
  5.0 1.3 collective-permute-start.5
  7.2 4.0 %collective-permute-start = (f32[4,2,3,256]{3,2,1,0:T(4,128)S(1)}, f32[4,2,3,256]{3,2,1,0:T(4,128)S(1)}, u32[]{:S(2)}, u32[]{:S(2)}) collective-permute-start(f32[4,2,3,256]{3,2,1,0:T(4,128)S(1)} %get-tuple-element.24), channel_id=1, source_target_pairs={{0,1},{1,2},{2,3},{3,4},{4,5},{5,6},{6,7},{8,9},{9,10},{10,11},{11... | collective-permute-start | bytes 73736 | tf_op jit(solution)/shard_map/ppermute | solution.py:44
  11.2 1.3 collective-permute-start.1
  12.5 1.3 collective-permute-done.5
  13.8 1.3 pad_maximum_fusion
  15.2 7.2 %collective-permute-start.6 = (bf16[2,8,64,256]{3,2,1,0:T(8,128)(2,1)S(1)}, bf16[2,8,64,256]{3,2,1,0:T(8,128)(2,1)S(1)}, u32[]{:S(2)}, u32[]{:S(2)}) collective-permute-start(bf16[2,8,64,256]{3,2,1,0:T(8,128)(2,1)S(1)} %get-tuple-element.16), channel_id=1, source_target_pairs={{0,8},{8,16},{16,24},{1,9},{9,17},{17,25},{2,10},{10,18},{18,26},{... | collective-permute-start | bytes 1572872 | tf_op jit(solution)/shard_map/ppermute | solution.py:48
  22.4 1.9 %collective-permute-start.7 = (bf16[2,8,64,256]{3,2,1,0:T(8,128)(2,1)S(1)}, bf16[2,8,64,256]{3,2,1,0:T(8,128)(2,1)S(1)}, u32[]{:S(2)}, u32[]{:S(2)}) collective-permute-start(bf16[2,8,64,256]{3,2,1,0:T(8,128)(2,1)S(1)} %get-tuple-element.15), channel_id=1, source_target_pairs={{8,0},{16,8},{24,16},{9,1},{17,9},{25,17},{10,2},{18,10},{26,18},{... | collective-permute-start | bytes 1572872 | tf_op jit(solution)/shard_map/ppermute | solution.py:49
  25.2 3.6 %collective-permute-start.2 = (f32[2,8,3,256]{3,2,1,0:T(4,128)S(1)}, f32[2,8,3,256]{3,2,1,0:T(4,128)S(1)}, u32[]{:S(2)}, u32[]{:S(2)}) collective-permute-start(f32[2,8,3,256]{3,2,1,0:T(4,128)S(1)} %get-tuple-element.22), channel_id=1, source_target_pairs={{0,8},{8,16},{16,24},{1,9},{9,17},{17,25},{2,10},{10,18},{18,26},{... | collective-permute-start | bytes 147464 | tf_op jit(solution)/shard_map/ppermute | solution.py:48
  28.9 1.9 %collective-permute-start.3 = (f32[2,8,3,256]{3,2,1,0:T(4,128)S(1)}, f32[2,8,3,256]{3,2,1,0:T(4,128)S(1)}, u32[]{:S(2)}, u32[]{:S(2)}) collective-permute-start(f32[2,8,3,256]{3,2,1,0:T(4,128)S(1)} %get-tuple-element.21), channel_id=1, source_target_pairs={{8,0},{16,8},{24,16},{9,1},{17,9},{25,17},{10,2},{18,10},{26,18},{... | collective-permute-start | bytes 147464 | tf_op jit(solution)/shard_map/ppermute | solution.py:49
  32.1 1.3 copy.20.factor_ref
  33.4 1.3 copy.21.onset_ref
  34.8 1.3 reshape.99.kelvin_ref
  37.1 30.2 %first_step.1 = (bf16[16,64,256]{2,1,0:T(8,128)(2,1)}, bf16[16,4096,256]{2,1,0:T(8,128)(2,1)}, f32[16,1,256]{2,1,0:T(1,128)}) custom-call(s32[256]{0:T(256)} %reshape.88.near_ref, s32[4]{0:T(128)} %pad_add_fusion.meta_ref, f32[16,3,256]{2,1,0:T(4,128)} %copy-done.2, f32[8,3,256]{2,1,0:T(4,128)} %bitcast.35, f32[8,3,256]{2,1,0:T(4,128)} %bitcast.36, ...), custom_call_target="tpu_custom_call" | custom-call | tf_op jit(solution)/shard_map/first_step/pallas_call | solution.py:304
  68.4 4.1 %collective-permute-start.8 = (bf16[4,2,64,256]{3,2,1,0:T(8,128)(2,1)S(1)}, bf16[4,2,64,256]{3,2,1,0:T(8,128)(2,1)S(1)}, u32[]{:S(2)}, u32[]{:S(2)}) collective-permute-start(bf16[4,2,64,256]{3,2,1,0:T(8,128)(2,1)S(1)} %get-tuple-element.18), channel_id=1, source_target_pairs={{0,1},{1,2},{2,3},{3,4},{4,5},{5,6},{6,7},{8,9},{9,10},{10,11},{11... | collective-permute-start | bytes 786440 | tf_op jit(solution)/shard_map/ppermute | solution.py:44
  72.5 1.3 collective-permute-start.9
  73.8 9.0 %collective-permute-done.8 = bf16[4,2,64,256]{3,2,1,0:T(8,128)(2,1)S(1)} collective-permute-done((bf16[4,2,64,256]{3,2,1,0:T(8,128)(2,1)S(1)}, bf16[4,2,64,256]{3,2,1,0:T(8,128)(2,1)S(1)}, u32[]{:S(2)}, u32[]{:S(2)}) %collective-permute-start.8) | collective-permute-done | bytes 262176 | tf_op jit(solution)/shard_map/ppermute | solution.py:44
  82.8 1.3 pad_maximum_fusion.1
  84.3 3.7 %collective-permute-start.10 = (bf16[2,8,64,256]{3,2,1,0:T(8,128)(2,1)S(1)}, bf16[2,8,64,256]{3,2,1,0:T(8,128)(2,1)S(1)}, u32[]{:S(2)}, u32[]{:S(2)}) collective-permute-start(bf16[2,8,64,256]{3,2,1,0:T(8,128)(2,1)S(1)} %get-tuple-element.14), channel_id=1, source_target_pairs={{0,8},{8,16},{16,24},{1,9},{9,17},{17,25},{2,10},{10,18},{18,26},{... | collective-permute-start | bytes 1572872 | tf_op jit(solution)/shard_map/ppermute | solution.py:48
  88.0 1.9 %collective-permute-start.11 = (bf16[2,8,64,256]{3,2,1,0:T(8,128)(2,1)S(1)}, bf16[2,8,64,256]{3,2,1,0:T(8,128)(2,1)S(1)}, u32[]{:S(2)}, u32[]{:S(2)}) collective-permute-start(bf16[2,8,64,256]{3,2,1,0:T(8,128)(2,1)S(1)} %get-tuple-element.13), channel_id=1, source_target_pairs={{8,0},{16,8},{24,16},{9,1},{17,9},{25,17},{10,2},{18,10},{26,18},{... | collective-permute-start | bytes 1572872 | tf_op jit(solution)/shard_map/ppermute | solution.py:49
  92.2 1.9 %collective-permute-done.10 = bf16[2,8,64,256]{3,2,1,0:T(8,128)(2,1)S(1)} collective-permute-done((bf16[2,8,64,256]{3,2,1,0:T(8,128)(2,1)S(1)}, bf16[2,8,64,256]{3,2,1,0:T(8,128)(2,1)S(1)}, u32[]{:S(2)}, u32[]{:S(2)}) %collective-permute-start.10) | collective-permute-done | bytes 524320 | tf_op jit(solution)/shard_map/ppermute | solution.py:48
  94.1 4.4 %collective-permute-done.11 = bf16[2,8,64,256]{3,2,1,0:T(8,128)(2,1)S(1)} collective-permute-done((bf16[2,8,64,256]{3,2,1,0:T(8,128)(2,1)S(1)}, bf16[2,8,64,256]{3,2,1,0:T(8,128)(2,1)S(1)}, u32[]{:S(2)}, u32[]{:S(2)}) %collective-permute-start.11) | collective-permute-done | bytes 524320 | tf_op jit(solution)/shard_map/ppermute | solution.py:49
  99.3 21.8 %last_step.1 = bf16[16,64,256]{2,1,0:T(8,128)(2,1)} custom-call(s32[256]{0:T(256)} %reshape.88.near_ref, s32[16]{0:T(128)} %get-tuple-element.12.bin_ref, s32[16]{0:T(128)} %get-tuple-element.11.used_ref, bf16[16,64,256]{2,1,0:T(8,128)(2,1)} %get-tuple-element.8.s0, bf16[8,64,256]{2,1,0:T(8,128)(2,1)} %bitcast.25, bf16[8,64,256]{2,1,0:T(8,128)(2,1)} %bitcast.26, ...), custom_call_target="tpu_custom_call" | custom-call | tf_op jit(solution)/shard_map/last_step/pallas_call | solution.py:345
  121.1 16.4 %all_to_all.5 = bf16[16,64,256]{2,1,0:T(8,128)(2,1)S(1)} all-to-all(bf16[16,64,256]{2,1,0:T(8,128)(2,1)} %last_step.1), channel_id=1, replica_groups=mesh['gx'=4,'gy'=8] {'gy'}, dimensions={0} | all-to-all | bytes 1048576 | tf_op jit(solution)/shard_map/all_to_all | solution.py:364
  (50 shorter events, 10.2 us)
Async XLA Ops:
  1.1 11.4 %collective-permute-start.4 = (bf16[4,2,64,256]{3,2,1,0:T(8,128)(2,1)S(1)}, bf16[4,2,64,256]{3,2,1,0:T(8,128)(2,1)S(1)}, u32[]{:S(2)}, u32[]{:S(2)}) collective-permute-start(bf16[4,2,64,256]{3,2,1,0:T(8,128)(2,1)S(1)} %get-tuple-element.20), channel_id=1, source_target_pairs={{0,1},{1,2},{2,3},{3,4},{4,5},{5,6},{6,7},{8,9},{9,10},{10,11},{11... | collective-permute-start | bytes 786440 | tf_op jit(solution)/shard_map/ppermute | solution.py:44
  5.0 8.8 %collective-permute-start.5 = (bf16[4,2,64,256]{3,2,1,0:T(8,128)(2,1)S(1)}, bf16[4,2,64,256]{3,2,1,0:T(8,128)(2,1)S(1)}, u32[]{:S(2)}, u32[]{:S(2)}) collective-permute-start(bf16[4,2,64,256]{3,2,1,0:T(8,128)(2,1)S(1)} %get-tuple-element.19), channel_id=1, source_target_pairs={{1,0},{2,1},{3,2},{4,3},{5,4},{6,5},{7,6},{9,8},{10,9},{11,10},{12... | collective-permute-start | bytes 786440 | tf_op jit(solution)/shard_map/ppermute | solution.py:45
  7.2 29.0 %copy-start.2 = (f32[16,3,256]{2,1,0:T(4,128)}, f32[16,3,256]{2,1,0:T(4,128)S(1)}, u32[]{:S(2)}) copy-start(f32[16,3,256]{2,1,0:T(4,128)S(1)} %copy.19.p0) | copy-start | bytes 147460
  7.2 17.9 %collective-permute-start = (f32[4,2,3,256]{3,2,1,0:T(4,128)S(1)}, f32[4,2,3,256]{3,2,1,0:T(4,128)S(1)}, u32[]{:S(2)}, u32[]{:S(2)}) collective-permute-start(f32[4,2,3,256]{3,2,1,0:T(4,128)S(1)} %get-tuple-element.24), channel_id=1, source_target_pairs={{0,1},{1,2},{2,3},{3,4},{4,5},{5,6},{6,7},{8,9},{9,10},{10,11},{11... | collective-permute-start | bytes 73736 | tf_op jit(solution)/shard_map/ppermute | solution.py:44
  11.2 13.9 %collective-permute-start.1 = (f32[4,2,3,256]{3,2,1,0:T(4,128)S(1)}, f32[4,2,3,256]{3,2,1,0:T(4,128)S(1)}, u32[]{:S(2)}, u32[]{:S(2)}) collective-permute-start(f32[4,2,3,256]{3,2,1,0:T(4,128)S(1)} %get-tuple-element.23), channel_id=1, source_target_pairs={{1,0},{2,1},{3,2},{4,3},{5,4},{6,5},{7,6},{9,8},{10,9},{11,10},{12... | collective-permute-start | bytes 73736 | tf_op jit(solution)/shard_map/ppermute | solution.py:45
  12.5 23.7 %copy-start.3 = (bf16[4,2,64,256]{3,2,1,0:T(8,128)(2,1)}, bf16[4,2,64,256]{3,2,1,0:T(8,128)(2,1)S(1)}, u32[]{:S(2)}) copy-start(bf16[4,2,64,256]{3,2,1,0:T(8,128)(2,1)S(1)} %collective-permute-done.4) | copy-start | bytes 786436
  13.8 22.4 %copy-start.4 = (bf16[4,2,64,256]{3,2,1,0:T(8,128)(2,1)}, bf16[4,2,64,256]{3,2,1,0:T(8,128)(2,1)S(1)}, u32[]{:S(2)}) copy-start(bf16[4,2,64,256]{3,2,1,0:T(8,128)(2,1)S(1)} %collective-permute-done.5) | copy-start | bytes 786436
  15.2 20.9 %collective-permute-start.6 = (bf16[2,8,64,256]{3,2,1,0:T(8,128)(2,1)S(1)}, bf16[2,8,64,256]{3,2,1,0:T(8,128)(2,1)S(1)}, u32[]{:S(2)}, u32[]{:S(2)}) collective-permute-start(bf16[2,8,64,256]{3,2,1,0:T(8,128)(2,1)S(1)} %get-tuple-element.16), channel_id=1, source_target_pairs={{0,8},{8,16},{16,24},{1,9},{9,17},{17,25},{2,10},{10,18},{18,26},{... | collective-permute-start | bytes 1572872 | tf_op jit(solution)/shard_map/ppermute | solution.py:48
  22.4 13.8 %collective-permute-start.7 = (bf16[2,8,64,256]{3,2,1,0:T(8,128)(2,1)S(1)}, bf16[2,8,64,256]{3,2,1,0:T(8,128)(2,1)S(1)}, u32[]{:S(2)}, u32[]{:S(2)}) collective-permute-start(bf16[2,8,64,256]{3,2,1,0:T(8,128)(2,1)S(1)} %get-tuple-element.15), channel_id=1, source_target_pairs={{8,0},{16,8},{24,16},{9,1},{17,9},{25,17},{10,2},{18,10},{26,18},{... | collective-permute-start | bytes 1572872 | tf_op jit(solution)/shard_map/ppermute | solution.py:49
  25.1 11.1 %copy-start.9 = (f32[4,2,3,256]{3,2,1,0:T(4,128)}, f32[4,2,3,256]{3,2,1,0:T(4,128)S(1)}, u32[]{:S(2)}) copy-start(f32[4,2,3,256]{3,2,1,0:T(4,128)S(1)} %collective-permute-done) | copy-start | bytes 73732
  25.1 11.1 %copy-start.10 = (f32[4,2,3,256]{3,2,1,0:T(4,128)}, f32[4,2,3,256]{3,2,1,0:T(4,128)S(1)}, u32[]{:S(2)}) copy-start(f32[4,2,3,256]{3,2,1,0:T(4,128)S(1)} %collective-permute-done.1) | copy-start | bytes 73732
  25.2 10.9 %collective-permute-start.2 = (f32[2,8,3,256]{3,2,1,0:T(4,128)S(1)}, f32[2,8,3,256]{3,2,1,0:T(4,128)S(1)}, u32[]{:S(2)}, u32[]{:S(2)}) collective-permute-start(f32[2,8,3,256]{3,2,1,0:T(4,128)S(1)} %get-tuple-element.22), channel_id=1, source_target_pairs={{0,8},{8,16},{16,24},{1,9},{9,17},{17,25},{2,10},{10,18},{18,26},{... | collective-permute-start | bytes 147464 | tf_op jit(solution)/shard_map/ppermute | solution.py:48
  28.9 7.3 %collective-permute-start.3 = (f32[2,8,3,256]{3,2,1,0:T(4,128)S(1)}, f32[2,8,3,256]{3,2,1,0:T(4,128)S(1)}, u32[]{:S(2)}, u32[]{:S(2)}) collective-permute-start(f32[2,8,3,256]{3,2,1,0:T(4,128)S(1)} %get-tuple-element.21), channel_id=1, source_target_pairs={{8,0},{16,8},{24,16},{9,1},{17,9},{25,17},{10,2},{18,10},{26,18},{... | collective-permute-start | bytes 147464 | tf_op jit(solution)/shard_map/ppermute | solution.py:49
  36.1 0.6 copy-start.12
  36.1 0.8 copy-start.7
  36.2 1.0 copy-start.8
  68.4 14.4 %collective-permute-start.8 = (bf16[4,2,64,256]{3,2,1,0:T(8,128)(2,1)S(1)}, bf16[4,2,64,256]{3,2,1,0:T(8,128)(2,1)S(1)}, u32[]{:S(2)}, u32[]{:S(2)}) collective-permute-start(bf16[4,2,64,256]{3,2,1,0:T(8,128)(2,1)S(1)} %get-tuple-element.18), channel_id=1, source_target_pairs={{0,1},{1,2},{2,3},{3,4},{4,5},{5,6},{6,7},{8,9},{9,10},{10,11},{11... | collective-permute-start | bytes 786440 | tf_op jit(solution)/shard_map/ppermute | solution.py:44
  72.5 10.3 %collective-permute-start.9 = (bf16[4,2,64,256]{3,2,1,0:T(8,128)(2,1)S(1)}, bf16[4,2,64,256]{3,2,1,0:T(8,128)(2,1)S(1)}, u32[]{:S(2)}, u32[]{:S(2)}) collective-permute-start(bf16[4,2,64,256]{3,2,1,0:T(8,128)(2,1)S(1)} %get-tuple-element.17), channel_id=1, source_target_pairs={{1,0},{2,1},{3,2},{4,3},{5,4},{6,5},{7,6},{9,8},{10,9},{11,10},{12... | collective-permute-start | bytes 786440 | tf_op jit(solution)/shard_map/ppermute | solution.py:45
  82.8 15.7 %copy-start = (bf16[4,2,64,256]{3,2,1,0:T(8,128)(2,1)}, bf16[4,2,64,256]{3,2,1,0:T(8,128)(2,1)S(1)}, u32[]{:S(2)}) copy-start(bf16[4,2,64,256]{3,2,1,0:T(8,128)(2,1)S(1)} %collective-permute-done.8) | copy-start | bytes 786436
  82.8 15.7 %copy-start.1 = (bf16[4,2,64,256]{3,2,1,0:T(8,128)(2,1)}, bf16[4,2,64,256]{3,2,1,0:T(8,128)(2,1)S(1)}, u32[]{:S(2)}) copy-start(bf16[4,2,64,256]{3,2,1,0:T(8,128)(2,1)S(1)} %collective-permute-done.9) | copy-start | bytes 786436
  84.3 9.8 %collective-permute-start.10 = (bf16[2,8,64,256]{3,2,1,0:T(8,128)(2,1)S(1)}, bf16[2,8,64,256]{3,2,1,0:T(8,128)(2,1)S(1)}, u32[]{:S(2)}, u32[]{:S(2)}) collective-permute-start(bf16[2,8,64,256]{3,2,1,0:T(8,128)(2,1)S(1)} %get-tuple-element.14), channel_id=1, source_target_pairs={{0,8},{8,16},{16,24},{1,9},{9,17},{17,25},{2,10},{10,18},{18,26},{... | collective-permute-start | bytes 1572872 | tf_op jit(solution)/shard_map/ppermute | solution.py:48
  88.0 10.5 %collective-permute-start.11 = (bf16[2,8,64,256]{3,2,1,0:T(8,128)(2,1)S(1)}, bf16[2,8,64,256]{3,2,1,0:T(8,128)(2,1)S(1)}, u32[]{:S(2)}, u32[]{:S(2)}) collective-permute-start(bf16[2,8,64,256]{3,2,1,0:T(8,128)(2,1)S(1)} %get-tuple-element.13), channel_id=1, source_target_pairs={{8,0},{16,8},{24,16},{9,1},{17,9},{25,17},{10,2},{18,10},{26,18},{... | collective-permute-start | bytes 1572872 | tf_op jit(solution)/shard_map/ppermute | solution.py:49
  94.1 4.4 %copy-start.5 = (bf16[2,8,64,256]{3,2,1,0:T(8,128)(2,1)}, bf16[2,8,64,256]{3,2,1,0:T(8,128)(2,1)S(1)}, u32[]{:S(2)}) copy-start(bf16[2,8,64,256]{3,2,1,0:T(8,128)(2,1)S(1)} %collective-permute-done.10) | copy-start | bytes 1572868
  98.5 0.8 copy-start.6
  (1 other events, 0.6 us)

commit v2 on v0

v2 whole, which is shorter than its diff:
```python
import math

import jax
import jax.numpy as jnp
from jax import lax
from jax.experimental import pallas as pl
from jax.experimental.pallas import tpu as pltpu
from jax.sharding import PartitionSpec as P


BX = 4
BY = 4
CAP = 2
HALO = 2
WIDTH = 2 * HALO + 1

inverse_width = 4.0
SCALE = math.sqrt(inverse_width * math.log2(math.e))
FAR = -1e30
FEATURES = 48

f32 = jnp.float32
bf16 = jnp.bfloat16
i32 = jnp.int32

SIDE = BX * HALO
QUAD = HALO * HALO
BAND = 4 * QUAD
EXT = 4 * SIDE + 2 * BAND
COUNTS = (SIDE, SIDE, SIDE, SIDE, BAND, BAND)
STARTS = (0, SIDE, 2 * SIDE, 3 * SIDE, 4 * SIDE, 4 * SIDE + BAND)


def swaps(count):
    def both(first):
        out = []
        for i in range(first, count - 1, 2):
            out += [(i, i + 1), (i + 1, i)]
        return out

    return both(0), both(1)


def slot_of(ex, ey, odd_lane, odd_band):
    low = ey < BY // 2
    by_a = low == (odd_lane == 1)
    own = (ey >= 0) & (ey < BY)
    piece = jnp.where(by_a, 0, 1) + jnp.where(own, 0, 2)
    column = (ey + HALO) % HALO
    inner = piece * SIDE + ex * HALO + column
    from_a = (ex < 0) == (odd_band == 1)
    row = jnp.where(ex < 0, ex + HALO, ex - BX)
    outer = jnp.where(from_a, STARTS[4], STARTS[5]) + piece * QUAD + row * HALO + column
    return jnp.where((ex >= 0) & (ex < BX), inner, outer)


def place_of(piece, i, odd_lane, odd_band):
    if piece < 4:
        part, ex = piece, i // HALO
    else:
        part, row = i // QUAD, i % QUAD // HALO
        up = (odd_band == 1) if piece == 4 else (odd_band == 0)
        ex = jnp.where(up, row - HALO, row + BX)
    by_a = part % 2 == 0
    low = (by_a == (odd_lane == 1)) if not isinstance(by_a, bool) else (odd_lane == int(by_a))
    outside = part >= 2
    base = jnp.where(low, jnp.where(outside, -HALO, 0), jnp.where(outside, BY, BY - HALO))
    return ex, base + i % HALO


def split(meta_ref, zone_ref, x0, x1, a0, b0, a1, b1, row_ref, taken):
    sources, outs = (x0, x1), (a0, b0, a1, b1)
    for z in range(taken.shape[0]):
        taken[z] = 0

    def place(b, _):
        zone = zone_ref[b, 0]
        order = taken[zone]
        taken[zone] = order + 1
        row_ref[b] = zone * CAP + order
        return 0

    lax.fori_loop(0, BX * BY, place, 0)
    low_a = jnp.where(meta_ref[4] == 1, 0, BY - HALO)
    for n, x in enumerate(sources):
        for r in range(BX):
            outs[2 * n][pl.ds(r * HALO, HALO)] = x[pl.ds(r * BY + low_a, HALO)]
            outs[2 * n + 1][pl.ds(r * HALO, HALO)] = x[pl.ds(r * BY + BY - HALO - low_a, HALO)]


def pack(meta_ref, p0, p1, p2, p3, out_a, out_b):
    size = BX * HALO
    from_a = jnp.where(meta_ref[5] == 1, 0, size - QUAD)
    for n, x in enumerate((p0, p1, p2, p3)):
        out_a[pl.ds(n * QUAD, QUAD)] = x[pl.ds(from_a, QUAD)]
        out_b[pl.ds(n * QUAD, QUAD)] = x[pl.ds(size - QUAD - from_a, QUAD)]


def swap(by_a, by_b, axis):
    pairs_a, pairs_b = swaps(lax.axis_size(axis))
    from_b = lax.ppermute(by_b, axis, pairs_b)
    from_a = lax.ppermute(by_a, axis, pairs_a)
    return from_a, from_b


def three_parts(x):
    high = x.astype(bf16).astype(f32)
    rest = x - high
    middle = rest.astype(bf16).astype(f32)
    return high, middle, rest - middle


def coordinates(pos, ex, ey):
    row = lax.broadcasted_iota(i32, (8, pos.shape[-1]), 0)
    padded = jnp.concatenate([pos, jnp.zeros((5, pos.shape[-1]), f32)], axis=0)
    middle = jnp.where(
        row == 0,
        ex.astype(f32) - (BX - 1) / 2,
        jnp.where(row == 1, ey.astype(f32) - (BY - 1) / 2, 0.0),
    )
    return (padded + middle) * SCALE, row


def features(pos, ex, ey, inside, as_target):
    x, row = coordinates(pos, ex, ey)
    norm = jnp.sum(x * x, axis=0, keepdims=True)
    high, middle, low = three_parts(x)
    nh, nm, nl = three_parts(norm)
    last = row == 3
    pick = lambda a, b: jnp.where(last, a, b)
    source = (
        pick(jnp.where(inside, -nh, FAR), high),
        pick(-nm, high),
        pick(-nl, middle),
        pick(1.0, high),
        pick(1.0, low),
        pick(1.0, middle),
    )
    source = jnp.concatenate(source, axis=0).T.astype(bf16)
    if not as_target:
        return source, None
    high, middle, low = 2.0 * high, 2.0 * middle, 2.0 * low
    target = (
        pick(1.0, high),
        pick(1.0, middle),
        pick(1.0, high),
        pick(-nh, low),
        pick(-nm, high),
        pick(-nl, middle),
    )
    return source, jnp.concatenate(target, axis=0).astype(bf16)


def build_rows(near_ref, source, target, w_refs, inv_ref, first_row):
    parts = source.shape[1]
    neighbours = near_ref.shape[0] // (BX * BY)
    for g, w_ref in enumerate(w_refs):

        def one(c, _, g=g, w_ref=w_ref):
            b = (first_row + g) * BY + c
            f = target[b]
            total = jnp.zeros((8, parts), f32)
            for k in range(neighbours):
                q = near_ref[b * neighbours + k]
                w = jnp.exp2(jnp.dot(source[q], f, preferred_element_type=f32))
                total = total + w.reshape(parts // 8, 8, parts).sum(0)
                w_ref[c, pl.ds(k * parts, parts)] = w.astype(bf16)
            inv_ref[pl.ds(g * BY + c, 1)] = 1.0 / jnp.sum(total, axis=0, keepdims=True)
            return 0

        lax.fori_loop(0, BY, one, 0)


def build_first(near_ref, meta_ref, own, c0, c1, r0, r1, w0, w1, inv_ref, source, target):
    odd_lane, odd_band = meta_ref[4], meta_ref[5]

    def put(pos, ex, ey, slot, as_target):
        gx = meta_ref[0] + ex
        gy = meta_ref[1] + ey
        inside = (gx >= 0) & (gx < meta_ref[2]) & (gy >= 0) & (gy < meta_ref[3])
        s, t = features(pos, ex, ey, inside, as_target)
        source[slot] = s
        return t

    def mine(b, _):
        ex, ey = b // BY, b % BY
        target[b] = put(own[b], ex, ey, slot_of(ex, ey, odd_lane, odd_band), True)
        return 0

    lax.fori_loop(0, BX * BY, mine, 0)
    for piece, ref in ((2, c0), (3, c1), (4, r0), (5, r1)):

        def one(i, _, piece=piece, ref=ref):
            ex, ey = place_of(piece, i, odd_lane, odd_band)
            put(ref[i], ex, ey, STARTS[piece] + i, False)
            return 0

        lax.fori_loop(0, COUNTS[piece], one, 0)
    build_rows(near_ref, source, target, (w0, w1), inv_ref, 0)


def build_second(near_ref, source, target, w2, w3, inv_ref):
    build_rows(near_ref, source, target, (w2, w3), inv_ref, BX // 2)


def column(row_ref):
    n = row_ref.shape[1]
    shape = (n, n)
    same = lax.broadcasted_iota(i32, shape, 0) == lax.broadcasted_iota(i32, shape, 1)
    return jnp.sum(jnp.where(same, row_ref[...], 0.0), axis=1, keepdims=True)


def react(mixture, kelvin, factor, onset):
    half = mixture.shape[0] // 2
    u = mixture[:half]
    v = mixture[half:]
    speed = factor * jnp.exp(-onset / kelvin)
    reacted = speed * u * v / (1.0 + speed * (u + v))
    return jnp.concatenate([u - reacted, v - reacted], axis=0).astype(bf16)


def mix(near_ref, species, gathered, w, b):
    neighbours = near_ref.shape[0] // (BX * BY)
    parts = species.shape[2]
    for k in range(neighbours):
        q = near_ref[b * neighbours + k]
        gathered[:, k * parts : (k + 1) * parts] = species[q]
    return jnp.dot(gathered[...], w, preferred_element_type=f32)


def join(pieces, species):
    for start, count, ref in zip(STARTS, COUNTS, pieces):
        species[pl.ds(start, count)] = ref[...]


def inverse_of(inv_refs, g, c):
    half = BX // 2
    return inv_refs[g // half][pl.ds((g % half) * BY + c, 1)]


def step_columns(near_ref, species, gathered, w_refs, inv_refs, consts, low, out_ref):
    kelvin_ref, factor_ref, onset_ref = consts
    factor, onset = column(factor_ref), column(onset_ref)
    for g, w_ref in enumerate(w_refs):

        def one(i, _, g=g, w_ref=w_ref):
            c = low + i
            b = g * BY + c
            mixed = mix(near_ref, species, gathered, w_ref[c], b)
            mixed = mixed * inverse_of(inv_refs, g, c)
            out_ref[g * HALO + i] = react(mixed, kelvin_ref[pl.ds(b, 1)], factor, onset)
            return 0

        lax.fori_loop(0, HALO, one, 0)


def step_b(near_ref, meta_ref, p0, p1, p2, p3, p4, p5, w0, w1, w2, w3, i0, i1, t, a, o, out, species, gathered):
    join((p0, p1, p2, p3, p4, p5), species)
    low = jnp.where(meta_ref[4] == 1, BY - HALO, 0)
    step_columns(near_ref, species, gathered, (w0, w1, w2, w3), (i0, i1), (t, a, o), low, out)


def step_a(near_ref, meta_ref, species, w0, w1, w2, w3, i0, i1, t, a, o, out, gathered):
    low = jnp.where(meta_ref[4] == 1, 0, BY - HALO)
    step_columns(near_ref, species, gathered, (w0, w1, w2, w3), (i0, i1), (t, a, o), low, out)


def last_step(near_ref, row_ref, p0, p1, p2, p3, p4, p5, w0, w1, w2, w3, i0, i1, t, a, o, out, species, gathered):
    join((p0, p1, p2, p3, p4, p5), species)
    if out.shape[0] > BX * BY:
        out[...] = jnp.zeros_like(out)
    factor, onset = column(a), column(o)
    for g, w_ref in enumerate((w0, w1, w2, w3)):

        def one(c, _, g=g, w_ref=w_ref):
            b = g * BY + c
            mixed = mix(near_ref, species, gathered, w_ref[c], b)
            mixed = mixed * inverse_of((i0, i1), g, c)
            out[row_ref[b]] = react(mixed, t[pl.ds(b, 1)], factor, onset)
            return 0

        lax.fori_loop(0, BY, one, 0)


VM = pl.BlockSpec(memory_space=pltpu.VMEM)
SM = pl.BlockSpec(memory_space=pltpu.SMEM)


def call(kernel, operands, scalars, outs, scratch, flops):
    single = not isinstance(outs, (list, tuple))
    return pl.pallas_call(
        kernel,
        out_shape=outs,
        in_specs=[SM] * scalars + [VM] * (len(operands) - scalars),
        out_specs=VM if single else [SM if o.dtype == i32 else VM for o in outs],
        scratch_shapes=scratch,
        compiler_params=pltpu.CompilerParams(vmem_limit_bytes=8 << 20),
        cost_estimate=pl.CostEstimate(
            flops=flops, bytes_accessed=1 << 20, transcendentals=0
        ),
    )(*operands)


def body(
    solute_load,
    walker_displacement,
    local_kelvin,
    couple_kinetic_factor,
    arrhenius_onset,
    adjacent_cell_keys,
    downstream_zone,
):
    lane_count = lax.axis_size("gy")
    bins, kinds, parts = solute_load.shape
    neighbours = adjacent_cell_keys.shape[1]
    band, lane = lax.axis_index("gx"), lax.axis_index("gy")
    odd_band, odd_lane = band % 2, lane % 2

    meta = jnp.stack(
        [
            band * BX,
            lane * BY,
            jnp.int32(lax.axis_size("gx") * BX),
            jnp.int32(lane_count * BY),
            odd_lane,
            odd_band,
        ]
    ).astype(i32)
    like = lambda x, n: pltpu.VMEM((n,) + x.shape[1:], x.dtype)
    pos_a, pos_b, own_a, own_b, row = call(
        split,
        (meta, downstream_zone, walker_displacement, solute_load),
        2,
        [like(walker_displacement, SIDE)] * 2
        + [like(solute_load, SIDE)] * 2
        + [jax.ShapeDtypeStruct((bins,), i32)],
        [pltpu.SMEM((lane_count,), i32)],
        1 << 20,
    )

    def rows(pieces):
        by_a, by_b = call(pack, (meta,) + pieces, 1, [like(pieces[0], BAND)] * 2, [], 1 << 20)
        return swap(by_a, by_b, "gx")

    pos_sides = swap(pos_a, pos_b, "gy")
    pos_bands = rows((pos_a, pos_b) + pos_sides)
    own = (own_a, own_b)
    sides = swap(own_a, own_b, "gy")
    bands = rows(own + sides)

    ids = jnp.arange(bins, dtype=i32)
    near = slot_of(
        (ids // BY)[:, None] + adjacent_cell_keys // WIDTH - HALO,
        (ids % BY)[:, None] + adjacent_cell_keys % WIDTH - HALO,
        odd_lane,
        odd_band,
    ).reshape(-1)
    consts = (local_kelvin, couple_kinetic_factor[None], arrhenius_onset[None])

    w_row = pltpu.VMEM((BY, neighbours * parts, parts), bf16)
    inv_half = pltpu.VMEM((bins // 2, parts), f32)
    half = pltpu.VMEM((SIDE, kinds, parts), bf16)
    gathered = pltpu.VMEM((kinds, neighbours * parts), bf16)
    all_species = pltpu.VMEM((EXT, kinds, parts), bf16)
    work = 2 * bins * neighbours * parts * parts * 128
    w0, w1, inv0, source, target = call(
        build_first,
        (near, meta, walker_displacement) + pos_sides + pos_bands,
        2,
        [
            w_row,
            w_row,
            inv_half,
            pltpu.VMEM((EXT, parts, FEATURES), bf16),
            pltpu.VMEM((bins, FEATURES, parts), bf16),
        ],
        [],
        work,
    )
    w2, w3, inv1 = call(build_second, (near, source, target), 1, [w_row, w_row, inv_half], [], work)
    built = (w0, w1, w2, w3, inv0, inv1) + consts
    by_b, species = call(
        step_b,
        (near, meta) + own + sides + bands + built,
        2,
        [half, all_species],
        [gathered],
        work // 2,
    )
    by_a = call(step_a, (near, meta, species) + built, 2, half, [gathered], work // 2)

    own = (by_a, by_b)
    sides = swap(by_a, by_b, "gy")
    bands = rows(own + sides)
    packed = call(
        last_step,
        (near, row) + own + sides + bands + built,
        2,
        jax.ShapeDtypeStruct((lane_count * CAP, kinds, parts), bf16),
        [all_species, gathered],
        work,
    )
    return lax.all_to_all(packed, "gy", split_axis=0, concat_axis=0, tiled=True)


def solution(mesh):
    in_specs = (
        P(("gx", "gy"), None, None),
        P(("gx", "gy"), None, None),
        P(("gx", "gy"), None),
        P(),
        P(),
        P(("gx", "gy"), None),
        P(("gx", "gy"), None),
    )
    out_specs = P(("gx", "gy"), None, None)
    return jax.shard_map(body, mesh=mesh, in_specs=in_specs, out_specs=out_specs, check_vma=False)
```

time: 263 us -> 104 us (0.40); the launches traced: 260 us -> 104 us
  other arithmetic: 99.6 us -> 0.79 us
  matrix products: 48.3 us -> 0 us
  Pallas kernels: 0 us -> 41.7 us
  local copies, waits for them, and re-layouts: 30.2 us -> 3.59 us
  starting transfers between devices: 34.9 us -> 23.7 us
  waiting for transfers between devices: 26 us -> 19.3 us
  blocking collectives: 19.8 us -> 14.5 us
    dot_general x9 -> x0, matrix products: 48.3 us -> none  [the longest x8 48 us: apply_weights(): jnp.einsum('gksq,gkpq->gsp', sources, weights, preferred_element_type=jnp...]
    dynamic_update_slice x12 -> x0, other arithmetic: 47.3 us -> none  [the longest x4 47.2 us: body(): lax.map(build_one, grouped((centre, neighbour_idx, adjacent_cell_keys, in...]
    pallas_call x0 -> x9, Pallas kernels: none -> 41.7 us  [call(): pl.pallas_call(kernel, out_shape=outs, in_specs=[SM] * scalars + [VM] * (...]
    reduce_sum x5 -> x0, other arithmetic: 40.5 us -> none  [the longest x4 40.3 us: build_weights(): row_total = jnp.sum(kernel, axis=(1, 3))]
    gather x16 -> x0, local copies, waits for them, and re-layouts: 23.3 us -> none  [the longest x8 18.2 us: apply_weights(): sources = ext_species[neighbour_idx]]
    ppermute x12, starting transfers between devices: 34.9 us -> 23.7 us  [the longest x6 12 us: swap(): from_a = lax.ppermute(by_a, axis, pairs_a)]
    ppermute x12, waiting for transfers between devices: 26 us -> 19.3 us  [the longest x6 12.1 us: swap(): from_a = lax.ppermute(by_a, axis, pairs_a)]
    concatenate x21 -> x0, other arithmetic: 6.4 us -> none  [the longest x5 5.23 us: with_halo(): block = jnp.concatenate([low, block, high], axis=dim)]
  transfers between devices with their start and end apart: 12 -> 12, of which waited for: 4 -> 3; matrix products, arithmetic and copies ran while one was open for 39% -> 1% of each run, Pallas kernels for 0% -> 21%
where the time goes in v2:
time: 104 us
  Pallas kernels  41.7 us (40%)
  starting transfers between devices  23.7 us (23%)
  waiting for transfers between devices  19.3 us (19%)
  blocking collectives  14.5 us (14%)
  local copies, waits for them, and re-layouts  3.59 us (3%)
    pallas_call x9, Pallas kernels, call(): pl.pallas_call(kernel, out_shape=outs, in_specs=[SM] * scalars + [VM] * (...  41.7 us
    all_to_all x1, blocking collectives, body(): return lax.all_to_all(packed, 'gy', split_axis=0, concat_axis=0, tiled=True)  14.5 us
    ppermute x6, waiting for transfers between devices, swap(): from_a = lax.ppermute(by_a, axis, pairs_a)  12.1 us
    ppermute x6, starting transfers between devices, swap(): from_a = lax.ppermute(by_a, axis, pairs_a)  12 us
    ppermute x6, starting transfers between devices, swap(): from_b = lax.ppermute(by_b, axis, pairs_b)  11.7 us
    ppermute x6, waiting for transfers between devices, swap(): from_b = lax.ppermute(by_b, axis, pairs_b)  7.22 us
    unnamed x11, local copies, waits for them, and re-layouts  3.42 us
  transfers between devices with their start and end apart: 12, of which 3 were waited for; matrix products, arithmetic and copies ran while one was open for 1% of the time, Pallas kernels for 21%

profile of v2, /device:TPU:1, one launch (start us, length us, event | category | flops | bytes accessed | tf_op | source)
XLA Modules:
  0.0 103.9 jit_solution(13993307431833164513)
XLA Ops:
  0.0 0.8 copy.9.x0.own
  0.8 0.7 copy.8.zone_ref
  1.7 1.0 %copy-done = bf16[16,64,256]{2,1,0:T(8,128)(2,1)S(1)} copy-done((bf16[16,64,256]{2,1,0:T(8,128)(2,1)S(1)}, bf16[16,64,256]{2,1,0:T(8,128)(2,1)}, u32[]{:S(2)}) %copy-start) | copy-done | bytes 524312
  2.7 1.4 %shard_map.73 = (f32[8,3,256]{2,1,0:T(4,128)S(1)}, f32[8,3,256]{2,1,0:T(4,128)S(1)}, bf16[8,64,256]{2,1,0:T(8,128)(2,1)S(1)}, bf16[8,64,256]{2,1,0:T(8,128)(2,1)S(1)}, s32[16]{0:T(128)S(1)}) custom-call(s32[6]{0:T(128)S(1)} %stack.19.meta_ref, s32[16,1]{1,0:T(8,128)S(1)} %copy.8.zone_ref, f32[16,3,256]{2,1,0:T(4,128)S(1)} %copy.9.x0.own, ...), custom_call_target="tpu_custom_call" | custom-call | flops 1048576 | bytes 1048576 | tf_op jit(solution)/shard_map/pallas_call | solution.py:291
  4.1 2.1 %collective-permute-start.4 = (f32[8,3,256]{2,1,0:T(4,128)S(1)}, f32[8,3,256]{2,1,0:T(4,128)S(1)}, u32[]{:S(2)}, u32[]{:S(2)}) collective-permute-start(f32[8,3,256]{2,1,0:T(4,128)S(1)} %get-tuple-element.31.p0), channel_id=1, source_target_pairs={{0,1},{1,0},{2,3},{3,2},{4,5},{5,4},{6,7},{7,6},{8,9},{9,8},{10,11... | collective-permute-start | bytes 73736 | tf_op jit(solution)/shard_map/ppermute | solution.py:102
  6.9 3.8 %collective-permute-start = (bf16[8,64,256]{2,1,0:T(8,128)(2,1)S(1)}, bf16[8,64,256]{2,1,0:T(8,128)(2,1)S(1)}, u32[]{:S(2)}, u32[]{:S(2)}) collective-permute-start(bf16[8,64,256]{2,1,0:T(8,128)(2,1)S(1)} %get-tuple-element.27.p0), channel_id=1, source_target_pairs={{0,1},{1,0},{2,3},{3,2},{4,5},{5,4},{6,7},{7,6},{8,9},{9,8},{10,11... | collective-permute-start | bytes 786440 | tf_op jit(solution)/shard_map/ppermute | solution.py:102
  10.7 0.7 collective-permute-start.1
  11.9 1.6 %collective-permute-start.6 = (f32[16,3,256]{2,1,0:T(4,128)S(1)}, f32[16,3,256]{2,1,0:T(4,128)S(1)}, u32[]{:S(2)}, u32[]{:S(2)}) collective-permute-start(f32[16,3,256]{2,1,0:T(4,128)S(1)} %get-tuple-element.33), channel_id=1, source_target_pairs={{0,8},{8,0},{16,24},{24,16},{1,9},{9,1},{17,25},{25,17},{2,10},{10... | collective-permute-start | bytes 147464 | tf_op jit(solution)/shard_map/ppermute | solution.py:102
  13.5 3.0 %collective-permute-start.7 = (f32[16,3,256]{2,1,0:T(4,128)S(1)}, f32[16,3,256]{2,1,0:T(4,128)S(1)}, u32[]{:S(2)}, u32[]{:S(2)}) collective-permute-start(f32[16,3,256]{2,1,0:T(4,128)S(1)} %get-tuple-element.34), channel_id=1, source_target_pairs={{8,16},{16,8},{9,17},{17,9},{10,18},{18,10},{11,19},{19,11},{12,20... | collective-permute-start | bytes 147464 | tf_op jit(solution)/shard_map/ppermute | solution.py:101
  16.6 0.8 fusion.6
  17.4 3.3 %collective-permute-done.p2 = bf16[8,64,256]{2,1,0:T(8,128)(2,1)S(1)} collective-permute-done((bf16[8,64,256]{2,1,0:T(8,128)(2,1)S(1)}, bf16[8,64,256]{2,1,0:T(8,128)(2,1)S(1)}, u32[]{:S(2)}, u32[]{:S(2)}) %collective-permute-start) | collective-permute-done | bytes 262176 | tf_op jit(solution)/shard_map/ppermute | solution.py:102
  21.3 2.2 %collective-permute-start.2 = (bf16[16,64,256]{2,1,0:T(8,128)(2,1)S(1)}, bf16[16,64,256]{2,1,0:T(8,128)(2,1)S(1)}, u32[]{:S(2)}, u32[]{:S(2)}) collective-permute-start(bf16[16,64,256]{2,1,0:T(8,128)(2,1)S(1)} %get-tuple-element.29), channel_id=1, source_target_pairs={{0,8},{8,0},{16,24},{24,16},{1,9},{9,1},{17,25},{25,17},{2,10},{10... | collective-permute-start | bytes 1572872 | tf_op jit(solution)/shard_map/ppermute | solution.py:102
  23.5 3.4 %collective-permute-start.3 = (bf16[16,64,256]{2,1,0:T(8,128)(2,1)S(1)}, bf16[16,64,256]{2,1,0:T(8,128)(2,1)S(1)}, u32[]{:S(2)}, u32[]{:S(2)}) collective-permute-start(bf16[16,64,256]{2,1,0:T(8,128)(2,1)S(1)} %get-tuple-element.30), channel_id=1, source_target_pairs={{8,16},{16,8},{9,17},{17,9},{10,18},{18,10},{11,19},{19,11},{12,20... | collective-permute-start | bytes 1572872 | tf_op jit(solution)/shard_map/ppermute | solution.py:101
  26.9 14.4 %shard_map.76 = (bf16[4,4096,256]{2,1,0:T(8,128)(2,1)S(1)}, bf16[4,4096,256]{2,1,0:T(8,128)(2,1)S(1)}, f32[8,256]{1,0:T(8,128)S(1)}, bf16[64,256,48]{2,1,0:T(8,128)(2,1)S(1)}, bf16[16,48,256]{2,1,0:T(8,128)(2,1)S(1)}) custom-call(s32[256]{0:T(256)S(1)} %reshape.25.near_ref, s32[6]{0:T(128)S(1)} %stack.19.meta_ref, f32[16,3,256]{2,1,0:T(4,128)S(1)} %copy.9.x0.own, ...), custom_call_target="tpu_custom_call" | custom-call | flops 4294967296 | bytes 1048576 | tf_op jit(solution)/shard_map/pallas_call | solution.py:291
  41.3 6.1 %shard_map.77 = (bf16[4,4096,256]{2,1,0:T(8,128)(2,1)S(1)}, bf16[4,4096,256]{2,1,0:T(8,128)(2,1)S(1)}, f32[8,256]{1,0:T(8,128)S(1)}) custom-call(s32[256]{0:T(256)S(1)} %reshape.25.near_ref, bf16[64,256,48]{2,1,0:T(8,128)(2,1)S(1)} %get-tuple-element.37.source, bf16[16,48,256]{2,1,0:T(8,128)(2,1)S(1)} %get-tuple-element.38.target), custom_call_target="tpu_custom_call" | custom-call | flops 4294967296 | bytes 1048576 | tf_op jit(solution)/shard_map/pallas_call | solution.py:291
  47.5 4.7 %shard_map.78 = (bf16[8,64,256]{2,1,0:T(8,128)(2,1)S(1)}, bf16[64,64,256]{2,1,0:T(8,128)(2,1)S(1)}) custom-call(s32[256]{0:T(256)S(1)} %reshape.25.near_ref, s32[6]{0:T(128)S(1)} %stack.19.meta_ref, bf16[8,64,256]{2,1,0:T(8,128)(2,1)S(1)} %get-tuple-element.27.p0, bf16[8,64,256]{2,1,0:T(8,128)(2,1)S(1)} %get-tuple-element.28.p1, ...), custom_call_target="tpu_custom_call" | custom-call | flops 2147483648 | bytes 1048576 | tf_op jit(solution)/shard_map/pallas_call | solution.py:291
  52.2 4.6 %shard_map.79.p0 = bf16[8,64,256]{2,1,0:T(8,128)(2,1)S(1)} custom-call(s32[256]{0:T(256)S(1)} %reshape.25.near_ref, s32[6]{0:T(128)S(1)} %stack.19.meta_ref, bf16[64,64,256]{2,1,0:T(8,128)(2,1)S(1)} %get-tuple-element.43.species, bf16[4,4096,256]{2,1,0:T(8,128)(2,1)S(1)} %get-tuple-element.35.w0, bf16[4,4096,256]{2,1,0:T(8,128)(2,1)S(1)} %get-tuple-element.36.w1, ...), custom_call_target="tpu_custom_call" | custom-call | flops 2147483648 | bytes 1048576 | tf_op jit(solution)/shard_map/pallas_call | solution.py:291
  56.9 2.3 %collective-permute-start.8 = (bf16[8,64,256]{2,1,0:T(8,128)(2,1)S(1)}, bf16[8,64,256]{2,1,0:T(8,128)(2,1)S(1)}, u32[]{:S(2)}, u32[]{:S(2)}) collective-permute-start(bf16[8,64,256]{2,1,0:T(8,128)(2,1)S(1)} %shard_map.79.p0), channel_id=1, source_target_pairs={{0,1},{1,0},{2,3},{3,2},{4,5},{5,4},{6,7},{7,6},{8,9},{9,8},{10,11... | collective-permute-start | bytes 786440 | tf_op jit(solution)/shard_map/ppermute | solution.py:102
  59.8 8.8 %collective-permute-done.8.p2 = bf16[8,64,256]{2,1,0:T(8,128)(2,1)S(1)} collective-permute-done((bf16[8,64,256]{2,1,0:T(8,128)(2,1)S(1)}, bf16[8,64,256]{2,1,0:T(8,128)(2,1)S(1)}, u32[]{:S(2)}, u32[]{:S(2)}) %collective-permute-start.8) | collective-permute-done | bytes 262176 | tf_op jit(solution)/shard_map/ppermute | solution.py:102
  69.4 3.3 %collective-permute-start.11 = (bf16[16,64,256]{2,1,0:T(8,128)(2,1)S(1)}, bf16[16,64,256]{2,1,0:T(8,128)(2,1)S(1)}, u32[]{:S(2)}, u32[]{:S(2)}) collective-permute-start(bf16[16,64,256]{2,1,0:T(8,128)(2,1)S(1)} %get-tuple-element.46), channel_id=1, source_target_pairs={{8,16},{16,8},{9,17},{17,9},{10,18},{18,10},{11,19},{19,11},{12,20... | collective-permute-start | bytes 1572872 | tf_op jit(solution)/shard_map/ppermute | solution.py:101
  72.7 7.2 %collective-permute-done.11.p5 = bf16[16,64,256]{2,1,0:T(8,128)(2,1)S(1)} collective-permute-done((bf16[16,64,256]{2,1,0:T(8,128)(2,1)S(1)}, bf16[16,64,256]{2,1,0:T(8,128)(2,1)S(1)}, u32[]{:S(2)}, u32[]{:S(2)}) %collective-permute-start.11) | collective-permute-done | bytes 524320 | tf_op jit(solution)/shard_map/ppermute | solution.py:101
  79.9 8.6 %shard_map.81 = bf16[16,64,256]{2,1,0:T(8,128)(2,1)S(1)} custom-call(s32[256]{0:T(256)S(1)} %reshape.25.near_ref, s32[16]{0:T(128)S(1)} %get-tuple-element.26.row_ref, bf16[8,64,256]{2,1,0:T(8,128)(2,1)S(1)} %shard_map.79.p0, bf16[8,64,256]{2,1,0:T(8,128)(2,1)S(1)} %get-tuple-element.44.p1, bf16[8,64,256]{2,1,0:T(8,128)(2,1)S(1)} %collective-permute-done.8.p2, ...), custom_call_target="tpu_custom_call" | custom-call | flops 4294967296 | bytes 1048576 | tf_op jit(solution)/shard_map/pallas_call | solution.py:291
  88.5 14.5 %all_to_all.5 = bf16[16,64,256]{2,1,0:T(8,128)(2,1)S(1)} all-to-all(bf16[16,64,256]{2,1,0:T(8,128)(2,1)S(1)} %shard_map.81), channel_id=1, replica_groups=mesh['gx'=4,'gy'=8] {'gy'}, dimensions={0} | all-to-all | bytes 1048576 | tf_op jit(solution)/shard_map/all_to_all | solution.py:403
  103.1 0.8 copy.12
  (25 shorter events, 3.4 us)
Async XLA Ops:
  1.7 1.0 %copy-start = (bf16[16,64,256]{2,1,0:T(8,128)(2,1)S(1)}, bf16[16,64,256]{2,1,0:T(8,128)(2,1)}, u32[]{:S(2)}) copy-start(bf16[16,64,256]{2,1,0:T(8,128)(2,1)} %x1.1) | copy-start | bytes 1572868
  4.1 7.2 %collective-permute-start.4 = (f32[8,3,256]{2,1,0:T(4,128)S(1)}, f32[8,3,256]{2,1,0:T(4,128)S(1)}, u32[]{:S(2)}, u32[]{:S(2)}) collective-permute-start(f32[8,3,256]{2,1,0:T(4,128)S(1)} %get-tuple-element.31.p0), channel_id=1, source_target_pairs={{0,1},{1,0},{2,3},{3,2},{4,5},{5,4},{6,7},{7,6},{8,9},{9,8},{10,11... | collective-permute-start | bytes 73736 | tf_op jit(solution)/shard_map/ppermute | solution.py:102
  6.2 5.2 %collective-permute-start.5 = (f32[8,3,256]{2,1,0:T(4,128)S(1)}, f32[8,3,256]{2,1,0:T(4,128)S(1)}, u32[]{:S(2)}, u32[]{:S(2)}) collective-permute-start(f32[8,3,256]{2,1,0:T(4,128)S(1)} %get-tuple-element.32.p1), channel_id=1, source_target_pairs={{1,2},{2,1},{3,4},{4,3},{5,6},{6,5},{9,10},{10,9},{11,12},{12,11},... | collective-permute-start | bytes 73736 | tf_op jit(solution)/shard_map/ppermute | solution.py:101
  6.9 13.8 %collective-permute-start = (bf16[8,64,256]{2,1,0:T(8,128)(2,1)S(1)}, bf16[8,64,256]{2,1,0:T(8,128)(2,1)S(1)}, u32[]{:S(2)}, u32[]{:S(2)}) collective-permute-start(bf16[8,64,256]{2,1,0:T(8,128)(2,1)S(1)} %get-tuple-element.27.p0), channel_id=1, source_target_pairs={{0,1},{1,0},{2,3},{3,2},{4,5},{5,4},{6,7},{7,6},{8,9},{9,8},{10,11... | collective-permute-start | bytes 786440 | tf_op jit(solution)/shard_map/ppermute | solution.py:102
  10.7 10.0 %collective-permute-start.1 = (bf16[8,64,256]{2,1,0:T(8,128)(2,1)S(1)}, bf16[8,64,256]{2,1,0:T(8,128)(2,1)S(1)}, u32[]{:S(2)}, u32[]{:S(2)}) collective-permute-start(bf16[8,64,256]{2,1,0:T(8,128)(2,1)S(1)} %get-tuple-element.28.p1), channel_id=1, source_target_pairs={{1,2},{2,1},{3,4},{4,3},{5,6},{6,5},{9,10},{10,9},{11,12},{12,11},... | collective-permute-start | bytes 786440 | tf_op jit(solution)/shard_map/ppermute | solution.py:101
  11.9 15.0 %collective-permute-start.6 = (f32[16,3,256]{2,1,0:T(4,128)S(1)}, f32[16,3,256]{2,1,0:T(4,128)S(1)}, u32[]{:S(2)}, u32[]{:S(2)}) collective-permute-start(f32[16,3,256]{2,1,0:T(4,128)S(1)} %get-tuple-element.33), channel_id=1, source_target_pairs={{0,8},{8,0},{16,24},{24,16},{1,9},{9,1},{17,25},{25,17},{2,10},{10... | collective-permute-start | bytes 147464 | tf_op jit(solution)/shard_map/ppermute | solution.py:102
  13.5 13.4 %collective-permute-start.7 = (f32[16,3,256]{2,1,0:T(4,128)S(1)}, f32[16,3,256]{2,1,0:T(4,128)S(1)}, u32[]{:S(2)}, u32[]{:S(2)}) collective-permute-start(f32[16,3,256]{2,1,0:T(4,128)S(1)} %get-tuple-element.34), channel_id=1, source_target_pairs={{8,16},{16,8},{9,17},{17,9},{10,18},{18,10},{11,19},{19,11},{12,20... | collective-permute-start | bytes 147464 | tf_op jit(solution)/shard_map/ppermute | solution.py:101
  21.3 26.2 %collective-permute-start.2 = (bf16[16,64,256]{2,1,0:T(8,128)(2,1)S(1)}, bf16[16,64,256]{2,1,0:T(8,128)(2,1)S(1)}, u32[]{:S(2)}, u32[]{:S(2)}) collective-permute-start(bf16[16,64,256]{2,1,0:T(8,128)(2,1)S(1)} %get-tuple-element.29), channel_id=1, source_target_pairs={{0,8},{8,0},{16,24},{24,16},{1,9},{9,1},{17,25},{25,17},{2,10},{10... | collective-permute-start | bytes 1572872 | tf_op jit(solution)/shard_map/ppermute | solution.py:102
  23.5 24.0 %collective-permute-start.3 = (bf16[16,64,256]{2,1,0:T(8,128)(2,1)S(1)}, bf16[16,64,256]{2,1,0:T(8,128)(2,1)S(1)}, u32[]{:S(2)}, u32[]{:S(2)}) collective-permute-start(bf16[16,64,256]{2,1,0:T(8,128)(2,1)S(1)} %get-tuple-element.30), channel_id=1, source_target_pairs={{8,16},{16,8},{9,17},{17,9},{10,18},{18,10},{11,19},{19,11},{12,20... | collective-permute-start | bytes 1572872 | tf_op jit(solution)/shard_map/ppermute | solution.py:101
  41.3 6.2 %copy-start.1 = (f32[16,256]{1,0:T(8,128)S(1)}, f32[16,256]{1,0:T(8,128)}, u32[]{:S(2)}) copy-start(f32[16,256]{1,0:T(8,128)} %t.5) | copy-start | bytes 49156
  41.3 6.2 %copy-start.2 = (f32[32]{0:T(128)S(1)}, f32[32]{0:T(128)}, u32[]{:S(2)}) copy-start(f32[32]{0:T(128)} %param.10) | copy-start | bytes 388
  41.3 6.2 %copy-start.3 = (f32[32]{0:T(128)S(1)}, f32[32]{0:T(128)}, u32[]{:S(2)}) copy-start(f32[32]{0:T(128)} %param.11) | copy-start | bytes 388
  56.9 11.8 %collective-permute-start.8 = (bf16[8,64,256]{2,1,0:T(8,128)(2,1)S(1)}, bf16[8,64,256]{2,1,0:T(8,128)(2,1)S(1)}, u32[]{:S(2)}, u32[]{:S(2)}) collective-permute-start(bf16[8,64,256]{2,1,0:T(8,128)(2,1)S(1)} %shard_map.79.p0), channel_id=1, source_target_pairs={{0,1},{1,0},{2,3},{3,2},{4,5},{5,4},{6,7},{7,6},{8,9},{9,8},{10,11... | collective-permute-start | bytes 786440 | tf_op jit(solution)/shard_map/ppermute | solution.py:102
  59.2 9.5 %collective-permute-start.9 = (bf16[8,64,256]{2,1,0:T(8,128)(2,1)S(1)}, bf16[8,64,256]{2,1,0:T(8,128)(2,1)S(1)}, u32[]{:S(2)}, u32[]{:S(2)}) collective-permute-start(bf16[8,64,256]{2,1,0:T(8,128)(2,1)S(1)} %get-tuple-element.44.p1), channel_id=1, source_target_pairs={{1,2},{2,1},{3,4},{4,3},{5,6},{6,5},{9,10},{10,9},{11,12},{12,11},... | collective-permute-start | bytes 786440 | tf_op jit(solution)/shard_map/ppermute | solution.py:101
  69.3 3.4 %collective-permute-start.10 = (bf16[16,64,256]{2,1,0:T(8,128)(2,1)S(1)}, bf16[16,64,256]{2,1,0:T(8,128)(2,1)S(1)}, u32[]{:S(2)}, u32[]{:S(2)}) collective-permute-start(bf16[16,64,256]{2,1,0:T(8,128)(2,1)S(1)} %get-tuple-element.45), channel_id=1, source_target_pairs={{0,8},{8,0},{16,24},{24,16},{1,9},{9,1},{17,25},{25,17},{2,10},{10... | collective-permute-start | bytes 1572872 | tf_op jit(solution)/shard_map/ppermute | solution.py:102
  69.4 10.5 %collective-permute-start.11 = (bf16[16,64,256]{2,1,0:T(8,128)(2,1)S(1)}, bf16[16,64,256]{2,1,0:T(8,128)(2,1)S(1)}, u32[]{:S(2)}, u32[]{:S(2)}) collective-permute-start(bf16[16,64,256]{2,1,0:T(8,128)(2,1)S(1)} %get-tuple-element.46), channel_id=1, source_target_pairs={{8,16},{16,8},{9,17},{17,9},{10,18},{18,10},{11,19},{19,11},{12,20... | collective-permute-start | bytes 1572872 | tf_op jit(solution)/shard_map/ppermute | solution.py:101

commit v3 on v2

--- a/solution.py
+++ b/solution.py
@@ -28,6 +28,7 @@
 BAND = 4 * QUAD
 EXT = 4 * SIDE + 2 * BAND
 COUNTS = (SIDE, SIDE, SIDE, SIDE, BAND, BAND)
+UNROLL = QUAD * HALO
 STARTS = (0, SIDE, 2 * SIDE, 3 * SIDE, 4 * SIDE, 4 * SIDE + BAND)
 
 
@@ -68,30 +69,31 @@
     return ex, base + i % HALO
 
 
-def split(meta_ref, zone_ref, x0, x1, a0, b0, a1, b1, row_ref, taken):
-    sources, outs = (x0, x1), (a0, b0, a1, b1)
-    for z in range(taken.shape[0]):
-        taken[z] = 0
-
-    def place(b, _):
-        zone = zone_ref[b, 0]
-        order = taken[zone]
-        taken[zone] = order + 1
-        row_ref[b] = zone * CAP + order
-        return 0
-
-    lax.fori_loop(0, BX * BY, place, 0)
+def split(meta_ref, x, pos, a, b, pos_a, pos_b, sem):
     low_a = jnp.where(meta_ref[4] == 1, 0, BY - HALO)
-    for n, x in enumerate(sources):
+    lows = (low_a, BY - HALO - low_a)
+    copies = []
+    for m, (out, low) in enumerate(zip((a, b), lows)):
         for r in range(BX):
-            outs[2 * n][pl.ds(r * HALO, HALO)] = x[pl.ds(r * BY + low_a, HALO)]
-            outs[2 * n + 1][pl.ds(r * HALO, HALO)] = x[pl.ds(r * BY + BY - HALO - low_a, HALO)]
-
-
-def pack(meta_ref, p0, p1, p2, p3, out_a, out_b):
+            source = x.at[pl.ds(r * BY + low, HALO)]
+            target = out.at[pl.ds(r * HALO, HALO)]
+            copies.append(pltpu.make_async_copy(source, target, sem.at[m, r]))
+    for copy in copies:
+        copy.start()
+    for out, low in zip((pos_a, pos_b), lows):
+        for r in range(BX):
+            for i in range(HALO):
+                for c in range(pos.shape[0]):
+                    out[r * HALO + i, c : c + 1] = pos[c, pl.ds(r * BY + low + i, 1)]
+    for copy in copies:
+        copy.wait()
+
+
+def pack(meta_ref, *refs):
+    pieces, (out_a, out_b) = refs[:-2], refs[-2:]
     size = BX * HALO
     from_a = jnp.where(meta_ref[5] == 1, 0, size - QUAD)
-    for n, x in enumerate((p0, p1, p2, p3)):
+    for n, x in enumerate(pieces):
         out_a[pl.ds(n * QUAD, QUAD)] = x[pl.ds(from_a, QUAD)]
         out_b[pl.ds(n * QUAD, QUAD)] = x[pl.ds(size - QUAD - from_a, QUAD)]
 
@@ -136,7 +138,7 @@
         pick(1.0, low),
         pick(1.0, middle),
     )
-    source = jnp.concatenate(source, axis=0).T.astype(bf16)
+    source = jnp.concatenate(source, axis=0).astype(bf16).T
     if not as_target:
         return source, None
     high, middle, low = 2.0 * high, 2.0 * middle, 2.0 * low
@@ -171,31 +173,37 @@
         lax.fori_loop(0, BY, one, 0)
 
 
-def build_first(near_ref, meta_ref, own, c0, c1, r0, r1, w0, w1, inv_ref, source, target):
+def build_first(
+    near_ref, meta_ref, zone_ref, o0, o1, c0, c1, r0, r1, w0, w1, inv_ref, source, target, row_ref, taken
+):
     odd_lane, odd_band = meta_ref[4], meta_ref[5]
-
-    def put(pos, ex, ey, slot, as_target):
-        gx = meta_ref[0] + ex
-        gy = meta_ref[1] + ey
-        inside = (gx >= 0) & (gx < meta_ref[2]) & (gy >= 0) & (gy < meta_ref[3])
-        s, t = features(pos, ex, ey, inside, as_target)
-        source[slot] = s
-        return t
-
-    def mine(b, _):
-        ex, ey = b // BY, b % BY
-        target[b] = put(own[b], ex, ey, slot_of(ex, ey, odd_lane, odd_band), True)
+    for piece, ref in enumerate((o0, o1, c0, c1, r0, r1)):
+
+        def some(j, _, piece=piece, ref=ref):
+            for n in range(UNROLL):
+                i = j * UNROLL + n
+                ex, ey = place_of(piece, i, odd_lane, odd_band)
+                gx = meta_ref[0] + ex
+                gy = meta_ref[1] + ey
+                inside = (gx >= 0) & (gx < meta_ref[2]) & (gy >= 0) & (gy < meta_ref[3])
+                s, t = features(ref[i], ex, ey, inside, piece < 2)
+                source[STARTS[piece] + i] = s
+                if piece < 2:
+                    target[ex * BY + ey] = t
+            return 0
+
+        lax.fori_loop(0, COUNTS[piece] // UNROLL, some, 0)
+    for z in range(taken.shape[0]):
+        taken[z] = 0
+
+    def place(b, _):
+        zone = zone_ref[0, b]
+        order = taken[zone]
+        taken[zone] = order + 1
+        row_ref[b] = zone * CAP + order
         return 0
 
-    lax.fori_loop(0, BX * BY, mine, 0)
-    for piece, ref in ((2, c0), (3, c1), (4, r0), (5, r1)):
-
-        def one(i, _, piece=piece, ref=ref):
-            ex, ey = place_of(piece, i, odd_lane, odd_band)
-            put(ref[i], ex, ey, STARTS[piece] + i, False)
-            return 0
-
-        lax.fori_loop(0, COUNTS[piece], one, 0)
+    lax.fori_loop(0, BX * BY, place, 0)
     build_rows(near_ref, source, target, (w0, w1), inv_ref, 0)
 
 
@@ -229,8 +237,10 @@
 
 
 def join(pieces, species):
-    for start, count, ref in zip(STARTS, COUNTS, pieces):
-        species[pl.ds(start, count)] = ref[...]
+    start = 0
+    for ref in pieces:
+        species[pl.ds(start, ref.shape[0])] = ref[...]
+        start += ref.shape[0]
 
 
 def inverse_of(inv_refs, g, c):
@@ -265,8 +275,8 @@
     step_columns(near_ref, species, gathered, (w0, w1, w2, w3), (i0, i1), (t, a, o), low, out)
 
 
-def last_step(near_ref, row_ref, p0, p1, p2, p3, p4, p5, w0, w1, w2, w3, i0, i1, t, a, o, out, species, gathered):
-    join((p0, p1, p2, p3, p4, p5), species)
+def last_step(near_ref, row_ref, p0, p1, p2, p3, p4, p5, p6, p7, w0, w1, w2, w3, i0, i1, t, a, o, out, species, gathered):
+    join((p0, p1, p2, p3, p4, p5, p6, p7), species)
     if out.shape[0] > BX * BY:
         out[...] = jnp.zeros_like(out)
     factor, onset = column(a), column(o)
@@ -284,6 +294,7 @@
 
 VM = pl.BlockSpec(memory_space=pltpu.VMEM)
 SM = pl.BlockSpec(memory_space=pltpu.SMEM)
+HBM = pl.BlockSpec(memory_space=pltpu.HBM)
 
 
 def call(kernel, operands, scalars, outs, scratch, flops):
@@ -327,19 +338,25 @@
         ]
     ).astype(i32)
     like = lambda x, n: pltpu.VMEM((n,) + x.shape[1:], x.dtype)
-    pos_a, pos_b, own_a, own_b, row = call(
+    axes = walker_displacement.shape[1]
+    own_a, own_b, pos_a, pos_b = pl.pallas_call(
         split,
-        (meta, downstream_zone, walker_displacement, solute_load),
-        2,
-        [like(walker_displacement, SIDE)] * 2
-        + [like(solute_load, SIDE)] * 2
-        + [jax.ShapeDtypeStruct((bins,), i32)],
-        [pltpu.SMEM((lane_count,), i32)],
-        1 << 20,
+        out_shape=[pltpu.VMEM((SIDE, kinds, parts), bf16)] * 2
+        + [pltpu.VMEM((SIDE, axes, parts), f32)] * 2,
+        in_specs=[SM, HBM, VM],
+        out_specs=[VM] * 4,
+        scratch_shapes=[pltpu.SemaphoreType.DMA((2, BX))],
+        compiler_params=pltpu.CompilerParams(vmem_limit_bytes=8 << 20),
+        name="split",
+    )(
+        meta,
+        pltpu.with_memory_space_constraint(solute_load, pltpu.HBM),
+        walker_displacement.transpose(1, 0, 2),
     )
 
     def rows(pieces):
-        by_a, by_b = call(pack, (meta,) + pieces, 1, [like(pieces[0], BAND)] * 2, [], 1 << 20)
+        size = len(pieces) * QUAD
+        by_a, by_b = call(pack, (meta,) + pieces, 1, [like(pieces[0], size)] * 2, [], 1 << 20)
         return swap(by_a, by_b, "gx")
 
     pos_sides = swap(pos_a, pos_b, "gy")
@@ -363,18 +380,19 @@
     gathered = pltpu.VMEM((kinds, neighbours * parts), bf16)
     all_species = pltpu.VMEM((EXT, kinds, parts), bf16)
     work = 2 * bins * neighbours * parts * parts * 128
-    w0, w1, inv0, source, target = call(
+    w0, w1, inv0, source, target, row = call(
         build_first,
-        (near, meta, walker_displacement) + pos_sides + pos_bands,
-        2,
+        (near, meta, downstream_zone.T, pos_a, pos_b) + pos_sides + pos_bands,
+        3,
         [
             w_row,
             w_row,
             inv_half,
             pltpu.VMEM((EXT, parts, FEATURES), bf16),
             pltpu.VMEM((bins, FEATURES, parts), bf16),
+            jax.ShapeDtypeStruct((bins,), i32),
         ],
-        [],
+        [pltpu.SMEM((lane_count,), i32)],
         work,
     )
     w2, w3, inv1 = call(build_second, (near, source, target), 1, [w_row, w_row, inv_half], [], work)
@@ -391,10 +409,12 @@
 
     own = (by_a, by_b)
     sides = swap(by_a, by_b, "gy")
-    bands = rows(own + sides)
+    own_bands = rows(own)
+    corners = rows(sides)
+    pieces = own + sides + (own_bands[0], corners[0], own_bands[1], corners[1])
     packed = call(
         last_step,
-        (near, row) + own + sides + bands + built,
+        (near, row) + pieces + built,
         2,
         jax.ShapeDtypeStruct((lane_count * CAP, kinds, parts), bf16),
         [all_species, gathered],

time: 104 us -> 94.8 us (0.912)
  waiting for transfers between devices: 19.3 us -> 13.4 us
  Pallas kernels: 41.7 us -> 36.4 us
  starting transfers between devices: 23.7 us -> 26.2 us
  local copies, waits for them, and re-layouts: 3.59 us -> 2.43 us
    pallas_call x9, Pallas kernels: 41.7 us -> 34.8 us  [call(): pl.pallas_call(kernel, out_shape=outs, in_specs=[SM] * scalars + [VM] * (...]
    ppermute x6 -> x7, waiting for transfers between devices: 12.1 us -> 8.99 us  [swap(): from_a = lax.ppermute(by_a, axis, pairs_a)]
    ppermute x6 -> x7, waiting for transfers between devices: 7.22 us -> 4.37 us  [swap(): from_b = lax.ppermute(by_b, axis, pairs_b)]
    ppermute x6 -> x7, starting transfers between devices: 11.7 us -> 14.2 us  [swap(): from_b = lax.ppermute(by_b, axis, pairs_b)]
    pallas_call x0 -> x1, Pallas kernels: none -> 1.67 us  [body(): pl.pallas_call(split, out_shape=[pltpu.VMEM((SIDE, kinds, parts), bf16)]...]
    unnamed x11, local copies, waits for them, and re-layouts: 3.42 us -> 2.26 us
    ppermute x6 -> x7, starting transfers between devices: 12 us -> 12 us  [swap(): from_a = lax.ppermute(by_a, axis, pairs_a)]
  transfers between devices with their start and end apart: 12 -> 14, of which waited for: 3 -> 3; matrix products, arithmetic and copies ran while one was open for 1% -> 1% of each run, Pallas kernels for 21% -> 18%
where the time goes in v3:
time: 94.8 us; the launch traced here: 94.3 us
  Pallas kernels  36.4 us (38%)
  starting transfers between devices  26.2 us (28%)
  blocking collectives  14.8 us (16%)
  waiting for transfers between devices  13.4 us (14%)
  local copies, waits for them, and re-layouts  2.43 us (3%)
    pallas_call x9, Pallas kernels, call(): pl.pallas_call(kernel, out_shape=outs, in_specs=[SM] * scalars + [VM] * (...  34.8 us
    all_to_all x1, blocking collectives, body(): return lax.all_to_all(packed, 'gy', split_axis=0, concat_axis=0, tiled=True)  14.8 us
    ppermute x7, starting transfers between devices, swap(): from_b = lax.ppermute(by_b, axis, pairs_b)  14.2 us
    ppermute x7, starting transfers between devices, swap(): from_a = lax.ppermute(by_a, axis, pairs_a)  12 us
    ppermute x7, waiting for transfers between devices, swap(): from_a = lax.ppermute(by_a, axis, pairs_a)  8.99 us
    ppermute x7, waiting for transfers between devices, swap(): from_b = lax.ppermute(by_b, axis, pairs_b)  4.37 us
    unnamed x11, local copies, waits for them, and re-layouts  2.26 us
  transfers between devices with their start and end apart: 14, of which 3 were waited for; matrix products, arithmetic and copies ran while one was open for 1% of the time, Pallas kernels for 18%

profile of v3, /device:TPU:1, one launch (start us, length us, event | category | flops | bytes accessed | tf_op | source)
XLA Modules:
  0.0 94.3 jit_solution(663347620114879303)
XLA Ops:
  0.1 0.8 copy-done.1
  0.9 1.7 %split.1 = (bf16[8,64,256]{2,1,0:T(8,128)(2,1)S(1)}, bf16[8,64,256]{2,1,0:T(8,128)(2,1)S(1)}, f32[8,3,256]{2,1,0:T(4,128)S(1)}, f32[8,3,256]{2,1,0:T(4,128)S(1)}) custom-call(s32[6]{0:T(128)S(1)} %stack.19.meta_ref, bf16[16,64,256]{2,1,0:T(8,128)(2,1)} %x.1, f32[3,16,256]{2,1,0:T(8,128)S(1)} %bitcast.8), custom_call_target="tpu_custom_call" | custom-call | tf_op jit(solution)/shard_map/split/pallas_call | solution.py:342
  2.6 2.1 %collective-permute-start = (f32[8,3,256]{2,1,0:T(4,128)S(1)}, f32[8,3,256]{2,1,0:T(4,128)S(1)}, u32[]{:S(2)}, u32[]{:S(2)}) collective-permute-start(f32[8,3,256]{2,1,0:T(4,128)S(1)} %get-tuple-element.28.refs_0_.o0), channel_id=1, source_target_pairs={{0,1},{1,0},{2,3},{3,2},{4,5},{5,4},{6,7},{7,6},{8,9},{9,8},{10,11... | collective-permute-start | bytes 73736 | tf_op jit(solution)/shard_map/ppermute | solution.py:104
  5.3 3.8 %collective-permute-start.4 = (bf16[8,64,256]{2,1,0:T(8,128)(2,1)S(1)}, bf16[8,64,256]{2,1,0:T(8,128)(2,1)S(1)}, u32[]{:S(2)}, u32[]{:S(2)}) collective-permute-start(bf16[8,64,256]{2,1,0:T(8,128)(2,1)S(1)} %get-tuple-element.33.refs_0_.p0), channel_id=1, source_target_pairs={{0,1},{1,0},{2,3},{3,2},{4,5},{5,4},{6,7},{7,6},{8,9},{9,8},{10,11... | collective-permute-start | bytes 786440 | tf_op jit(solution)/shard_map/ppermute | solution.py:104
  9.1 0.7 collective-permute-start.5
  10.4 1.6 %collective-permute-start.2 = (f32[16,3,256]{2,1,0:T(4,128)S(1)}, f32[16,3,256]{2,1,0:T(4,128)S(1)}, u32[]{:S(2)}, u32[]{:S(2)}) collective-permute-start(f32[16,3,256]{2,1,0:T(4,128)S(1)} %get-tuple-element.30), channel_id=1, source_target_pairs={{0,8},{8,0},{16,24},{24,16},{1,9},{9,1},{17,25},{25,17},{2,10},{10... | collective-permute-start | bytes 147464 | tf_op jit(solution)/shard_map/ppermute | solution.py:104
  12.0 3.0 %collective-permute-start.3 = (f32[16,3,256]{2,1,0:T(4,128)S(1)}, f32[16,3,256]{2,1,0:T(4,128)S(1)}, u32[]{:S(2)}, u32[]{:S(2)}) collective-permute-start(f32[16,3,256]{2,1,0:T(4,128)S(1)} %get-tuple-element.31), channel_id=1, source_target_pairs={{8,16},{16,8},{9,17},{17,9},{10,18},{18,10},{11,19},{19,11},{12,20... | collective-permute-start | bytes 147464 | tf_op jit(solution)/shard_map/ppermute | solution.py:103
  15.0 0.8 fusion.6
  15.9 3.3 %collective-permute-done.4.refs_2_.p2 = bf16[8,64,256]{2,1,0:T(8,128)(2,1)S(1)} collective-permute-done((bf16[8,64,256]{2,1,0:T(8,128)(2,1)S(1)}, bf16[8,64,256]{2,1,0:T(8,128)(2,1)S(1)}, u32[]{:S(2)}, u32[]{:S(2)}) %collective-permute-start.4) | collective-permute-done | bytes 262176 | tf_op jit(solution)/shard_map/ppermute | solution.py:104
  19.8 2.2 %collective-permute-start.6 = (bf16[16,64,256]{2,1,0:T(8,128)(2,1)S(1)}, bf16[16,64,256]{2,1,0:T(8,128)(2,1)S(1)}, u32[]{:S(2)}, u32[]{:S(2)}) collective-permute-start(bf16[16,64,256]{2,1,0:T(8,128)(2,1)S(1)} %get-tuple-element.35), channel_id=1, source_target_pairs={{0,8},{8,0},{16,24},{24,16},{1,9},{9,1},{17,25},{25,17},{2,10},{10... | collective-permute-start | bytes 1572872 | tf_op jit(solution)/shard_map/ppermute | solution.py:104
  21.9 3.4 %collective-permute-start.7 = (bf16[16,64,256]{2,1,0:T(8,128)(2,1)S(1)}, bf16[16,64,256]{2,1,0:T(8,128)(2,1)S(1)}, u32[]{:S(2)}, u32[]{:S(2)}) collective-permute-start(bf16[16,64,256]{2,1,0:T(8,128)(2,1)S(1)} %get-tuple-element.36), channel_id=1, source_target_pairs={{8,16},{16,8},{9,17},{17,9},{10,18},{18,10},{11,19},{19,11},{12,20... | collective-permute-start | bytes 1572872 | tf_op jit(solution)/shard_map/ppermute | solution.py:103
  26.0 8.4 %shard_map.74 = (bf16[4,4096,256]{2,1,0:T(8,128)(2,1)S(1)}, bf16[4,4096,256]{2,1,0:T(8,128)(2,1)S(1)}, f32[8,256]{1,0:T(8,128)S(1)}, bf16[64,256,48]{2,1,0:T(8,1...) custom-call(s32[256]{0:T(256)S(1)} %reshape.25.near_ref, s32[6]{0:T(128)S(1)} %stack.19.meta_ref, ...), custom_call_target="tpu_custom_call" | custom-call | flops 4294967296 | bytes 1048576 | tf_op jit(solution)/shard_map/pallas_call | solution.py:302
  34.5 6.1 %shard_map.76 = (bf16[4,4096,256]{2,1,0:T(8,128)(2,1)S(1)}, bf16[4,4096,256]{2,1,0:T(8,128)(2,1)S(1)}, f32[8,256]{1,0:T(8,128)S(1)}) custom-call(s32[256]{0:T(256)S(1)} %reshape.25.near_ref, bf16[64,256,48]{2,1,0:T(8,128)(2,1)S(1)} %get-tuple-element.39.source, bf16[16,48,256]{2,1,0:T(8,128)(2,1)S(1)} %get-tuple-element.40.target), custom_call_target="tpu_custom_call" | custom-call | flops 4294967296 | bytes 1048576 | tf_op jit(solution)/shard_map/pallas_call | solution.py:302
  40.7 4.7 %shard_map.77 = (bf16[8,64,256]{2,1,0:T(8,128)(2,1)S(1)}, bf16[64,64,256]{2,1,0:T(8,128)(2,1)S(1)}) custom-call(s32[256]{0:T(256)S(1)} %reshape.25.near_ref, s32[6]{0:T(128)S(1)} %stack.19.meta_ref, bf16[8,64,256]{2,1,0:T(8,128)(2,1)S(1)} %get-tuple-element.33.refs_0_.p0, bf16[8,64,256]{2,1,0:T(8,128)(2,1)S(1)} %get-tuple-element.34.refs_1_.p1, ...), custom_call_target="tpu_custom_call" | custom-call | flops 2147483648 | bytes 1048576 | tf_op jit(solution)/shard_map/pallas_call | solution.py:302
  45.3 4.6 %shard_map.78.refs_0_.p0 = bf16[8,64,256]{2,1,0:T(8,128)(2,1)S(1)} custom-call(s32[256]{0:T(256)S(1)} %reshape.25.near_ref, s32[6]{0:T(128)S(1)} %stack.19.meta_ref, bf16[64,64,256]{2,1,0:T(8,128)(2,1)S(1)} %get-tuple-element.45.species, bf16[4,4096,256]{2,1,0:T(8,128)(2,1)S(1)} %get-tuple-element.37.w0, bf16[4,4096,256]{2,1,0:T(8,128)(2,1)S(1)} %get-tuple-element.38.w1, ...), custom_call_target="tpu_custom_call" | custom-call | flops 2147483648 | bytes 1048576 | tf_op jit(solution)/shard_map/pallas_call | solution.py:302
  49.9 2.3 %collective-permute-start.8 = (bf16[8,64,256]{2,1,0:T(8,128)(2,1)S(1)}, bf16[8,64,256]{2,1,0:T(8,128)(2,1)S(1)}, u32[]{:S(2)}, u32[]{:S(2)}) collective-permute-start(bf16[8,64,256]{2,1,0:T(8,128)(2,1)S(1)} %shard_map.78.refs_0_.p0), channel_id=1, source_target_pairs={{0,1},{1,0},{2,3},{3,2},{4,5},{5,4},{6,7},{7,6},{8,9},{9,8},{10,11... | collective-permute-start | bytes 786440 | tf_op jit(solution)/shard_map/ppermute | solution.py:104
  52.2 0.7 collective-permute-start.9
  53.6 2.4 %collective-permute-start.12 = (bf16[8,64,256]{2,1,0:T(8,128)(2,1)S(1)}, bf16[8,64,256]{2,1,0:T(8,128)(2,1)S(1)}, u32[]{:S(2)}, u32[]{:S(2)}) collective-permute-start(bf16[8,64,256]{2,1,0:T(8,128)(2,1)S(1)} %get-tuple-element.49), channel_id=1, source_target_pairs={{8,16},{16,8},{9,17},{17,9},{10,18},{18,10},{11,19},{19,11},{12,20... | collective-permute-start | bytes 786440 | tf_op jit(solution)/shard_map/ppermute | solution.py:103
  56.0 5.7 %collective-permute-done.8.refs_0_.p2 = bf16[8,64,256]{2,1,0:T(8,128)(2,1)S(1)} collective-permute-done((bf16[8,64,256]{2,1,0:T(8,128)(2,1)S(1)}, bf16[8,64,256]{2,1,0:T(8,128)(2,1)S(1)}, u32[]{:S(2)}, u32[]{:S(2)}) %collective-permute-start.8) | collective-permute-done | bytes 262176 | tf_op jit(solution)/shard_map/ppermute | solution.py:104
  62.4 3.3 %collective-permute-start.13 = (bf16[8,64,256]{2,1,0:T(8,128)(2,1)S(1)}, bf16[8,64,256]{2,1,0:T(8,128)(2,1)S(1)}, u32[]{:S(2)}, u32[]{:S(2)}) collective-permute-start(bf16[8,64,256]{2,1,0:T(8,128)(2,1)S(1)} %get-tuple-element.50), channel_id=1, source_target_pairs={{8,16},{16,8},{9,17},{17,9},{10,18},{18,10},{11,19},{19,11},{12,20... | collective-permute-start | bytes 786440 | tf_op jit(solution)/shard_map/ppermute | solution.py:103
  65.7 4.4 %collective-permute-done.13.p7 = bf16[8,64,256]{2,1,0:T(8,128)(2,1)S(1)} collective-permute-done((bf16[8,64,256]{2,1,0:T(8,128)(2,1)S(1)}, bf16[8,64,256]{2,1,0:T(8,128)(2,1)S(1)}, u32[]{:S(2)}, u32[]{:S(2)}) %collective-permute-start.13) | collective-permute-done | bytes 262176 | tf_op jit(solution)/shard_map/ppermute | solution.py:103
  70.1 8.6 %shard_map.81 = bf16[16,64,256]{2,1,0:T(8,128)(2,1)S(1)} custom-call(s32[256]{0:T(256)S(1)} %reshape.25.near_ref, s32[16]{0:T(128)S(1)} %get-tuple-element.32.row_ref, bf16[8,64,256]{2,1,0:T(8,128)(2,1)S(1)} %shard_map.78.refs_0_.p0, bf16[8,64,256]{2,1,0:T(8,128)(2,1)S(1)} %get-tuple-element.46.refs_1_.p1, ...), custom_call_target="tpu_custom_call" | custom-call | flops 4294967296 | bytes 1048576 | tf_op jit(solution)/shard_map/pallas_call | solution.py:302
  78.7 14.8 %all_to_all.5 = bf16[16,64,256]{2,1,0:T(8,128)(2,1)S(1)} all-to-all(bf16[16,64,256]{2,1,0:T(8,128)(2,1)S(1)} %shard_map.81), channel_id=1, replica_groups=mesh['gx'=4,'gy'=8] {'gy'}, dimensions={0} | all-to-all | bytes 1048576 | tf_op jit(solution)/shard_map/all_to_all | solution.py:423
  93.5 0.8 copy.9
  (30 shorter events, 4.0 us)
Async XLA Ops:
  0.1 0.8 copy-start.1
  2.6 7.2 %collective-permute-start = (f32[8,3,256]{2,1,0:T(4,128)S(1)}, f32[8,3,256]{2,1,0:T(4,128)S(1)}, u32[]{:S(2)}, u32[]{:S(2)}) collective-permute-start(f32[8,3,256]{2,1,0:T(4,128)S(1)} %get-tuple-element.28.refs_0_.o0), channel_id=1, source_target_pairs={{0,1},{1,0},{2,3},{3,2},{4,5},{5,4},{6,7},{7,6},{8,9},{9,8},{10,11... | collective-permute-start | bytes 73736 | tf_op jit(solution)/shard_map/ppermute | solution.py:104
  4.7 5.2 %collective-permute-start.1 = (f32[8,3,256]{2,1,0:T(4,128)S(1)}, f32[8,3,256]{2,1,0:T(4,128)S(1)}, u32[]{:S(2)}, u32[]{:S(2)}) collective-permute-start(f32[8,3,256]{2,1,0:T(4,128)S(1)} %get-tuple-element.29.refs_1_.o1), channel_id=1, source_target_pairs={{1,2},{2,1},{3,4},{4,3},{5,6},{6,5},{9,10},{10,9},{11,12},{12,11},... | collective-permute-start | bytes 73736 | tf_op jit(solution)/shard_map/ppermute | solution.py:103
  5.3 13.8 %collective-permute-start.4 = (bf16[8,64,256]{2,1,0:T(8,128)(2,1)S(1)}, bf16[8,64,256]{2,1,0:T(8,128)(2,1)S(1)}, u32[]{:S(2)}, u32[]{:S(2)}) collective-permute-start(bf16[8,64,256]{2,1,0:T(8,128)(2,1)S(1)} %get-tuple-element.33.refs_0_.p0), channel_id=1, source_target_pairs={{0,1},{1,0},{2,3},{3,2},{4,5},{5,4},{6,7},{7,6},{8,9},{9,8},{10,11... | collective-permute-start | bytes 786440 | tf_op jit(solution)/shard_map/ppermute | solution.py:104
  9.1 10.0 %collective-permute-start.5 = (bf16[8,64,256]{2,1,0:T(8,128)(2,1)S(1)}, bf16[8,64,256]{2,1,0:T(8,128)(2,1)S(1)}, u32[]{:S(2)}, u32[]{:S(2)}) collective-permute-start(bf16[8,64,256]{2,1,0:T(8,128)(2,1)S(1)} %get-tuple-element.34.refs_1_.p1), channel_id=1, source_target_pairs={{1,2},{2,1},{3,4},{4,3},{5,6},{6,5},{9,10},{10,9},{11,12},{12,11},... | collective-permute-start | bytes 786440 | tf_op jit(solution)/shard_map/ppermute | solution.py:103
  10.4 15.0 %collective-permute-start.2 = (f32[16,3,256]{2,1,0:T(4,128)S(1)}, f32[16,3,256]{2,1,0:T(4,128)S(1)}, u32[]{:S(2)}, u32[]{:S(2)}) collective-permute-start(f32[16,3,256]{2,1,0:T(4,128)S(1)} %get-tuple-element.30), channel_id=1, source_target_pairs={{0,8},{8,0},{16,24},{24,16},{1,9},{9,1},{17,25},{25,17},{2,10},{10... | collective-permute-start | bytes 147464 | tf_op jit(solution)/shard_map/ppermute | solution.py:104
  12.0 13.4 %collective-permute-start.3 = (f32[16,3,256]{2,1,0:T(4,128)S(1)}, f32[16,3,256]{2,1,0:T(4,128)S(1)}, u32[]{:S(2)}, u32[]{:S(2)}) collective-permute-start(f32[16,3,256]{2,1,0:T(4,128)S(1)} %get-tuple-element.31), channel_id=1, source_target_pairs={{8,16},{16,8},{9,17},{17,9},{10,18},{18,10},{11,19},{19,11},{12,20... | collective-permute-start | bytes 147464 | tf_op jit(solution)/shard_map/ppermute | solution.py:103
  19.8 20.8 %collective-permute-start.6 = (bf16[16,64,256]{2,1,0:T(8,128)(2,1)S(1)}, bf16[16,64,256]{2,1,0:T(8,128)(2,1)S(1)}, u32[]{:S(2)}, u32[]{:S(2)}) collective-permute-start(bf16[16,64,256]{2,1,0:T(8,128)(2,1)S(1)} %get-tuple-element.35), channel_id=1, source_target_pairs={{0,8},{8,0},{16,24},{24,16},{1,9},{9,1},{17,25},{25,17},{2,10},{10... | collective-permute-start | bytes 1572872 | tf_op jit(solution)/shard_map/ppermute | solution.py:104
  21.9 18.7 %collective-permute-start.7 = (bf16[16,64,256]{2,1,0:T(8,128)(2,1)S(1)}, bf16[16,64,256]{2,1,0:T(8,128)(2,1)S(1)}, u32[]{:S(2)}, u32[]{:S(2)}) collective-permute-start(bf16[16,64,256]{2,1,0:T(8,128)(2,1)S(1)} %get-tuple-element.36), channel_id=1, source_target_pairs={{8,16},{16,8},{9,17},{17,9},{10,18},{18,10},{11,19},{19,11},{12,20... | collective-permute-start | bytes 1572872 | tf_op jit(solution)/shard_map/ppermute | solution.py:103
  25.4 0.7 copy-start.4
  34.4 6.2 %copy-start = (f32[16,256]{1,0:T(8,128)S(1)}, f32[16,256]{1,0:T(8,128)}, u32[]{:S(2)}) copy-start(f32[16,256]{1,0:T(8,128)} %t.5) | copy-start | bytes 49156
  34.5 6.2 %copy-start.2 = (f32[32]{0:T(128)S(1)}, f32[32]{0:T(128)}, u32[]{:S(2)}) copy-start(f32[32]{0:T(128)} %param.10) | copy-start | bytes 388
  34.5 6.2 %copy-start.3 = (f32[32]{0:T(128)S(1)}, f32[32]{0:T(128)}, u32[]{:S(2)}) copy-start(f32[32]{0:T(128)} %param.11) | copy-start | bytes 388
  49.9 11.8 %collective-permute-start.8 = (bf16[8,64,256]{2,1,0:T(8,128)(2,1)S(1)}, bf16[8,64,256]{2,1,0:T(8,128)(2,1)S(1)}, u32[]{:S(2)}, u32[]{:S(2)}) collective-permute-start(bf16[8,64,256]{2,1,0:T(8,128)(2,1)S(1)} %shard_map.78.refs_0_.p0), channel_id=1, source_target_pairs={{0,1},{1,0},{2,3},{3,2},{4,5},{5,4},{6,7},{7,6},{8,9},{9,8},{10,11... | collective-permute-start | bytes 786440 | tf_op jit(solution)/shard_map/ppermute | solution.py:104
  52.2 9.5 %collective-permute-start.9 = (bf16[8,64,256]{2,1,0:T(8,128)(2,1)S(1)}, bf16[8,64,256]{2,1,0:T(8,128)(2,1)S(1)}, u32[]{:S(2)}, u32[]{:S(2)}) collective-permute-start(bf16[8,64,256]{2,1,0:T(8,128)(2,1)S(1)} %get-tuple-element.46.refs_1_.p1), channel_id=1, source_target_pairs={{1,2},{2,1},{3,4},{4,3},{5,6},{6,5},{9,10},{10,9},{11,12},{12,11},... | collective-permute-start | bytes 786440 | tf_op jit(solution)/shard_map/ppermute | solution.py:103
  53.5 12.2 %collective-permute-start.10 = (bf16[8,64,256]{2,1,0:T(8,128)(2,1)S(1)}, bf16[8,64,256]{2,1,0:T(8,128)(2,1)S(1)}, u32[]{:S(2)}, u32[]{:S(2)}) collective-permute-start(bf16[8,64,256]{2,1,0:T(8,128)(2,1)S(1)} %get-tuple-element.47), channel_id=1, source_target_pairs={{0,8},{8,0},{16,24},{24,16},{1,9},{9,1},{17,25},{25,17},{2,10},{10... | collective-permute-start | bytes 786440 | tf_op jit(solution)/shard_map/ppermute | solution.py:104
  53.6 12.2 %collective-permute-start.12 = (bf16[8,64,256]{2,1,0:T(8,128)(2,1)S(1)}, bf16[8,64,256]{2,1,0:T(8,128)(2,1)S(1)}, u32[]{:S(2)}, u32[]{:S(2)}) collective-permute-start(bf16[8,64,256]{2,1,0:T(8,128)(2,1)S(1)} %get-tuple-element.49), channel_id=1, source_target_pairs={{8,16},{16,8},{9,17},{17,9},{10,18},{18,10},{11,19},{19,11},{12,20... | collective-permute-start | bytes 786440 | tf_op jit(solution)/shard_map/ppermute | solution.py:103
  62.3 3.4 %collective-permute-start.11 = (bf16[8,64,256]{2,1,0:T(8,128)(2,1)S(1)}, bf16[8,64,256]{2,1,0:T(8,128)(2,1)S(1)}, u32[]{:S(2)}, u32[]{:S(2)}) collective-permute-start(bf16[8,64,256]{2,1,0:T(8,128)(2,1)S(1)} %get-tuple-element.48), channel_id=1, source_target_pairs={{0,8},{8,0},{16,24},{24,16},{1,9},{9,1},{17,25},{25,17},{2,10},{10... | collective-permute-start | bytes 786440 | tf_op jit(solution)/shard_map/ppermute | solution.py:104
  62.4 7.7 %collective-permute-start.13 = (bf16[8,64,256]{2,1,0:T(8,128)(2,1)S(1)}, bf16[8,64,256]{2,1,0:T(8,128)(2,1)S(1)}, u32[]{:S(2)}, u32[]{:S(2)}) collective-permute-start(bf16[8,64,256]{2,1,0:T(8,128)(2,1)S(1)} %get-tuple-element.50), channel_id=1, source_target_pairs={{8,16},{16,8},{9,17},{17,9},{10,18},{18,10},{11,19},{19,11},{12,20... | collective-permute-start | bytes 786440 | tf_op jit(solution)/shard_map/ppermute | solution.py:103

commit v4 on v3

--- a/solution.py
+++ b/solution.py
@@ -32,14 +32,28 @@
 STARTS = (0, SIDE, 2 * SIDE, 3 * SIDE, 4 * SIDE, 4 * SIDE + BAND)
 
 
-def swaps(count):
-    def both(first):
-        out = []
-        for i in range(first, count - 1, 2):
-            out += [(i, i + 1), (i + 1, i)]
-        return out
-
-    return both(0), both(1)
+def swaps(axis):
+    bands, lanes = lax.axis_size("gx"), lax.axis_size("gy")
+
+    def partner(g, l, first):
+        i, count = (l, lanes) if axis == "gy" else (g, bands)
+        other = i + 1 if (i - first) % 2 == 0 else i - 1
+        if 0 <= other < count:
+            return (g, other) if axis == "gy" else (other, l)
+        if axis == "gy":
+            return (g ^ 1, l) if bands % 2 == 0 else None
+        return (g, l ^ 2) if lanes % 4 == 0 else None
+
+    out = []
+    for first in range(2):
+        pairs = []
+        for g in range(bands):
+            for l in range(lanes):
+                to = partner(g, l, first)
+                if to is not None:
+                    pairs.append((g * lanes + l, to[0] * lanes + to[1]))
+        out.append(pairs)
+    return out
 
 
 def slot_of(ex, ey, odd_lane, odd_band):
@@ -99,7 +113,8 @@
 
 
 def swap(by_a, by_b, axis):
-    pairs_a, pairs_b = swaps(lax.axis_size(axis))
+    pairs_a, pairs_b = swaps(axis)
+    axis = ("gx", "gy")
     from_b = lax.ppermute(by_b, axis, pairs_b)
     from_a = lax.ppermute(by_a, axis, pairs_a)
     return from_a, from_b
@@ -153,9 +168,13 @@
     return source, jnp.concatenate(target, axis=0).astype(bf16)
 
 
+def neighbours_of(near_ref):
+    return near_ref.shape[0] // (BX * BY) - 1
+
+
 def build_rows(near_ref, source, target, w_refs, inv_ref, first_row):
     parts = source.shape[1]
-    neighbours = near_ref.shape[0] // (BX * BY)
+    neighbours = neighbours_of(near_ref)
     for g, w_ref in enumerate(w_refs):
 
         def one(c, _, g=g, w_ref=w_ref):
@@ -174,7 +193,7 @@
 
 
 def build_first(
-    near_ref, meta_ref, zone_ref, o0, o1, c0, c1, r0, r1, w0, w1, inv_ref, source, target, row_ref, taken
+    near_ref, meta_ref, o0, o1, c0, c1, r0, r1, w0, w1, inv_ref, source, target, row_ref, taken
 ):
     odd_lane, odd_band = meta_ref[4], meta_ref[5]
     for piece, ref in enumerate((o0, o1, c0, c1, r0, r1)):
@@ -197,7 +216,7 @@
         taken[z] = 0
 
     def place(b, _):
-        zone = zone_ref[0, b]
+        zone = near_ref[BX * BY * neighbours_of(near_ref) + b]
         order = taken[zone]
         taken[zone] = order + 1
         row_ref[b] = zone * CAP + order
@@ -228,7 +247,7 @@
 
 
 def mix(near_ref, species, gathered, w, b):
-    neighbours = near_ref.shape[0] // (BX * BY)
+    neighbours = neighbours_of(near_ref)
     parts = species.shape[2]
     for k in range(neighbours):
         q = near_ref[b * neighbours + k]
@@ -372,6 +391,7 @@
         odd_lane,
         odd_band,
     ).reshape(-1)
+    near = jnp.concatenate([near, downstream_zone[:, 0]])
     consts = (local_kelvin, couple_kinetic_factor[None], arrhenius_onset[None])
 
     w_row = pltpu.VMEM((BY, neighbours * parts, parts), bf16)
@@ -382,8 +402,8 @@
     work = 2 * bins * neighbours * parts * parts * 128
     w0, w1, inv0, source, target, row = call(
         build_first,
-        (near, meta, downstream_zone.T, pos_a, pos_b) + pos_sides + pos_bands,
-        3,
+        (near, meta, pos_a, pos_b) + pos_sides + pos_bands,
+        2,
         [
             w_row,
             w_row,

time: 94.8 us -> 96.5 us (1.018)
  the two profiles are of different devices: /device:TPU:1 before, /device:TPU:0 now
where the time goes in v4:
time: 96.5 us; the launch traced here: 96.2 us
  Pallas kernels  36.5 us (38%)
  blocking collectives  19.8 us (21%)
  waiting for transfers between devices  19.2 us (20%)
  starting transfers between devices  17.3 us (18%)
  local copies, waits for them, and re-layouts  1.78 us (2%)
  other arithmetic  1.45 us (2%)
    pallas_call x9, Pallas kernels, call(): pl.pallas_call(kernel, out_shape=outs, in_specs=[SM] * scalars + [VM] * (...  34.8 us
    all_to_all x1, blocking collectives, body(): return lax.all_to_all(packed, 'gy', split_axis=0, concat_axis=0, tiled=True)  19.8 us
    ppermute x7, waiting for transfers between devices, swap(): from_a = lax.ppermute(by_a, axis, pairs_a)  14.5 us
    ppermute x7, starting transfers between devices, swap(): from_a = lax.ppermute(by_a, axis, pairs_a)  8.93 us
    ppermute x7, starting transfers between devices, swap(): from_b = lax.ppermute(by_b, axis, pairs_b)  8.38 us
    ppermute x7, waiting for transfers between devices, swap(): from_b = lax.ppermute(by_b, axis, pairs_b)  4.7 us
  transfers between devices with their start and end apart: 14, of which 3 were waited for; matrix products, arithmetic and copies ran while one was open for 2% of the time, Pallas kernels for 18%

profile of v4, /device:TPU:0, one launch (start us, length us, event | category | flops | bytes accessed | tf_op | source)
XLA Modules:
  0.0 96.2 jit_solution(17147152622093916391)
XLA Ops:
  0.1 0.8 copy-done.1
  0.9 1.7 %split.1 = (bf16[8,64,256]{2,1,0:T(8,128)(2,1)S(1)}, bf16[8,64,256]{2,1,0:T(8,128)(2,1)S(1)}, f32[8,3,256]{2,1,0:T(4,128)S(1)}, f32[8,3,256]{2,1,0:T(4,128)S(1)}) custom-call(s32[6]{0:T(128)S(1)} %stack.19.meta_ref, bf16[16,64,256]{2,1,0:T(8,128)(2,1)} %x.1, f32[3,16,256]{2,1,0:T(8,128)S(1)} %bitcast.8), custom_call_target="tpu_custom_call" | custom-call | tf_op jit(solution)/shard_map/split/pallas_call | solution.py:361
  2.6 3.0 %collective-permute-start = (f32[8,3,256]{2,1,0:T(4,128)S(1)}, f32[8,3,256]{2,1,0:T(4,128)S(1)}, u32[]{:S(2)}, u32[]{:S(2)}) collective-permute-start(f32[8,3,256]{2,1,0:T(4,128)S(1)} %get-tuple-element.28.refs_0_.o0), channel_id=1, source_target_pairs={{0,1},{1,0},{2,3},{3,2},{4,5},{5,4},{6,7},{7,6},{8,9},{9,8},{10,11... | collective-permute-start | bytes 73736 | tf_op jit(solution)/shard_map/ppermute | solution.py:119
  5.6 3.0 %collective-permute-start.4 = (bf16[8,64,256]{2,1,0:T(8,128)(2,1)S(1)}, bf16[8,64,256]{2,1,0:T(8,128)(2,1)S(1)}, u32[]{:S(2)}, u32[]{:S(2)}) collective-permute-start(bf16[8,64,256]{2,1,0:T(8,128)(2,1)S(1)} %get-tuple-element.33.refs_0_.p0), channel_id=1, source_target_pairs={{0,1},{1,0},{2,3},{3,2},{4,5},{5,4},{6,7},{7,6},{8,9},{9,8},{10,11... | collective-permute-start | bytes 786440 | tf_op jit(solution)/shard_map/ppermute | solution.py:119
  8.6 0.8 fusion.6
  10.7 2.1 %collective-permute-start.3 = (f32[16,3,256]{2,1,0:T(4,128)S(1)}, f32[16,3,256]{2,1,0:T(4,128)S(1)}, u32[]{:S(2)}, u32[]{:S(2)}) collective-permute-start(f32[16,3,256]{2,1,0:T(4,128)S(1)} %get-tuple-element.31), channel_id=1, source_target_pairs={{0,2},{1,3},{2,0},{3,1},{4,6},{5,7},{6,4},{7,5},{8,16},{9,17},{10,... | collective-permute-start | bytes 147464 | tf_op jit(solution)/shard_map/ppermute | solution.py:118
  12.8 0.7 pad_add_fusion.near_ref
  13.5 5.8 %collective-permute-done.4.refs_2_.p2 = bf16[8,64,256]{2,1,0:T(8,128)(2,1)S(1)} collective-permute-done((bf16[8,64,256]{2,1,0:T(8,128)(2,1)S(1)}, bf16[8,64,256]{2,1,0:T(8,128)(2,1)S(1)}, u32[]{:S(2)}, u32[]{:S(2)}) %collective-permute-start.4) | collective-permute-done | bytes 262176 | tf_op jit(solution)/shard_map/ppermute | solution.py:119
  19.3 0.6 shard_map.75
  20.0 2.9 %collective-permute-start.7 = (bf16[16,64,256]{2,1,0:T(8,128)(2,1)S(1)}, bf16[16,64,256]{2,1,0:T(8,128)(2,1)S(1)}, u32[]{:S(2)}, u32[]{:S(2)}) collective-permute-start(bf16[16,64,256]{2,1,0:T(8,128)(2,1)S(1)} %get-tuple-element.36), channel_id=1, source_target_pairs={{0,2},{1,3},{2,0},{3,1},{4,6},{5,7},{6,4},{7,5},{8,16},{9,17},{10,... | collective-permute-start | bytes 1572872 | tf_op jit(solution)/shard_map/ppermute | solution.py:118
  22.9 8.4 %shard_map.74 = (bf16[4,4096,256]{2,1,0:T(8,128)(2,1)S(1)}, bf16[4,4096,256]{2,1,0:T(8,128)(2,1)S(1)}, f32[8,256]{1,0:T(8,128)S(1)}, bf16[64,256,48]{2,1,0:T(8,1...) custom-call(s32[272]{0:T(512)S(1)} %pad_add_fusion.near_ref, s32[6]{0:T(128)S(1)} %stack.19.meta_ref, ...), custom_call_target="tpu_custom_call" | custom-call | flops 4294967296 | bytes 1048576 | tf_op jit(solution)/shard_map/pallas_call | solution.py:321
  31.4 6.1 %shard_map.76 = (bf16[4,4096,256]{2,1,0:T(8,128)(2,1)S(1)}, bf16[4,4096,256]{2,1,0:T(8,128)(2,1)S(1)}, f32[8,256]{1,0:T(8,128)S(1)}) custom-call(s32[272]{0:T(512)S(1)} %pad_add_fusion.near_ref, bf16[64,256,48]{2,1,0:T(8,128)(2,1)S(1)} %get-tuple-element.39.source, bf16[16,48,256]{2,1,0:T(8,128)(2,1)S(1)} %get-tuple-element.40.target), custom_call_target="tpu_custom_call" | custom-call | flops 4294967296 | bytes 1048576 | tf_op jit(solution)/shard_map/pallas_call | solution.py:321
  37.6 4.7 %shard_map.77 = (bf16[8,64,256]{2,1,0:T(8,128)(2,1)S(1)}, bf16[64,64,256]{2,1,0:T(8,128)(2,1)S(1)}) custom-call(s32[272]{0:T(512)S(1)} %pad_add_fusion.near_ref, s32[6]{0:T(128)S(1)} %stack.19.meta_ref, bf16[8,64,256]{2,1,0:T(8,128)(2,1)S(1)} %get-tuple-element.33.refs_0_.p0, bf16[8,64,256]{2,1,0:T(8,128)(2,1)S(1)} %get-tuple-element.34.refs_1_.p1, ...), custom_call_target="tpu_custom_call" | custom-call | flops 2147483648 | bytes 1048576 | tf_op jit(solution)/shard_map/pallas_call | solution.py:321
  42.3 4.6 %shard_map.78.refs_0_.p0 = bf16[8,64,256]{2,1,0:T(8,128)(2,1)S(1)} custom-call(s32[272]{0:T(512)S(1)} %pad_add_fusion.near_ref, s32[6]{0:T(128)S(1)} %stack.19.meta_ref, bf16[64,64,256]{2,1,0:T(8,128)(2,1)S(1)} %get-tuple-element.45.species, bf16[4,4096,256]{2,1,0:T(8,128)(2,1)S(1)} %get-tuple-element.37.w0, bf16[4,4096,256]{2,1,0:T(8,128)(2,1)S(1)} %get-tuple-element.38.w1, ...), custom_call_target="tpu_custom_call" | custom-call | flops 2147483648 | bytes 1048576 | tf_op jit(solution)/shard_map/pallas_call | solution.py:321
  46.9 1.6 %collective-permute-start.8 = (bf16[8,64,256]{2,1,0:T(8,128)(2,1)S(1)}, bf16[8,64,256]{2,1,0:T(8,128)(2,1)S(1)}, u32[]{:S(2)}, u32[]{:S(2)}) collective-permute-start(bf16[8,64,256]{2,1,0:T(8,128)(2,1)S(1)} %shard_map.78.refs_0_.p0), channel_id=1, source_target_pairs={{0,1},{1,0},{2,3},{3,2},{4,5},{5,4},{6,7},{7,6},{8,9},{9,8},{10,11... | collective-permute-start | bytes 786440 | tf_op jit(solution)/shard_map/ppermute | solution.py:119
  48.5 0.6 shard_map.79
  49.6 1.6 %collective-permute-start.12 = (bf16[8,64,256]{2,1,0:T(8,128)(2,1)S(1)}, bf16[8,64,256]{2,1,0:T(8,128)(2,1)S(1)}, u32[]{:S(2)}, u32[]{:S(2)}) collective-permute-start(bf16[8,64,256]{2,1,0:T(8,128)(2,1)S(1)} %get-tuple-element.49), channel_id=1, source_target_pairs={{0,2},{1,3},{2,0},{3,1},{4,6},{5,7},{6,4},{7,5},{8,16},{9,17},{10,... | collective-permute-start | bytes 786440 | tf_op jit(solution)/shard_map/ppermute | solution.py:118
  51.2 8.7 %collective-permute-done.8.refs_0_.p2 = bf16[8,64,256]{2,1,0:T(8,128)(2,1)S(1)} collective-permute-done((bf16[8,64,256]{2,1,0:T(8,128)(2,1)S(1)}, bf16[8,64,256]{2,1,0:T(8,128)(2,1)S(1)}, u32[]{:S(2)}, u32[]{:S(2)}) %collective-permute-start.8) | collective-permute-done | bytes 262176 | tf_op jit(solution)/shard_map/ppermute | solution.py:119
  59.9 0.6 shard_map.80
  60.5 1.7 %collective-permute-start.13 = (bf16[8,64,256]{2,1,0:T(8,128)(2,1)S(1)}, bf16[8,64,256]{2,1,0:T(8,128)(2,1)S(1)}, u32[]{:S(2)}, u32[]{:S(2)}) collective-permute-start(bf16[8,64,256]{2,1,0:T(8,128)(2,1)S(1)} %get-tuple-element.50), channel_id=1, source_target_pairs={{0,2},{1,3},{2,0},{3,1},{4,6},{5,7},{6,4},{7,5},{8,16},{9,17},{10,... | collective-permute-start | bytes 786440 | tf_op jit(solution)/shard_map/ppermute | solution.py:118
  62.3 4.7 %collective-permute-done.13.p7 = bf16[8,64,256]{2,1,0:T(8,128)(2,1)S(1)} collective-permute-done((bf16[8,64,256]{2,1,0:T(8,128)(2,1)S(1)}, bf16[8,64,256]{2,1,0:T(8,128)(2,1)S(1)}, u32[]{:S(2)}, u32[]{:S(2)}) %collective-permute-start.13) | collective-permute-done | bytes 262176 | tf_op jit(solution)/shard_map/ppermute | solution.py:118
  67.0 8.6 %shard_map.81 = bf16[16,64,256]{2,1,0:T(8,128)(2,1)S(1)} custom-call(s32[272]{0:T(512)S(1)} %pad_add_fusion.near_ref, s32[16]{0:T(128)S(1)} %get-tuple-element.32.row_ref, bf16[8,64,256]{2,1,0:T(8,128)(2,1)S(1)} %shard_map.78.refs_0_.p0, bf16[8,64,256]{2,1,0:T(8,128)(2,1)S(1)} %get-tuple-element.46.refs_1_.p1, ...), custom_call_target="tpu_custom_call" | custom-call | flops 4294967296 | bytes 1048576 | tf_op jit(solution)/shard_map/pallas_call | solution.py:321
  75.6 19.8 %all_to_all.5 = bf16[16,64,256]{2,1,0:T(8,128)(2,1)S(1)} all-to-all(bf16[16,64,256]{2,1,0:T(8,128)(2,1)S(1)} %shard_map.81), channel_id=1, replica_groups=mesh['gx'=4,'gy'=8] {'gy'}, dimensions={0} | all-to-all | bytes 1048576 | tf_op jit(solution)/shard_map/all_to_all | solution.py:443
  95.4 0.8 copy.9
  (29 shorter events, 2.1 us)
Async XLA Ops:
  0.1 0.8 copy-start.1
  2.6 6.9 %collective-permute-start = (f32[8,3,256]{2,1,0:T(4,128)S(1)}, f32[8,3,256]{2,1,0:T(4,128)S(1)}, u32[]{:S(2)}, u32[]{:S(2)}) collective-permute-start(f32[8,3,256]{2,1,0:T(4,128)S(1)} %get-tuple-element.28.refs_0_.o0), channel_id=1, source_target_pairs={{0,1},{1,0},{2,3},{3,2},{4,5},{5,4},{6,7},{7,6},{8,9},{9,8},{10,11... | collective-permute-start | bytes 73736 | tf_op jit(solution)/shard_map/ppermute | solution.py:119
  5.6 3.9 %collective-permute-start.1 = (f32[8,3,256]{2,1,0:T(4,128)S(1)}, f32[8,3,256]{2,1,0:T(4,128)S(1)}, u32[]{:S(2)}, u32[]{:S(2)}) collective-permute-start(f32[8,3,256]{2,1,0:T(4,128)S(1)} %get-tuple-element.29.refs_1_.o1), channel_id=1, source_target_pairs={{0,8},{1,2},{2,1},{3,4},{4,3},{5,6},{6,5},{7,15},{8,0},{9,10},{10,... | collective-permute-start | bytes 73736 | tf_op jit(solution)/shard_map/ppermute | solution.py:118
  5.6 13.7 %collective-permute-start.4 = (bf16[8,64,256]{2,1,0:T(8,128)(2,1)S(1)}, bf16[8,64,256]{2,1,0:T(8,128)(2,1)S(1)}, u32[]{:S(2)}, u32[]{:S(2)}) collective-permute-start(bf16[8,64,256]{2,1,0:T(8,128)(2,1)S(1)} %get-tuple-element.33.refs_0_.p0), channel_id=1, source_target_pairs={{0,1},{1,0},{2,3},{3,2},{4,5},{5,4},{6,7},{7,6},{8,9},{9,8},{10,11... | collective-permute-start | bytes 786440 | tf_op jit(solution)/shard_map/ppermute | solution.py:119
  8.6 10.6 %collective-permute-start.5 = (bf16[8,64,256]{2,1,0:T(8,128)(2,1)S(1)}, bf16[8,64,256]{2,1,0:T(8,128)(2,1)S(1)}, u32[]{:S(2)}, u32[]{:S(2)}) collective-permute-start(bf16[8,64,256]{2,1,0:T(8,128)(2,1)S(1)} %get-tuple-element.34.refs_1_.p1), channel_id=1, source_target_pairs={{0,8},{1,2},{2,1},{3,4},{4,3},{5,6},{6,5},{7,15},{8,0},{9,10},{10,... | collective-permute-start | bytes 786440 | tf_op jit(solution)/shard_map/ppermute | solution.py:118
  10.1 12.8 %collective-permute-start.2 = (f32[16,3,256]{2,1,0:T(4,128)S(1)}, f32[16,3,256]{2,1,0:T(4,128)S(1)}, u32[]{:S(2)}, u32[]{:S(2)}) collective-permute-start(f32[16,3,256]{2,1,0:T(4,128)S(1)} %get-tuple-element.30), channel_id=1, source_target_pairs={{0,8},{1,9},{2,10},{3,11},{4,12},{5,13},{6,14},{7,15},{8,0},{9,1},... | collective-permute-start | bytes 147464 | tf_op jit(solution)/shard_map/ppermute | solution.py:119
  10.7 12.3 %collective-permute-start.3 = (f32[16,3,256]{2,1,0:T(4,128)S(1)}, f32[16,3,256]{2,1,0:T(4,128)S(1)}, u32[]{:S(2)}, u32[]{:S(2)}) collective-permute-start(f32[16,3,256]{2,1,0:T(4,128)S(1)} %get-tuple-element.31), channel_id=1, source_target_pairs={{0,2},{1,3},{2,0},{3,1},{4,6},{5,7},{6,4},{7,5},{8,16},{9,17},{10,... | collective-permute-start | bytes 147464 | tf_op jit(solution)/shard_map/ppermute | solution.py:118
  19.9 17.6 %collective-permute-start.6 = (bf16[16,64,256]{2,1,0:T(8,128)(2,1)S(1)}, bf16[16,64,256]{2,1,0:T(8,128)(2,1)S(1)}, u32[]{:S(2)}, u32[]{:S(2)}) collective-permute-start(bf16[16,64,256]{2,1,0:T(8,128)(2,1)S(1)} %get-tuple-element.35), channel_id=1, source_target_pairs={{0,8},{1,9},{2,10},{3,11},{4,12},{5,13},{6,14},{7,15},{8,0},{9,1},... | collective-permute-start | bytes 1572872 | tf_op jit(solution)/shard_map/ppermute | solution.py:119
  20.0 17.6 %collective-permute-start.7 = (bf16[16,64,256]{2,1,0:T(8,128)(2,1)S(1)}, bf16[16,64,256]{2,1,0:T(8,128)(2,1)S(1)}, u32[]{:S(2)}, u32[]{:S(2)}) collective-permute-start(bf16[16,64,256]{2,1,0:T(8,128)(2,1)S(1)} %get-tuple-element.36), channel_id=1, source_target_pairs={{0,2},{1,3},{2,0},{3,1},{4,6},{5,7},{6,4},{7,5},{8,16},{9,17},{10,... | collective-permute-start | bytes 1572872 | tf_op jit(solution)/shard_map/ppermute | solution.py:118
  31.4 6.2 %copy-start = (f32[16,256]{1,0:T(8,128)S(1)}, f32[16,256]{1,0:T(8,128)}, u32[]{:S(2)}) copy-start(f32[16,256]{1,0:T(8,128)} %t.5) | copy-start | bytes 49156
  31.4 6.2 %copy-start.2 = (f32[32]{0:T(128)S(1)}, f32[32]{0:T(128)}, u32[]{:S(2)}) copy-start(f32[32]{0:T(128)} %param.10) | copy-start | bytes 388
  31.4 6.2 %copy-start.3 = (f32[32]{0:T(128)S(1)}, f32[32]{0:T(128)}, u32[]{:S(2)}) copy-start(f32[32]{0:T(128)} %param.11) | copy-start | bytes 388
  46.9 13.0 %collective-permute-start.8 = (bf16[8,64,256]{2,1,0:T(8,128)(2,1)S(1)}, bf16[8,64,256]{2,1,0:T(8,128)(2,1)S(1)}, u32[]{:S(2)}, u32[]{:S(2)}) collective-permute-start(bf16[8,64,256]{2,1,0:T(8,128)(2,1)S(1)} %shard_map.78.refs_0_.p0), channel_id=1, source_target_pairs={{0,1},{1,0},{2,3},{3,2},{4,5},{5,4},{6,7},{7,6},{8,9},{9,8},{10,11... | collective-permute-start | bytes 786440 | tf_op jit(solution)/shard_map/ppermute | solution.py:119
  48.5 11.4 %collective-permute-start.9 = (bf16[8,64,256]{2,1,0:T(8,128)(2,1)S(1)}, bf16[8,64,256]{2,1,0:T(8,128)(2,1)S(1)}, u32[]{:S(2)}, u32[]{:S(2)}) collective-permute-start(bf16[8,64,256]{2,1,0:T(8,128)(2,1)S(1)} %get-tuple-element.46.refs_1_.p1), channel_id=1, source_target_pairs={{0,8},{1,2},{2,1},{3,4},{4,3},{5,6},{6,5},{7,15},{8,0},{9,10},{10,... | collective-permute-start | bytes 786440 | tf_op jit(solution)/shard_map/ppermute | solution.py:118
  49.1 13.2 %collective-permute-start.10 = (bf16[8,64,256]{2,1,0:T(8,128)(2,1)S(1)}, bf16[8,64,256]{2,1,0:T(8,128)(2,1)S(1)}, u32[]{:S(2)}, u32[]{:S(2)}) collective-permute-start(bf16[8,64,256]{2,1,0:T(8,128)(2,1)S(1)} %get-tuple-element.47), channel_id=1, source_target_pairs={{0,8},{1,9},{2,10},{3,11},{4,12},{5,13},{6,14},{7,15},{8,0},{9,1},... | collective-permute-start | bytes 786440 | tf_op jit(solution)/shard_map/ppermute | solution.py:119
  49.6 12.7 %collective-permute-start.12 = (bf16[8,64,256]{2,1,0:T(8,128)(2,1)S(1)}, bf16[8,64,256]{2,1,0:T(8,128)(2,1)S(1)}, u32[]{:S(2)}, u32[]{:S(2)}) collective-permute-start(bf16[8,64,256]{2,1,0:T(8,128)(2,1)S(1)} %get-tuple-element.49), channel_id=1, source_target_pairs={{0,2},{1,3},{2,0},{3,1},{4,6},{5,7},{6,4},{7,5},{8,16},{9,17},{10,... | collective-permute-start | bytes 786440 | tf_op jit(solution)/shard_map/ppermute | solution.py:118
  60.5 1.8 %collective-permute-start.11 = (bf16[8,64,256]{2,1,0:T(8,128)(2,1)S(1)}, bf16[8,64,256]{2,1,0:T(8,128)(2,1)S(1)}, u32[]{:S(2)}, u32[]{:S(2)}) collective-permute-start(bf16[8,64,256]{2,1,0:T(8,128)(2,1)S(1)} %get-tuple-element.48), channel_id=1, source_target_pairs={{0,8},{1,9},{2,10},{3,11},{4,12},{5,13},{6,14},{7,15},{8,0},{9,1},... | collective-permute-start | bytes 786440 | tf_op jit(solution)/shard_map/ppermute | solution.py:119
  60.5 6.4 %collective-permute-start.13 = (bf16[8,64,256]{2,1,0:T(8,128)(2,1)S(1)}, bf16[8,64,256]{2,1,0:T(8,128)(2,1)S(1)}, u32[]{:S(2)}, u32[]{:S(2)}) collective-permute-start(bf16[8,64,256]{2,1,0:T(8,128)(2,1)S(1)} %get-tuple-element.50), channel_id=1, source_target_pairs={{0,2},{1,3},{2,0},{3,1},{4,6},{5,7},{6,4},{7,5},{8,16},{9,17},{10,... | collective-permute-start | bytes 786440 | tf_op jit(solution)/shard_map/ppermute | solution.py:118

commit v5 on v4

--- a/solution.py
+++ b/solution.py
@@ -18,6 +18,7 @@
 SCALE = math.sqrt(inverse_width * math.log2(math.e))
 FAR = -1e30
 FEATURES = 48
+
 
 f32 = jnp.float32
 bf16 = jnp.bfloat16
@@ -294,21 +295,61 @@
     step_columns(near_ref, species, gathered, (w0, w1, w2, w3), (i0, i1), (t, a, o), low, out)
 
 
-def last_step(near_ref, row_ref, p0, p1, p2, p3, p4, p5, p6, p7, w0, w1, w2, w3, i0, i1, t, a, o, out, species, gathered):
-    join((p0, p1, p2, p3, p4, p5, p6, p7), species)
-    if out.shape[0] > BX * BY:
-        out[...] = jnp.zeros_like(out)
-    factor, onset = column(a), column(o)
-    for g, w_ref in enumerate((w0, w1, w2, w3)):
+def deliver(tables, species, gathered, staged, w_refs, inv_refs, consts, first, outs):
+    near_ref, meta_ref, row_ref = tables
+    kelvin_ref, factor_ref, onset_ref = consts
+    factor, onset = column(factor_ref), column(onset_ref)
+    lane = meta_ref[1] // BY
+    if 2 * staged.shape[0] > BX * BY:
+        staged[...] = jnp.zeros_like(staged)
+    for g, w_ref in enumerate(w_refs):
 
         def one(c, _, g=g, w_ref=w_ref):
             b = g * BY + c
-            mixed = mix(near_ref, species, gathered, w_ref[c], b)
-            mixed = mixed * inverse_of((i0, i1), g, c)
-            out[row_ref[b]] = react(mixed, t[pl.ds(b, 1)], factor, onset)
+            row = row_ref[b]
+            way = ((row // CAP) ^ lane) - first
+
+            @pl.when((way >= 0) & (way < len(outs)))
+            def _():
+                mixed = mix(near_ref, species, gathered, w_ref[c], b)
+                mixed = mixed * inverse_of(inv_refs, g, c)
+                moved = react(mixed, kelvin_ref[pl.ds(b, 1)], factor, onset)
+                staged[way * CAP + row % CAP] = moved
+
             return 0
 
         lax.fori_loop(0, BY, one, 0)
+    for i, out in enumerate(outs):
+        out[...] = staged[i * CAP : (i + 1) * CAP]
+
+
+def last_far(near_ref, meta_ref, row_ref, *refs):
+    pieces, rest = refs[:8], refs[8:]
+    w, inv, consts, rest = rest[:4], rest[4:6], rest[6:9], rest[9:]
+    outs, (species, gathered, staged) = rest[:-3], rest[-3:]
+    join(pieces, species)
+    tables = (near_ref, meta_ref, row_ref)
+    deliver(tables, species, gathered, staged, w, inv, consts, len(outs), outs)
+
+
+def last_near(near_ref, meta_ref, row_ref, species, *refs):
+    w, inv, consts, rest = refs[:4], refs[4:6], refs[6:9], refs[9:]
+    outs, (gathered, staged) = rest[:-2], rest[-2:]
+    tables = (near_ref, meta_ref, row_ref)
+    deliver(tables, species, gathered, staged, w, inv, consts, 0, outs)
+
+
+def place(meta_ref, *refs):
+    blocks, (out, sem) = refs[:-2], refs[-2:]
+    lane = meta_ref[1] // BY
+    copies = [
+        pltpu.make_async_copy(x, out.at[pl.ds((lane ^ way) * CAP, CAP)], sem.at[way])
+        for way, x in enumerate(blocks)
+    ]
+    for copy in copies:
+        copy.start()
+    for copy in copies:
+        copy.wait()
 
 
 VM = pl.BlockSpec(memory_space=pltpu.VMEM)
@@ -432,15 +473,38 @@
     own_bands = rows(own)
     corners = rows(sides)
     pieces = own + sides + (own_bands[0], corners[0], own_bands[1], corners[1])
-    packed = call(
-        last_step,
-        (near, row) + pieces + built,
-        2,
-        jax.ShapeDtypeStruct((lane_count * CAP, kinds, parts), bf16),
-        [all_species, gathered],
-        work,
-    )
-    return lax.all_to_all(packed, "gy", split_axis=0, concat_axis=0, tiled=True)
+    half_lanes = lane_count // 2
+    block = pltpu.VMEM((CAP, kinds, parts), bf16)
+    staged = pltpu.VMEM((half_lanes * CAP, kinds, parts), bf16)
+    *far, species = call(
+        last_far,
+        (near, meta, row) + pieces + built,
+        3,
+        [block] * half_lanes + [all_species],
+        [gathered, staged],
+        work // 2,
+    )
+    close = call(
+        last_near,
+        (near, meta, row, species) + built,
+        3,
+        [block] * half_lanes,
+        [gathered, staged],
+        work // 2,
+    )
+    blocks = list(close) + far
+    for way in list(range(half_lanes, lane_count)) + list(range(1, half_lanes)):
+        pairs = [(l, l ^ way) for l in range(lane_count)]
+        blocks[way] = lax.ppermute(blocks[way], "gy", pairs)
+    return pl.pallas_call(
+        place,
+        out_shape=jax.ShapeDtypeStruct((lane_count * CAP, kinds, parts), bf16),
+        in_specs=[SM] + [VM] * lane_count,
+        out_specs=HBM,
+        scratch_shapes=[pltpu.SemaphoreType.DMA((lane_count,))],
+        compiler_params=pltpu.CompilerParams(vmem_limit_bytes=8 << 20),
+        name="place",
+    )(meta, *blocks)
 
 
 def solution(mesh):

time: 96.5 us -> 96 us (level)
  the two profiles are of different devices: /device:TPU:0 before, /device:TPU:9 now
where the time goes in v5:
time: 96 us; the launch traced here: 95.7 us
  Pallas kernels  39.2 us (41%)
  waiting for transfers between devices  30.8 us (32%)
  starting transfers between devices  23.1 us (24%)
  other arithmetic  1.45 us (2%)
  local copies, waits for them, and re-layouts  0.98 us (1%)
    pallas_call x10, Pallas kernels, call(): pl.pallas_call(kernel, out_shape=outs, in_specs=[SM] * scalars + [VM] * (...  36.1 us
    ppermute x7, waiting for transfers between devices, swap(): from_a = lax.ppermute(by_a, axis, pairs_a)  15.6 us
    ppermute x7, waiting for transfers between devices, body(): blocks[way] = lax.ppermute(blocks[way], 'gy', pairs)  10.3 us
    ppermute x7, starting transfers between devices, swap(): from_a = lax.ppermute(by_a, axis, pairs_a)  10.2 us
    ppermute x7, starting transfers between devices, body(): blocks[way] = lax.ppermute(blocks[way], 'gy', pairs)  8.51 us
    ppermute x7, waiting for transfers between devices, swap(): from_b = lax.ppermute(by_b, axis, pairs_b)  4.98 us
    ppermute x7, starting transfers between devices, swap(): from_b = lax.ppermute(by_b, axis, pairs_b)  4.37 us
  transfers between devices with their start and end apart: 21, of which 9 were waited for; matrix products, arithmetic and copies ran while one was open for 2% of the time, Pallas kernels for 18%

profile of v5, /device:TPU:9, one launch (start us, length us, event | category | flops | bytes accessed | tf_op | source)
XLA Modules:
  0.0 95.7 jit_solution(17267812851935712502)
XLA Ops:
  0.9 1.7 %split.1 = (bf16[8,64,256]{2,1,0:T(8,128)(2,1)S(1)}, bf16[8,64,256]{2,1,0:T(8,128)(2,1)S(1)}, f32[8,3,256]{2,1,0:T(4,128)S(1)}, f32[8,3,256]{2,1,0:T(4,128)S(1)}) custom-call(s32[6]{0:T(128)S(1)} %stack.19.meta_ref, bf16[16,64,256]{2,1,0:T(8,128)(2,1)} %x.1, f32[3,16,256]{2,1,0:T(8,128)S(1)} %bitcast.8), custom_call_target="tpu_custom_call" | custom-call | tf_op jit(solution)/shard_map/split/pallas_call | solution.py:402
  2.6 1.3 %collective-permute-start = (f32[8,3,256]{2,1,0:T(4,128)S(1)}, f32[8,3,256]{2,1,0:T(4,128)S(1)}, u32[]{:S(2)}, u32[]{:S(2)}) collective-permute-start(f32[8,3,256]{2,1,0:T(4,128)S(1)} %get-tuple-element.37.refs_0_.o0), channel_id=1, source_target_pairs={{0,1},{1,0},{2,3},{3,2},{4,5},{5,4},{6,7},{7,6},{8,9},{9,8},{10,11... | collective-permute-start | bytes 73736 | tf_op jit(solution)/shard_map/ppermute | solution.py:120
  3.8 2.5 %collective-permute-start.4 = (bf16[8,64,256]{2,1,0:T(8,128)(2,1)S(1)}, bf16[8,64,256]{2,1,0:T(8,128)(2,1)S(1)}, u32[]{:S(2)}, u32[]{:S(2)}) collective-permute-start(bf16[8,64,256]{2,1,0:T(8,128)(2,1)S(1)} %get-tuple-element.42.refs_0_.p0), channel_id=1, source_target_pairs={{0,1},{1,0},{2,3},{3,2},{4,5},{5,4},{6,7},{7,6},{8,9},{9,8},{10,11... | collective-permute-start | bytes 786440 | tf_op jit(solution)/shard_map/ppermute | solution.py:120
  8.1 2.2 %collective-permute-start.2 = (f32[16,3,256]{2,1,0:T(4,128)S(1)}, f32[16,3,256]{2,1,0:T(4,128)S(1)}, u32[]{:S(2)}, u32[]{:S(2)}) collective-permute-start(f32[16,3,256]{2,1,0:T(4,128)S(1)} %get-tuple-element.39), channel_id=1, source_target_pairs={{0,8},{1,9},{2,10},{3,11},{4,12},{5,13},{6,14},{7,15},{8,0},{9,1},... | collective-permute-start | bytes 147464 | tf_op jit(solution)/shard_map/ppermute | solution.py:120
  10.3 1.2 %collective-permute-start.3 = (f32[16,3,256]{2,1,0:T(4,128)S(1)}, f32[16,3,256]{2,1,0:T(4,128)S(1)}, u32[]{:S(2)}, u32[]{:S(2)}) collective-permute-start(f32[16,3,256]{2,1,0:T(4,128)S(1)} %get-tuple-element.40), channel_id=1, source_target_pairs={{0,2},{1,3},{2,0},{3,1},{4,6},{5,7},{6,4},{7,5},{8,16},{9,17},{10,... | collective-permute-start | bytes 147464 | tf_op jit(solution)/shard_map/ppermute | solution.py:119
  12.2 6.0 %collective-permute-done.4.refs_2_.p2 = bf16[8,64,256]{2,1,0:T(8,128)(2,1)S(1)} collective-permute-done((bf16[8,64,256]{2,1,0:T(8,128)(2,1)S(1)}, bf16[8,64,256]{2,1,0:T(8,128)(2,1)S(1)}, u32[]{:S(2)}, u32[]{:S(2)}) %collective-permute-start.4) | collective-permute-done | bytes 262176 | tf_op jit(solution)/shard_map/ppermute | solution.py:120
  18.9 1.6 %collective-permute-start.6 = (bf16[16,64,256]{2,1,0:T(8,128)(2,1)S(1)}, bf16[16,64,256]{2,1,0:T(8,128)(2,1)S(1)}, u32[]{:S(2)}, u32[]{:S(2)}) collective-permute-start(bf16[16,64,256]{2,1,0:T(8,128)(2,1)S(1)} %get-tuple-element.44), channel_id=1, source_target_pairs={{0,8},{1,9},{2,10},{3,11},{4,12},{5,13},{6,14},{7,15},{8,0},{9,1},... | collective-permute-start | bytes 1572872 | tf_op jit(solution)/shard_map/ppermute | solution.py:120
  20.5 1.2 %collective-permute-start.7 = (bf16[16,64,256]{2,1,0:T(8,128)(2,1)S(1)}, bf16[16,64,256]{2,1,0:T(8,128)(2,1)S(1)}, u32[]{:S(2)}, u32[]{:S(2)}) collective-permute-start(bf16[16,64,256]{2,1,0:T(8,128)(2,1)S(1)} %get-tuple-element.45), channel_id=1, source_target_pairs={{0,2},{1,3},{2,0},{3,1},{4,6},{5,7},{6,4},{7,5},{8,16},{9,17},{10,... | collective-permute-start | bytes 1572872 | tf_op jit(solution)/shard_map/ppermute | solution.py:119
  21.7 8.4 %shard_map.74 = (bf16[4,4096,256]{2,1,0:T(8,128)(2,1)S(1)}, bf16[4,4096,256]{2,1,0:T(8,128)(2,1)S(1)}, f32[8,256]{1,0:T(8,128)S(1)}, bf16[64,256,48]{2,1,0:T(8,1...) custom-call(s32[272]{0:T(512)S(1)} %pad_add_fusion.near_ref, s32[6]{0:T(128)S(1)} %stack.19.meta_ref, ...), custom_call_target="tpu_custom_call" | custom-call | flops 4294967296 | bytes 1048576 | tf_op jit(solution)/shard_map/pallas_call | solution.py:362
  30.2 6.1 %shard_map.76 = (bf16[4,4096,256]{2,1,0:T(8,128)(2,1)S(1)}, bf16[4,4096,256]{2,1,0:T(8,128)(2,1)S(1)}, f32[8,256]{1,0:T(8,128)S(1)}) custom-call(s32[272]{0:T(512)S(1)} %pad_add_fusion.near_ref, bf16[64,256,48]{2,1,0:T(8,128)(2,1)S(1)} %get-tuple-element.48.source, bf16[16,48,256]{2,1,0:T(8,128)(2,1)S(1)} %get-tuple-element.49.target), custom_call_target="tpu_custom_call" | custom-call | flops 4294967296 | bytes 1048576 | tf_op jit(solution)/shard_map/pallas_call | solution.py:362
  36.4 4.7 %shard_map.77 = (bf16[8,64,256]{2,1,0:T(8,128)(2,1)S(1)}, bf16[64,64,256]{2,1,0:T(8,128)(2,1)S(1)}) custom-call(s32[272]{0:T(512)S(1)} %pad_add_fusion.near_ref, s32[6]{0:T(128)S(1)} %stack.19.meta_ref, bf16[8,64,256]{2,1,0:T(8,128)(2,1)S(1)} %get-tuple-element.42.refs_0_.p0, bf16[8,64,256]{2,1,0:T(8,128)(2,1)S(1)} %get-tuple-element.43.refs_1_.p1, ...), custom_call_target="tpu_custom_call" | custom-call | flops 2147483648 | bytes 1048576 | tf_op jit(solution)/shard_map/pallas_call | solution.py:362
  41.1 4.6 %shard_map.78.refs_0_ = bf16[8,64,256]{2,1,0:T(8,128)(2,1)S(1)} custom-call(s32[272]{0:T(512)S(1)} %pad_add_fusion.near_ref, s32[6]{0:T(128)S(1)} %stack.19.meta_ref, bf16[64,64,256]{2,1,0:T(8,128)(2,1)S(1)} %get-tuple-element.54.species, bf16[4,4096,256]{2,1,0:T(8,128)(2,1)S(1)} %get-tuple-element.46.w0.refs_8_.refs_0_, ...), custom_call_target="tpu_custom_call" | custom-call | flops 2147483648 | bytes 1048576 | tf_op jit(solution)/shard_map/pallas_call | solution.py:362
  45.7 1.3 %collective-permute-start.8 = (bf16[8,64,256]{2,1,0:T(8,128)(2,1)S(1)}, bf16[8,64,256]{2,1,0:T(8,128)(2,1)S(1)}, u32[]{:S(2)}, u32[]{:S(2)}) collective-permute-start(bf16[8,64,256]{2,1,0:T(8,128)(2,1)S(1)} %shard_map.78.refs_0_), channel_id=1, source_target_pairs={{0,1},{1,0},{2,3},{3,2},{4,5},{5,4},{6,7},{7,6},{8,9},{9,8},{10,11... | collective-permute-start | bytes 786440 | tf_op jit(solution)/shard_map/ppermute | solution.py:120
  49.5 9.3 %collective-permute-done.8.refs_0_.refs_2_ = bf16[8,64,256]{2,1,0:T(8,128)(2,1)S(1)} collective-permute-done((bf16[8,64,256]{2,1,0:T(8,128)(2,1)S(1)}, bf16[8,64,256]{2,1,0:T(8,128)(2,1)S(1)}, u32[]{:S(2)}, u32[]{:S(2)}) %collective-permute-start.8) | collective-permute-done | bytes 262176 | tf_op jit(solution)/shard_map/ppermute | solution.py:120
  59.5 1.2 %collective-permute-start.13 = (bf16[8,64,256]{2,1,0:T(8,128)(2,1)S(1)}, bf16[8,64,256]{2,1,0:T(8,128)(2,1)S(1)}, u32[]{:S(2)}, u32[]{:S(2)}) collective-permute-start(bf16[8,64,256]{2,1,0:T(8,128)(2,1)S(1)} %get-tuple-element.59), channel_id=1, source_target_pairs={{0,2},{1,3},{2,0},{3,1},{4,6},{5,7},{6,4},{7,5},{8,16},{9,17},{10,... | collective-permute-start | bytes 786440 | tf_op jit(solution)/shard_map/ppermute | solution.py:119
  61.0 4.6 %collective-permute-done.13.refs_7_ = bf16[8,64,256]{2,1,0:T(8,128)(2,1)S(1)} collective-permute-done((bf16[8,64,256]{2,1,0:T(8,128)(2,1)S(1)}, bf16[8,64,256]{2,1,0:T(8,128)(2,1)S(1)}, u32[]{:S(2)}, u32[]{:S(2)}) %collective-permute-start.13) | collective-permute-done | bytes 262176 | tf_op jit(solution)/shard_map/ppermute | solution.py:119
  65.6 4.9 %shard_map.81 = (bf16[2,64,256]{2,1,0:T(8,128)(2,1)S(1)}, bf16[2,64,256]{2,1,0:T(8,128)(2,1)S(1)}, bf16[2,64,256]{2,1,0:T(8,128)(2,1)S(1)}, bf16[2,64,256]{2,1,0:T(8,128)(2,1)S(1)}, bf16[64,64,256]{2,1,0:T(8,128)(2,1)S(1)}) custom-call(s32[272]{0:T(512)S(1)} %pad_add_fusion.near_ref, s32[6]{0:T(128)S(1)} %stack.19.meta_ref, ...), custom_call_target="tpu_custom_call" | custom-call | flops 2147483648 | bytes 1048576 | tf_op jit(solution)/shard_map/pallas_call | solution.py:362
  70.6 4.9 %shard_map.82 = (bf16[2,64,256]{2,1,0:T(8,128)(2,1)S(1)}, bf16[2,64,256]{2,1,0:T(8,128)(2,1)S(1)}, bf16[2,64,256]{2,1,0:T(8,128)(2,1)S(1)}, bf16[2,64,256]{2,1,0:T(8,128)(2,1)S(1)}) custom-call(s32[272]{0:T(512)S(1)} %pad_add_fusion.near_ref, s32[6]{0:T(128)S(1)} %stack.19.meta_ref, s32[16]{0:T(128)S(1)} %get-tuple-element.41.row_ref, ...), custom_call_target="tpu_custom_call" | custom-call | flops 2147483648 | bytes 1048576 | tf_op jit(solution)/shard_map/pallas_call | solution.py:362
  75.5 1.4 %collective-permute-start.14 = (bf16[2,64,256]{2,1,0:T(8,128)(2,1)S(1)}, bf16[2,64,256]{2,1,0:T(8,128)(2,1)S(1)}, u32[]{:S(2)}, u32[]{:S(2)}) collective-permute-start(bf16[2,64,256]{2,1,0:T(8,128)(2,1)S(1)} %get-tuple-element.62), channel_id=1, source_target_pairs={{0,1},{1,0},{2,3},{3,2},{4,5},{5,4},{6,7},{7,6},{8,9},{9,8},{10,11... | collective-permute-start | bytes 196616 | tf_op jit(solution)/shard_map/ppermute | solution.py:498
  78.2 2.9 %collective-permute-start.17 = (bf16[2,64,256]{2,1,0:T(8,128)(2,1)S(1)}, bf16[2,64,256]{2,1,0:T(8,128)(2,1)S(1)}, u32[]{:S(2)}, u32[]{:S(2)}) collective-permute-start(bf16[2,64,256]{2,1,0:T(8,128)(2,1)S(1)} %get-tuple-element.65), channel_id=1, source_target_pairs={{0,4},{1,5},{2,6},{3,7},{4,0},{5,1},{6,2},{7,3},{8,12},{9,13},{10,... | collective-permute-start | bytes 196616 | tf_op jit(solution)/shard_map/ppermute | solution.py:498
  84.3 4.2 %collective-permute-done.18.refs_5_ = bf16[2,64,256]{2,1,0:T(8,128)(2,1)S(1)} collective-permute-done((bf16[2,64,256]{2,1,0:T(8,128)(2,1)S(1)}, bf16[2,64,256]{2,1,0:T(8,128)(2,1)S(1)}, u32[]{:S(2)}, u32[]{:S(2)}) %collective-permute-start.18) | collective-permute-done | bytes 65568 | tf_op jit(solution)/shard_map/ppermute | solution.py:498
  88.5 2.7 %collective-permute-done.19.refs_6_ = bf16[2,64,256]{2,1,0:T(8,128)(2,1)S(1)} collective-permute-done((bf16[2,64,256]{2,1,0:T(8,128)(2,1)S(1)}, bf16[2,64,256]{2,1,0:T(8,128)(2,1)S(1)}, u32[]{:S(2)}, u32[]{:S(2)}) %collective-permute-start.19) | collective-permute-done | bytes 65568 | tf_op jit(solution)/shard_map/ppermute | solution.py:498
  91.2 3.1 %collective-permute-done.20.refs_7_ = bf16[2,64,256]{2,1,0:T(8,128)(2,1)S(1)} collective-permute-done((bf16[2,64,256]{2,1,0:T(8,128)(2,1)S(1)}, bf16[2,64,256]{2,1,0:T(8,128)(2,1)S(1)}, u32[]{:S(2)}, u32[]{:S(2)}) %collective-permute-start.20) | collective-permute-done | bytes 65568 | tf_op jit(solution)/shard_map/ppermute | solution.py:498
  94.3 1.4 %place.1 = bf16[16,64,256]{2,1,0:T(8,128)(2,1)} custom-call(s32[6]{0:T(128)S(1)} %stack.19.meta_ref, bf16[2,64,256]{2,1,0:T(8,128)(2,1)S(1)} %get-tuple-element.61.refs_0_, bf16[2,64,256]{2,1,0:T(8,128)(2,1)S(1)} %collective-permute-done.14.refs_1_, bf16[2,64,256]{2,1,0:T(8,128)(2,1)S(1)} %collective-permute-done.15.refs_2_, ...), custom_call_target="tpu_custom_call" | custom-call | tf_op jit(solution)/shard_map/place/pallas_call | solution.py:499
  (43 shorter events, 11.9 us)
Async XLA Ops:
  2.6 4.6 %collective-permute-start = (f32[8,3,256]{2,1,0:T(4,128)S(1)}, f32[8,3,256]{2,1,0:T(4,128)S(1)}, u32[]{:S(2)}, u32[]{:S(2)}) collective-permute-start(f32[8,3,256]{2,1,0:T(4,128)S(1)} %get-tuple-element.37.refs_0_.o0), channel_id=1, source_target_pairs={{0,1},{1,0},{2,3},{3,2},{4,5},{5,4},{6,7},{7,6},{8,9},{9,8},{10,11... | collective-permute-start | bytes 73736 | tf_op jit(solution)/shard_map/ppermute | solution.py:120
  3.8 3.7 %collective-permute-start.1 = (f32[8,3,256]{2,1,0:T(4,128)S(1)}, f32[8,3,256]{2,1,0:T(4,128)S(1)}, u32[]{:S(2)}, u32[]{:S(2)}) collective-permute-start(f32[8,3,256]{2,1,0:T(4,128)S(1)} %get-tuple-element.38.refs_1_.o1), channel_id=1, source_target_pairs={{0,8},{1,2},{2,1},{3,4},{4,3},{5,6},{6,5},{7,15},{8,0},{9,10},{10,... | collective-permute-start | bytes 73736 | tf_op jit(solution)/shard_map/ppermute | solution.py:119
  3.8 14.4 %collective-permute-start.4 = (bf16[8,64,256]{2,1,0:T(8,128)(2,1)S(1)}, bf16[8,64,256]{2,1,0:T(8,128)(2,1)S(1)}, u32[]{:S(2)}, u32[]{:S(2)}) collective-permute-start(bf16[8,64,256]{2,1,0:T(8,128)(2,1)S(1)} %get-tuple-element.42.refs_0_.p0), channel_id=1, source_target_pairs={{0,1},{1,0},{2,3},{3,2},{4,5},{5,4},{6,7},{7,6},{8,9},{9,8},{10,11... | collective-permute-start | bytes 786440 | tf_op jit(solution)/shard_map/ppermute | solution.py:120
  6.3 11.9 %collective-permute-start.5 = (bf16[8,64,256]{2,1,0:T(8,128)(2,1)S(1)}, bf16[8,64,256]{2,1,0:T(8,128)(2,1)S(1)}, u32[]{:S(2)}, u32[]{:S(2)}) collective-permute-start(bf16[8,64,256]{2,1,0:T(8,128)(2,1)S(1)} %get-tuple-element.43.refs_1_.p1), channel_id=1, source_target_pairs={{0,8},{1,2},{2,1},{3,4},{4,3},{5,6},{6,5},{7,15},{8,0},{9,10},{10,... | collective-permute-start | bytes 786440 | tf_op jit(solution)/shard_map/ppermute | solution.py:119
  8.1 13.6 %collective-permute-start.2 = (f32[16,3,256]{2,1,0:T(4,128)S(1)}, f32[16,3,256]{2,1,0:T(4,128)S(1)}, u32[]{:S(2)}, u32[]{:S(2)}) collective-permute-start(f32[16,3,256]{2,1,0:T(4,128)S(1)} %get-tuple-element.39), channel_id=1, source_target_pairs={{0,8},{1,9},{2,10},{3,11},{4,12},{5,13},{6,14},{7,15},{8,0},{9,1},... | collective-permute-start | bytes 147464 | tf_op jit(solution)/shard_map/ppermute | solution.py:120
  10.3 11.3 %collective-permute-start.3 = (f32[16,3,256]{2,1,0:T(4,128)S(1)}, f32[16,3,256]{2,1,0:T(4,128)S(1)}, u32[]{:S(2)}, u32[]{:S(2)}) collective-permute-start(f32[16,3,256]{2,1,0:T(4,128)S(1)} %get-tuple-element.40), channel_id=1, source_target_pairs={{0,2},{1,3},{2,0},{3,1},{4,6},{5,7},{6,4},{7,5},{8,16},{9,17},{10,... | collective-permute-start | bytes 147464 | tf_op jit(solution)/shard_map/ppermute | solution.py:119
  18.9 17.5 %collective-permute-start.6 = (bf16[16,64,256]{2,1,0:T(8,128)(2,1)S(1)}, bf16[16,64,256]{2,1,0:T(8,128)(2,1)S(1)}, u32[]{:S(2)}, u32[]{:S(2)}) collective-permute-start(bf16[16,64,256]{2,1,0:T(8,128)(2,1)S(1)} %get-tuple-element.44), channel_id=1, source_target_pairs={{0,8},{1,9},{2,10},{3,11},{4,12},{5,13},{6,14},{7,15},{8,0},{9,1},... | collective-permute-start | bytes 1572872 | tf_op jit(solution)/shard_map/ppermute | solution.py:120
  20.5 15.8 %collective-permute-start.7 = (bf16[16,64,256]{2,1,0:T(8,128)(2,1)S(1)}, bf16[16,64,256]{2,1,0:T(8,128)(2,1)S(1)}, u32[]{:S(2)}, u32[]{:S(2)}) collective-permute-start(bf16[16,64,256]{2,1,0:T(8,128)(2,1)S(1)} %get-tuple-element.45), channel_id=1, source_target_pairs={{0,2},{1,3},{2,0},{3,1},{4,6},{5,7},{6,4},{7,5},{8,16},{9,17},{10,... | collective-permute-start | bytes 1572872 | tf_op jit(solution)/shard_map/ppermute | solution.py:119
  30.1 6.2 %copy-start = (f32[16,256]{1,0:T(8,128)S(1)}, f32[16,256]{1,0:T(8,128)}, u32[]{:S(2)}) copy-start(f32[16,256]{1,0:T(8,128)} %refs_6_.1) | copy-start | bytes 49156
  30.1 6.2 %copy-start.2 = (f32[32]{0:T(128)S(1)}, f32[32]{0:T(128)}, u32[]{:S(2)}) copy-start(f32[32]{0:T(128)} %param.10) | copy-start | bytes 388
  30.1 6.2 %copy-start.3 = (f32[32]{0:T(128)S(1)}, f32[32]{0:T(128)}, u32[]{:S(2)}) copy-start(f32[32]{0:T(128)} %param.11) | copy-start | bytes 388
  45.7 13.1 %collective-permute-start.8 = (bf16[8,64,256]{2,1,0:T(8,128)(2,1)S(1)}, bf16[8,64,256]{2,1,0:T(8,128)(2,1)S(1)}, u32[]{:S(2)}, u32[]{:S(2)}) collective-permute-start(bf16[8,64,256]{2,1,0:T(8,128)(2,1)S(1)} %shard_map.78.refs_0_), channel_id=1, source_target_pairs={{0,1},{1,0},{2,3},{3,2},{4,5},{5,4},{6,7},{7,6},{8,9},{9,8},{10,11... | collective-permute-start | bytes 786440 | tf_op jit(solution)/shard_map/ppermute | solution.py:120
  47.0 11.8 %collective-permute-start.9 = (bf16[8,64,256]{2,1,0:T(8,128)(2,1)S(1)}, bf16[8,64,256]{2,1,0:T(8,128)(2,1)S(1)}, u32[]{:S(2)}, u32[]{:S(2)}) collective-permute-start(bf16[8,64,256]{2,1,0:T(8,128)(2,1)S(1)} %get-tuple-element.55.refs_1_), channel_id=1, source_target_pairs={{0,8},{1,2},{2,1},{3,4},{4,3},{5,6},{6,5},{7,15},{8,0},{9,10},{10,... | collective-permute-start | bytes 786440 | tf_op jit(solution)/shard_map/ppermute | solution.py:119
  47.6 13.2 %collective-permute-start.10 = (bf16[8,64,256]{2,1,0:T(8,128)(2,1)S(1)}, bf16[8,64,256]{2,1,0:T(8,128)(2,1)S(1)}, u32[]{:S(2)}, u32[]{:S(2)}) collective-permute-start(bf16[8,64,256]{2,1,0:T(8,128)(2,1)S(1)} %get-tuple-element.56), channel_id=1, source_target_pairs={{0,8},{1,9},{2,10},{3,11},{4,12},{5,13},{6,14},{7,15},{8,0},{9,1},... | collective-permute-start | bytes 786440 | tf_op jit(solution)/shard_map/ppermute | solution.py:120
  48.8 12.0 %collective-permute-start.12 = (bf16[8,64,256]{2,1,0:T(8,128)(2,1)S(1)}, bf16[8,64,256]{2,1,0:T(8,128)(2,1)S(1)}, u32[]{:S(2)}, u32[]{:S(2)}) collective-permute-start(bf16[8,64,256]{2,1,0:T(8,128)(2,1)S(1)} %get-tuple-element.58), channel_id=1, source_target_pairs={{0,2},{1,3},{2,0},{3,1},{4,6},{5,7},{6,4},{7,5},{8,16},{9,17},{10,... | collective-permute-start | bytes 786440 | tf_op jit(solution)/shard_map/ppermute | solution.py:119
  59.4 1.6 %collective-permute-start.11 = (bf16[8,64,256]{2,1,0:T(8,128)(2,1)S(1)}, bf16[8,64,256]{2,1,0:T(8,128)(2,1)S(1)}, u32[]{:S(2)}, u32[]{:S(2)}) collective-permute-start(bf16[8,64,256]{2,1,0:T(8,128)(2,1)S(1)} %get-tuple-element.57), channel_id=1, source_target_pairs={{0,8},{1,9},{2,10},{3,11},{4,12},{5,13},{6,14},{7,15},{8,0},{9,1},... | collective-permute-start | bytes 786440 | tf_op jit(solution)/shard_map/ppermute | solution.py:120
  59.5 6.1 %collective-permute-start.13 = (bf16[8,64,256]{2,1,0:T(8,128)(2,1)S(1)}, bf16[8,64,256]{2,1,0:T(8,128)(2,1)S(1)}, u32[]{:S(2)}, u32[]{:S(2)}) collective-permute-start(bf16[8,64,256]{2,1,0:T(8,128)(2,1)S(1)} %get-tuple-element.59), channel_id=1, source_target_pairs={{0,2},{1,3},{2,0},{3,1},{4,6},{5,7},{6,4},{7,5},{8,16},{9,17},{10,... | collective-permute-start | bytes 786440 | tf_op jit(solution)/shard_map/ppermute | solution.py:119
  75.5 6.2 %collective-permute-start.14 = (bf16[2,64,256]{2,1,0:T(8,128)(2,1)S(1)}, bf16[2,64,256]{2,1,0:T(8,128)(2,1)S(1)}, u32[]{:S(2)}, u32[]{:S(2)}) collective-permute-start(bf16[2,64,256]{2,1,0:T(8,128)(2,1)S(1)} %get-tuple-element.62), channel_id=1, source_target_pairs={{0,1},{1,0},{2,3},{3,2},{4,5},{5,4},{6,7},{7,6},{8,9},{9,8},{10,11... | collective-permute-start | bytes 196616 | tf_op jit(solution)/shard_map/ppermute | solution.py:498
  76.9 5.9 %collective-permute-start.15 = (bf16[2,64,256]{2,1,0:T(8,128)(2,1)S(1)}, bf16[2,64,256]{2,1,0:T(8,128)(2,1)S(1)}, u32[]{:S(2)}, u32[]{:S(2)}) collective-permute-start(bf16[2,64,256]{2,1,0:T(8,128)(2,1)S(1)} %get-tuple-element.63), channel_id=1, source_target_pairs={{0,2},{1,3},{2,0},{3,1},{4,6},{5,7},{6,4},{7,5},{8,10},{9,11},{10,... | collective-permute-start | bytes 196616 | tf_op jit(solution)/shard_map/ppermute | solution.py:498
  78.1 5.9 %collective-permute-start.16 = (bf16[2,64,256]{2,1,0:T(8,128)(2,1)S(1)}, bf16[2,64,256]{2,1,0:T(8,128)(2,1)S(1)}, u32[]{:S(2)}, u32[]{:S(2)}) collective-permute-start(bf16[2,64,256]{2,1,0:T(8,128)(2,1)S(1)} %get-tuple-element.64), channel_id=1, source_target_pairs={{0,3},{1,2},{2,1},{3,0},{4,7},{5,6},{6,5},{7,4},{8,11},{9,10},{10,... | collective-permute-start | bytes 196616 | tf_op jit(solution)/shard_map/ppermute | solution.py:498
  78.2 6.1 %collective-permute-start.17 = (bf16[2,64,256]{2,1,0:T(8,128)(2,1)S(1)}, bf16[2,64,256]{2,1,0:T(8,128)(2,1)S(1)}, u32[]{:S(2)}, u32[]{:S(2)}) collective-permute-start(bf16[2,64,256]{2,1,0:T(8,128)(2,1)S(1)} %get-tuple-element.65), channel_id=1, source_target_pairs={{0,4},{1,5},{2,6},{3,7},{4,0},{5,1},{6,2},{7,3},{8,12},{9,13},{10,... | collective-permute-start | bytes 196616 | tf_op jit(solution)/shard_map/ppermute | solution.py:498
  81.1 7.4 %collective-permute-start.18 = (bf16[2,64,256]{2,1,0:T(8,128)(2,1)S(1)}, bf16[2,64,256]{2,1,0:T(8,128)(2,1)S(1)}, u32[]{:S(2)}, u32[]{:S(2)}) collective-permute-start(bf16[2,64,256]{2,1,0:T(8,128)(2,1)S(1)} %get-tuple-element.66), channel_id=1, source_target_pairs={{0,5},{1,4},{2,7},{3,6},{4,1},{5,0},{6,3},{7,2},{8,13},{9,12},{10,... | collective-permute-start | bytes 196616 | tf_op jit(solution)/shard_map/ppermute | solution.py:498
  81.7 9.6 %collective-permute-start.19 = (bf16[2,64,256]{2,1,0:T(8,128)(2,1)S(1)}, bf16[2,64,256]{2,1,0:T(8,128)(2,1)S(1)}, u32[]{:S(2)}, u32[]{:S(2)}) collective-permute-start(bf16[2,64,256]{2,1,0:T(8,128)(2,1)S(1)} %get-tuple-element.67), channel_id=1, source_target_pairs={{0,6},{1,7},{2,4},{3,5},{4,2},{5,3},{6,0},{7,1},{8,14},{9,15},{10,... | collective-permute-start | bytes 196616 | tf_op jit(solution)/shard_map/ppermute | solution.py:498
  82.8 11.5 %collective-permute-start.20 = (bf16[2,64,256]{2,1,0:T(8,128)(2,1)S(1)}, bf16[2,64,256]{2,1,0:T(8,128)(2,1)S(1)}, u32[]{:S(2)}, u32[]{:S(2)}) collective-permute-start(bf16[2,64,256]{2,1,0:T(8,128)(2,1)S(1)} %get-tuple-element.68), channel_id=1, source_target_pairs={{0,7},{1,6},{2,5},{3,4},{4,3},{5,2},{6,1},{7,0},{8,15},{9,14},{10,... | collective-permute-start | bytes 196616 | tf_op jit(solution)/shard_map/ppermute | solution.py:498
  (1 other events, 0.8 us)

commit v6 on v5

--- a/solution.py
+++ b/solution.py
@@ -273,15 +273,12 @@
     factor, onset = column(factor_ref), column(onset_ref)
     for g, w_ref in enumerate(w_refs):
 
-        def one(i, _, g=g, w_ref=w_ref):
+        for i in range(HALO):
             c = low + i
             b = g * BY + c
-            mixed = mix(near_ref, species, gathered, w_ref[c], b)
+            mixed = mix(near_ref, species, gathered.at[i], w_ref[c], b)
             mixed = mixed * inverse_of(inv_refs, g, c)
             out_ref[g * HALO + i] = react(mixed, kelvin_ref[pl.ds(b, 1)], factor, onset)
-            return 0
-
-        lax.fori_loop(0, HALO, one, 0)
 
 
 def step_b(near_ref, meta_ref, p0, p1, p2, p3, p4, p5, w0, w1, w2, w3, i0, i1, t, a, o, out, species, gathered):
@@ -295,48 +292,32 @@
     step_columns(near_ref, species, gathered, (w0, w1, w2, w3), (i0, i1), (t, a, o), low, out)
 
 
-def deliver(tables, species, gathered, staged, w_refs, inv_refs, consts, first, outs):
-    near_ref, meta_ref, row_ref = tables
-    kelvin_ref, factor_ref, onset_ref = consts
+def last_step(near_ref, meta_ref, row_ref, *refs):
+    pieces, refs = refs[:8], refs[8:]
+    w_refs, inv_refs, refs = refs[:4], refs[4:6], refs[6:]
+    (kelvin_ref, factor_ref, onset_ref), refs = refs[:3], refs[3:]
+    outs, (species, gathered, staged) = refs[:-3], refs[-3:]
+    join(pieces, species)
     factor, onset = column(factor_ref), column(onset_ref)
     lane = meta_ref[1] // BY
-    if 2 * staged.shape[0] > BX * BY:
+    if staged.shape[0] > BX * BY:
         staged[...] = jnp.zeros_like(staged)
     for g, w_ref in enumerate(w_refs):
 
-        def one(c, _, g=g, w_ref=w_ref):
-            b = g * BY + c
-            row = row_ref[b]
-            way = ((row // CAP) ^ lane) - first
-
-            @pl.when((way >= 0) & (way < len(outs)))
-            def _():
-                mixed = mix(near_ref, species, gathered, w_ref[c], b)
+        def some(j, _, g=g, w_ref=w_ref):
+            for i in range(HALO):
+                c = j * HALO + i
+                b = g * BY + c
+                row = row_ref[b]
+                mixed = mix(near_ref, species, gathered.at[i], w_ref[c], b)
                 mixed = mixed * inverse_of(inv_refs, g, c)
                 moved = react(mixed, kelvin_ref[pl.ds(b, 1)], factor, onset)
-                staged[way * CAP + row % CAP] = moved
-
+                staged[((row // CAP) ^ lane) * CAP + row % CAP] = moved
             return 0
 
-        lax.fori_loop(0, BY, one, 0)
+        lax.fori_loop(0, BY // HALO, some, 0)
     for i, out in enumerate(outs):
         out[...] = staged[i * CAP : (i + 1) * CAP]
-
-
-def last_far(near_ref, meta_ref, row_ref, *refs):
-    pieces, rest = refs[:8], refs[8:]
-    w, inv, consts, rest = rest[:4], rest[4:6], rest[6:9], rest[9:]
-    outs, (species, gathered, staged) = rest[:-3], rest[-3:]
-    join(pieces, species)
-    tables = (near_ref, meta_ref, row_ref)
-    deliver(tables, species, gathered, staged, w, inv, consts, len(outs), outs)
-
-
-def last_near(near_ref, meta_ref, row_ref, species, *refs):
-    w, inv, consts, rest = refs[:4], refs[4:6], refs[6:9], refs[9:]
-    outs, (gathered, staged) = rest[:-2], rest[-2:]
-    tables = (near_ref, meta_ref, row_ref)
-    deliver(tables, species, gathered, staged, w, inv, consts, 0, outs)
 
 
 def place(meta_ref, *refs):
@@ -438,7 +419,7 @@
     w_row = pltpu.VMEM((BY, neighbours * parts, parts), bf16)
     inv_half = pltpu.VMEM((bins // 2, parts), f32)
     half = pltpu.VMEM((SIDE, kinds, parts), bf16)
-    gathered = pltpu.VMEM((kinds, neighbours * parts), bf16)
+    gathered = pltpu.VMEM((HALO, kinds, neighbours * parts), bf16)
     all_species = pltpu.VMEM((EXT, kinds, parts), bf16)
     work = 2 * bins * neighbours * parts * parts * 128
     w0, w1, inv0, source, target, row = call(
@@ -473,27 +454,17 @@
     own_bands = rows(own)
     corners = rows(sides)
     pieces = own + sides + (own_bands[0], corners[0], own_bands[1], corners[1])
-    half_lanes = lane_count // 2
-    block = pltpu.VMEM((CAP, kinds, parts), bf16)
-    staged = pltpu.VMEM((half_lanes * CAP, kinds, parts), bf16)
-    *far, species = call(
-        last_far,
-        (near, meta, row) + pieces + built,
-        3,
-        [block] * half_lanes + [all_species],
-        [gathered, staged],
-        work // 2,
-    )
-    close = call(
-        last_near,
-        (near, meta, row, species) + built,
-        3,
-        [block] * half_lanes,
-        [gathered, staged],
-        work // 2,
-    )
-    blocks = list(close) + far
-    for way in list(range(half_lanes, lane_count)) + list(range(1, half_lanes)):
+    blocks = list(
+        call(
+            last_step,
+            (near, meta, row) + pieces + built,
+            3,
+            [pltpu.VMEM((CAP, kinds, parts), bf16)] * lane_count,
+            [all_species, gathered, pltpu.VMEM((lane_count * CAP, kinds, parts), bf16)],
+            work,
+        )
+    )
+    for way in range(lane_count - 1, 0, -1):
         pairs = [(l, l ^ way) for l in range(lane_count)]
         blocks[way] = lax.ppermute(blocks[way], "gy", pairs)
     return pl.pallas_call(

time: 96 us -> 91.9 us (0.957)
  Pallas kernels: 39.2 us -> 35.1 us
    pallas_call x10 -> x9, Pallas kernels: 36.1 us -> 32 us  [call(): pl.pallas_call(kernel, out_shape=outs, in_specs=[SM] * scalars + [VM] * (...]
where the time goes in v6:
time: 91.9 us; the launch traced here: 91.6 us
  Pallas kernels  35.1 us (38%)
  waiting for transfers between devices  30.8 us (34%)
  starting transfers between devices  23.2 us (25%)
  other arithmetic  1.45 us (2%)
  local copies, waits for them, and re-layouts  0.98 us (1%)
    pallas_call x9, Pallas kernels, call(): pl.pallas_call(kernel, out_shape=outs, in_specs=[SM] * scalars + [VM] * (...  32 us
    ppermute x7, waiting for transfers between devices, swap(): from_a = lax.ppermute(by_a, axis, pairs_a)  15.5 us
    ppermute x7, waiting for transfers between devices, body(): blocks[way] = lax.ppermute(blocks[way], 'gy', pairs)  10.3 us
    ppermute x7, starting transfers between devices, swap(): from_a = lax.ppermute(by_a, axis, pairs_a)  10.2 us
    ppermute x7, starting transfers between devices, body(): blocks[way] = lax.ppermute(blocks[way], 'gy', pairs)  8.54 us
    ppermute x7, waiting for transfers between devices, swap(): from_b = lax.ppermute(by_b, axis, pairs_b)  4.98 us
    ppermute x7, starting transfers between devices, swap(): from_b = lax.ppermute(by_b, axis, pairs_b)  4.38 us
  transfers between devices with their start and end apart: 21, of which 9 were waited for; matrix products, arithmetic and copies ran while one was open for 2% of the time, Pallas kernels for 18%

profile of v6, /device:TPU:9, one launch (start us, length us, event | category | flops | bytes accessed | tf_op | source)
XLA Modules:
  0.0 91.6 jit_solution(882054480760749346)
XLA Ops:
  0.9 1.7 %split.1 = (bf16[8,64,256]{2,1,0:T(8,128)(2,1)S(1)}, bf16[8,64,256]{2,1,0:T(8,128)(2,1)S(1)}, f32[8,3,256]{2,1,0:T(4,128)S(1)}, f32[8,3,256]{2,1,0:T(4,128)S(1)}) custom-call(s32[6]{0:T(128)S(1)} %stack.19.meta_ref, bf16[16,64,256]{2,1,0:T(8,128)(2,1)} %x.1, f32[3,16,256]{2,1,0:T(8,128)S(1)} %bitcast.8), custom_call_target="tpu_custom_call" | custom-call | tf_op jit(solution)/shard_map/split/pallas_call | solution.py:383
  2.6 1.3 %collective-permute-start = (f32[8,3,256]{2,1,0:T(4,128)S(1)}, f32[8,3,256]{2,1,0:T(4,128)S(1)}, u32[]{:S(2)}, u32[]{:S(2)}) collective-permute-start(f32[8,3,256]{2,1,0:T(4,128)S(1)} %get-tuple-element.36.refs_0_.o0), channel_id=1, source_target_pairs={{0,1},{1,0},{2,3},{3,2},{4,5},{5,4},{6,7},{7,6},{8,9},{9,8},{10,11... | collective-permute-start | bytes 73736 | tf_op jit(solution)/shard_map/ppermute | solution.py:120
  3.8 2.5 %collective-permute-start.4 = (bf16[8,64,256]{2,1,0:T(8,128)(2,1)S(1)}, bf16[8,64,256]{2,1,0:T(8,128)(2,1)S(1)}, u32[]{:S(2)}, u32[]{:S(2)}) collective-permute-start(bf16[8,64,256]{2,1,0:T(8,128)(2,1)S(1)} %get-tuple-element.41.refs_0_.p0), channel_id=1, source_target_pairs={{0,1},{1,0},{2,3},{3,2},{4,5},{5,4},{6,7},{7,6},{8,9},{9,8},{10,11... | collective-permute-start | bytes 786440 | tf_op jit(solution)/shard_map/ppermute | solution.py:120
  8.1 2.2 %collective-permute-start.2 = (f32[16,3,256]{2,1,0:T(4,128)S(1)}, f32[16,3,256]{2,1,0:T(4,128)S(1)}, u32[]{:S(2)}, u32[]{:S(2)}) collective-permute-start(f32[16,3,256]{2,1,0:T(4,128)S(1)} %get-tuple-element.38), channel_id=1, source_target_pairs={{0,8},{1,9},{2,10},{3,11},{4,12},{5,13},{6,14},{7,15},{8,0},{9,1},... | collective-permute-start | bytes 147464 | tf_op jit(solution)/shard_map/ppermute | solution.py:120
  10.3 1.2 %collective-permute-start.3 = (f32[16,3,256]{2,1,0:T(4,128)S(1)}, f32[16,3,256]{2,1,0:T(4,128)S(1)}, u32[]{:S(2)}, u32[]{:S(2)}) collective-permute-start(f32[16,3,256]{2,1,0:T(4,128)S(1)} %get-tuple-element.39), channel_id=1, source_target_pairs={{0,2},{1,3},{2,0},{3,1},{4,6},{5,7},{6,4},{7,5},{8,16},{9,17},{10,... | collective-permute-start | bytes 147464 | tf_op jit(solution)/shard_map/ppermute | solution.py:119
  12.2 6.0 %collective-permute-done.4.refs_2_.p2 = bf16[8,64,256]{2,1,0:T(8,128)(2,1)S(1)} collective-permute-done((bf16[8,64,256]{2,1,0:T(8,128)(2,1)S(1)}, bf16[8,64,256]{2,1,0:T(8,128)(2,1)S(1)}, u32[]{:S(2)}, u32[]{:S(2)}) %collective-permute-start.4) | collective-permute-done | bytes 262176 | tf_op jit(solution)/shard_map/ppermute | solution.py:120
  18.9 1.6 %collective-permute-start.6 = (bf16[16,64,256]{2,1,0:T(8,128)(2,1)S(1)}, bf16[16,64,256]{2,1,0:T(8,128)(2,1)S(1)}, u32[]{:S(2)}, u32[]{:S(2)}) collective-permute-start(bf16[16,64,256]{2,1,0:T(8,128)(2,1)S(1)} %get-tuple-element.43), channel_id=1, source_target_pairs={{0,8},{1,9},{2,10},{3,11},{4,12},{5,13},{6,14},{7,15},{8,0},{9,1},... | collective-permute-start | bytes 1572872 | tf_op jit(solution)/shard_map/ppermute | solution.py:120
  21.7 8.4 %shard_map.74 = (bf16[4,4096,256]{2,1,0:T(8,128)(2,1)S(1)}, bf16[4,4096,256]{2,1,0:T(8,128)(2,1)S(1)}, f32[8,256]{1,0:T(8,128)S(1)}, bf16[64,256,48]{2,1,0:T(8,1...) custom-call(s32[272]{0:T(512)S(1)} %pad_add_fusion.near_ref, s32[6]{0:T(128)S(1)} %stack.19.meta_ref, ...), custom_call_target="tpu_custom_call" | custom-call | flops 4294967296 | bytes 1048576 | tf_op jit(solution)/shard_map/pallas_call | solution.py:343
  30.2 6.1 %shard_map.76 = (bf16[4,4096,256]{2,1,0:T(8,128)(2,1)S(1)}, bf16[4,4096,256]{2,1,0:T(8,128)(2,1)S(1)}, f32[8,256]{1,0:T(8,128)S(1)}) custom-call(s32[272]{0:T(512)S(1)} %pad_add_fusion.near_ref, bf16[64,256,48]{2,1,0:T(8,128)(2,1)S(1)} %get-tuple-element.47.source, bf16[16,48,256]{2,1,0:T(8,128)(2,1)S(1)} %get-tuple-element.48.target), custom_call_target="tpu_custom_call" | custom-call | flops 4294967296 | bytes 1048576 | tf_op jit(solution)/shard_map/pallas_call | solution.py:343
  36.4 3.8 %shard_map.77 = (bf16[8,64,256]{2,1,0:T(8,128)(2,1)S(1)}, bf16[64,64,256]{2,1,0:T(8,128)(2,1)S(1)}) custom-call(s32[272]{0:T(512)S(1)} %pad_add_fusion.near_ref, s32[6]{0:T(128)S(1)} %stack.19.meta_ref, bf16[8,64,256]{2,1,0:T(8,128)(2,1)S(1)} %get-tuple-element.41.refs_0_.p0, bf16[8,64,256]{2,1,0:T(8,128)(2,1)S(1)} %get-tuple-element.42.refs_1_.p1, ...), custom_call_target="tpu_custom_call" | custom-call | flops 2147483648 | bytes 1048576 | tf_op jit(solution)/shard_map/pallas_call | solution.py:343
  40.1 3.6 %shard_map.78.refs_0_ = bf16[8,64,256]{2,1,0:T(8,128)(2,1)S(1)} custom-call(s32[272]{0:T(512)S(1)} %pad_add_fusion.near_ref, s32[6]{0:T(128)S(1)} %stack.19.meta_ref, bf16[64,64,256]{2,1,0:T(8,128)(2,1)S(1)} %get-tuple-element.53.species, bf16[4,4096,256]{2,1,0:T(8,128)(2,1)S(1)} %get-tuple-element.45.w0.refs_8_, ...), custom_call_target="tpu_custom_call" | custom-call | flops 2147483648 | bytes 1048576 | tf_op jit(solution)/shard_map/pallas_call | solution.py:343
  43.8 1.3 %collective-permute-start.8 = (bf16[8,64,256]{2,1,0:T(8,128)(2,1)S(1)}, bf16[8,64,256]{2,1,0:T(8,128)(2,1)S(1)}, u32[]{:S(2)}, u32[]{:S(2)}) collective-permute-start(bf16[8,64,256]{2,1,0:T(8,128)(2,1)S(1)} %shard_map.78.refs_0_), channel_id=1, source_target_pairs={{0,1},{1,0},{2,3},{3,2},{4,5},{5,4},{6,7},{7,6},{8,9},{9,8},{10,11... | collective-permute-start | bytes 786440 | tf_op jit(solution)/shard_map/ppermute | solution.py:120
  47.6 9.3 %collective-permute-done.8.refs_0_.refs_2_ = bf16[8,64,256]{2,1,0:T(8,128)(2,1)S(1)} collective-permute-done((bf16[8,64,256]{2,1,0:T(8,128)(2,1)S(1)}, bf16[8,64,256]{2,1,0:T(8,128)(2,1)S(1)}, u32[]{:S(2)}, u32[]{:S(2)}) %collective-permute-start.8) | collective-permute-done | bytes 262176 | tf_op jit(solution)/shard_map/ppermute | solution.py:120
  57.6 1.3 %collective-permute-start.13 = (bf16[8,64,256]{2,1,0:T(8,128)(2,1)S(1)}, bf16[8,64,256]{2,1,0:T(8,128)(2,1)S(1)}, u32[]{:S(2)}, u32[]{:S(2)}) collective-permute-start(bf16[8,64,256]{2,1,0:T(8,128)(2,1)S(1)} %get-tuple-element.58), channel_id=1, source_target_pairs={{0,2},{1,3},{2,0},{3,1},{4,6},{5,7},{6,4},{7,5},{8,16},{9,17},{10,... | collective-permute-start | bytes 786440 | tf_op jit(solution)/shard_map/ppermute | solution.py:119
  59.1 4.6 %collective-permute-done.13.refs_7_ = bf16[8,64,256]{2,1,0:T(8,128)(2,1)S(1)} collective-permute-done((bf16[8,64,256]{2,1,0:T(8,128)(2,1)S(1)}, bf16[8,64,256]{2,1,0:T(8,128)(2,1)S(1)}, u32[]{:S(2)}, u32[]{:S(2)}) %collective-permute-start.13) | collective-permute-done | bytes 262176 | tf_op jit(solution)/shard_map/ppermute | solution.py:119
  63.7 7.7 %shard_map.81 = (bf16[2,64,256]{2,1,0:T(8,128)(2,1)S(1)}, bf16[2,64,256]{2,1,0:T(8,128)(2,1)S(1)}, bf16[2,64,256]{2,1,0:T(8,128)(2,1)S(1)}, bf16[2,64,256]{2,1,0...) custom-call(s32[272]{0:T(512)S(1)} %pad_add_fusion.near_ref, ...), custom_call_target="tpu_custom_call" | custom-call | flops 4294967296 | bytes 1048576 | tf_op jit(solution)/shard_map/pallas_call | solution.py:343
  71.4 1.4 %collective-permute-start.14 = (bf16[2,64,256]{2,1,0:T(8,128)(2,1)S(1)}, bf16[2,64,256]{2,1,0:T(8,128)(2,1)S(1)}, u32[]{:S(2)}, u32[]{:S(2)}) collective-permute-start(bf16[2,64,256]{2,1,0:T(8,128)(2,1)S(1)} %get-tuple-element.60), channel_id=1, source_target_pairs={{0,1},{1,0},{2,3},{3,2},{4,5},{5,4},{6,7},{7,6},{8,9},{9,8},{10,11... | collective-permute-start | bytes 196616 | tf_op jit(solution)/shard_map/ppermute | solution.py:469
  72.8 1.2 %collective-permute-start.15 = (bf16[2,64,256]{2,1,0:T(8,128)(2,1)S(1)}, bf16[2,64,256]{2,1,0:T(8,128)(2,1)S(1)}, u32[]{:S(2)}, u32[]{:S(2)}) collective-permute-start(bf16[2,64,256]{2,1,0:T(8,128)(2,1)S(1)} %get-tuple-element.61), channel_id=1, source_target_pairs={{0,2},{1,3},{2,0},{3,1},{4,6},{5,7},{6,4},{7,5},{8,10},{9,11},{10,... | collective-permute-start | bytes 196616 | tf_op jit(solution)/shard_map/ppermute | solution.py:469
  74.1 2.9 %collective-permute-start.17 = (bf16[2,64,256]{2,1,0:T(8,128)(2,1)S(1)}, bf16[2,64,256]{2,1,0:T(8,128)(2,1)S(1)}, u32[]{:S(2)}, u32[]{:S(2)}) collective-permute-start(bf16[2,64,256]{2,1,0:T(8,128)(2,1)S(1)} %get-tuple-element.63), channel_id=1, source_target_pairs={{0,4},{1,5},{2,6},{3,7},{4,0},{5,1},{6,2},{7,3},{8,12},{9,13},{10,... | collective-permute-start | bytes 196616 | tf_op jit(solution)/shard_map/ppermute | solution.py:469
  77.6 1.2 %collective-permute-start.19 = (bf16[2,64,256]{2,1,0:T(8,128)(2,1)S(1)}, bf16[2,64,256]{2,1,0:T(8,128)(2,1)S(1)}, u32[]{:S(2)}, u32[]{:S(2)}) collective-permute-start(bf16[2,64,256]{2,1,0:T(8,128)(2,1)S(1)} %get-tuple-element.65), channel_id=1, source_target_pairs={{0,6},{1,7},{2,4},{3,5},{4,2},{5,3},{6,0},{7,1},{8,14},{9,15},{10,... | collective-permute-start | bytes 196616 | tf_op jit(solution)/shard_map/ppermute | solution.py:469
  80.3 4.1 %collective-permute-done.18.refs_5_ = bf16[2,64,256]{2,1,0:T(8,128)(2,1)S(1)} collective-permute-done((bf16[2,64,256]{2,1,0:T(8,128)(2,1)S(1)}, bf16[2,64,256]{2,1,0:T(8,128)(2,1)S(1)}, u32[]{:S(2)}, u32[]{:S(2)}) %collective-permute-start.18) | collective-permute-done | bytes 65568 | tf_op jit(solution)/shard_map/ppermute | solution.py:469
  84.4 2.7 %collective-permute-done.19.refs_6_ = bf16[2,64,256]{2,1,0:T(8,128)(2,1)S(1)} collective-permute-done((bf16[2,64,256]{2,1,0:T(8,128)(2,1)S(1)}, bf16[2,64,256]{2,1,0:T(8,128)(2,1)S(1)}, u32[]{:S(2)}, u32[]{:S(2)}) %collective-permute-start.19) | collective-permute-done | bytes 65568 | tf_op jit(solution)/shard_map/ppermute | solution.py:469
  87.2 3.1 %collective-permute-done.20.refs_7_ = bf16[2,64,256]{2,1,0:T(8,128)(2,1)S(1)} collective-permute-done((bf16[2,64,256]{2,1,0:T(8,128)(2,1)S(1)}, bf16[2,64,256]{2,1,0:T(8,128)(2,1)S(1)}, u32[]{:S(2)}, u32[]{:S(2)}) %collective-permute-start.20) | collective-permute-done | bytes 65568 | tf_op jit(solution)/shard_map/ppermute | solution.py:469
  90.2 1.4 %place.1 = bf16[16,64,256]{2,1,0:T(8,128)(2,1)} custom-call(s32[6]{0:T(128)S(1)} %stack.19.meta_ref, bf16[2,64,256]{2,1,0:T(8,128)(2,1)S(1)} %get-tuple-element.59.refs_0_, bf16[2,64,256]{2,1,0:T(8,128)(2,1)S(1)} %collective-permute-done.14.refs_1_, bf16[2,64,256]{2,1,0:T(8,128)(2,1)S(1)} %collective-permute-done.15.refs_2_, ...), custom_call_target="tpu_custom_call" | custom-call | tf_op jit(solution)/shard_map/place/pallas_call | solution.py:470
  (42 shorter events, 10.7 us)
Async XLA Ops:
  2.6 4.6 %collective-permute-start = (f32[8,3,256]{2,1,0:T(4,128)S(1)}, f32[8,3,256]{2,1,0:T(4,128)S(1)}, u32[]{:S(2)}, u32[]{:S(2)}) collective-permute-start(f32[8,3,256]{2,1,0:T(4,128)S(1)} %get-tuple-element.36.refs_0_.o0), channel_id=1, source_target_pairs={{0,1},{1,0},{2,3},{3,2},{4,5},{5,4},{6,7},{7,6},{8,9},{9,8},{10,11... | collective-permute-start | bytes 73736 | tf_op jit(solution)/shard_map/ppermute | solution.py:120
  3.8 3.7 %collective-permute-start.1 = (f32[8,3,256]{2,1,0:T(4,128)S(1)}, f32[8,3,256]{2,1,0:T(4,128)S(1)}, u32[]{:S(2)}, u32[]{:S(2)}) collective-permute-start(f32[8,3,256]{2,1,0:T(4,128)S(1)} %get-tuple-element.37.refs_1_.o1), channel_id=1, source_target_pairs={{0,8},{1,2},{2,1},{3,4},{4,3},{5,6},{6,5},{7,15},{8,0},{9,10},{10,... | collective-permute-start | bytes 73736 | tf_op jit(solution)/shard_map/ppermute | solution.py:119
  3.8 14.4 %collective-permute-start.4 = (bf16[8,64,256]{2,1,0:T(8,128)(2,1)S(1)}, bf16[8,64,256]{2,1,0:T(8,128)(2,1)S(1)}, u32[]{:S(2)}, u32[]{:S(2)}) collective-permute-start(bf16[8,64,256]{2,1,0:T(8,128)(2,1)S(1)} %get-tuple-element.41.refs_0_.p0), channel_id=1, source_target_pairs={{0,1},{1,0},{2,3},{3,2},{4,5},{5,4},{6,7},{7,6},{8,9},{9,8},{10,11... | collective-permute-start | bytes 786440 | tf_op jit(solution)/shard_map/ppermute | solution.py:120
  6.3 11.9 %collective-permute-start.5 = (bf16[8,64,256]{2,1,0:T(8,128)(2,1)S(1)}, bf16[8,64,256]{2,1,0:T(8,128)(2,1)S(1)}, u32[]{:S(2)}, u32[]{:S(2)}) collective-permute-start(bf16[8,64,256]{2,1,0:T(8,128)(2,1)S(1)} %get-tuple-element.42.refs_1_.p1), channel_id=1, source_target_pairs={{0,8},{1,2},{2,1},{3,4},{4,3},{5,6},{6,5},{7,15},{8,0},{9,10},{10,... | collective-permute-start | bytes 786440 | tf_op jit(solution)/shard_map/ppermute | solution.py:119
  8.1 13.6 %collective-permute-start.2 = (f32[16,3,256]{2,1,0:T(4,128)S(1)}, f32[16,3,256]{2,1,0:T(4,128)S(1)}, u32[]{:S(2)}, u32[]{:S(2)}) collective-permute-start(f32[16,3,256]{2,1,0:T(4,128)S(1)} %get-tuple-element.38), channel_id=1, source_target_pairs={{0,8},{1,9},{2,10},{3,11},{4,12},{5,13},{6,14},{7,15},{8,0},{9,1},... | collective-permute-start | bytes 147464 | tf_op jit(solution)/shard_map/ppermute | solution.py:120
  10.3 11.3 %collective-permute-start.3 = (f32[16,3,256]{2,1,0:T(4,128)S(1)}, f32[16,3,256]{2,1,0:T(4,128)S(1)}, u32[]{:S(2)}, u32[]{:S(2)}) collective-permute-start(f32[16,3,256]{2,1,0:T(4,128)S(1)} %get-tuple-element.39), channel_id=1, source_target_pairs={{0,2},{1,3},{2,0},{3,1},{4,6},{5,7},{6,4},{7,5},{8,16},{9,17},{10,... | collective-permute-start | bytes 147464 | tf_op jit(solution)/shard_map/ppermute | solution.py:119
  18.9 17.5 %collective-permute-start.6 = (bf16[16,64,256]{2,1,0:T(8,128)(2,1)S(1)}, bf16[16,64,256]{2,1,0:T(8,128)(2,1)S(1)}, u32[]{:S(2)}, u32[]{:S(2)}) collective-permute-start(bf16[16,64,256]{2,1,0:T(8,128)(2,1)S(1)} %get-tuple-element.43), channel_id=1, source_target_pairs={{0,8},{1,9},{2,10},{3,11},{4,12},{5,13},{6,14},{7,15},{8,0},{9,1},... | collective-permute-start | bytes 1572872 | tf_op jit(solution)/shard_map/ppermute | solution.py:120
  20.5 15.8 %collective-permute-start.7 = (bf16[16,64,256]{2,1,0:T(8,128)(2,1)S(1)}, bf16[16,64,256]{2,1,0:T(8,128)(2,1)S(1)}, u32[]{:S(2)}, u32[]{:S(2)}) collective-permute-start(bf16[16,64,256]{2,1,0:T(8,128)(2,1)S(1)} %get-tuple-element.44), channel_id=1, source_target_pairs={{0,2},{1,3},{2,0},{3,1},{4,6},{5,7},{6,4},{7,5},{8,16},{9,17},{10,... | collective-permute-start | bytes 1572872 | tf_op jit(solution)/shard_map/ppermute | solution.py:119
  30.1 6.2 %copy-start = (f32[16,256]{1,0:T(8,128)S(1)}, f32[16,256]{1,0:T(8,128)}, u32[]{:S(2)}) copy-start(f32[16,256]{1,0:T(8,128)} %refs_14_.1) | copy-start | bytes 49156
  30.1 6.2 %copy-start.2 = (f32[32]{0:T(128)S(1)}, f32[32]{0:T(128)}, u32[]{:S(2)}) copy-start(f32[32]{0:T(128)} %param.10) | copy-start | bytes 388
  30.1 6.2 %copy-start.3 = (f32[32]{0:T(128)S(1)}, f32[32]{0:T(128)}, u32[]{:S(2)}) copy-start(f32[32]{0:T(128)} %param.11) | copy-start | bytes 388
  43.8 13.1 %collective-permute-start.8 = (bf16[8,64,256]{2,1,0:T(8,128)(2,1)S(1)}, bf16[8,64,256]{2,1,0:T(8,128)(2,1)S(1)}, u32[]{:S(2)}, u32[]{:S(2)}) collective-permute-start(bf16[8,64,256]{2,1,0:T(8,128)(2,1)S(1)} %shard_map.78.refs_0_), channel_id=1, source_target_pairs={{0,1},{1,0},{2,3},{3,2},{4,5},{5,4},{6,7},{7,6},{8,9},{9,8},{10,11... | collective-permute-start | bytes 786440 | tf_op jit(solution)/shard_map/ppermute | solution.py:120
  45.1 11.8 %collective-permute-start.9 = (bf16[8,64,256]{2,1,0:T(8,128)(2,1)S(1)}, bf16[8,64,256]{2,1,0:T(8,128)(2,1)S(1)}, u32[]{:S(2)}, u32[]{:S(2)}) collective-permute-start(bf16[8,64,256]{2,1,0:T(8,128)(2,1)S(1)} %get-tuple-element.54.refs_1_), channel_id=1, source_target_pairs={{0,8},{1,2},{2,1},{3,4},{4,3},{5,6},{6,5},{7,15},{8,0},{9,10},{10,... | collective-permute-start | bytes 786440 | tf_op jit(solution)/shard_map/ppermute | solution.py:119
  45.6 13.2 %collective-permute-start.10 = (bf16[8,64,256]{2,1,0:T(8,128)(2,1)S(1)}, bf16[8,64,256]{2,1,0:T(8,128)(2,1)S(1)}, u32[]{:S(2)}, u32[]{:S(2)}) collective-permute-start(bf16[8,64,256]{2,1,0:T(8,128)(2,1)S(1)} %get-tuple-element.55), channel_id=1, source_target_pairs={{0,8},{1,9},{2,10},{3,11},{4,12},{5,13},{6,14},{7,15},{8,0},{9,1},... | collective-permute-start | bytes 786440 | tf_op jit(solution)/shard_map/ppermute | solution.py:120
  46.9 12.0 %collective-permute-start.12 = (bf16[8,64,256]{2,1,0:T(8,128)(2,1)S(1)}, bf16[8,64,256]{2,1,0:T(8,128)(2,1)S(1)}, u32[]{:S(2)}, u32[]{:S(2)}) collective-permute-start(bf16[8,64,256]{2,1,0:T(8,128)(2,1)S(1)} %get-tuple-element.57), channel_id=1, source_target_pairs={{0,2},{1,3},{2,0},{3,1},{4,6},{5,7},{6,4},{7,5},{8,16},{9,17},{10,... | collective-permute-start | bytes 786440 | tf_op jit(solution)/shard_map/ppermute | solution.py:119
  57.5 1.6 %collective-permute-start.11 = (bf16[8,64,256]{2,1,0:T(8,128)(2,1)S(1)}, bf16[8,64,256]{2,1,0:T(8,128)(2,1)S(1)}, u32[]{:S(2)}, u32[]{:S(2)}) collective-permute-start(bf16[8,64,256]{2,1,0:T(8,128)(2,1)S(1)} %get-tuple-element.56), channel_id=1, source_target_pairs={{0,8},{1,9},{2,10},{3,11},{4,12},{5,13},{6,14},{7,15},{8,0},{9,1},... | collective-permute-start | bytes 786440 | tf_op jit(solution)/shard_map/ppermute | solution.py:120
  57.6 6.1 %collective-permute-start.13 = (bf16[8,64,256]{2,1,0:T(8,128)(2,1)S(1)}, bf16[8,64,256]{2,1,0:T(8,128)(2,1)S(1)}, u32[]{:S(2)}, u32[]{:S(2)}) collective-permute-start(bf16[8,64,256]{2,1,0:T(8,128)(2,1)S(1)} %get-tuple-element.58), channel_id=1, source_target_pairs={{0,2},{1,3},{2,0},{3,1},{4,6},{5,7},{6,4},{7,5},{8,16},{9,17},{10,... | collective-permute-start | bytes 786440 | tf_op jit(solution)/shard_map/ppermute | solution.py:119
  71.4 6.2 %collective-permute-start.14 = (bf16[2,64,256]{2,1,0:T(8,128)(2,1)S(1)}, bf16[2,64,256]{2,1,0:T(8,128)(2,1)S(1)}, u32[]{:S(2)}, u32[]{:S(2)}) collective-permute-start(bf16[2,64,256]{2,1,0:T(8,128)(2,1)S(1)} %get-tuple-element.60), channel_id=1, source_target_pairs={{0,1},{1,0},{2,3},{3,2},{4,5},{5,4},{6,7},{7,6},{8,9},{9,8},{10,11... | collective-permute-start | bytes 196616 | tf_op jit(solution)/shard_map/ppermute | solution.py:469
  72.8 5.9 %collective-permute-start.15 = (bf16[2,64,256]{2,1,0:T(8,128)(2,1)S(1)}, bf16[2,64,256]{2,1,0:T(8,128)(2,1)S(1)}, u32[]{:S(2)}, u32[]{:S(2)}) collective-permute-start(bf16[2,64,256]{2,1,0:T(8,128)(2,1)S(1)} %get-tuple-element.61), channel_id=1, source_target_pairs={{0,2},{1,3},{2,0},{3,1},{4,6},{5,7},{6,4},{7,5},{8,10},{9,11},{10,... | collective-permute-start | bytes 196616 | tf_op jit(solution)/shard_map/ppermute | solution.py:469
  74.1 5.9 %collective-permute-start.16 = (bf16[2,64,256]{2,1,0:T(8,128)(2,1)S(1)}, bf16[2,64,256]{2,1,0:T(8,128)(2,1)S(1)}, u32[]{:S(2)}, u32[]{:S(2)}) collective-permute-start(bf16[2,64,256]{2,1,0:T(8,128)(2,1)S(1)} %get-tuple-element.62), channel_id=1, source_target_pairs={{0,3},{1,2},{2,1},{3,0},{4,7},{5,6},{6,5},{7,4},{8,11},{9,10},{10,... | collective-permute-start | bytes 196616 | tf_op jit(solution)/shard_map/ppermute | solution.py:469
  74.1 6.2 %collective-permute-start.17 = (bf16[2,64,256]{2,1,0:T(8,128)(2,1)S(1)}, bf16[2,64,256]{2,1,0:T(8,128)(2,1)S(1)}, u32[]{:S(2)}, u32[]{:S(2)}) collective-permute-start(bf16[2,64,256]{2,1,0:T(8,128)(2,1)S(1)} %get-tuple-element.63), channel_id=1, source_target_pairs={{0,4},{1,5},{2,6},{3,7},{4,0},{5,1},{6,2},{7,3},{8,12},{9,13},{10,... | collective-permute-start | bytes 196616 | tf_op jit(solution)/shard_map/ppermute | solution.py:469
  77.0 7.4 %collective-permute-start.18 = (bf16[2,64,256]{2,1,0:T(8,128)(2,1)S(1)}, bf16[2,64,256]{2,1,0:T(8,128)(2,1)S(1)}, u32[]{:S(2)}, u32[]{:S(2)}) collective-permute-start(bf16[2,64,256]{2,1,0:T(8,128)(2,1)S(1)} %get-tuple-element.64), channel_id=1, source_target_pairs={{0,5},{1,4},{2,7},{3,6},{4,1},{5,0},{6,3},{7,2},{8,13},{9,12},{10,... | collective-permute-start | bytes 196616 | tf_op jit(solution)/shard_map/ppermute | solution.py:469
  77.6 9.6 %collective-permute-start.19 = (bf16[2,64,256]{2,1,0:T(8,128)(2,1)S(1)}, bf16[2,64,256]{2,1,0:T(8,128)(2,1)S(1)}, u32[]{:S(2)}, u32[]{:S(2)}) collective-permute-start(bf16[2,64,256]{2,1,0:T(8,128)(2,1)S(1)} %get-tuple-element.65), channel_id=1, source_target_pairs={{0,6},{1,7},{2,4},{3,5},{4,2},{5,3},{6,0},{7,1},{8,14},{9,15},{10,... | collective-permute-start | bytes 196616 | tf_op jit(solution)/shard_map/ppermute | solution.py:469
  78.8 11.5 %collective-permute-start.20 = (bf16[2,64,256]{2,1,0:T(8,128)(2,1)S(1)}, bf16[2,64,256]{2,1,0:T(8,128)(2,1)S(1)}, u32[]{:S(2)}, u32[]{:S(2)}) collective-permute-start(bf16[2,64,256]{2,1,0:T(8,128)(2,1)S(1)} %get-tuple-element.66), channel_id=1, source_target_pairs={{0,7},{1,6},{2,5},{3,4},{4,3},{5,2},{6,1},{7,0},{8,15},{9,14},{10,... | collective-permute-start | bytes 196616 | tf_op jit(solution)/shard_map/ppermute | solution.py:469
  (1 other events, 0.8 us)

commit v7 on v6

--- a/solution.py
+++ b/solution.py
@@ -173,7 +173,7 @@
     return near_ref.shape[0] // (BX * BY) - 1
 
 
-def build_rows(near_ref, source, target, w_refs, inv_ref, first_row):
+def build_rows(near_ref, source, target, w_refs, first_row):
     parts = source.shape[1]
     neighbours = neighbours_of(near_ref)
     for g, w_ref in enumerate(w_refs):
@@ -181,20 +181,17 @@
         def one(c, _, g=g, w_ref=w_ref):
             b = (first_row + g) * BY + c
             f = target[b]
-            total = jnp.zeros((8, parts), f32)
             for k in range(neighbours):
                 q = near_ref[b * neighbours + k]
-                w = jnp.exp2(jnp.dot(source[q], f, preferred_element_type=f32))
-                total = total + w.reshape(parts // 8, 8, parts).sum(0)
-                w_ref[c, pl.ds(k * parts, parts)] = w.astype(bf16)
-            inv_ref[pl.ds(g * BY + c, 1)] = 1.0 / jnp.sum(total, axis=0, keepdims=True)
+                e = jnp.dot(source[q], f, preferred_element_type=f32)
+                w_ref[c, pl.ds(k * parts, parts)] = jnp.exp2(e.astype(bf16))
             return 0
 
         lax.fori_loop(0, BY, one, 0)
 
 
 def build_first(
-    near_ref, meta_ref, o0, o1, c0, c1, r0, r1, w0, w1, inv_ref, source, target, row_ref, taken
+    near_ref, meta_ref, o0, o1, c0, c1, r0, r1, w0, w1, source, target, row_ref, taken
 ):
     odd_lane, odd_band = meta_ref[4], meta_ref[5]
     for piece, ref in enumerate((o0, o1, c0, c1, r0, r1)):
@@ -224,11 +221,11 @@
         return 0
 
     lax.fori_loop(0, BX * BY, place, 0)
-    build_rows(near_ref, source, target, (w0, w1), inv_ref, 0)
-
-
-def build_second(near_ref, source, target, w2, w3, inv_ref):
-    build_rows(near_ref, source, target, (w2, w3), inv_ref, BX // 2)
+    build_rows(near_ref, source, target, (w0, w1), 0)
+
+
+def build_second(near_ref, source, target, w2, w3):
+    build_rows(near_ref, source, target, (w2, w3), BX // 2)
 
 
 def column(row_ref):
@@ -250,9 +247,10 @@
 def mix(near_ref, species, gathered, w, b):
     neighbours = neighbours_of(near_ref)
     parts = species.shape[2]
+    kinds = species.shape[1]
     for k in range(neighbours):
         q = near_ref[b * neighbours + k]
-        gathered[:, k * parts : (k + 1) * parts] = species[q]
+        gathered[:kinds, k * parts : (k + 1) * parts] = species[q]
     return jnp.dot(gathered[...], w, preferred_element_type=f32)
 
 
@@ -263,12 +261,9 @@
         start += ref.shape[0]
 
 
-def inverse_of(inv_refs, g, c):
-    half = BX // 2
-    return inv_refs[g // half][pl.ds((g % half) * BY + c, 1)]
-
-
-def step_columns(near_ref, species, gathered, w_refs, inv_refs, consts, low, out_ref):
+def step_columns(near_ref, species, gathered, w_refs, consts, low, out_ref, inv_ref):
+    kinds = species.shape[1]
+    gathered[:, kinds:] = jnp.ones_like(gathered[:, kinds:])
     kelvin_ref, factor_ref, onset_ref = consts
     factor, onset = column(factor_ref), column(onset_ref)
     for g, w_ref in enumerate(w_refs):
@@ -277,40 +272,49 @@
             c = low + i
             b = g * BY + c
             mixed = mix(near_ref, species, gathered.at[i], w_ref[c], b)
-            mixed = mixed * inverse_of(inv_refs, g, c)
+            inv = 1.0 / mixed[kinds : kinds + 1]
+            inv_ref[pl.ds(g * HALO + i, 1)] = inv
+            mixed = mixed[:kinds] * inv
             out_ref[g * HALO + i] = react(mixed, kelvin_ref[pl.ds(b, 1)], factor, onset)
 
 
-def step_b(near_ref, meta_ref, p0, p1, p2, p3, p4, p5, w0, w1, w2, w3, i0, i1, t, a, o, out, species, gathered):
-    join((p0, p1, p2, p3, p4, p5), species)
+def step_b(near_ref, meta_ref, *refs):
+    pieces, w_refs, consts = refs[:6], refs[6:10], refs[10:13]
+    out, inv_ref, species, gathered = refs[13:]
+    join(pieces, species)
     low = jnp.where(meta_ref[4] == 1, BY - HALO, 0)
-    step_columns(near_ref, species, gathered, (w0, w1, w2, w3), (i0, i1), (t, a, o), low, out)
-
-
-def step_a(near_ref, meta_ref, species, w0, w1, w2, w3, i0, i1, t, a, o, out, gathered):
+    step_columns(near_ref, species, gathered, w_refs, consts, low, out, inv_ref)
+
+
+def step_a(near_ref, meta_ref, species, *refs):
+    w_refs, consts = refs[:4], refs[4:7]
+    out, inv_ref, gathered = refs[7:]
     low = jnp.where(meta_ref[4] == 1, 0, BY - HALO)
-    step_columns(near_ref, species, gathered, (w0, w1, w2, w3), (i0, i1), (t, a, o), low, out)
+    step_columns(near_ref, species, gathered, w_refs, consts, low, out, inv_ref)
 
 
 def last_step(near_ref, meta_ref, row_ref, *refs):
     pieces, refs = refs[:8], refs[8:]
-    w_refs, inv_refs, refs = refs[:4], refs[4:6], refs[6:]
+    w_refs, (inv_a, inv_b), refs = refs[:4], refs[4:6], refs[6:]
     (kelvin_ref, factor_ref, onset_ref), refs = refs[:3], refs[3:]
     outs, (species, gathered, staged) = refs[:-3], refs[-3:]
     join(pieces, species)
     factor, onset = column(factor_ref), column(onset_ref)
     lane = meta_ref[1] // BY
+    a_first = meta_ref[4] == 1
     if staged.shape[0] > BX * BY:
         staged[...] = jnp.zeros_like(staged)
     for g, w_ref in enumerate(w_refs):
 
         def some(j, _, g=g, w_ref=w_ref):
+            by_a = (j == 0) == a_first
             for i in range(HALO):
                 c = j * HALO + i
+                at = pl.ds(g * HALO + i, 1)
                 b = g * BY + c
                 row = row_ref[b]
                 mixed = mix(near_ref, species, gathered.at[i], w_ref[c], b)
-                mixed = mixed * inverse_of(inv_refs, g, c)
+                mixed = mixed * jnp.where(by_a, inv_a[at], inv_b[at])
                 moved = react(mixed, kelvin_ref[pl.ds(b, 1)], factor, onset)
                 staged[((row // CAP) ^ lane) * CAP + row % CAP] = moved
             return 0
@@ -397,7 +401,9 @@
 
     def rows(pieces):
         size = len(pieces) * QUAD
-        by_a, by_b = call(pack, (meta,) + pieces, 1, [like(pieces[0], size)] * 2, [], 1 << 20)
+        by_a, by_b = call(
+            pack, (meta,) + pieces, 1, [like(pieces[0], size)] * 2, [], 1 << 20
+        )
         return swap(by_a, by_b, "gx")
 
     pos_sides = swap(pos_a, pos_b, "gy")
@@ -417,19 +423,19 @@
     consts = (local_kelvin, couple_kinetic_factor[None], arrhenius_onset[None])
 
     w_row = pltpu.VMEM((BY, neighbours * parts, parts), bf16)
-    inv_half = pltpu.VMEM((bins // 2, parts), f32)
+    inv = pltpu.VMEM((SIDE, parts), f32)
+    counted = pltpu.VMEM((HALO, kinds + 16, neighbours * parts), bf16)
     half = pltpu.VMEM((SIDE, kinds, parts), bf16)
     gathered = pltpu.VMEM((HALO, kinds, neighbours * parts), bf16)
     all_species = pltpu.VMEM((EXT, kinds, parts), bf16)
     work = 2 * bins * neighbours * parts * parts * 128
-    w0, w1, inv0, source, target, row = call(
+    w0, w1, source, target, row = call(
         build_first,
         (near, meta, pos_a, pos_b) + pos_sides + pos_bands,
         2,
         [
             w_row,
             w_row,
-            inv_half,
             pltpu.VMEM((EXT, parts, FEATURES), bf16),
             pltpu.VMEM((bins, FEATURES, parts), bf16),
             jax.ShapeDtypeStruct((bins,), i32),
@@ -437,17 +443,24 @@
         [pltpu.SMEM((lane_count,), i32)],
         work,
     )
-    w2, w3, inv1 = call(build_second, (near, source, target), 1, [w_row, w_row, inv_half], [], work)
-    built = (w0, w1, w2, w3, inv0, inv1) + consts
-    by_b, species = call(
+    w2, w3 = call(build_second, (near, source, target), 1, [w_row, w_row], [], work)
+    built = (w0, w1, w2, w3)
+    by_b, inv_b, species = call(
         step_b,
-        (near, meta) + own + sides + bands + built,
+        (near, meta) + own + sides + bands + built + consts,
         2,
-        [half, all_species],
-        [gathered],
+        [half, inv, all_species],
+        [counted],
         work // 2,
     )
-    by_a = call(step_a, (near, meta, species) + built, 2, half, [gathered], work // 2)
+    by_a, inv_a = call(
+        step_a,
+        (near, meta, species) + built + consts,
+        2,
+        [half, inv],
+        [counted],
+        work // 2,
+    )
 
     own = (by_a, by_b)
     sides = swap(by_a, by_b, "gy")
@@ -457,7 +470,7 @@
     blocks = list(
         call(
             last_step,
-            (near, meta, row) + pieces + built,
+            (near, meta, row) + pieces + built + (inv_a, inv_b) + consts,
             3,
             [pltpu.VMEM((CAP, kinds, parts), bf16)] * lane_count,
             [all_species, gathered, pltpu.VMEM((lane_count * CAP, kinds, parts), bf16)],
@@ -489,4 +502,6 @@
         P(("gx", "gy"), None),
     )
     out_specs = P(("gx", "gy"), None, None)
-    return jax.shard_map(body, mesh=mesh, in_specs=in_specs, out_specs=out_specs, check_vma=False)
+    return jax.shard_map(
+        body, mesh=mesh, in_specs=in_specs, out_specs=out_specs, check_vma=False
+    )

time: 91.9 us -> 91.5 us (level)
  no operation moved by 1% of the time
where the time goes in v7:
time: 91.5 us; the launch traced here: 91.2 us
  Pallas kernels  34.7 us (38%)
  waiting for transfers between devices  30.8 us (34%)
  starting transfers between devices  23.2 us (25%)
  other arithmetic  1.45 us (2%)
  local copies, waits for them, and re-layouts  0.98 us (1%)
    pallas_call x9, Pallas kernels, call(): pl.pallas_call(kernel, out_shape=outs, in_specs=[SM] * scalars + [VM] * (...  31.6 us
    ppermute x7, waiting for transfers between devices, swap(): from_a = lax.ppermute(by_a, axis, pairs_a)  15.5 us
    ppermute x7, waiting for transfers between devices, body(): blocks[way] = lax.ppermute(blocks[way], 'gy', pairs)  10.3 us
    ppermute x7, starting transfers between devices, swap(): from_a = lax.ppermute(by_a, axis, pairs_a)  10.2 us
    ppermute x7, starting transfers between devices, body(): blocks[way] = lax.ppermute(blocks[way], 'gy', pairs)  8.56 us
    ppermute x7, waiting for transfers between devices, swap(): from_b = lax.ppermute(by_b, axis, pairs_b)  4.98 us
    ppermute x7, starting transfers between devices, swap(): from_b = lax.ppermute(by_b, axis, pairs_b)  4.43 us
  transfers between devices with their start and end apart: 21, of which 9 were waited for; matrix products, arithmetic and copies ran while one was open for 2% of the time, Pallas kernels for 18%

profile of v7, /device:TPU:9, one launch (start us, length us, event | category | flops | bytes accessed | tf_op | source)
XLA Modules:
  0.0 91.2 jit_solution(3479627650092962050)
XLA Ops:
  0.9 1.7 %split.1 = (bf16[8,64,256]{2,1,0:T(8,128)(2,1)S(1)}, bf16[8,64,256]{2,1,0:T(8,128)(2,1)S(1)}, f32[8,3,256]{2,1,0:T(4,128)S(1)}, f32[8,3,256]{2,1,0:T(4,128)S(1)}) custom-call(s32[6]{0:T(128)S(1)} %stack.19.meta_ref, bf16[16,64,256]{2,1,0:T(8,128)(2,1)} %x.1, f32[3,16,256]{2,1,0:T(8,128)S(1)} %bitcast.8), custom_call_target="tpu_custom_call" | custom-call | tf_op jit(solution)/shard_map/split/pallas_call | solution.py:387
  2.6 1.3 %collective-permute-start = (f32[8,3,256]{2,1,0:T(4,128)S(1)}, f32[8,3,256]{2,1,0:T(4,128)S(1)}, u32[]{:S(2)}, u32[]{:S(2)}) collective-permute-start(f32[8,3,256]{2,1,0:T(4,128)S(1)} %get-tuple-element.37.refs_0_.o0), channel_id=1, source_target_pairs={{0,1},{1,0},{2,3},{3,2},{4,5},{5,4},{6,7},{7,6},{8,9},{9,8},{10,11... | collective-permute-start | bytes 73736 | tf_op jit(solution)/shard_map/ppermute | solution.py:120
  3.8 2.5 %collective-permute-start.4 = (bf16[8,64,256]{2,1,0:T(8,128)(2,1)S(1)}, bf16[8,64,256]{2,1,0:T(8,128)(2,1)S(1)}, u32[]{:S(2)}, u32[]{:S(2)}) collective-permute-start(bf16[8,64,256]{2,1,0:T(8,128)(2,1)S(1)} %get-tuple-element.42.refs_0_), channel_id=1, source_target_pairs={{0,1},{1,0},{2,3},{3,2},{4,5},{5,4},{6,7},{7,6},{8,9},{9,8},{10,11... | collective-permute-start | bytes 786440 | tf_op jit(solution)/shard_map/ppermute | solution.py:120
  8.1 2.2 %collective-permute-start.2 = (f32[16,3,256]{2,1,0:T(4,128)S(1)}, f32[16,3,256]{2,1,0:T(4,128)S(1)}, u32[]{:S(2)}, u32[]{:S(2)}) collective-permute-start(f32[16,3,256]{2,1,0:T(4,128)S(1)} %get-tuple-element.39), channel_id=1, source_target_pairs={{0,8},{1,9},{2,10},{3,11},{4,12},{5,13},{6,14},{7,15},{8,0},{9,1},... | collective-permute-start | bytes 147464 | tf_op jit(solution)/shard_map/ppermute | solution.py:120
  10.3 1.2 %collective-permute-start.3 = (f32[16,3,256]{2,1,0:T(4,128)S(1)}, f32[16,3,256]{2,1,0:T(4,128)S(1)}, u32[]{:S(2)}, u32[]{:S(2)}) collective-permute-start(f32[16,3,256]{2,1,0:T(4,128)S(1)} %get-tuple-element.40), channel_id=1, source_target_pairs={{0,2},{1,3},{2,0},{3,1},{4,6},{5,7},{6,4},{7,5},{8,16},{9,17},{10,... | collective-permute-start | bytes 147464 | tf_op jit(solution)/shard_map/ppermute | solution.py:119
  12.2 6.0 %collective-permute-done.4.refs_2_ = bf16[8,64,256]{2,1,0:T(8,128)(2,1)S(1)} collective-permute-done((bf16[8,64,256]{2,1,0:T(8,128)(2,1)S(1)}, bf16[8,64,256]{2,1,0:T(8,128)(2,1)S(1)}, u32[]{:S(2)}, u32[]{:S(2)}) %collective-permute-start.4) | collective-permute-done | bytes 262176 | tf_op jit(solution)/shard_map/ppermute | solution.py:120
  18.9 1.6 %collective-permute-start.6 = (bf16[16,64,256]{2,1,0:T(8,128)(2,1)S(1)}, bf16[16,64,256]{2,1,0:T(8,128)(2,1)S(1)}, u32[]{:S(2)}, u32[]{:S(2)}) collective-permute-start(bf16[16,64,256]{2,1,0:T(8,128)(2,1)S(1)} %get-tuple-element.44), channel_id=1, source_target_pairs={{0,8},{1,9},{2,10},{3,11},{4,12},{5,13},{6,14},{7,15},{8,0},{9,1},... | collective-permute-start | bytes 1572872 | tf_op jit(solution)/shard_map/ppermute | solution.py:120
  20.5 1.2 %collective-permute-start.7 = (bf16[16,64,256]{2,1,0:T(8,128)(2,1)S(1)}, bf16[16,64,256]{2,1,0:T(8,128)(2,1)S(1)}, u32[]{:S(2)}, u32[]{:S(2)}) collective-permute-start(bf16[16,64,256]{2,1,0:T(8,128)(2,1)S(1)} %get-tuple-element.45), channel_id=1, source_target_pairs={{0,2},{1,3},{2,0},{3,1},{4,6},{5,7},{6,4},{7,5},{8,16},{9,17},{10,... | collective-permute-start | bytes 1572872 | tf_op jit(solution)/shard_map/ppermute | solution.py:119
  21.7 8.0 %shard_map.74 = (bf16[4,4096,256]{2,1,0:T(8,128)(2,1)S(1)}, bf16[4,4096,256]{2,1,0:T(8,128)(2,1)S(1)}, bf16[64,256,48]{2,1,0:T(8,128)(2,1)S(1)}, bf16[16,48,256]{2,1,0:T(8,128)(2,1)S(1)}, s32[16]{0:T(128)S(1)}) custom-call(s32[272]{0:T(512)S(1)} %pad_add_fusion.near_ref, s32[6]{0:T(128)S(1)} %stack.19.meta_ref, ...), custom_call_target="tpu_custom_call" | custom-call | flops 4294967296 | bytes 1048576 | tf_op jit(solution)/shard_map/pallas_call | solution.py:347
  29.8 6.0 %shard_map.76 = (bf16[4,4096,256]{2,1,0:T(8,128)(2,1)S(1)}, bf16[4,4096,256]{2,1,0:T(8,128)(2,1)S(1)}) custom-call(s32[272]{0:T(512)S(1)} %pad_add_fusion.near_ref, bf16[64,256,48]{2,1,0:T(8,128)(2,1)S(1)} %get-tuple-element.48.source, bf16[16,48,256]{2,1,0:T(8,128)(2,1)S(1)} %get-tuple-element.49.target), custom_call_target="tpu_custom_call" | custom-call | flops 4294967296 | bytes 1048576 | tf_op jit(solution)/shard_map/pallas_call | solution.py:347
  35.9 3.7 %shard_map.77 = (bf16[8,64,256]{2,1,0:T(8,128)(2,1)S(1)}, f32[8,256]{1,0:T(8,128)S(1)}, bf16[64,64,256]{2,1,0:T(8,128)(2,1)S(1)}) custom-call(s32[272]{0:T(512)S(1)} %pad_add_fusion.near_ref, s32[6]{0:T(128)S(1)} %stack.19.meta_ref, bf16[8,64,256]{2,1,0:T(8,128)(2,1)S(1)} %get-tuple-element.42.refs_0_, bf16[8,64,256]{2,1,0:T(8,128)(2,1)S(1)} %get-tuple-element.43.refs_1_, ...), custom_call_target="tpu_custom_call" | custom-call | flops 2147483648 | bytes 1048576 | tf_op jit(solution)/shard_map/pallas_call | solution.py:347
  39.6 3.6 %shard_map.78 = (bf16[8,64,256]{2,1,0:T(8,128)(2,1)S(1)}, f32[8,256]{1,0:T(8,128)S(1)}) custom-call(s32[272]{0:T(512)S(1)} %pad_add_fusion.near_ref, s32[6]{0:T(128)S(1)} %stack.19.meta_ref, bf16[64,64,256]{2,1,0:T(8,128)(2,1)S(1)} %get-tuple-element.52.species, bf16[4,4096,256]{2,1,0:T(8,128)(2,1)S(1)} %get-tuple-element.46.refs_6_.refs_0_.refs_8_, ...), custom_call_target="tpu_custom_call" | custom-call | flops 2147483648 | bytes 1048576 | tf_op jit(solution)/shard_map/pallas_call | solution.py:347
  43.3 1.3 %collective-permute-start.8 = (bf16[8,64,256]{2,1,0:T(8,128)(2,1)S(1)}, bf16[8,64,256]{2,1,0:T(8,128)(2,1)S(1)}, u32[]{:S(2)}, u32[]{:S(2)}) collective-permute-start(bf16[8,64,256]{2,1,0:T(8,128)(2,1)S(1)} %get-tuple-element.53.refs_0_), channel_id=1, source_target_pairs={{0,1},{1,0},{2,3},{3,2},{4,5},{5,4},{6,7},{7,6},{8,9},{9,8},{10,11... | collective-permute-start | bytes 786440 | tf_op jit(solution)/shard_map/ppermute | solution.py:120
  47.1 9.3 %collective-permute-done.8.refs_0_.refs_2_ = bf16[8,64,256]{2,1,0:T(8,128)(2,1)S(1)} collective-permute-done((bf16[8,64,256]{2,1,0:T(8,128)(2,1)S(1)}, bf16[8,64,256]{2,1,0:T(8,128)(2,1)S(1)}, u32[]{:S(2)}, u32[]{:S(2)}) %collective-permute-start.8) | collective-permute-done | bytes 262176 | tf_op jit(solution)/shard_map/ppermute | solution.py:120
  57.0 1.3 %collective-permute-start.13 = (bf16[8,64,256]{2,1,0:T(8,128)(2,1)S(1)}, bf16[8,64,256]{2,1,0:T(8,128)(2,1)S(1)}, u32[]{:S(2)}, u32[]{:S(2)}) collective-permute-start(bf16[8,64,256]{2,1,0:T(8,128)(2,1)S(1)} %get-tuple-element.58), channel_id=1, source_target_pairs={{0,2},{1,3},{2,0},{3,1},{4,6},{5,7},{6,4},{7,5},{8,16},{9,17},{10,... | collective-permute-start | bytes 786440 | tf_op jit(solution)/shard_map/ppermute | solution.py:119
  58.5 4.6 %collective-permute-done.13.refs_7_ = bf16[8,64,256]{2,1,0:T(8,128)(2,1)S(1)} collective-permute-done((bf16[8,64,256]{2,1,0:T(8,128)(2,1)S(1)}, bf16[8,64,256]{2,1,0:T(8,128)(2,1)S(1)}, u32[]{:S(2)}, u32[]{:S(2)}) %collective-permute-start.13) | collective-permute-done | bytes 262176 | tf_op jit(solution)/shard_map/ppermute | solution.py:119
  63.2 7.8 %shard_map.81 = (bf16[2,64,256]{2,1,0:T(8,128)(2,1)S(1)}, bf16[2,64,256]{2,1,0:T(8,128)(2,1)S(1)}, bf16[2,64,256]{2,1,0:T(8,128)(2,1)S(1)}, bf16[2,64,256]{2,1,0...) custom-call(s32[272]{0:T(512)S(1)} %pad_add_fusion.near_ref, ...), custom_call_target="tpu_custom_call" | custom-call | flops 4294967296 | bytes 1048576 | tf_op jit(solution)/shard_map/pallas_call | solution.py:347
  71.0 1.5 %collective-permute-start.14 = (bf16[2,64,256]{2,1,0:T(8,128)(2,1)S(1)}, bf16[2,64,256]{2,1,0:T(8,128)(2,1)S(1)}, u32[]{:S(2)}, u32[]{:S(2)}) collective-permute-start(bf16[2,64,256]{2,1,0:T(8,128)(2,1)S(1)} %get-tuple-element.62), channel_id=1, source_target_pairs={{0,1},{1,0},{2,3},{3,2},{4,5},{5,4},{6,7},{7,6},{8,9},{9,8},{10,11... | collective-permute-start | bytes 196616 | tf_op jit(solution)/shard_map/ppermute | solution.py:482
  72.4 1.2 %collective-permute-start.15 = (bf16[2,64,256]{2,1,0:T(8,128)(2,1)S(1)}, bf16[2,64,256]{2,1,0:T(8,128)(2,1)S(1)}, u32[]{:S(2)}, u32[]{:S(2)}) collective-permute-start(bf16[2,64,256]{2,1,0:T(8,128)(2,1)S(1)} %get-tuple-element.63), channel_id=1, source_target_pairs={{0,2},{1,3},{2,0},{3,1},{4,6},{5,7},{6,4},{7,5},{8,10},{9,11},{10,... | collective-permute-start | bytes 196616 | tf_op jit(solution)/shard_map/ppermute | solution.py:482
  73.7 2.9 %collective-permute-start.17 = (bf16[2,64,256]{2,1,0:T(8,128)(2,1)S(1)}, bf16[2,64,256]{2,1,0:T(8,128)(2,1)S(1)}, u32[]{:S(2)}, u32[]{:S(2)}) collective-permute-start(bf16[2,64,256]{2,1,0:T(8,128)(2,1)S(1)} %get-tuple-element.65), channel_id=1, source_target_pairs={{0,4},{1,5},{2,6},{3,7},{4,0},{5,1},{6,2},{7,3},{8,12},{9,13},{10,... | collective-permute-start | bytes 196616 | tf_op jit(solution)/shard_map/ppermute | solution.py:482
  79.9 4.1 %collective-permute-done.18.refs_5_ = bf16[2,64,256]{2,1,0:T(8,128)(2,1)S(1)} collective-permute-done((bf16[2,64,256]{2,1,0:T(8,128)(2,1)S(1)}, bf16[2,64,256]{2,1,0:T(8,128)(2,1)S(1)}, u32[]{:S(2)}, u32[]{:S(2)}) %collective-permute-start.18) | collective-permute-done | bytes 65568 | tf_op jit(solution)/shard_map/ppermute | solution.py:482
  84.0 2.8 %collective-permute-done.19.refs_6_ = bf16[2,64,256]{2,1,0:T(8,128)(2,1)S(1)} collective-permute-done((bf16[2,64,256]{2,1,0:T(8,128)(2,1)S(1)}, bf16[2,64,256]{2,1,0:T(8,128)(2,1)S(1)}, u32[]{:S(2)}, u32[]{:S(2)}) %collective-permute-start.19) | collective-permute-done | bytes 65568 | tf_op jit(solution)/shard_map/ppermute | solution.py:482
  86.8 3.1 %collective-permute-done.20.refs_7_ = bf16[2,64,256]{2,1,0:T(8,128)(2,1)S(1)} collective-permute-done((bf16[2,64,256]{2,1,0:T(8,128)(2,1)S(1)}, bf16[2,64,256]{2,1,0:T(8,128)(2,1)S(1)}, u32[]{:S(2)}, u32[]{:S(2)}) %collective-permute-start.20) | collective-permute-done | bytes 65568 | tf_op jit(solution)/shard_map/ppermute | solution.py:482
  89.8 1.4 %place.1 = bf16[16,64,256]{2,1,0:T(8,128)(2,1)} custom-call(s32[6]{0:T(128)S(1)} %stack.19.meta_ref, bf16[2,64,256]{2,1,0:T(8,128)(2,1)S(1)} %get-tuple-element.61.refs_0_, bf16[2,64,256]{2,1,0:T(8,128)(2,1)S(1)} %collective-permute-done.14.refs_1_, bf16[2,64,256]{2,1,0:T(8,128)(2,1)S(1)} %collective-permute-done.15.refs_2_, ...), custom_call_target="tpu_custom_call" | custom-call | tf_op jit(solution)/shard_map/place/pallas_call | solution.py:483
  (42 shorter events, 10.7 us)
Async XLA Ops:
  2.6 4.6 %collective-permute-start = (f32[8,3,256]{2,1,0:T(4,128)S(1)}, f32[8,3,256]{2,1,0:T(4,128)S(1)}, u32[]{:S(2)}, u32[]{:S(2)}) collective-permute-start(f32[8,3,256]{2,1,0:T(4,128)S(1)} %get-tuple-element.37.refs_0_.o0), channel_id=1, source_target_pairs={{0,1},{1,0},{2,3},{3,2},{4,5},{5,4},{6,7},{7,6},{8,9},{9,8},{10,11... | collective-permute-start | bytes 73736 | tf_op jit(solution)/shard_map/ppermute | solution.py:120
  3.8 3.7 %collective-permute-start.1 = (f32[8,3,256]{2,1,0:T(4,128)S(1)}, f32[8,3,256]{2,1,0:T(4,128)S(1)}, u32[]{:S(2)}, u32[]{:S(2)}) collective-permute-start(f32[8,3,256]{2,1,0:T(4,128)S(1)} %get-tuple-element.38.refs_1_.o1), channel_id=1, source_target_pairs={{0,8},{1,2},{2,1},{3,4},{4,3},{5,6},{6,5},{7,15},{8,0},{9,10},{10,... | collective-permute-start | bytes 73736 | tf_op jit(solution)/shard_map/ppermute | solution.py:119
  3.8 14.4 %collective-permute-start.4 = (bf16[8,64,256]{2,1,0:T(8,128)(2,1)S(1)}, bf16[8,64,256]{2,1,0:T(8,128)(2,1)S(1)}, u32[]{:S(2)}, u32[]{:S(2)}) collective-permute-start(bf16[8,64,256]{2,1,0:T(8,128)(2,1)S(1)} %get-tuple-element.42.refs_0_), channel_id=1, source_target_pairs={{0,1},{1,0},{2,3},{3,2},{4,5},{5,4},{6,7},{7,6},{8,9},{9,8},{10,11... | collective-permute-start | bytes 786440 | tf_op jit(solution)/shard_map/ppermute | solution.py:120
  6.3 11.9 %collective-permute-start.5 = (bf16[8,64,256]{2,1,0:T(8,128)(2,1)S(1)}, bf16[8,64,256]{2,1,0:T(8,128)(2,1)S(1)}, u32[]{:S(2)}, u32[]{:S(2)}) collective-permute-start(bf16[8,64,256]{2,1,0:T(8,128)(2,1)S(1)} %get-tuple-element.43.refs_1_), channel_id=1, source_target_pairs={{0,8},{1,2},{2,1},{3,4},{4,3},{5,6},{6,5},{7,15},{8,0},{9,10},{10,... | collective-permute-start | bytes 786440 | tf_op jit(solution)/shard_map/ppermute | solution.py:119
  8.1 13.6 %collective-permute-start.2 = (f32[16,3,256]{2,1,0:T(4,128)S(1)}, f32[16,3,256]{2,1,0:T(4,128)S(1)}, u32[]{:S(2)}, u32[]{:S(2)}) collective-permute-start(f32[16,3,256]{2,1,0:T(4,128)S(1)} %get-tuple-element.39), channel_id=1, source_target_pairs={{0,8},{1,9},{2,10},{3,11},{4,12},{5,13},{6,14},{7,15},{8,0},{9,1},... | collective-permute-start | bytes 147464 | tf_op jit(solution)/shard_map/ppermute | solution.py:120
  10.3 11.3 %collective-permute-start.3 = (f32[16,3,256]{2,1,0:T(4,128)S(1)}, f32[16,3,256]{2,1,0:T(4,128)S(1)}, u32[]{:S(2)}, u32[]{:S(2)}) collective-permute-start(f32[16,3,256]{2,1,0:T(4,128)S(1)} %get-tuple-element.40), channel_id=1, source_target_pairs={{0,2},{1,3},{2,0},{3,1},{4,6},{5,7},{6,4},{7,5},{8,16},{9,17},{10,... | collective-permute-start | bytes 147464 | tf_op jit(solution)/shard_map/ppermute | solution.py:119
  18.9 17.0 %collective-permute-start.6 = (bf16[16,64,256]{2,1,0:T(8,128)(2,1)S(1)}, bf16[16,64,256]{2,1,0:T(8,128)(2,1)S(1)}, u32[]{:S(2)}, u32[]{:S(2)}) collective-permute-start(bf16[16,64,256]{2,1,0:T(8,128)(2,1)S(1)} %get-tuple-element.44), channel_id=1, source_target_pairs={{0,8},{1,9},{2,10},{3,11},{4,12},{5,13},{6,14},{7,15},{8,0},{9,1},... | collective-permute-start | bytes 1572872 | tf_op jit(solution)/shard_map/ppermute | solution.py:120
  20.5 15.4 %collective-permute-start.7 = (bf16[16,64,256]{2,1,0:T(8,128)(2,1)S(1)}, bf16[16,64,256]{2,1,0:T(8,128)(2,1)S(1)}, u32[]{:S(2)}, u32[]{:S(2)}) collective-permute-start(bf16[16,64,256]{2,1,0:T(8,128)(2,1)S(1)} %get-tuple-element.45), channel_id=1, source_target_pairs={{0,2},{1,3},{2,0},{3,1},{4,6},{5,7},{6,4},{7,5},{8,16},{9,17},{10,... | collective-permute-start | bytes 1572872 | tf_op jit(solution)/shard_map/ppermute | solution.py:119
  29.7 6.1 %copy-start = (f32[16,256]{1,0:T(8,128)S(1)}, f32[16,256]{1,0:T(8,128)}, u32[]{:S(2)}) copy-start(f32[16,256]{1,0:T(8,128)} %refs_14_.1) | copy-start | bytes 49156
  29.8 6.1 %copy-start.2 = (f32[32]{0:T(128)S(1)}, f32[32]{0:T(128)}, u32[]{:S(2)}) copy-start(f32[32]{0:T(128)} %param.10) | copy-start | bytes 388
  29.8 6.1 %copy-start.3 = (f32[32]{0:T(128)S(1)}, f32[32]{0:T(128)}, u32[]{:S(2)}) copy-start(f32[32]{0:T(128)} %param.11) | copy-start | bytes 388
  43.3 13.1 %collective-permute-start.8 = (bf16[8,64,256]{2,1,0:T(8,128)(2,1)S(1)}, bf16[8,64,256]{2,1,0:T(8,128)(2,1)S(1)}, u32[]{:S(2)}, u32[]{:S(2)}) collective-permute-start(bf16[8,64,256]{2,1,0:T(8,128)(2,1)S(1)} %get-tuple-element.53.refs_0_), channel_id=1, source_target_pairs={{0,1},{1,0},{2,3},{3,2},{4,5},{5,4},{6,7},{7,6},{8,9},{9,8},{10,11... | collective-permute-start | bytes 786440 | tf_op jit(solution)/shard_map/ppermute | solution.py:120
  44.6 11.8 %collective-permute-start.9 = (bf16[8,64,256]{2,1,0:T(8,128)(2,1)S(1)}, bf16[8,64,256]{2,1,0:T(8,128)(2,1)S(1)}, u32[]{:S(2)}, u32[]{:S(2)}) collective-permute-start(bf16[8,64,256]{2,1,0:T(8,128)(2,1)S(1)} %get-tuple-element.54.refs_1_), channel_id=1, source_target_pairs={{0,8},{1,2},{2,1},{3,4},{4,3},{5,6},{6,5},{7,15},{8,0},{9,10},{10,... | collective-permute-start | bytes 786440 | tf_op jit(solution)/shard_map/ppermute | solution.py:119
  45.1 13.2 %collective-permute-start.10 = (bf16[8,64,256]{2,1,0:T(8,128)(2,1)S(1)}, bf16[8,64,256]{2,1,0:T(8,128)(2,1)S(1)}, u32[]{:S(2)}, u32[]{:S(2)}) collective-permute-start(bf16[8,64,256]{2,1,0:T(8,128)(2,1)S(1)} %get-tuple-element.55), channel_id=1, source_target_pairs={{0,8},{1,9},{2,10},{3,11},{4,12},{5,13},{6,14},{7,15},{8,0},{9,1},... | collective-permute-start | bytes 786440 | tf_op jit(solution)/shard_map/ppermute | solution.py:120
  46.3 12.0 %collective-permute-start.12 = (bf16[8,64,256]{2,1,0:T(8,128)(2,1)S(1)}, bf16[8,64,256]{2,1,0:T(8,128)(2,1)S(1)}, u32[]{:S(2)}, u32[]{:S(2)}) collective-permute-start(bf16[8,64,256]{2,1,0:T(8,128)(2,1)S(1)} %get-tuple-element.57), channel_id=1, source_target_pairs={{0,2},{1,3},{2,0},{3,1},{4,6},{5,7},{6,4},{7,5},{8,16},{9,17},{10,... | collective-permute-start | bytes 786440 | tf_op jit(solution)/shard_map/ppermute | solution.py:119
  56.9 1.6 %collective-permute-start.11 = (bf16[8,64,256]{2,1,0:T(8,128)(2,1)S(1)}, bf16[8,64,256]{2,1,0:T(8,128)(2,1)S(1)}, u32[]{:S(2)}, u32[]{:S(2)}) collective-permute-start(bf16[8,64,256]{2,1,0:T(8,128)(2,1)S(1)} %get-tuple-element.56), channel_id=1, source_target_pairs={{0,8},{1,9},{2,10},{3,11},{4,12},{5,13},{6,14},{7,15},{8,0},{9,1},... | collective-permute-start | bytes 786440 | tf_op jit(solution)/shard_map/ppermute | solution.py:120
  57.0 6.1 %collective-permute-start.13 = (bf16[8,64,256]{2,1,0:T(8,128)(2,1)S(1)}, bf16[8,64,256]{2,1,0:T(8,128)(2,1)S(1)}, u32[]{:S(2)}, u32[]{:S(2)}) collective-permute-start(bf16[8,64,256]{2,1,0:T(8,128)(2,1)S(1)} %get-tuple-element.58), channel_id=1, source_target_pairs={{0,2},{1,3},{2,0},{3,1},{4,6},{5,7},{6,4},{7,5},{8,16},{9,17},{10,... | collective-permute-start | bytes 786440 | tf_op jit(solution)/shard_map/ppermute | solution.py:119
  71.0 6.2 %collective-permute-start.14 = (bf16[2,64,256]{2,1,0:T(8,128)(2,1)S(1)}, bf16[2,64,256]{2,1,0:T(8,128)(2,1)S(1)}, u32[]{:S(2)}, u32[]{:S(2)}) collective-permute-start(bf16[2,64,256]{2,1,0:T(8,128)(2,1)S(1)} %get-tuple-element.62), channel_id=1, source_target_pairs={{0,1},{1,0},{2,3},{3,2},{4,5},{5,4},{6,7},{7,6},{8,9},{9,8},{10,11... | collective-permute-start | bytes 196616 | tf_op jit(solution)/shard_map/ppermute | solution.py:482
  72.4 5.9 %collective-permute-start.15 = (bf16[2,64,256]{2,1,0:T(8,128)(2,1)S(1)}, bf16[2,64,256]{2,1,0:T(8,128)(2,1)S(1)}, u32[]{:S(2)}, u32[]{:S(2)}) collective-permute-start(bf16[2,64,256]{2,1,0:T(8,128)(2,1)S(1)} %get-tuple-element.63), channel_id=1, source_target_pairs={{0,2},{1,3},{2,0},{3,1},{4,6},{5,7},{6,4},{7,5},{8,10},{9,11},{10,... | collective-permute-start | bytes 196616 | tf_op jit(solution)/shard_map/ppermute | solution.py:482
  73.7 5.9 %collective-permute-start.16 = (bf16[2,64,256]{2,1,0:T(8,128)(2,1)S(1)}, bf16[2,64,256]{2,1,0:T(8,128)(2,1)S(1)}, u32[]{:S(2)}, u32[]{:S(2)}) collective-permute-start(bf16[2,64,256]{2,1,0:T(8,128)(2,1)S(1)} %get-tuple-element.64), channel_id=1, source_target_pairs={{0,3},{1,2},{2,1},{3,0},{4,7},{5,6},{6,5},{7,4},{8,11},{9,10},{10,... | collective-permute-start | bytes 196616 | tf_op jit(solution)/shard_map/ppermute | solution.py:482
  73.7 6.2 %collective-permute-start.17 = (bf16[2,64,256]{2,1,0:T(8,128)(2,1)S(1)}, bf16[2,64,256]{2,1,0:T(8,128)(2,1)S(1)}, u32[]{:S(2)}, u32[]{:S(2)}) collective-permute-start(bf16[2,64,256]{2,1,0:T(8,128)(2,1)S(1)} %get-tuple-element.65), channel_id=1, source_target_pairs={{0,4},{1,5},{2,6},{3,7},{4,0},{5,1},{6,2},{7,3},{8,12},{9,13},{10,... | collective-permute-start | bytes 196616 | tf_op jit(solution)/shard_map/ppermute | solution.py:482
  76.6 7.4 %collective-permute-start.18 = (bf16[2,64,256]{2,1,0:T(8,128)(2,1)S(1)}, bf16[2,64,256]{2,1,0:T(8,128)(2,1)S(1)}, u32[]{:S(2)}, u32[]{:S(2)}) collective-permute-start(bf16[2,64,256]{2,1,0:T(8,128)(2,1)S(1)} %get-tuple-element.66), channel_id=1, source_target_pairs={{0,5},{1,4},{2,7},{3,6},{4,1},{5,0},{6,3},{7,2},{8,13},{9,12},{10,... | collective-permute-start | bytes 196616 | tf_op jit(solution)/shard_map/ppermute | solution.py:482
  77.2 9.6 %collective-permute-start.19 = (bf16[2,64,256]{2,1,0:T(8,128)(2,1)S(1)}, bf16[2,64,256]{2,1,0:T(8,128)(2,1)S(1)}, u32[]{:S(2)}, u32[]{:S(2)}) collective-permute-start(bf16[2,64,256]{2,1,0:T(8,128)(2,1)S(1)} %get-tuple-element.67), channel_id=1, source_target_pairs={{0,6},{1,7},{2,4},{3,5},{4,2},{5,3},{6,0},{7,1},{8,14},{9,15},{10,... | collective-permute-start | bytes 196616 | tf_op jit(solution)/shard_map/ppermute | solution.py:482
  78.4 11.5 %collective-permute-start.20 = (bf16[2,64,256]{2,1,0:T(8,128)(2,1)S(1)}, bf16[2,64,256]{2,1,0:T(8,128)(2,1)S(1)}, u32[]{:S(2)}, u32[]{:S(2)}) collective-permute-start(bf16[2,64,256]{2,1,0:T(8,128)(2,1)S(1)} %get-tuple-element.68), channel_id=1, source_target_pairs={{0,7},{1,6},{2,5},{3,4},{4,3},{5,2},{6,1},{7,0},{8,15},{9,14},{10,... | collective-permute-start | bytes 196616 | tf_op jit(solution)/shard_map/ppermute | solution.py:482
  (1 other events, 0.8 us)

commit v8 on v7

--- a/solution.py
+++ b/solution.py
@@ -61,7 +61,7 @@
     low = ey < BY // 2
     by_a = low == (odd_lane == 1)
     own = (ey >= 0) & (ey < BY)
-    piece = jnp.where(by_a, 0, 1) + jnp.where(own, 0, 2)
+    piece = jnp.where(own, jnp.where(by_a, 0, 1), jnp.where(by_a, 3, 2))
     column = (ey + HALO) % HALO
     inner = piece * SIDE + ex * HALO + column
     from_a = (ex < 0) == (odd_band == 1)
@@ -77,14 +77,16 @@
         part, row = i // QUAD, i % QUAD // HALO
         up = (odd_band == 1) if piece == 4 else (odd_band == 0)
         ex = jnp.where(up, row - HALO, row + BX)
-    by_a = part % 2 == 0
+    by_a = (part == 0) | (part == 3)
     low = (by_a == (odd_lane == 1)) if not isinstance(by_a, bool) else (odd_lane == int(by_a))
     outside = part >= 2
     base = jnp.where(low, jnp.where(outside, -HALO, 0), jnp.where(outside, BY, BY - HALO))
     return ex, base + i % HALO
 
 
-def split(meta_ref, x, pos, a, b, pos_a, pos_b, sem):
+def split(meta_ref, x, pos_hbm, a, b, pos_a, pos_b, pos, sem, pos_sem):
+    pos_copy = pltpu.make_async_copy(pos_hbm, pos, pos_sem)
+    pos_copy.start()
     low_a = jnp.where(meta_ref[4] == 1, 0, BY - HALO)
     lows = (low_a, BY - HALO - low_a)
     copies = []
@@ -95,6 +97,7 @@
             copies.append(pltpu.make_async_copy(source, target, sem.at[m, r]))
     for copy in copies:
         copy.start()
+    pos_copy.wait()
     for out, low in zip((pos_a, pos_b), lows):
         for r in range(BX):
             for i in range(HALO):
@@ -388,15 +391,19 @@
         split,
         out_shape=[pltpu.VMEM((SIDE, kinds, parts), bf16)] * 2
         + [pltpu.VMEM((SIDE, axes, parts), f32)] * 2,
-        in_specs=[SM, HBM, VM],
+        in_specs=[SM, HBM, HBM],
         out_specs=[VM] * 4,
-        scratch_shapes=[pltpu.SemaphoreType.DMA((2, BX))],
+        scratch_shapes=[
+            pltpu.VMEM((axes, bins, parts), f32),
+            pltpu.SemaphoreType.DMA((2, BX)),
+            pltpu.SemaphoreType.DMA,
+        ],
         compiler_params=pltpu.CompilerParams(vmem_limit_bytes=8 << 20),
         name="split",
     )(
         meta,
         pltpu.with_memory_space_constraint(solute_load, pltpu.HBM),
-        walker_displacement.transpose(1, 0, 2),
+        pltpu.with_memory_space_constraint(walker_displacement.transpose(1, 0, 2), pltpu.HBM),
     )
 
     def rows(pieces):
@@ -406,10 +413,10 @@
         )
         return swap(by_a, by_b, "gx")
 
-    pos_sides = swap(pos_a, pos_b, "gy")
+    pos_sides = swap(pos_a, pos_b, "gy")[::-1]
     pos_bands = rows((pos_a, pos_b) + pos_sides)
     own = (own_a, own_b)
-    sides = swap(own_a, own_b, "gy")
+    sides = swap(own_a, own_b, "gy")[::-1]
     bands = rows(own + sides)
 
     ids = jnp.arange(bins, dtype=i32)
@@ -463,10 +470,10 @@
     )
 
     own = (by_a, by_b)
-    sides = swap(by_a, by_b, "gy")
-    own_bands = rows(own)
-    corners = rows(sides)
-    pieces = own + sides + (own_bands[0], corners[0], own_bands[1], corners[1])
+    sides = swap(by_a, by_b, "gy")[::-1]
+    early = rows(own + sides[:1])
+    corners = rows(sides[1:])
+    pieces = own + sides + (early[0], corners[0], early[1], corners[1])
     blocks = list(
         call(
             last_step,

time: 91.5 us -> 86.6 us (0.946)
  the two profiles are of different devices: /device:TPU:9 before, /device:TPU:0 now
where the time goes in v8:
time: 86.6 us; the launch traced here: 86.4 us
  Pallas kernels  34.6 us (40%)
  starting transfers between devices  33.4 us (39%)
  waiting for transfers between devices  16.5 us (19%)
  other arithmetic  1.45 us (2%)
    pallas_call x9, Pallas kernels, call(): pl.pallas_call(kernel, out_shape=outs, in_specs=[SM] * scalars + [VM] * (...  31.5 us
    ppermute x7, starting transfers between devices, swap(): from_b = lax.ppermute(by_b, axis, pairs_b)  11.8 us
    ppermute x7, starting transfers between devices, body(): blocks[way] = lax.ppermute(blocks[way], 'gy', pairs)  11.5 us
    ppermute x7, starting transfers between devices, swap(): from_a = lax.ppermute(by_a, axis, pairs_a)  10.1 us
    ppermute x7, waiting for transfers between devices, swap(): from_a = lax.ppermute(by_a, axis, pairs_a)  7.94 us
    ppermute x7, waiting for transfers between devices, body(): blocks[way] = lax.ppermute(blocks[way], 'gy', pairs)  5.59 us
    ppermute x7, waiting for transfers between devices, swap(): from_b = lax.ppermute(by_b, axis, pairs_b)  2.96 us
  transfers between devices with their start and end apart: 21, of which 7 were waited for; matrix products, arithmetic and copies ran while one was open for 2% of the time, Pallas kernels for 23%

profile of v8, /device:TPU:0, one launch (start us, length us, event | category | flops | bytes accessed | tf_op | source)
XLA Modules:
  0.0 86.4 jit_solution(14153889562468668408)
XLA Ops:
  0.1 1.7 %split.1 = (bf16[8,64,256]{2,1,0:T(8,128)(2,1)S(1)}, bf16[8,64,256]{2,1,0:T(8,128)(2,1)S(1)}, f32[8,3,256]{2,1,0:T(4,128)S(1)}, f32[8,3,256]{2,1,0:T(4,128)S(1)}) custom-call(s32[6]{0:T(128)S(1)} %stack.19.meta_ref, bf16[16,64,256]{2,1,0:T(8,128)(2,1)} %x.1, f32[3,16,256]{2,1,0:T(8,128)} %bitcast.14), custom_call_target="tpu_custom_call" | custom-call | tf_op jit(solution)/shard_map/split/pallas_call | solution.py:390
  2.4 4.0 %collective-permute-start.1 = (f32[8,3,256]{2,1,0:T(4,128)S(1)}, f32[8,3,256]{2,1,0:T(4,128)S(1)}, u32[]{:S(2)}, u32[]{:S(2)}) collective-permute-start(f32[8,3,256]{2,1,0:T(4,128)S(1)} %get-tuple-element.37.refs_0_.o0), channel_id=1, source_target_pairs={{0,1},{1,0},{2,3},{3,2},{4,5},{5,4},{6,7},{7,6},{8,9},{9,8},{10,11... | collective-permute-start | bytes 73736 | tf_op jit(solution)/shard_map/ppermute | solution.py:123
  6.4 3.0 %collective-permute-start.5 = (bf16[8,64,256]{2,1,0:T(8,128)(2,1)S(1)}, bf16[8,64,256]{2,1,0:T(8,128)(2,1)S(1)}, u32[]{:S(2)}, u32[]{:S(2)}) collective-permute-start(bf16[8,64,256]{2,1,0:T(8,128)(2,1)S(1)} %get-tuple-element.42.refs_0_), channel_id=1, source_target_pairs={{0,1},{1,0},{2,3},{3,2},{4,5},{5,4},{6,7},{7,6},{8,9},{9,8},{10,11... | collective-permute-start | bytes 786440 | tf_op jit(solution)/shard_map/ppermute | solution.py:123
  10.3 3.0 %collective-permute-done.1.refs_3_.c1 = f32[8,3,256]{2,1,0:T(4,128)S(1)} collective-permute-done((f32[8,3,256]{2,1,0:T(4,128)S(1)}, f32[8,3,256]{2,1,0:T(4,128)S(1)}, u32[]{:S(2)}, u32[]{:S(2)}) %collective-permute-start.1) | collective-permute-done | bytes 24608 | tf_op jit(solution)/shard_map/ppermute | solution.py:123
  13.9 1.6 %collective-permute-start.3 = (f32[16,3,256]{2,1,0:T(4,128)S(1)}, f32[16,3,256]{2,1,0:T(4,128)S(1)}, u32[]{:S(2)}, u32[]{:S(2)}) collective-permute-start(f32[16,3,256]{2,1,0:T(4,128)S(1)} %get-tuple-element.40), channel_id=1, source_target_pairs={{0,2},{1,3},{2,0},{3,1},{4,6},{5,7},{6,4},{7,5},{8,16},{9,17},{10,... | collective-permute-start | bytes 147464 | tf_op jit(solution)/shard_map/ppermute | solution.py:122
  16.2 2.6 %collective-permute-done.5.refs_3_ = bf16[8,64,256]{2,1,0:T(8,128)(2,1)S(1)} collective-permute-done((bf16[8,64,256]{2,1,0:T(8,128)(2,1)S(1)}, bf16[8,64,256]{2,1,0:T(8,128)(2,1)S(1)}, u32[]{:S(2)}, u32[]{:S(2)}) %collective-permute-start.5) | collective-permute-done | bytes 262176 | tf_op jit(solution)/shard_map/ppermute | solution.py:123
  19.5 3.3 %collective-permute-start.7 = (bf16[16,64,256]{2,1,0:T(8,128)(2,1)S(1)}, bf16[16,64,256]{2,1,0:T(8,128)(2,1)S(1)}, u32[]{:S(2)}, u32[]{:S(2)}) collective-permute-start(bf16[16,64,256]{2,1,0:T(8,128)(2,1)S(1)} %get-tuple-element.45), channel_id=1, source_target_pairs={{0,2},{1,3},{2,0},{3,1},{4,6},{5,7},{6,4},{7,5},{8,16},{9,17},{10,... | collective-permute-start | bytes 1572872 | tf_op jit(solution)/shard_map/ppermute | solution.py:122
  22.7 8.0 %shard_map.74 = (bf16[4,4096,256]{2,1,0:T(8,128)(2,1)S(1)}, bf16[4,4096,256]{2,1,0:T(8,128)(2,1)S(1)}, bf16[64,256,48]{2,1,0:T(8,128)(2,1)S(1)}, bf16[16,48,256]{2,1,0:T(8,128)(2,1)S(1)}, s32[16]{0:T(128)S(1)}) custom-call(s32[272]{0:T(512)S(1)} %pad_add_fusion.near_ref, s32[6]{0:T(128)S(1)} %stack.19.meta_ref, ...), custom_call_target="tpu_custom_call" | custom-call | flops 4294967296 | bytes 1048576 | tf_op jit(solution)/shard_map/pallas_call | solution.py:350
  30.8 6.0 %shard_map.76 = (bf16[4,4096,256]{2,1,0:T(8,128)(2,1)S(1)}, bf16[4,4096,256]{2,1,0:T(8,128)(2,1)S(1)}) custom-call(s32[272]{0:T(512)S(1)} %pad_add_fusion.near_ref, bf16[64,256,48]{2,1,0:T(8,128)(2,1)S(1)} %get-tuple-element.48.source, bf16[16,48,256]{2,1,0:T(8,128)(2,1)S(1)} %get-tuple-element.49.target), custom_call_target="tpu_custom_call" | custom-call | flops 4294967296 | bytes 1048576 | tf_op jit(solution)/shard_map/pallas_call | solution.py:350
  36.8 3.7 %shard_map.77 = (bf16[8,64,256]{2,1,0:T(8,128)(2,1)S(1)}, f32[8,256]{1,0:T(8,128)S(1)}, bf16[64,64,256]{2,1,0:T(8,128)(2,1)S(1)}) custom-call(s32[272]{0:T(512)S(1)} %pad_add_fusion.near_ref, s32[6]{0:T(128)S(1)} %stack.19.meta_ref, bf16[8,64,256]{2,1,0:T(8,128)(2,1)S(1)} %get-tuple-element.42.refs_0_, bf16[8,64,256]{2,1,0:T(8,128)(2,1)S(1)} %get-tuple-element.43.refs_1_, ...), custom_call_target="tpu_custom_call" | custom-call | flops 2147483648 | bytes 1048576 | tf_op jit(solution)/shard_map/pallas_call | solution.py:350
  40.7 3.6 %shard_map.78 = (bf16[8,64,256]{2,1,0:T(8,128)(2,1)S(1)}, f32[8,256]{1,0:T(8,128)S(1)}) custom-call(s32[272]{0:T(512)S(1)} %pad_add_fusion.near_ref, s32[6]{0:T(128)S(1)} %stack.19.meta_ref, bf16[64,64,256]{2,1,0:T(8,128)(2,1)S(1)} %get-tuple-element.52.species, bf16[4,4096,256]{2,1,0:T(8,128)(2,1)S(1)} %get-tuple-element.46.refs_6_.refs_0_.refs_8_, ...), custom_call_target="tpu_custom_call" | custom-call | flops 2147483648 | bytes 1048576 | tf_op jit(solution)/shard_map/pallas_call | solution.py:350
  44.3 1.5 %collective-permute-start.9 = (bf16[8,64,256]{2,1,0:T(8,128)(2,1)S(1)}, bf16[8,64,256]{2,1,0:T(8,128)(2,1)S(1)}, u32[]{:S(2)}, u32[]{:S(2)}) collective-permute-start(bf16[8,64,256]{2,1,0:T(8,128)(2,1)S(1)} %get-tuple-element.53.refs_0_), channel_id=1, source_target_pairs={{0,1},{1,0},{2,3},{3,2},{4,5},{5,4},{6,7},{7,6},{8,9},{9,8},{10,11... | collective-permute-start | bytes 786440 | tf_op jit(solution)/shard_map/ppermute | solution.py:123
  47.6 3.8 %collective-permute-start.12 = (bf16[12,64,256]{2,1,0:T(8,128)(2,1)S(1)}, bf16[12,64,256]{2,1,0:T(8,128)(2,1)S(1)}, u32[]{:S(2)}, u32[]{:S(2)}) collective-permute-start(bf16[12,64,256]{2,1,0:T(8,128)(2,1)S(1)} %get-tuple-element.57), channel_id=1, source_target_pairs={{0,2},{1,3},{2,0},{3,1},{4,6},{5,7},{6,4},{7,5},{8,16},{9,17},{10,... | collective-permute-start | bytes 1179656 | tf_op jit(solution)/shard_map/ppermute | solution.py:122
  51.4 2.4 %collective-permute-done.9.refs_0_.refs_3_ = bf16[8,64,256]{2,1,0:T(8,128)(2,1)S(1)} collective-permute-done((bf16[8,64,256]{2,1,0:T(8,128)(2,1)S(1)}, bf16[8,64,256]{2,1,0:T(8,128)(2,1)S(1)}, u32[]{:S(2)}, u32[]{:S(2)}) %collective-permute-start.9) | collective-permute-done | bytes 262176 | tf_op jit(solution)/shard_map/ppermute | solution.py:123
  54.6 2.5 %collective-permute-start.13 = (bf16[4,64,256]{2,1,0:T(8,128)(2,1)S(1)}, bf16[4,64,256]{2,1,0:T(8,128)(2,1)S(1)}, u32[]{:S(2)}, u32[]{:S(2)}) collective-permute-start(bf16[4,64,256]{2,1,0:T(8,128)(2,1)S(1)} %get-tuple-element.58), channel_id=1, source_target_pairs={{0,2},{1,3},{2,0},{3,1},{4,6},{5,7},{6,4},{7,5},{8,16},{9,17},{10,... | collective-permute-start | bytes 393224 | tf_op jit(solution)/shard_map/ppermute | solution.py:122
  57.1 2.9 %collective-permute-done.13.refs_7_ = bf16[4,64,256]{2,1,0:T(8,128)(2,1)S(1)} collective-permute-done((bf16[4,64,256]{2,1,0:T(8,128)(2,1)S(1)}, bf16[4,64,256]{2,1,0:T(8,128)(2,1)S(1)}, u32[]{:S(2)}, u32[]{:S(2)}) %collective-permute-start.13) | collective-permute-done | bytes 131104 | tf_op jit(solution)/shard_map/ppermute | solution.py:122
  60.1 7.8 %shard_map.81 = (bf16[2,64,256]{2,1,0:T(8,128)(2,1)S(1)}, bf16[2,64,256]{2,1,0:T(8,128)(2,1)S(1)}, bf16[2,64,256]{2,1,0:T(8,128)(2,1)S(1)}, bf16[2,64,256]{2,1,0...) custom-call(s32[272]{0:T(512)S(1)} %pad_add_fusion.near_ref, ...), custom_call_target="tpu_custom_call" | custom-call | flops 4294967296 | bytes 1048576 | tf_op jit(solution)/shard_map/pallas_call | solution.py:350
  67.9 2.0 %collective-permute-start.14 = (bf16[2,64,256]{2,1,0:T(8,128)(2,1)S(1)}, bf16[2,64,256]{2,1,0:T(8,128)(2,1)S(1)}, u32[]{:S(2)}, u32[]{:S(2)}) collective-permute-start(bf16[2,64,256]{2,1,0:T(8,128)(2,1)S(1)} %get-tuple-element.62), channel_id=1, source_target_pairs={{0,1},{1,0},{2,3},{3,2},{4,5},{5,4},{6,7},{7,6},{8,9},{9,8},{10,11... | collective-permute-start | bytes 196616 | tf_op jit(solution)/shard_map/ppermute | solution.py:489
  71.5 3.2 %collective-permute-start.17 = (bf16[2,64,256]{2,1,0:T(8,128)(2,1)S(1)}, bf16[2,64,256]{2,1,0:T(8,128)(2,1)S(1)}, u32[]{:S(2)}, u32[]{:S(2)}) collective-permute-start(bf16[2,64,256]{2,1,0:T(8,128)(2,1)S(1)} %get-tuple-element.65), channel_id=1, source_target_pairs={{0,4},{1,5},{2,6},{3,7},{4,0},{5,1},{6,2},{7,3},{8,12},{9,13},{10,... | collective-permute-start | bytes 196616 | tf_op jit(solution)/shard_map/ppermute | solution.py:489
  75.8 2.1 %collective-permute-start.19 = (bf16[2,64,256]{2,1,0:T(8,128)(2,1)S(1)}, bf16[2,64,256]{2,1,0:T(8,128)(2,1)S(1)}, u32[]{:S(2)}, u32[]{:S(2)}) collective-permute-start(bf16[2,64,256]{2,1,0:T(8,128)(2,1)S(1)} %get-tuple-element.67), channel_id=1, source_target_pairs={{0,6},{1,7},{2,4},{3,5},{4,2},{5,3},{6,0},{7,1},{8,14},{9,15},{10,... | collective-permute-start | bytes 196616 | tf_op jit(solution)/shard_map/ppermute | solution.py:489
  77.9 1.5 %collective-permute-start.20 = (bf16[2,64,256]{2,1,0:T(8,128)(2,1)S(1)}, bf16[2,64,256]{2,1,0:T(8,128)(2,1)S(1)}, u32[]{:S(2)}, u32[]{:S(2)}) collective-permute-start(bf16[2,64,256]{2,1,0:T(8,128)(2,1)S(1)} %get-tuple-element.68), channel_id=1, source_target_pairs={{0,7},{1,6},{2,5},{3,4},{4,3},{5,2},{6,1},{7,0},{8,15},{9,14},{10,... | collective-permute-start | bytes 196616 | tf_op jit(solution)/shard_map/ppermute | solution.py:489
  79.4 1.4 %collective-permute-done.17.refs_4_ = bf16[2,64,256]{2,1,0:T(8,128)(2,1)S(1)} collective-permute-done((bf16[2,64,256]{2,1,0:T(8,128)(2,1)S(1)}, bf16[2,64,256]{2,1,0:T(8,128)(2,1)S(1)}, u32[]{:S(2)}, u32[]{:S(2)}) %collective-permute-start.17) | collective-permute-done | bytes 65568 | tf_op jit(solution)/shard_map/ppermute | solution.py:489
  80.8 3.4 %collective-permute-done.18.refs_5_ = bf16[2,64,256]{2,1,0:T(8,128)(2,1)S(1)} collective-permute-done((bf16[2,64,256]{2,1,0:T(8,128)(2,1)S(1)}, bf16[2,64,256]{2,1,0:T(8,128)(2,1)S(1)}, u32[]{:S(2)}, u32[]{:S(2)}) %collective-permute-start.18) | collective-permute-done | bytes 65568 | tf_op jit(solution)/shard_map/ppermute | solution.py:489
  85.0 1.4 %place.1 = bf16[16,64,256]{2,1,0:T(8,128)(2,1)} custom-call(s32[6]{0:T(128)S(1)} %stack.19.meta_ref, bf16[2,64,256]{2,1,0:T(8,128)(2,1)S(1)} %get-tuple-element.61.refs_0_, bf16[2,64,256]{2,1,0:T(8,128)(2,1)S(1)} %collective-permute-done.14.refs_1_, bf16[2,64,256]{2,1,0:T(8,128)(2,1)S(1)} %collective-permute-done.15.refs_2_, ...), custom_call_target="tpu_custom_call" | custom-call | tf_op jit(solution)/shard_map/place/pallas_call | solution.py:490
  (40 shorter events, 9.6 us)
Async XLA Ops:
  1.8 8.5 %collective-permute-start = (f32[8,3,256]{2,1,0:T(4,128)S(1)}, f32[8,3,256]{2,1,0:T(4,128)S(1)}, u32[]{:S(2)}, u32[]{:S(2)}) collective-permute-start(f32[8,3,256]{2,1,0:T(4,128)S(1)} %get-tuple-element.38.refs_1_.o1), channel_id=1, source_target_pairs={{0,8},{1,2},{2,1},{3,4},{4,3},{5,6},{6,5},{7,15},{8,0},{9,10},{10,... | collective-permute-start | bytes 73736 | tf_op jit(solution)/shard_map/ppermute | solution.py:122
  2.4 10.9 %collective-permute-start.1 = (f32[8,3,256]{2,1,0:T(4,128)S(1)}, f32[8,3,256]{2,1,0:T(4,128)S(1)}, u32[]{:S(2)}, u32[]{:S(2)}) collective-permute-start(f32[8,3,256]{2,1,0:T(4,128)S(1)} %get-tuple-element.37.refs_0_.o0), channel_id=1, source_target_pairs={{0,1},{1,0},{2,3},{3,2},{4,5},{5,4},{6,7},{7,6},{8,9},{9,8},{10,11... | collective-permute-start | bytes 73736 | tf_op jit(solution)/shard_map/ppermute | solution.py:123
  6.4 9.8 %collective-permute-start.4 = (bf16[8,64,256]{2,1,0:T(8,128)(2,1)S(1)}, bf16[8,64,256]{2,1,0:T(8,128)(2,1)S(1)}, u32[]{:S(2)}, u32[]{:S(2)}) collective-permute-start(bf16[8,64,256]{2,1,0:T(8,128)(2,1)S(1)} %get-tuple-element.43.refs_1_), channel_id=1, source_target_pairs={{0,8},{1,2},{2,1},{3,4},{4,3},{5,6},{6,5},{7,15},{8,0},{9,10},{10,... | collective-permute-start | bytes 786440 | tf_op jit(solution)/shard_map/ppermute | solution.py:122
  6.4 12.4 %collective-permute-start.5 = (bf16[8,64,256]{2,1,0:T(8,128)(2,1)S(1)}, bf16[8,64,256]{2,1,0:T(8,128)(2,1)S(1)}, u32[]{:S(2)}, u32[]{:S(2)}) collective-permute-start(bf16[8,64,256]{2,1,0:T(8,128)(2,1)S(1)} %get-tuple-element.42.refs_0_), channel_id=1, source_target_pairs={{0,1},{1,0},{2,3},{3,2},{4,5},{5,4},{6,7},{7,6},{8,9},{9,8},{10,11... | collective-permute-start | bytes 786440 | tf_op jit(solution)/shard_map/ppermute | solution.py:123
  13.8 8.9 %collective-permute-start.2 = (f32[16,3,256]{2,1,0:T(4,128)S(1)}, f32[16,3,256]{2,1,0:T(4,128)S(1)}, u32[]{:S(2)}, u32[]{:S(2)}) collective-permute-start(f32[16,3,256]{2,1,0:T(4,128)S(1)} %get-tuple-element.39), channel_id=1, source_target_pairs={{0,8},{1,9},{2,10},{3,11},{4,12},{5,13},{6,14},{7,15},{8,0},{9,1},... | collective-permute-start | bytes 147464 | tf_op jit(solution)/shard_map/ppermute | solution.py:123
  13.9 8.8 %collective-permute-start.3 = (f32[16,3,256]{2,1,0:T(4,128)S(1)}, f32[16,3,256]{2,1,0:T(4,128)S(1)}, u32[]{:S(2)}, u32[]{:S(2)}) collective-permute-start(f32[16,3,256]{2,1,0:T(4,128)S(1)} %get-tuple-element.40), channel_id=1, source_target_pairs={{0,2},{1,3},{2,0},{3,1},{4,6},{5,7},{6,4},{7,5},{8,16},{9,17},{10,... | collective-permute-start | bytes 147464 | tf_op jit(solution)/shard_map/ppermute | solution.py:122
  19.4 17.4 %collective-permute-start.6 = (bf16[16,64,256]{2,1,0:T(8,128)(2,1)S(1)}, bf16[16,64,256]{2,1,0:T(8,128)(2,1)S(1)}, u32[]{:S(2)}, u32[]{:S(2)}) collective-permute-start(bf16[16,64,256]{2,1,0:T(8,128)(2,1)S(1)} %get-tuple-element.44), channel_id=1, source_target_pairs={{0,8},{1,9},{2,10},{3,11},{4,12},{5,13},{6,14},{7,15},{8,0},{9,1},... | collective-permute-start | bytes 1572872 | tf_op jit(solution)/shard_map/ppermute | solution.py:123
  19.5 17.4 %collective-permute-start.7 = (bf16[16,64,256]{2,1,0:T(8,128)(2,1)S(1)}, bf16[16,64,256]{2,1,0:T(8,128)(2,1)S(1)}, u32[]{:S(2)}, u32[]{:S(2)}) collective-permute-start(bf16[16,64,256]{2,1,0:T(8,128)(2,1)S(1)} %get-tuple-element.45), channel_id=1, source_target_pairs={{0,2},{1,3},{2,0},{3,1},{4,6},{5,7},{6,4},{7,5},{8,16},{9,17},{10,... | collective-permute-start | bytes 1572872 | tf_op jit(solution)/shard_map/ppermute | solution.py:122
  30.7 6.1 %copy-start = (f32[16,256]{1,0:T(8,128)S(1)}, f32[16,256]{1,0:T(8,128)}, u32[]{:S(2)}) copy-start(f32[16,256]{1,0:T(8,128)} %refs_14_.1) | copy-start | bytes 49156
  30.7 6.1 %copy-start.1 = (f32[32]{0:T(128)S(1)}, f32[32]{0:T(128)}, u32[]{:S(2)}) copy-start(f32[32]{0:T(128)} %param.10) | copy-start | bytes 388
  30.7 6.1 %copy-start.2 = (f32[32]{0:T(128)S(1)}, f32[32]{0:T(128)}, u32[]{:S(2)}) copy-start(f32[32]{0:T(128)} %param.11) | copy-start | bytes 388
  40.6 5.3 %collective-permute-start.8 = (bf16[8,64,256]{2,1,0:T(8,128)(2,1)S(1)}, bf16[8,64,256]{2,1,0:T(8,128)(2,1)S(1)}, u32[]{:S(2)}, u32[]{:S(2)}) collective-permute-start(bf16[8,64,256]{2,1,0:T(8,128)(2,1)S(1)} %get-tuple-element.54.refs_1_), channel_id=1, source_target_pairs={{0,8},{1,2},{2,1},{3,4},{4,3},{5,6},{6,5},{7,15},{8,0},{9,10},{10,... | collective-permute-start | bytes 786440 | tf_op jit(solution)/shard_map/ppermute | solution.py:122
  44.3 9.5 %collective-permute-start.9 = (bf16[8,64,256]{2,1,0:T(8,128)(2,1)S(1)}, bf16[8,64,256]{2,1,0:T(8,128)(2,1)S(1)}, u32[]{:S(2)}, u32[]{:S(2)}) collective-permute-start(bf16[8,64,256]{2,1,0:T(8,128)(2,1)S(1)} %get-tuple-element.53.refs_0_), channel_id=1, source_target_pairs={{0,1},{1,0},{2,3},{3,2},{4,5},{5,4},{6,7},{7,6},{8,9},{9,8},{10,11... | collective-permute-start | bytes 786440 | tf_op jit(solution)/shard_map/ppermute | solution.py:123
  46.5 13.6 %collective-permute-start.10 = (bf16[12,64,256]{2,1,0:T(8,128)(2,1)S(1)}, bf16[12,64,256]{2,1,0:T(8,128)(2,1)S(1)}, u32[]{:S(2)}, u32[]{:S(2)}) collective-permute-start(bf16[12,64,256]{2,1,0:T(8,128)(2,1)S(1)} %get-tuple-element.55), channel_id=1, source_target_pairs={{0,8},{1,9},{2,10},{3,11},{4,12},{5,13},{6,14},{7,15},{8,0},{9,1},... | collective-permute-start | bytes 1179656 | tf_op jit(solution)/shard_map/ppermute | solution.py:123
  47.6 12.5 %collective-permute-start.12 = (bf16[12,64,256]{2,1,0:T(8,128)(2,1)S(1)}, bf16[12,64,256]{2,1,0:T(8,128)(2,1)S(1)}, u32[]{:S(2)}, u32[]{:S(2)}) collective-permute-start(bf16[12,64,256]{2,1,0:T(8,128)(2,1)S(1)} %get-tuple-element.57), channel_id=1, source_target_pairs={{0,2},{1,3},{2,0},{3,1},{4,6},{5,7},{6,4},{7,5},{8,16},{9,17},{10,... | collective-permute-start | bytes 1179656 | tf_op jit(solution)/shard_map/ppermute | solution.py:122
  54.4 2.7 %collective-permute-start.11 = (bf16[4,64,256]{2,1,0:T(8,128)(2,1)S(1)}, bf16[4,64,256]{2,1,0:T(8,128)(2,1)S(1)}, u32[]{:S(2)}, u32[]{:S(2)}) collective-permute-start(bf16[4,64,256]{2,1,0:T(8,128)(2,1)S(1)} %get-tuple-element.56), channel_id=1, source_target_pairs={{0,8},{1,9},{2,10},{3,11},{4,12},{5,13},{6,14},{7,15},{8,0},{9,1},... | collective-permute-start | bytes 393224 | tf_op jit(solution)/shard_map/ppermute | solution.py:123
  54.6 5.5 %collective-permute-start.13 = (bf16[4,64,256]{2,1,0:T(8,128)(2,1)S(1)}, bf16[4,64,256]{2,1,0:T(8,128)(2,1)S(1)}, u32[]{:S(2)}, u32[]{:S(2)}) collective-permute-start(bf16[4,64,256]{2,1,0:T(8,128)(2,1)S(1)} %get-tuple-element.58), channel_id=1, source_target_pairs={{0,2},{1,3},{2,0},{3,1},{4,6},{5,7},{6,4},{7,5},{8,16},{9,17},{10,... | collective-permute-start | bytes 393224 | tf_op jit(solution)/shard_map/ppermute | solution.py:122
  67.9 7.9 %collective-permute-start.14 = (bf16[2,64,256]{2,1,0:T(8,128)(2,1)S(1)}, bf16[2,64,256]{2,1,0:T(8,128)(2,1)S(1)}, u32[]{:S(2)}, u32[]{:S(2)}) collective-permute-start(bf16[2,64,256]{2,1,0:T(8,128)(2,1)S(1)} %get-tuple-element.62), channel_id=1, source_target_pairs={{0,1},{1,0},{2,3},{3,2},{4,5},{5,4},{6,7},{7,6},{8,9},{9,8},{10,11... | collective-permute-start | bytes 196616 | tf_op jit(solution)/shard_map/ppermute | solution.py:489
  69.9 8.0 %collective-permute-start.15 = (bf16[2,64,256]{2,1,0:T(8,128)(2,1)S(1)}, bf16[2,64,256]{2,1,0:T(8,128)(2,1)S(1)}, u32[]{:S(2)}, u32[]{:S(2)}) collective-permute-start(bf16[2,64,256]{2,1,0:T(8,128)(2,1)S(1)} %get-tuple-element.63), channel_id=1, source_target_pairs={{0,2},{1,3},{2,0},{3,1},{4,6},{5,7},{6,4},{7,5},{8,10},{9,11},{10,... | collective-permute-start | bytes 196616 | tf_op jit(solution)/shard_map/ppermute | solution.py:489
  71.2 8.2 %collective-permute-start.16 = (bf16[2,64,256]{2,1,0:T(8,128)(2,1)S(1)}, bf16[2,64,256]{2,1,0:T(8,128)(2,1)S(1)}, u32[]{:S(2)}, u32[]{:S(2)}) collective-permute-start(bf16[2,64,256]{2,1,0:T(8,128)(2,1)S(1)} %get-tuple-element.64), channel_id=1, source_target_pairs={{0,3},{1,2},{2,1},{3,0},{4,7},{5,6},{6,5},{7,4},{8,11},{9,10},{10,... | collective-permute-start | bytes 196616 | tf_op jit(solution)/shard_map/ppermute | solution.py:489
  71.5 9.3 %collective-permute-start.17 = (bf16[2,64,256]{2,1,0:T(8,128)(2,1)S(1)}, bf16[2,64,256]{2,1,0:T(8,128)(2,1)S(1)}, u32[]{:S(2)}, u32[]{:S(2)}) collective-permute-start(bf16[2,64,256]{2,1,0:T(8,128)(2,1)S(1)} %get-tuple-element.65), channel_id=1, source_target_pairs={{0,4},{1,5},{2,6},{3,7},{4,0},{5,1},{6,2},{7,3},{8,12},{9,13},{10,... | collective-permute-start | bytes 196616 | tf_op jit(solution)/shard_map/ppermute | solution.py:489
  74.7 9.5 %collective-permute-start.18 = (bf16[2,64,256]{2,1,0:T(8,128)(2,1)S(1)}, bf16[2,64,256]{2,1,0:T(8,128)(2,1)S(1)}, u32[]{:S(2)}, u32[]{:S(2)}) collective-permute-start(bf16[2,64,256]{2,1,0:T(8,128)(2,1)S(1)} %get-tuple-element.66), channel_id=1, source_target_pairs={{0,5},{1,4},{2,7},{3,6},{4,1},{5,0},{6,3},{7,2},{8,13},{9,12},{10,... | collective-permute-start | bytes 196616 | tf_op jit(solution)/shard_map/ppermute | solution.py:489
  75.8 8.4 %collective-permute-start.19 = (bf16[2,64,256]{2,1,0:T(8,128)(2,1)S(1)}, bf16[2,64,256]{2,1,0:T(8,128)(2,1)S(1)}, u32[]{:S(2)}, u32[]{:S(2)}) collective-permute-start(bf16[2,64,256]{2,1,0:T(8,128)(2,1)S(1)} %get-tuple-element.67), channel_id=1, source_target_pairs={{0,6},{1,7},{2,4},{3,5},{4,2},{5,3},{6,0},{7,1},{8,14},{9,15},{10,... | collective-permute-start | bytes 196616 | tf_op jit(solution)/shard_map/ppermute | solution.py:489
  77.9 7.1 %collective-permute-start.20 = (bf16[2,64,256]{2,1,0:T(8,128)(2,1)S(1)}, bf16[2,64,256]{2,1,0:T(8,128)(2,1)S(1)}, u32[]{:S(2)}, u32[]{:S(2)}) collective-permute-start(bf16[2,64,256]{2,1,0:T(8,128)(2,1)S(1)} %get-tuple-element.68), channel_id=1, source_target_pairs={{0,7},{1,6},{2,5},{3,4},{4,3},{5,2},{6,1},{7,0},{8,15},{9,14},{10,... | collective-permute-start | bytes 196616 | tf_op jit(solution)/shard_map/ppermute | solution.py:489

commit v9 on v8

--- a/solution.py
+++ b/solution.py
@@ -309,11 +309,11 @@
         staged[...] = jnp.zeros_like(staged)
     for g, w_ref in enumerate(w_refs):
 
-        def some(j, _, g=g, w_ref=w_ref):
-            by_a = (j == 0) == a_first
-            for i in range(HALO):
-                c = j * HALO + i
-                at = pl.ds(g * HALO + i, 1)
+        def some(g=g, w_ref=w_ref):
+            for i in range(BY):
+                c = i
+                by_a = a_first if i < HALO else ~a_first
+                at = pl.ds(g * HALO + i % HALO, 1)
                 b = g * BY + c
                 row = row_ref[b]
                 mixed = mix(near_ref, species, gathered.at[i], w_ref[c], b)
@@ -322,7 +322,7 @@
                 staged[((row // CAP) ^ lane) * CAP + row % CAP] = moved
             return 0
 
-        lax.fori_loop(0, BY // HALO, some, 0)
+        some()
     for i, out in enumerate(outs):
         out[...] = staged[i * CAP : (i + 1) * CAP]
 
@@ -480,7 +480,7 @@
             (near, meta, row) + pieces + built + (inv_a, inv_b) + consts,
             3,
             [pltpu.VMEM((CAP, kinds, parts), bf16)] * lane_count,
-            [all_species, gathered, pltpu.VMEM((lane_count * CAP, kinds, parts), bf16)],
+            [all_species, pltpu.VMEM((BY, kinds, neighbours * parts), bf16), pltpu.VMEM((lane_count * CAP, kinds, parts), bf16)],
             work,
         )
     )

time: 86.6 us -> 86 us (level)
  the two profiles are of different devices: /device:TPU:0 before, /device:TPU:9 now
where the time goes in v9:
time: 86 us; the launch traced here: 85.8 us
  Pallas kernels  33.9 us (39%)
  starting transfers between devices  25.2 us (29%)
  waiting for transfers between devices  24.7 us (29%)
  other arithmetic  1.45 us (2%)
    pallas_call x9, Pallas kernels, call(): pl.pallas_call(kernel, out_shape=outs, in_specs=[SM] * scalars + [VM] * (...  30.8 us
    ppermute x7, starting transfers between devices, swap(): from_a = lax.ppermute(by_a, axis, pairs_a)  11.5 us
    ppermute x7, waiting for transfers between devices, body(): blocks[way] = lax.ppermute(blocks[way], 'gy', pairs)  10.3 us
    ppermute x7, waiting for transfers between devices, swap(): from_a = lax.ppermute(by_a, axis, pairs_a)  8.11 us
    ppermute x7, starting transfers between devices, body(): blocks[way] = lax.ppermute(blocks[way], 'gy', pairs)  7.57 us
    ppermute x7, waiting for transfers between devices, swap(): from_b = lax.ppermute(by_b, axis, pairs_b)  6.34 us
    ppermute x7, starting transfers between devices, swap(): from_b = lax.ppermute(by_b, axis, pairs_b)  6.11 us
  transfers between devices with their start and end apart: 21, of which 9 were waited for; matrix products, arithmetic and copies ran while one was open for 2% of the time, Pallas kernels for 24%

profile of v9, /device:TPU:9, one launch (start us, length us, event | category | flops | bytes accessed | tf_op | source)
XLA Modules:
  0.0 85.8 jit_solution(3653728201800718252)
XLA Ops:
  0.1 1.7 %split.1 = (bf16[8,64,256]{2,1,0:T(8,128)(2,1)S(1)}, bf16[8,64,256]{2,1,0:T(8,128)(2,1)S(1)}, f32[8,3,256]{2,1,0:T(4,128)S(1)}, f32[8,3,256]{2,1,0:T(4,128)S(1)}) custom-call(s32[6]{0:T(128)S(1)} %stack.19.meta_ref, bf16[16,64,256]{2,1,0:T(8,128)(2,1)} %x.1, f32[3,16,256]{2,1,0:T(8,128)} %bitcast.14), custom_call_target="tpu_custom_call" | custom-call | tf_op jit(solution)/shard_map/split/pallas_call | solution.py:390
  1.8 1.2 %collective-permute-start = (f32[8,3,256]{2,1,0:T(4,128)S(1)}, f32[8,3,256]{2,1,0:T(4,128)S(1)}, u32[]{:S(2)}, u32[]{:S(2)}) collective-permute-start(f32[8,3,256]{2,1,0:T(4,128)S(1)} %get-tuple-element.38.refs_1_.o1), channel_id=1, source_target_pairs={{0,8},{1,2},{2,1},{3,4},{4,3},{5,6},{6,5},{7,15},{8,0},{9,10},{10,... | collective-permute-start | bytes 73736 | tf_op jit(solution)/shard_map/ppermute | solution.py:122
  3.0 1.4 %collective-permute-start.1 = (f32[8,3,256]{2,1,0:T(4,128)S(1)}, f32[8,3,256]{2,1,0:T(4,128)S(1)}, u32[]{:S(2)}, u32[]{:S(2)}) collective-permute-start(f32[8,3,256]{2,1,0:T(4,128)S(1)} %get-tuple-element.37.refs_0_.o0), channel_id=1, source_target_pairs={{0,1},{1,0},{2,3},{3,2},{4,5},{5,4},{6,7},{7,6},{8,9},{9,8},{10,11... | collective-permute-start | bytes 73736 | tf_op jit(solution)/shard_map/ppermute | solution.py:123
  4.3 2.5 %collective-permute-start.5 = (bf16[8,64,256]{2,1,0:T(8,128)(2,1)S(1)}, bf16[8,64,256]{2,1,0:T(8,128)(2,1)S(1)}, u32[]{:S(2)}, u32[]{:S(2)}) collective-permute-start(bf16[8,64,256]{2,1,0:T(8,128)(2,1)S(1)} %get-tuple-element.42.refs_0_), channel_id=1, source_target_pairs={{0,1},{1,0},{2,3},{3,2},{4,5},{5,4},{6,7},{7,6},{8,9},{9,8},{10,11... | collective-permute-start | bytes 786440 | tf_op jit(solution)/shard_map/ppermute | solution.py:123
  8.3 4.8 %collective-permute-start.2 = (f32[16,3,256]{2,1,0:T(4,128)S(1)}, f32[16,3,256]{2,1,0:T(4,128)S(1)}, u32[]{:S(2)}, u32[]{:S(2)}) collective-permute-start(f32[16,3,256]{2,1,0:T(4,128)S(1)} %get-tuple-element.39), channel_id=1, source_target_pairs={{0,8},{1,9},{2,10},{3,11},{4,12},{5,13},{6,14},{7,15},{8,0},{9,1},... | collective-permute-start | bytes 147464 | tf_op jit(solution)/shard_map/ppermute | solution.py:123
  13.1 1.2 %collective-permute-start.3 = (f32[16,3,256]{2,1,0:T(4,128)S(1)}, f32[16,3,256]{2,1,0:T(4,128)S(1)}, u32[]{:S(2)}, u32[]{:S(2)}) collective-permute-start(f32[16,3,256]{2,1,0:T(4,128)S(1)} %get-tuple-element.40), channel_id=1, source_target_pairs={{0,2},{1,3},{2,0},{3,1},{4,6},{5,7},{6,4},{7,5},{8,16},{9,17},{10,... | collective-permute-start | bytes 147464 | tf_op jit(solution)/shard_map/ppermute | solution.py:122
  14.9 4.1 %collective-permute-done.5.refs_3_ = bf16[8,64,256]{2,1,0:T(8,128)(2,1)S(1)} collective-permute-done((bf16[8,64,256]{2,1,0:T(8,128)(2,1)S(1)}, bf16[8,64,256]{2,1,0:T(8,128)(2,1)S(1)}, u32[]{:S(2)}, u32[]{:S(2)}) %collective-permute-start.5) | collective-permute-done | bytes 262176 | tf_op jit(solution)/shard_map/ppermute | solution.py:123
  20.3 1.2 %collective-permute-start.7 = (bf16[16,64,256]{2,1,0:T(8,128)(2,1)S(1)}, bf16[16,64,256]{2,1,0:T(8,128)(2,1)S(1)}, u32[]{:S(2)}, u32[]{:S(2)}) collective-permute-start(bf16[16,64,256]{2,1,0:T(8,128)(2,1)S(1)} %get-tuple-element.45), channel_id=1, source_target_pairs={{0,2},{1,3},{2,0},{3,1},{4,6},{5,7},{6,4},{7,5},{8,16},{9,17},{10,... | collective-permute-start | bytes 1572872 | tf_op jit(solution)/shard_map/ppermute | solution.py:122
  21.5 8.0 %shard_map.74 = (bf16[4,4096,256]{2,1,0:T(8,128)(2,1)S(1)}, bf16[4,4096,256]{2,1,0:T(8,128)(2,1)S(1)}, bf16[64,256,48]{2,1,0:T(8,128)(2,1)S(1)}, bf16[16,48,256]{2,1,0:T(8,128)(2,1)S(1)}, s32[16]{0:T(128)S(1)}) custom-call(s32[272]{0:T(512)S(1)} %pad_add_fusion.near_ref, s32[6]{0:T(128)S(1)} %stack.19.meta_ref, ...), custom_call_target="tpu_custom_call" | custom-call | flops 4294967296 | bytes 1048576 | tf_op jit(solution)/shard_map/pallas_call | solution.py:350
  29.5 6.2 %shard_map.76 = (bf16[4,4096,256]{2,1,0:T(8,128)(2,1)S(1)}, bf16[4,4096,256]{2,1,0:T(8,128)(2,1)S(1)}) custom-call(s32[272]{0:T(512)S(1)} %pad_add_fusion.near_ref, bf16[64,256,48]{2,1,0:T(8,128)(2,1)S(1)} %get-tuple-element.48.source, bf16[16,48,256]{2,1,0:T(8,128)(2,1)S(1)} %get-tuple-element.49.target), custom_call_target="tpu_custom_call" | custom-call | flops 4294967296 | bytes 1048576 | tf_op jit(solution)/shard_map/pallas_call | solution.py:350
  35.8 3.7 %shard_map.77 = (bf16[8,64,256]{2,1,0:T(8,128)(2,1)S(1)}, f32[8,256]{1,0:T(8,128)S(1)}, bf16[64,64,256]{2,1,0:T(8,128)(2,1)S(1)}) custom-call(s32[272]{0:T(512)S(1)} %pad_add_fusion.near_ref, s32[6]{0:T(128)S(1)} %stack.19.meta_ref, bf16[8,64,256]{2,1,0:T(8,128)(2,1)S(1)} %get-tuple-element.42.refs_0_, bf16[8,64,256]{2,1,0:T(8,128)(2,1)S(1)} %get-tuple-element.43.refs_1_, ...), custom_call_target="tpu_custom_call" | custom-call | flops 2147483648 | bytes 1048576 | tf_op jit(solution)/shard_map/pallas_call | solution.py:350
  40.1 3.6 %shard_map.78 = (bf16[8,64,256]{2,1,0:T(8,128)(2,1)S(1)}, f32[8,256]{1,0:T(8,128)S(1)}) custom-call(s32[272]{0:T(512)S(1)} %pad_add_fusion.near_ref, s32[6]{0:T(128)S(1)} %stack.19.meta_ref, bf16[64,64,256]{2,1,0:T(8,128)(2,1)S(1)} %get-tuple-element.52.species, bf16[4,4096,256]{2,1,0:T(8,128)(2,1)S(1)} %get-tuple-element.46.refs_6_.refs_0_.refs_8_, ...), custom_call_target="tpu_custom_call" | custom-call | flops 2147483648 | bytes 1048576 | tf_op jit(solution)/shard_map/pallas_call | solution.py:350
  43.7 1.7 %collective-permute-start.9 = (bf16[8,64,256]{2,1,0:T(8,128)(2,1)S(1)}, bf16[8,64,256]{2,1,0:T(8,128)(2,1)S(1)}, u32[]{:S(2)}, u32[]{:S(2)}) collective-permute-start(bf16[8,64,256]{2,1,0:T(8,128)(2,1)S(1)} %get-tuple-element.53.refs_0_), channel_id=1, source_target_pairs={{0,1},{1,0},{2,3},{3,2},{4,5},{5,4},{6,7},{7,6},{8,9},{9,8},{10,11... | collective-permute-start | bytes 786440 | tf_op jit(solution)/shard_map/ppermute | solution.py:123
  45.3 2.7 %collective-permute-done.8.refs_2_ = bf16[8,64,256]{2,1,0:T(8,128)(2,1)S(1)} collective-permute-done((bf16[8,64,256]{2,1,0:T(8,128)(2,1)S(1)}, bf16[8,64,256]{2,1,0:T(8,128)(2,1)S(1)}, u32[]{:S(2)}, u32[]{:S(2)}) %collective-permute-start.8) | collective-permute-done | bytes 262176 | tf_op jit(solution)/shard_map/ppermute | solution.py:122
  48.7 1.3 %collective-permute-start.12 = (bf16[12,64,256]{2,1,0:T(8,128)(2,1)S(1)}, bf16[12,64,256]{2,1,0:T(8,128)(2,1)S(1)}, u32[]{:S(2)}, u32[]{:S(2)}) collective-permute-start(bf16[12,64,256]{2,1,0:T(8,128)(2,1)S(1)} %get-tuple-element.57), channel_id=1, source_target_pairs={{0,2},{1,3},{2,0},{3,1},{4,6},{5,7},{6,4},{7,5},{8,16},{9,17},{10,... | collective-permute-start | bytes 1179656 | tf_op jit(solution)/shard_map/ppermute | solution.py:122
  50.0 3.7 %collective-permute-done.9.refs_0_.refs_3_ = bf16[8,64,256]{2,1,0:T(8,128)(2,1)S(1)} collective-permute-done((bf16[8,64,256]{2,1,0:T(8,128)(2,1)S(1)}, bf16[8,64,256]{2,1,0:T(8,128)(2,1)S(1)}, u32[]{:S(2)}, u32[]{:S(2)}) %collective-permute-start.9) | collective-permute-done | bytes 262176 | tf_op jit(solution)/shard_map/ppermute | solution.py:123
  55.8 3.7 %collective-permute-done.13.refs_7_ = bf16[4,64,256]{2,1,0:T(8,128)(2,1)S(1)} collective-permute-done((bf16[4,64,256]{2,1,0:T(8,128)(2,1)S(1)}, bf16[4,64,256]{2,1,0:T(8,128)(2,1)S(1)}, u32[]{:S(2)}, u32[]{:S(2)}) %collective-permute-start.13) | collective-permute-done | bytes 131104 | tf_op jit(solution)/shard_map/ppermute | solution.py:122
  59.5 6.9 %shard_map.81 = (bf16[2,64,256]{2,1,0:T(8,128)(2,1)S(1)}, bf16[2,64,256]{2,1,0:T(8,128)(2,1)S(1)}, bf16[2,64,256]{2,1,0:T(8,128)(2,1)S(1)}, bf16[2,64,256]{2,1,0...) custom-call(s32[272]{0:T(512)S(1)} %pad_add_fusion.near_ref, ...), custom_call_target="tpu_custom_call" | custom-call | flops 4294967296 | bytes 1048576 | tf_op jit(solution)/shard_map/pallas_call | solution.py:350
  67.8 1.3 %collective-permute-start.16 = (bf16[2,64,256]{2,1,0:T(8,128)(2,1)S(1)}, bf16[2,64,256]{2,1,0:T(8,128)(2,1)S(1)}, u32[]{:S(2)}, u32[]{:S(2)}) collective-permute-start(bf16[2,64,256]{2,1,0:T(8,128)(2,1)S(1)} %get-tuple-element.64), channel_id=1, source_target_pairs={{0,3},{1,2},{2,1},{3,0},{4,7},{5,6},{6,5},{7,4},{8,11},{9,10},{10,... | collective-permute-start | bytes 196616 | tf_op jit(solution)/shard_map/ppermute | solution.py:489
  69.1 2.3 %collective-permute-start.17 = (bf16[2,64,256]{2,1,0:T(8,128)(2,1)S(1)}, bf16[2,64,256]{2,1,0:T(8,128)(2,1)S(1)}, u32[]{:S(2)}, u32[]{:S(2)}) collective-permute-start(bf16[2,64,256]{2,1,0:T(8,128)(2,1)S(1)} %get-tuple-element.65), channel_id=1, source_target_pairs={{0,4},{1,5},{2,6},{3,7},{4,0},{5,1},{6,2},{7,3},{8,12},{9,13},{10,... | collective-permute-start | bytes 196616 | tf_op jit(solution)/shard_map/ppermute | solution.py:489
  74.9 4.9 %collective-permute-done.18.refs_5_ = bf16[2,64,256]{2,1,0:T(8,128)(2,1)S(1)} collective-permute-done((bf16[2,64,256]{2,1,0:T(8,128)(2,1)S(1)}, bf16[2,64,256]{2,1,0:T(8,128)(2,1)S(1)}, u32[]{:S(2)}, u32[]{:S(2)}) %collective-permute-start.18) | collective-permute-done | bytes 65568 | tf_op jit(solution)/shard_map/ppermute | solution.py:489
  79.8 1.5 %collective-permute-done.19.refs_6_ = bf16[2,64,256]{2,1,0:T(8,128)(2,1)S(1)} collective-permute-done((bf16[2,64,256]{2,1,0:T(8,128)(2,1)S(1)}, bf16[2,64,256]{2,1,0:T(8,128)(2,1)S(1)}, u32[]{:S(2)}, u32[]{:S(2)}) %collective-permute-start.19) | collective-permute-done | bytes 65568 | tf_op jit(solution)/shard_map/ppermute | solution.py:489
  81.4 2.9 %collective-permute-done.20.refs_7_ = bf16[2,64,256]{2,1,0:T(8,128)(2,1)S(1)} collective-permute-done((bf16[2,64,256]{2,1,0:T(8,128)(2,1)S(1)}, bf16[2,64,256]{2,1,0:T(8,128)(2,1)S(1)}, u32[]{:S(2)}, u32[]{:S(2)}) %collective-permute-start.20) | collective-permute-done | bytes 65568 | tf_op jit(solution)/shard_map/ppermute | solution.py:489
  84.3 1.4 %place.1 = bf16[16,64,256]{2,1,0:T(8,128)(2,1)} custom-call(s32[6]{0:T(128)S(1)} %stack.19.meta_ref, bf16[2,64,256]{2,1,0:T(8,128)(2,1)S(1)} %get-tuple-element.61.refs_0_, bf16[2,64,256]{2,1,0:T(8,128)(2,1)S(1)} %collective-permute-done.14.refs_1_, bf16[2,64,256]{2,1,0:T(8,128)(2,1)S(1)} %collective-permute-done.15.refs_2_, ...), custom_call_target="tpu_custom_call" | custom-call | tf_op jit(solution)/shard_map/place/pallas_call | solution.py:490
  (40 shorter events, 11.7 us)
Async XLA Ops:
  1.8 5.9 %collective-permute-start = (f32[8,3,256]{2,1,0:T(4,128)S(1)}, f32[8,3,256]{2,1,0:T(4,128)S(1)}, u32[]{:S(2)}, u32[]{:S(2)}) collective-permute-start(f32[8,3,256]{2,1,0:T(4,128)S(1)} %get-tuple-element.38.refs_1_.o1), channel_id=1, source_target_pairs={{0,8},{1,2},{2,1},{3,4},{4,3},{5,6},{6,5},{7,15},{8,0},{9,10},{10,... | collective-permute-start | bytes 73736 | tf_op jit(solution)/shard_map/ppermute | solution.py:122
  3.0 4.7 %collective-permute-start.1 = (f32[8,3,256]{2,1,0:T(4,128)S(1)}, f32[8,3,256]{2,1,0:T(4,128)S(1)}, u32[]{:S(2)}, u32[]{:S(2)}) collective-permute-start(f32[8,3,256]{2,1,0:T(4,128)S(1)} %get-tuple-element.37.refs_0_.o0), channel_id=1, source_target_pairs={{0,1},{1,0},{2,3},{3,2},{4,5},{5,4},{6,7},{7,6},{8,9},{9,8},{10,11... | collective-permute-start | bytes 73736 | tf_op jit(solution)/shard_map/ppermute | solution.py:123
  4.3 10.6 %collective-permute-start.4 = (bf16[8,64,256]{2,1,0:T(8,128)(2,1)S(1)}, bf16[8,64,256]{2,1,0:T(8,128)(2,1)S(1)}, u32[]{:S(2)}, u32[]{:S(2)}) collective-permute-start(bf16[8,64,256]{2,1,0:T(8,128)(2,1)S(1)} %get-tuple-element.43.refs_1_), channel_id=1, source_target_pairs={{0,8},{1,2},{2,1},{3,4},{4,3},{5,6},{6,5},{7,15},{8,0},{9,10},{10,... | collective-permute-start | bytes 786440 | tf_op jit(solution)/shard_map/ppermute | solution.py:122
  4.3 14.7 %collective-permute-start.5 = (bf16[8,64,256]{2,1,0:T(8,128)(2,1)S(1)}, bf16[8,64,256]{2,1,0:T(8,128)(2,1)S(1)}, u32[]{:S(2)}, u32[]{:S(2)}) collective-permute-start(bf16[8,64,256]{2,1,0:T(8,128)(2,1)S(1)} %get-tuple-element.42.refs_0_), channel_id=1, source_target_pairs={{0,1},{1,0},{2,3},{3,2},{4,5},{5,4},{6,7},{7,6},{8,9},{9,8},{10,11... | collective-permute-start | bytes 786440 | tf_op jit(solution)/shard_map/ppermute | solution.py:123
  8.3 13.2 %collective-permute-start.2 = (f32[16,3,256]{2,1,0:T(4,128)S(1)}, f32[16,3,256]{2,1,0:T(4,128)S(1)}, u32[]{:S(2)}, u32[]{:S(2)}) collective-permute-start(f32[16,3,256]{2,1,0:T(4,128)S(1)} %get-tuple-element.39), channel_id=1, source_target_pairs={{0,8},{1,9},{2,10},{3,11},{4,12},{5,13},{6,14},{7,15},{8,0},{9,1},... | collective-permute-start | bytes 147464 | tf_op jit(solution)/shard_map/ppermute | solution.py:123
  13.1 8.4 %collective-permute-start.3 = (f32[16,3,256]{2,1,0:T(4,128)S(1)}, f32[16,3,256]{2,1,0:T(4,128)S(1)}, u32[]{:S(2)}, u32[]{:S(2)}) collective-permute-start(f32[16,3,256]{2,1,0:T(4,128)S(1)} %get-tuple-element.40), channel_id=1, source_target_pairs={{0,2},{1,3},{2,0},{3,1},{4,6},{5,7},{6,4},{7,5},{8,16},{9,17},{10,... | collective-permute-start | bytes 147464 | tf_op jit(solution)/shard_map/ppermute | solution.py:122
  19.7 16.0 %collective-permute-start.6 = (bf16[16,64,256]{2,1,0:T(8,128)(2,1)S(1)}, bf16[16,64,256]{2,1,0:T(8,128)(2,1)S(1)}, u32[]{:S(2)}, u32[]{:S(2)}) collective-permute-start(bf16[16,64,256]{2,1,0:T(8,128)(2,1)S(1)} %get-tuple-element.44), channel_id=1, source_target_pairs={{0,8},{1,9},{2,10},{3,11},{4,12},{5,13},{6,14},{7,15},{8,0},{9,1},... | collective-permute-start | bytes 1572872 | tf_op jit(solution)/shard_map/ppermute | solution.py:123
  20.3 15.5 %collective-permute-start.7 = (bf16[16,64,256]{2,1,0:T(8,128)(2,1)S(1)}, bf16[16,64,256]{2,1,0:T(8,128)(2,1)S(1)}, u32[]{:S(2)}, u32[]{:S(2)}) collective-permute-start(bf16[16,64,256]{2,1,0:T(8,128)(2,1)S(1)} %get-tuple-element.45), channel_id=1, source_target_pairs={{0,2},{1,3},{2,0},{3,1},{4,6},{5,7},{6,4},{7,5},{8,16},{9,17},{10,... | collective-permute-start | bytes 1572872 | tf_op jit(solution)/shard_map/ppermute | solution.py:122
  29.5 6.3 %copy-start = (f32[16,256]{1,0:T(8,128)S(1)}, f32[16,256]{1,0:T(8,128)}, u32[]{:S(2)}) copy-start(f32[16,256]{1,0:T(8,128)} %refs_14_.1) | copy-start | bytes 49156
  29.5 6.3 %copy-start.1 = (f32[32]{0:T(128)S(1)}, f32[32]{0:T(128)}, u32[]{:S(2)}) copy-start(f32[32]{0:T(128)} %param.10) | copy-start | bytes 388
  29.5 6.3 %copy-start.2 = (f32[32]{0:T(128)S(1)}, f32[32]{0:T(128)}, u32[]{:S(2)}) copy-start(f32[32]{0:T(128)} %param.11) | copy-start | bytes 388
  39.6 8.5 %collective-permute-start.8 = (bf16[8,64,256]{2,1,0:T(8,128)(2,1)S(1)}, bf16[8,64,256]{2,1,0:T(8,128)(2,1)S(1)}, u32[]{:S(2)}, u32[]{:S(2)}) collective-permute-start(bf16[8,64,256]{2,1,0:T(8,128)(2,1)S(1)} %get-tuple-element.54.refs_1_), channel_id=1, source_target_pairs={{0,8},{1,2},{2,1},{3,4},{4,3},{5,6},{6,5},{7,15},{8,0},{9,10},{10,... | collective-permute-start | bytes 786440 | tf_op jit(solution)/shard_map/ppermute | solution.py:122
  43.7 10.0 %collective-permute-start.9 = (bf16[8,64,256]{2,1,0:T(8,128)(2,1)S(1)}, bf16[8,64,256]{2,1,0:T(8,128)(2,1)S(1)}, u32[]{:S(2)}, u32[]{:S(2)}) collective-permute-start(bf16[8,64,256]{2,1,0:T(8,128)(2,1)S(1)} %get-tuple-element.53.refs_0_), channel_id=1, source_target_pairs={{0,1},{1,0},{2,3},{3,2},{4,5},{5,4},{6,7},{7,6},{8,9},{9,8},{10,11... | collective-permute-start | bytes 786440 | tf_op jit(solution)/shard_map/ppermute | solution.py:123
  48.6 10.9 %collective-permute-start.10 = (bf16[12,64,256]{2,1,0:T(8,128)(2,1)S(1)}, bf16[12,64,256]{2,1,0:T(8,128)(2,1)S(1)}, u32[]{:S(2)}, u32[]{:S(2)}) collective-permute-start(bf16[12,64,256]{2,1,0:T(8,128)(2,1)S(1)} %get-tuple-element.55), channel_id=1, source_target_pairs={{0,8},{1,9},{2,10},{3,11},{4,12},{5,13},{6,14},{7,15},{8,0},{9,1},... | collective-permute-start | bytes 1179656 | tf_op jit(solution)/shard_map/ppermute | solution.py:123
  48.7 10.8 %collective-permute-start.12 = (bf16[12,64,256]{2,1,0:T(8,128)(2,1)S(1)}, bf16[12,64,256]{2,1,0:T(8,128)(2,1)S(1)}, u32[]{:S(2)}, u32[]{:S(2)}) collective-permute-start(bf16[12,64,256]{2,1,0:T(8,128)(2,1)S(1)} %get-tuple-element.57), channel_id=1, source_target_pairs={{0,2},{1,3},{2,0},{3,1},{4,6},{5,7},{6,4},{7,5},{8,16},{9,17},{10,... | collective-permute-start | bytes 1179656 | tf_op jit(solution)/shard_map/ppermute | solution.py:122
  54.3 1.5 %collective-permute-start.11 = (bf16[4,64,256]{2,1,0:T(8,128)(2,1)S(1)}, bf16[4,64,256]{2,1,0:T(8,128)(2,1)S(1)}, u32[]{:S(2)}, u32[]{:S(2)}) collective-permute-start(bf16[4,64,256]{2,1,0:T(8,128)(2,1)S(1)} %get-tuple-element.56), channel_id=1, source_target_pairs={{0,8},{1,9},{2,10},{3,11},{4,12},{5,13},{6,14},{7,15},{8,0},{9,1},... | collective-permute-start | bytes 393224 | tf_op jit(solution)/shard_map/ppermute | solution.py:123
  54.8 4.7 %collective-permute-start.13 = (bf16[4,64,256]{2,1,0:T(8,128)(2,1)S(1)}, bf16[4,64,256]{2,1,0:T(8,128)(2,1)S(1)}, u32[]{:S(2)}, u32[]{:S(2)}) collective-permute-start(bf16[4,64,256]{2,1,0:T(8,128)(2,1)S(1)} %get-tuple-element.58), channel_id=1, source_target_pairs={{0,2},{1,3},{2,0},{3,1},{4,6},{5,7},{6,4},{7,5},{8,16},{9,17},{10,... | collective-permute-start | bytes 393224 | tf_op jit(solution)/shard_map/ppermute | solution.py:122
  66.4 5.8 %collective-permute-start.14 = (bf16[2,64,256]{2,1,0:T(8,128)(2,1)S(1)}, bf16[2,64,256]{2,1,0:T(8,128)(2,1)S(1)}, u32[]{:S(2)}, u32[]{:S(2)}) collective-permute-start(bf16[2,64,256]{2,1,0:T(8,128)(2,1)S(1)} %get-tuple-element.62), channel_id=1, source_target_pairs={{0,1},{1,0},{2,3},{3,2},{4,5},{5,4},{6,7},{7,6},{8,9},{9,8},{10,11... | collective-permute-start | bytes 196616 | tf_op jit(solution)/shard_map/ppermute | solution.py:489
  67.4 5.6 %collective-permute-start.15 = (bf16[2,64,256]{2,1,0:T(8,128)(2,1)S(1)}, bf16[2,64,256]{2,1,0:T(8,128)(2,1)S(1)}, u32[]{:S(2)}, u32[]{:S(2)}) collective-permute-start(bf16[2,64,256]{2,1,0:T(8,128)(2,1)S(1)} %get-tuple-element.63), channel_id=1, source_target_pairs={{0,2},{1,3},{2,0},{3,1},{4,6},{5,7},{6,4},{7,5},{8,10},{9,11},{10,... | collective-permute-start | bytes 196616 | tf_op jit(solution)/shard_map/ppermute | solution.py:489
  67.8 6.2 %collective-permute-start.16 = (bf16[2,64,256]{2,1,0:T(8,128)(2,1)S(1)}, bf16[2,64,256]{2,1,0:T(8,128)(2,1)S(1)}, u32[]{:S(2)}, u32[]{:S(2)}) collective-permute-start(bf16[2,64,256]{2,1,0:T(8,128)(2,1)S(1)} %get-tuple-element.64), channel_id=1, source_target_pairs={{0,3},{1,2},{2,1},{3,0},{4,7},{5,6},{6,5},{7,4},{8,11},{9,10},{10,... | collective-permute-start | bytes 196616 | tf_op jit(solution)/shard_map/ppermute | solution.py:489
  69.1 5.8 %collective-permute-start.17 = (bf16[2,64,256]{2,1,0:T(8,128)(2,1)S(1)}, bf16[2,64,256]{2,1,0:T(8,128)(2,1)S(1)}, u32[]{:S(2)}, u32[]{:S(2)}) collective-permute-start(bf16[2,64,256]{2,1,0:T(8,128)(2,1)S(1)} %get-tuple-element.65), channel_id=1, source_target_pairs={{0,4},{1,5},{2,6},{3,7},{4,0},{5,1},{6,2},{7,3},{8,12},{9,13},{10,... | collective-permute-start | bytes 196616 | tf_op jit(solution)/shard_map/ppermute | solution.py:489
  71.4 8.5 %collective-permute-start.18 = (bf16[2,64,256]{2,1,0:T(8,128)(2,1)S(1)}, bf16[2,64,256]{2,1,0:T(8,128)(2,1)S(1)}, u32[]{:S(2)}, u32[]{:S(2)}) collective-permute-start(bf16[2,64,256]{2,1,0:T(8,128)(2,1)S(1)} %get-tuple-element.66), channel_id=1, source_target_pairs={{0,5},{1,4},{2,7},{3,6},{4,1},{5,0},{6,3},{7,2},{8,13},{9,12},{10,... | collective-permute-start | bytes 196616 | tf_op jit(solution)/shard_map/ppermute | solution.py:489
  72.2 9.2 %collective-permute-start.19 = (bf16[2,64,256]{2,1,0:T(8,128)(2,1)S(1)}, bf16[2,64,256]{2,1,0:T(8,128)(2,1)S(1)}, u32[]{:S(2)}, u32[]{:S(2)}) collective-permute-start(bf16[2,64,256]{2,1,0:T(8,128)(2,1)S(1)} %get-tuple-element.67), channel_id=1, source_target_pairs={{0,6},{1,7},{2,4},{3,5},{4,2},{5,3},{6,0},{7,1},{8,14},{9,15},{10,... | collective-permute-start | bytes 196616 | tf_op jit(solution)/shard_map/ppermute | solution.py:489
  73.1 11.2 %collective-permute-start.20 = (bf16[2,64,256]{2,1,0:T(8,128)(2,1)S(1)}, bf16[2,64,256]{2,1,0:T(8,128)(2,1)S(1)}, u32[]{:S(2)}, u32[]{:S(2)}) collective-permute-start(bf16[2,64,256]{2,1,0:T(8,128)(2,1)S(1)} %get-tuple-element.68), channel_id=1, source_target_pairs={{0,7},{1,6},{2,5},{3,4},{4,3},{5,2},{6,1},{7,0},{8,15},{9,14},{10,... | collective-permute-start | bytes 196616 | tf_op jit(solution)/shard_map/ppermute | solution.py:489

commit v10 on v9

--- a/solution.py
+++ b/solution.py
@@ -194,7 +194,7 @@
 
 
 def build_first(
-    near_ref, meta_ref, o0, o1, c0, c1, r0, r1, w0, w1, source, target, row_ref, taken
+    near_ref, meta_ref, o0, o1, c0, c1, r0, r1, w0, source, target, row_ref, taken
 ):
     odd_lane, odd_band = meta_ref[4], meta_ref[5]
     for piece, ref in enumerate((o0, o1, c0, c1, r0, r1)):
@@ -224,11 +224,11 @@
         return 0
 
     lax.fori_loop(0, BX * BY, place, 0)
-    build_rows(near_ref, source, target, (w0, w1), 0)
-
-
-def build_second(near_ref, source, target, w2, w3):
-    build_rows(near_ref, source, target, (w2, w3), BX // 2)
+    build_rows(near_ref, source, target, (w0,), 0)
+
+
+def build_second(near_ref, source, target, *w_refs):
+    build_rows(near_ref, source, target, w_refs, BX - len(w_refs))
 
 
 def column(row_ref):
@@ -436,12 +436,11 @@
     gathered = pltpu.VMEM((HALO, kinds, neighbours * parts), bf16)
     all_species = pltpu.VMEM((EXT, kinds, parts), bf16)
     work = 2 * bins * neighbours * parts * parts * 128
-    w0, w1, source, target, row = call(
+    w0, source, target, row = call(
         build_first,
         (near, meta, pos_a, pos_b) + pos_sides + pos_bands,
         2,
         [
-            w_row,
             w_row,
             pltpu.VMEM((EXT, parts, FEATURES), bf16),
             pltpu.VMEM((bins, FEATURES, parts), bf16),
@@ -450,7 +449,7 @@
         [pltpu.SMEM((lane_count,), i32)],
         work,
     )
-    w2, w3 = call(build_second, (near, source, target), 1, [w_row, w_row], [], work)
+    w1, w2, w3 = call(build_second, (near, source, target), 1, [w_row] * 3, [], work)
     built = (w0, w1, w2, w3)
     by_b, inv_b, species = call(
         step_b,

time: 86 us -> 86 us (level)
  the two profiles are of different devices: /device:TPU:9 before, /device:TPU:0 now
where the time goes in v10:
time: 86 us; the launch traced here: 85.8 us
  Pallas kernels  33.8 us (39%)
  starting transfers between devices  33.5 us (39%)
  waiting for transfers between devices  16.5 us (19%)
  other arithmetic  1.45 us (2%)
    pallas_call x9, Pallas kernels, call(): pl.pallas_call(kernel, out_shape=outs, in_specs=[SM] * scalars + [VM] * (...  30.7 us
    ppermute x7, starting transfers between devices, swap(): from_b = lax.ppermute(by_b, axis, pairs_b)  11.9 us
    ppermute x7, starting transfers between devices, body(): blocks[way] = lax.ppermute(blocks[way], 'gy', pairs)  11.5 us
    ppermute x7, starting transfers between devices, swap(): from_a = lax.ppermute(by_a, axis, pairs_a)  10.1 us
    ppermute x7, waiting for transfers between devices, swap(): from_a = lax.ppermute(by_a, axis, pairs_a)  7.93 us
    ppermute x7, waiting for transfers between devices, body(): blocks[way] = lax.ppermute(blocks[way], 'gy', pairs)  5.59 us
    ppermute x7, waiting for transfers between devices, swap(): from_b = lax.ppermute(by_b, axis, pairs_b)  2.96 us
  transfers between devices with their start and end apart: 21, of which 7 were waited for; matrix products, arithmetic and copies ran while one was open for 2% of the time, Pallas kernels for 23%

profile of v10, /device:TPU:0, one launch (start us, length us, event | category | flops | bytes accessed | tf_op | source)
XLA Modules:
  0.0 85.8 jit_solution(6151885691143512148)
XLA Ops:
  0.1 1.7 %split.1 = (bf16[8,64,256]{2,1,0:T(8,128)(2,1)S(1)}, bf16[8,64,256]{2,1,0:T(8,128)(2,1)S(1)}, f32[8,3,256]{2,1,0:T(4,128)S(1)}, f32[8,3,256]{2,1,0:T(4,128)S(1)}) custom-call(s32[6]{0:T(128)S(1)} %stack.19.meta_ref, bf16[16,64,256]{2,1,0:T(8,128)(2,1)} %x.1, f32[3,16,256]{2,1,0:T(8,128)} %bitcast.14), custom_call_target="tpu_custom_call" | custom-call | tf_op jit(solution)/shard_map/split/pallas_call | solution.py:390
  2.4 4.0 %collective-permute-start.1 = (f32[8,3,256]{2,1,0:T(4,128)S(1)}, f32[8,3,256]{2,1,0:T(4,128)S(1)}, u32[]{:S(2)}, u32[]{:S(2)}) collective-permute-start(f32[8,3,256]{2,1,0:T(4,128)S(1)} %get-tuple-element.37.refs_0_.o0), channel_id=1, source_target_pairs={{0,1},{1,0},{2,3},{3,2},{4,5},{5,4},{6,7},{7,6},{8,9},{9,8},{10,11... | collective-permute-start | bytes 73736 | tf_op jit(solution)/shard_map/ppermute | solution.py:123
  6.4 3.0 %collective-permute-start.5 = (bf16[8,64,256]{2,1,0:T(8,128)(2,1)S(1)}, bf16[8,64,256]{2,1,0:T(8,128)(2,1)S(1)}, u32[]{:S(2)}, u32[]{:S(2)}) collective-permute-start(bf16[8,64,256]{2,1,0:T(8,128)(2,1)S(1)} %get-tuple-element.42.refs_0_), channel_id=1, source_target_pairs={{0,1},{1,0},{2,3},{3,2},{4,5},{5,4},{6,7},{7,6},{8,9},{9,8},{10,11... | collective-permute-start | bytes 786440 | tf_op jit(solution)/shard_map/ppermute | solution.py:123
  10.3 3.0 %collective-permute-done.1.refs_3_.c1 = f32[8,3,256]{2,1,0:T(4,128)S(1)} collective-permute-done((f32[8,3,256]{2,1,0:T(4,128)S(1)}, f32[8,3,256]{2,1,0:T(4,128)S(1)}, u32[]{:S(2)}, u32[]{:S(2)}) %collective-permute-start.1) | collective-permute-done | bytes 24608 | tf_op jit(solution)/shard_map/ppermute | solution.py:123
  13.9 1.6 %collective-permute-start.3 = (f32[16,3,256]{2,1,0:T(4,128)S(1)}, f32[16,3,256]{2,1,0:T(4,128)S(1)}, u32[]{:S(2)}, u32[]{:S(2)}) collective-permute-start(f32[16,3,256]{2,1,0:T(4,128)S(1)} %get-tuple-element.40), channel_id=1, source_target_pairs={{0,2},{1,3},{2,0},{3,1},{4,6},{5,7},{6,4},{7,5},{8,16},{9,17},{10,... | collective-permute-start | bytes 147464 | tf_op jit(solution)/shard_map/ppermute | solution.py:122
  16.2 2.6 %collective-permute-done.5.refs_3_ = bf16[8,64,256]{2,1,0:T(8,128)(2,1)S(1)} collective-permute-done((bf16[8,64,256]{2,1,0:T(8,128)(2,1)S(1)}, bf16[8,64,256]{2,1,0:T(8,128)(2,1)S(1)}, u32[]{:S(2)}, u32[]{:S(2)}) %collective-permute-start.5) | collective-permute-done | bytes 262176 | tf_op jit(solution)/shard_map/ppermute | solution.py:123
  19.5 3.3 %collective-permute-start.7 = (bf16[16,64,256]{2,1,0:T(8,128)(2,1)S(1)}, bf16[16,64,256]{2,1,0:T(8,128)(2,1)S(1)}, u32[]{:S(2)}, u32[]{:S(2)}) collective-permute-start(bf16[16,64,256]{2,1,0:T(8,128)(2,1)S(1)} %get-tuple-element.45), channel_id=1, source_target_pairs={{0,2},{1,3},{2,0},{3,1},{4,6},{5,7},{6,4},{7,5},{8,16},{9,17},{10,... | collective-permute-start | bytes 1572872 | tf_op jit(solution)/shard_map/ppermute | solution.py:122
  22.7 5.2 %shard_map.74 = (bf16[4,4096,256]{2,1,0:T(8,128)(2,1)S(1)}, bf16[64,256,48]{2,1,0:T(8,128)(2,1)S(1)}, bf16[16,48,256]{2,1,0:T(8,128)(2,1)S(1)}, s32[16]{0:T(128)S(1)}) custom-call(s32[272]{0:T(512)S(1)} %pad_add_fusion.near_ref, s32[6]{0:T(128)S(1)} %stack.19.meta_ref, f32[8,3,256]{2,1,0:T(4,128)S(1)} %get-tuple-element.37.refs_0_.o0, ...), custom_call_target="tpu_custom_call" | custom-call | flops 4294967296 | bytes 1048576 | tf_op jit(solution)/shard_map/pallas_call | solution.py:350
  28.0 9.0 %shard_map.76 = (bf16[4,4096,256]{2,1,0:T(8,128)(2,1)S(1)}, bf16[4,4096,256]{2,1,0:T(8,128)(2,1)S(1)}, bf16[4,4096,256]{2,1,0:T(8,128)(2,1)S(1)}) custom-call(s32[272]{0:T(512)S(1)} %pad_add_fusion.near_ref, bf16[64,256,48]{2,1,0:T(8,128)(2,1)S(1)} %get-tuple-element.47.source, bf16[16,48,256]{2,1,0:T(8,128)(2,1)S(1)} %get-tuple-element.48.target), custom_call_target="tpu_custom_call" | custom-call | flops 4294967296 | bytes 1048576 | tf_op jit(solution)/shard_map/pallas_call | solution.py:350
  37.0 3.7 %shard_map.77 = (bf16[8,64,256]{2,1,0:T(8,128)(2,1)S(1)}, f32[8,256]{1,0:T(8,128)S(1)}, bf16[64,64,256]{2,1,0:T(8,128)(2,1)S(1)}) custom-call(s32[272]{0:T(512)S(1)} %pad_add_fusion.near_ref, s32[6]{0:T(128)S(1)} %stack.19.meta_ref, bf16[8,64,256]{2,1,0:T(8,128)(2,1)S(1)} %get-tuple-element.42.refs_0_, bf16[8,64,256]{2,1,0:T(8,128)(2,1)S(1)} %get-tuple-element.43.refs_1_, ...), custom_call_target="tpu_custom_call" | custom-call | flops 2147483648 | bytes 1048576 | tf_op jit(solution)/shard_map/pallas_call | solution.py:350
  40.8 3.6 %shard_map.78 = (bf16[8,64,256]{2,1,0:T(8,128)(2,1)S(1)}, f32[8,256]{1,0:T(8,128)S(1)}) custom-call(s32[272]{0:T(512)S(1)} %pad_add_fusion.near_ref, s32[6]{0:T(128)S(1)} %stack.19.meta_ref, bf16[64,64,256]{2,1,0:T(8,128)(2,1)S(1)} %get-tuple-element.52.species, bf16[4,4096,256]{2,1,0:T(8,128)(2,1)S(1)} %get-tuple-element.46.refs_6_.refs_0_.refs_8_, ...), custom_call_target="tpu_custom_call" | custom-call | flops 2147483648 | bytes 1048576 | tf_op jit(solution)/shard_map/pallas_call | solution.py:350
  44.5 1.5 %collective-permute-start.9 = (bf16[8,64,256]{2,1,0:T(8,128)(2,1)S(1)}, bf16[8,64,256]{2,1,0:T(8,128)(2,1)S(1)}, u32[]{:S(2)}, u32[]{:S(2)}) collective-permute-start(bf16[8,64,256]{2,1,0:T(8,128)(2,1)S(1)} %get-tuple-element.53.refs_0_), channel_id=1, source_target_pairs={{0,1},{1,0},{2,3},{3,2},{4,5},{5,4},{6,7},{7,6},{8,9},{9,8},{10,11... | collective-permute-start | bytes 786440 | tf_op jit(solution)/shard_map/ppermute | solution.py:123
  47.7 3.8 %collective-permute-start.12 = (bf16[12,64,256]{2,1,0:T(8,128)(2,1)S(1)}, bf16[12,64,256]{2,1,0:T(8,128)(2,1)S(1)}, u32[]{:S(2)}, u32[]{:S(2)}) collective-permute-start(bf16[12,64,256]{2,1,0:T(8,128)(2,1)S(1)} %get-tuple-element.57), channel_id=1, source_target_pairs={{0,2},{1,3},{2,0},{3,1},{4,6},{5,7},{6,4},{7,5},{8,16},{9,17},{10,... | collective-permute-start | bytes 1179656 | tf_op jit(solution)/shard_map/ppermute | solution.py:122
  51.5 2.4 %collective-permute-done.9.refs_0_.refs_3_ = bf16[8,64,256]{2,1,0:T(8,128)(2,1)S(1)} collective-permute-done((bf16[8,64,256]{2,1,0:T(8,128)(2,1)S(1)}, bf16[8,64,256]{2,1,0:T(8,128)(2,1)S(1)}, u32[]{:S(2)}, u32[]{:S(2)}) %collective-permute-start.9) | collective-permute-done | bytes 262176 | tf_op jit(solution)/shard_map/ppermute | solution.py:123
  54.8 2.5 %collective-permute-start.13 = (bf16[4,64,256]{2,1,0:T(8,128)(2,1)S(1)}, bf16[4,64,256]{2,1,0:T(8,128)(2,1)S(1)}, u32[]{:S(2)}, u32[]{:S(2)}) collective-permute-start(bf16[4,64,256]{2,1,0:T(8,128)(2,1)S(1)} %get-tuple-element.58), channel_id=1, source_target_pairs={{0,2},{1,3},{2,0},{3,1},{4,6},{5,7},{6,4},{7,5},{8,16},{9,17},{10,... | collective-permute-start | bytes 393224 | tf_op jit(solution)/shard_map/ppermute | solution.py:122
  57.3 2.9 %collective-permute-done.13.refs_7_ = bf16[4,64,256]{2,1,0:T(8,128)(2,1)S(1)} collective-permute-done((bf16[4,64,256]{2,1,0:T(8,128)(2,1)S(1)}, bf16[4,64,256]{2,1,0:T(8,128)(2,1)S(1)}, u32[]{:S(2)}, u32[]{:S(2)}) %collective-permute-start.13) | collective-permute-done | bytes 131104 | tf_op jit(solution)/shard_map/ppermute | solution.py:122
  60.2 6.9 %shard_map.81 = (bf16[2,64,256]{2,1,0:T(8,128)(2,1)S(1)}, bf16[2,64,256]{2,1,0:T(8,128)(2,1)S(1)}, bf16[2,64,256]{2,1,0:T(8,128)(2,1)S(1)}, bf16[2,64,256]{2,1,0...) custom-call(s32[272]{0:T(512)S(1)} %pad_add_fusion.near_ref, ...), custom_call_target="tpu_custom_call" | custom-call | flops 4294967296 | bytes 1048576 | tf_op jit(solution)/shard_map/pallas_call | solution.py:350
  67.1 2.0 %collective-permute-start.14 = (bf16[2,64,256]{2,1,0:T(8,128)(2,1)S(1)}, bf16[2,64,256]{2,1,0:T(8,128)(2,1)S(1)}, u32[]{:S(2)}, u32[]{:S(2)}) collective-permute-start(bf16[2,64,256]{2,1,0:T(8,128)(2,1)S(1)} %get-tuple-element.62), channel_id=1, source_target_pairs={{0,1},{1,0},{2,3},{3,2},{4,5},{5,4},{6,7},{7,6},{8,9},{9,8},{10,11... | collective-permute-start | bytes 196616 | tf_op jit(solution)/shard_map/ppermute | solution.py:488
  70.7 3.2 %collective-permute-start.17 = (bf16[2,64,256]{2,1,0:T(8,128)(2,1)S(1)}, bf16[2,64,256]{2,1,0:T(8,128)(2,1)S(1)}, u32[]{:S(2)}, u32[]{:S(2)}) collective-permute-start(bf16[2,64,256]{2,1,0:T(8,128)(2,1)S(1)} %get-tuple-element.65), channel_id=1, source_target_pairs={{0,4},{1,5},{2,6},{3,7},{4,0},{5,1},{6,2},{7,3},{8,12},{9,13},{10,... | collective-permute-start | bytes 196616 | tf_op jit(solution)/shard_map/ppermute | solution.py:488
  75.0 2.1 %collective-permute-start.19 = (bf16[2,64,256]{2,1,0:T(8,128)(2,1)S(1)}, bf16[2,64,256]{2,1,0:T(8,128)(2,1)S(1)}, u32[]{:S(2)}, u32[]{:S(2)}) collective-permute-start(bf16[2,64,256]{2,1,0:T(8,128)(2,1)S(1)} %get-tuple-element.67), channel_id=1, source_target_pairs={{0,6},{1,7},{2,4},{3,5},{4,2},{5,3},{6,0},{7,1},{8,14},{9,15},{10,... | collective-permute-start | bytes 196616 | tf_op jit(solution)/shard_map/ppermute | solution.py:488
  77.1 1.5 %collective-permute-start.20 = (bf16[2,64,256]{2,1,0:T(8,128)(2,1)S(1)}, bf16[2,64,256]{2,1,0:T(8,128)(2,1)S(1)}, u32[]{:S(2)}, u32[]{:S(2)}) collective-permute-start(bf16[2,64,256]{2,1,0:T(8,128)(2,1)S(1)} %get-tuple-element.68), channel_id=1, source_target_pairs={{0,7},{1,6},{2,5},{3,4},{4,3},{5,2},{6,1},{7,0},{8,15},{9,14},{10,... | collective-permute-start | bytes 196616 | tf_op jit(solution)/shard_map/ppermute | solution.py:488
  78.6 1.3 %collective-permute-done.17.refs_4_ = bf16[2,64,256]{2,1,0:T(8,128)(2,1)S(1)} collective-permute-done((bf16[2,64,256]{2,1,0:T(8,128)(2,1)S(1)}, bf16[2,64,256]{2,1,0:T(8,128)(2,1)S(1)}, u32[]{:S(2)}, u32[]{:S(2)}) %collective-permute-start.17) | collective-permute-done | bytes 65568 | tf_op jit(solution)/shard_map/ppermute | solution.py:488
  80.0 3.4 %collective-permute-done.18.refs_5_ = bf16[2,64,256]{2,1,0:T(8,128)(2,1)S(1)} collective-permute-done((bf16[2,64,256]{2,1,0:T(8,128)(2,1)S(1)}, bf16[2,64,256]{2,1,0:T(8,128)(2,1)S(1)}, u32[]{:S(2)}, u32[]{:S(2)}) %collective-permute-start.18) | collective-permute-done | bytes 65568 | tf_op jit(solution)/shard_map/ppermute | solution.py:488
  84.2 1.4 %place.1 = bf16[16,64,256]{2,1,0:T(8,128)(2,1)} custom-call(s32[6]{0:T(128)S(1)} %stack.19.meta_ref, bf16[2,64,256]{2,1,0:T(8,128)(2,1)S(1)} %get-tuple-element.61.refs_0_, bf16[2,64,256]{2,1,0:T(8,128)(2,1)S(1)} %collective-permute-done.14.refs_1_, bf16[2,64,256]{2,1,0:T(8,128)(2,1)S(1)} %collective-permute-done.15.refs_2_, ...), custom_call_target="tpu_custom_call" | custom-call | tf_op jit(solution)/shard_map/place/pallas_call | solution.py:489
  (40 shorter events, 9.6 us)
Async XLA Ops:
  1.8 8.5 %collective-permute-start = (f32[8,3,256]{2,1,0:T(4,128)S(1)}, f32[8,3,256]{2,1,0:T(4,128)S(1)}, u32[]{:S(2)}, u32[]{:S(2)}) collective-permute-start(f32[8,3,256]{2,1,0:T(4,128)S(1)} %get-tuple-element.38.refs_1_.o1), channel_id=1, source_target_pairs={{0,8},{1,2},{2,1},{3,4},{4,3},{5,6},{6,5},{7,15},{8,0},{9,10},{10,... | collective-permute-start | bytes 73736 | tf_op jit(solution)/shard_map/ppermute | solution.py:122
  2.4 10.9 %collective-permute-start.1 = (f32[8,3,256]{2,1,0:T(4,128)S(1)}, f32[8,3,256]{2,1,0:T(4,128)S(1)}, u32[]{:S(2)}, u32[]{:S(2)}) collective-permute-start(f32[8,3,256]{2,1,0:T(4,128)S(1)} %get-tuple-element.37.refs_0_.o0), channel_id=1, source_target_pairs={{0,1},{1,0},{2,3},{3,2},{4,5},{5,4},{6,7},{7,6},{8,9},{9,8},{10,11... | collective-permute-start | bytes 73736 | tf_op jit(solution)/shard_map/ppermute | solution.py:123
  6.4 9.8 %collective-permute-start.4 = (bf16[8,64,256]{2,1,0:T(8,128)(2,1)S(1)}, bf16[8,64,256]{2,1,0:T(8,128)(2,1)S(1)}, u32[]{:S(2)}, u32[]{:S(2)}) collective-permute-start(bf16[8,64,256]{2,1,0:T(8,128)(2,1)S(1)} %get-tuple-element.43.refs_1_), channel_id=1, source_target_pairs={{0,8},{1,2},{2,1},{3,4},{4,3},{5,6},{6,5},{7,15},{8,0},{9,10},{10,... | collective-permute-start | bytes 786440 | tf_op jit(solution)/shard_map/ppermute | solution.py:122
  6.4 12.4 %collective-permute-start.5 = (bf16[8,64,256]{2,1,0:T(8,128)(2,1)S(1)}, bf16[8,64,256]{2,1,0:T(8,128)(2,1)S(1)}, u32[]{:S(2)}, u32[]{:S(2)}) collective-permute-start(bf16[8,64,256]{2,1,0:T(8,128)(2,1)S(1)} %get-tuple-element.42.refs_0_), channel_id=1, source_target_pairs={{0,1},{1,0},{2,3},{3,2},{4,5},{5,4},{6,7},{7,6},{8,9},{9,8},{10,11... | collective-permute-start | bytes 786440 | tf_op jit(solution)/shard_map/ppermute | solution.py:123
  13.8 8.9 %collective-permute-start.2 = (f32[16,3,256]{2,1,0:T(4,128)S(1)}, f32[16,3,256]{2,1,0:T(4,128)S(1)}, u32[]{:S(2)}, u32[]{:S(2)}) collective-permute-start(f32[16,3,256]{2,1,0:T(4,128)S(1)} %get-tuple-element.39), channel_id=1, source_target_pairs={{0,8},{1,9},{2,10},{3,11},{4,12},{5,13},{6,14},{7,15},{8,0},{9,1},... | collective-permute-start | bytes 147464 | tf_op jit(solution)/shard_map/ppermute | solution.py:123
  13.9 8.8 %collective-permute-start.3 = (f32[16,3,256]{2,1,0:T(4,128)S(1)}, f32[16,3,256]{2,1,0:T(4,128)S(1)}, u32[]{:S(2)}, u32[]{:S(2)}) collective-permute-start(f32[16,3,256]{2,1,0:T(4,128)S(1)} %get-tuple-element.40), channel_id=1, source_target_pairs={{0,2},{1,3},{2,0},{3,1},{4,6},{5,7},{6,4},{7,5},{8,16},{9,17},{10,... | collective-permute-start | bytes 147464 | tf_op jit(solution)/shard_map/ppermute | solution.py:122
  19.4 17.6 %collective-permute-start.6 = (bf16[16,64,256]{2,1,0:T(8,128)(2,1)S(1)}, bf16[16,64,256]{2,1,0:T(8,128)(2,1)S(1)}, u32[]{:S(2)}, u32[]{:S(2)}) collective-permute-start(bf16[16,64,256]{2,1,0:T(8,128)(2,1)S(1)} %get-tuple-element.44), channel_id=1, source_target_pairs={{0,8},{1,9},{2,10},{3,11},{4,12},{5,13},{6,14},{7,15},{8,0},{9,1},... | collective-permute-start | bytes 1572872 | tf_op jit(solution)/shard_map/ppermute | solution.py:123
  19.5 17.5 %collective-permute-start.7 = (bf16[16,64,256]{2,1,0:T(8,128)(2,1)S(1)}, bf16[16,64,256]{2,1,0:T(8,128)(2,1)S(1)}, u32[]{:S(2)}, u32[]{:S(2)}) collective-permute-start(bf16[16,64,256]{2,1,0:T(8,128)(2,1)S(1)} %get-tuple-element.45), channel_id=1, source_target_pairs={{0,2},{1,3},{2,0},{3,1},{4,6},{5,7},{6,4},{7,5},{8,16},{9,17},{10,... | collective-permute-start | bytes 1572872 | tf_op jit(solution)/shard_map/ppermute | solution.py:122
  28.0 9.0 %copy-start = (f32[16,256]{1,0:T(8,128)S(1)}, f32[16,256]{1,0:T(8,128)}, u32[]{:S(2)}) copy-start(f32[16,256]{1,0:T(8,128)} %refs_14_.1) | copy-start | bytes 49156
  28.0 9.0 %copy-start.1 = (f32[32]{0:T(128)S(1)}, f32[32]{0:T(128)}, u32[]{:S(2)}) copy-start(f32[32]{0:T(128)} %param.10) | copy-start | bytes 388
  28.0 9.0 %copy-start.2 = (f32[32]{0:T(128)S(1)}, f32[32]{0:T(128)}, u32[]{:S(2)}) copy-start(f32[32]{0:T(128)} %param.11) | copy-start | bytes 388
  40.8 5.2 %collective-permute-start.8 = (bf16[8,64,256]{2,1,0:T(8,128)(2,1)S(1)}, bf16[8,64,256]{2,1,0:T(8,128)(2,1)S(1)}, u32[]{:S(2)}, u32[]{:S(2)}) collective-permute-start(bf16[8,64,256]{2,1,0:T(8,128)(2,1)S(1)} %get-tuple-element.54.refs_1_), channel_id=1, source_target_pairs={{0,8},{1,2},{2,1},{3,4},{4,3},{5,6},{6,5},{7,15},{8,0},{9,10},{10,... | collective-permute-start | bytes 786440 | tf_op jit(solution)/shard_map/ppermute | solution.py:122
  44.5 9.5 %collective-permute-start.9 = (bf16[8,64,256]{2,1,0:T(8,128)(2,1)S(1)}, bf16[8,64,256]{2,1,0:T(8,128)(2,1)S(1)}, u32[]{:S(2)}, u32[]{:S(2)}) collective-permute-start(bf16[8,64,256]{2,1,0:T(8,128)(2,1)S(1)} %get-tuple-element.53.refs_0_), channel_id=1, source_target_pairs={{0,1},{1,0},{2,3},{3,2},{4,5},{5,4},{6,7},{7,6},{8,9},{9,8},{10,11... | collective-permute-start | bytes 786440 | tf_op jit(solution)/shard_map/ppermute | solution.py:123
  46.6 13.6 %collective-permute-start.10 = (bf16[12,64,256]{2,1,0:T(8,128)(2,1)S(1)}, bf16[12,64,256]{2,1,0:T(8,128)(2,1)S(1)}, u32[]{:S(2)}, u32[]{:S(2)}) collective-permute-start(bf16[12,64,256]{2,1,0:T(8,128)(2,1)S(1)} %get-tuple-element.55), channel_id=1, source_target_pairs={{0,8},{1,9},{2,10},{3,11},{4,12},{5,13},{6,14},{7,15},{8,0},{9,1},... | collective-permute-start | bytes 1179656 | tf_op jit(solution)/shard_map/ppermute | solution.py:123
  47.7 12.5 %collective-permute-start.12 = (bf16[12,64,256]{2,1,0:T(8,128)(2,1)S(1)}, bf16[12,64,256]{2,1,0:T(8,128)(2,1)S(1)}, u32[]{:S(2)}, u32[]{:S(2)}) collective-permute-start(bf16[12,64,256]{2,1,0:T(8,128)(2,1)S(1)} %get-tuple-element.57), channel_id=1, source_target_pairs={{0,2},{1,3},{2,0},{3,1},{4,6},{5,7},{6,4},{7,5},{8,16},{9,17},{10,... | collective-permute-start | bytes 1179656 | tf_op jit(solution)/shard_map/ppermute | solution.py:122
  54.5 2.8 %collective-permute-start.11 = (bf16[4,64,256]{2,1,0:T(8,128)(2,1)S(1)}, bf16[4,64,256]{2,1,0:T(8,128)(2,1)S(1)}, u32[]{:S(2)}, u32[]{:S(2)}) collective-permute-start(bf16[4,64,256]{2,1,0:T(8,128)(2,1)S(1)} %get-tuple-element.56), channel_id=1, source_target_pairs={{0,8},{1,9},{2,10},{3,11},{4,12},{5,13},{6,14},{7,15},{8,0},{9,1},... | collective-permute-start | bytes 393224 | tf_op jit(solution)/shard_map/ppermute | solution.py:123
  54.8 5.5 %collective-permute-start.13 = (bf16[4,64,256]{2,1,0:T(8,128)(2,1)S(1)}, bf16[4,64,256]{2,1,0:T(8,128)(2,1)S(1)}, u32[]{:S(2)}, u32[]{:S(2)}) collective-permute-start(bf16[4,64,256]{2,1,0:T(8,128)(2,1)S(1)} %get-tuple-element.58), channel_id=1, source_target_pairs={{0,2},{1,3},{2,0},{3,1},{4,6},{5,7},{6,4},{7,5},{8,16},{9,17},{10,... | collective-permute-start | bytes 393224 | tf_op jit(solution)/shard_map/ppermute | solution.py:122
  67.1 7.9 %collective-permute-start.14 = (bf16[2,64,256]{2,1,0:T(8,128)(2,1)S(1)}, bf16[2,64,256]{2,1,0:T(8,128)(2,1)S(1)}, u32[]{:S(2)}, u32[]{:S(2)}) collective-permute-start(bf16[2,64,256]{2,1,0:T(8,128)(2,1)S(1)} %get-tuple-element.62), channel_id=1, source_target_pairs={{0,1},{1,0},{2,3},{3,2},{4,5},{5,4},{6,7},{7,6},{8,9},{9,8},{10,11... | collective-permute-start | bytes 196616 | tf_op jit(solution)/shard_map/ppermute | solution.py:488
  69.1 8.0 %collective-permute-start.15 = (bf16[2,64,256]{2,1,0:T(8,128)(2,1)S(1)}, bf16[2,64,256]{2,1,0:T(8,128)(2,1)S(1)}, u32[]{:S(2)}, u32[]{:S(2)}) collective-permute-start(bf16[2,64,256]{2,1,0:T(8,128)(2,1)S(1)} %get-tuple-element.63), channel_id=1, source_target_pairs={{0,2},{1,3},{2,0},{3,1},{4,6},{5,7},{6,4},{7,5},{8,10},{9,11},{10,... | collective-permute-start | bytes 196616 | tf_op jit(solution)/shard_map/ppermute | solution.py:488
  70.5 8.2 %collective-permute-start.16 = (bf16[2,64,256]{2,1,0:T(8,128)(2,1)S(1)}, bf16[2,64,256]{2,1,0:T(8,128)(2,1)S(1)}, u32[]{:S(2)}, u32[]{:S(2)}) collective-permute-start(bf16[2,64,256]{2,1,0:T(8,128)(2,1)S(1)} %get-tuple-element.64), channel_id=1, source_target_pairs={{0,3},{1,2},{2,1},{3,0},{4,7},{5,6},{6,5},{7,4},{8,11},{9,10},{10,... | collective-permute-start | bytes 196616 | tf_op jit(solution)/shard_map/ppermute | solution.py:488
  70.7 9.3 %collective-permute-start.17 = (bf16[2,64,256]{2,1,0:T(8,128)(2,1)S(1)}, bf16[2,64,256]{2,1,0:T(8,128)(2,1)S(1)}, u32[]{:S(2)}, u32[]{:S(2)}) collective-permute-start(bf16[2,64,256]{2,1,0:T(8,128)(2,1)S(1)} %get-tuple-element.65), channel_id=1, source_target_pairs={{0,4},{1,5},{2,6},{3,7},{4,0},{5,1},{6,2},{7,3},{8,12},{9,13},{10,... | collective-permute-start | bytes 196616 | tf_op jit(solution)/shard_map/ppermute | solution.py:488
  73.9 9.5 %collective-permute-start.18 = (bf16[2,64,256]{2,1,0:T(8,128)(2,1)S(1)}, bf16[2,64,256]{2,1,0:T(8,128)(2,1)S(1)}, u32[]{:S(2)}, u32[]{:S(2)}) collective-permute-start(bf16[2,64,256]{2,1,0:T(8,128)(2,1)S(1)} %get-tuple-element.66), channel_id=1, source_target_pairs={{0,5},{1,4},{2,7},{3,6},{4,1},{5,0},{6,3},{7,2},{8,13},{9,12},{10,... | collective-permute-start | bytes 196616 | tf_op jit(solution)/shard_map/ppermute | solution.py:488
  75.0 8.4 %collective-permute-start.19 = (bf16[2,64,256]{2,1,0:T(8,128)(2,1)S(1)}, bf16[2,64,256]{2,1,0:T(8,128)(2,1)S(1)}, u32[]{:S(2)}, u32[]{:S(2)}) collective-permute-start(bf16[2,64,256]{2,1,0:T(8,128)(2,1)S(1)} %get-tuple-element.67), channel_id=1, source_target_pairs={{0,6},{1,7},{2,4},{3,5},{4,2},{5,3},{6,0},{7,1},{8,14},{9,15},{10,... | collective-permute-start | bytes 196616 | tf_op jit(solution)/shard_map/ppermute | solution.py:488
  77.1 7.1 %collective-permute-start.20 = (bf16[2,64,256]{2,1,0:T(8,128)(2,1)S(1)}, bf16[2,64,256]{2,1,0:T(8,128)(2,1)S(1)}, u32[]{:S(2)}, u32[]{:S(2)}) collective-permute-start(bf16[2,64,256]{2,1,0:T(8,128)(2,1)S(1)} %get-tuple-element.68), channel_id=1, source_target_pairs={{0,7},{1,6},{2,5},{3,4},{4,3},{5,2},{6,1},{7,0},{8,15},{9,14},{10,... | collective-permute-start | bytes 196616 | tf_op jit(solution)/shard_map/ppermute | solution.py:488

commit v11 on v10

--- a/solution.py
+++ b/solution.py
@@ -193,11 +193,9 @@
         lax.fori_loop(0, BY, one, 0)
 
 
-def build_first(
-    near_ref, meta_ref, o0, o1, c0, c1, r0, r1, w0, source, target, row_ref, taken
-):
+def put_features(meta_ref, first, refs, source, target):
     odd_lane, odd_band = meta_ref[4], meta_ref[5]
-    for piece, ref in enumerate((o0, o1, c0, c1, r0, r1)):
+    for piece, ref in enumerate(refs, first):
 
         def some(j, _, piece=piece, ref=ref):
             for n in range(UNROLL):
@@ -213,6 +211,14 @@
             return 0
 
         lax.fori_loop(0, COUNTS[piece] // UNROLL, some, 0)
+
+
+def prepare(meta_ref, o0, o1, c0, c1, source, target):
+    put_features(meta_ref, 0, (o0, o1, c0, c1), source, target)
+
+
+def build_first(near_ref, meta_ref, _, target, r0, r1, w0, source, row_ref, taken):
+    put_features(meta_ref, 4, (r0, r1), source, None)
     for z in range(taken.shape[0]):
         taken[z] = 0
 
@@ -345,7 +351,7 @@
 HBM = pl.BlockSpec(memory_space=pltpu.HBM)
 
 
-def call(kernel, operands, scalars, outs, scratch, flops):
+def call(kernel, operands, scalars, outs, scratch, flops, aliases=None):
     single = not isinstance(outs, (list, tuple))
     return pl.pallas_call(
         kernel,
@@ -353,6 +359,7 @@
         in_specs=[SM] * scalars + [VM] * (len(operands) - scalars),
         out_specs=VM if single else [SM if o.dtype == i32 else VM for o in outs],
         scratch_shapes=scratch,
+        input_output_aliases=aliases or {},
         compiler_params=pltpu.CompilerParams(vmem_limit_bytes=8 << 20),
         cost_estimate=pl.CostEstimate(
             flops=flops, bytes_accessed=1 << 20, transcendentals=0
@@ -411,18 +418,23 @@
         by_a, by_b = call(
             pack, (meta,) + pieces, 1, [like(pieces[0], size)] * 2, [], 1 << 20
         )
-        return swap(by_a, by_b, "gx")
+        return by_a, by_b
+
+    def swap_rows(pieces):
+        return swap(*rows(pieces), "gx")
 
     pos_sides = swap(pos_a, pos_b, "gy")[::-1]
-    pos_bands = rows((pos_a, pos_b) + pos_sides)
+    packed_a, packed_b = rows((pos_a, pos_b) + pos_sides)
+    packed_a, keys = lax.optimization_barrier((packed_a, adjacent_cell_keys))
+    pos_bands = swap(packed_a, packed_b, "gx")
     own = (own_a, own_b)
     sides = swap(own_a, own_b, "gy")[::-1]
-    bands = rows(own + sides)
+    bands = swap_rows(own + sides)
 
     ids = jnp.arange(bins, dtype=i32)
     near = slot_of(
-        (ids // BY)[:, None] + adjacent_cell_keys // WIDTH - HALO,
-        (ids % BY)[:, None] + adjacent_cell_keys % WIDTH - HALO,
+        (ids // BY)[:, None] + keys // WIDTH - HALO,
+        (ids % BY)[:, None] + keys % WIDTH - HALO,
         odd_lane,
         odd_band,
     ).reshape(-1)
@@ -436,18 +448,23 @@
     gathered = pltpu.VMEM((HALO, kinds, neighbours * parts), bf16)
     all_species = pltpu.VMEM((EXT, kinds, parts), bf16)
     work = 2 * bins * neighbours * parts * parts * 128
-    w0, source, target, row = call(
+    source_space = pltpu.VMEM((EXT, parts, FEATURES), bf16)
+    source, target = call(
+        prepare,
+        (meta, pos_a, pos_b) + pos_sides,
+        1,
+        [source_space, pltpu.VMEM((bins, FEATURES, parts), bf16)],
+        [],
+        1 << 20,
+    )
+    w0, source, row = call(
         build_first,
-        (near, meta, pos_a, pos_b) + pos_sides + pos_bands,
+        (near, meta, source, target) + pos_bands,
         2,
-        [
-            w_row,
-            pltpu.VMEM((EXT, parts, FEATURES), bf16),
-            pltpu.VMEM((bins, FEATURES, parts), bf16),
-            jax.ShapeDtypeStruct((bins,), i32),
-        ],
+        [w_row, source_space, jax.ShapeDtypeStruct((bins,), i32)],
         [pltpu.SMEM((lane_count,), i32)],
         work,
+        {2: 1},
     )
     w1, w2, w3 = call(build_second, (near, source, target), 1, [w_row] * 3, [], work)
     built = (w0, w1, w2, w3)
@@ -470,8 +487,8 @@
 
     own = (by_a, by_b)
     sides = swap(by_a, by_b, "gy")[::-1]
-    early = rows(own + sides[:1])
-    corners = rows(sides[1:])
+    early = swap_rows(own + sides[:1])
+    corners = swap_rows(sides[1:])
     pieces = own + sides + (early[0], corners[0], early[1], corners[1])
     blocks = list(
         call(

time: 86 us -> 85.3 us (level)
  waiting for transfers between devices: 16.5 us -> 15.3 us
    ppermute x7, waiting for transfers between devices: 7.93 us -> 6.73 us  [swap(): from_a = lax.ppermute(by_a, axis, pairs_a)]
    pallas_call x9 -> x10, Pallas kernels: 30.7 us -> 31.3 us  [call(): pl.pallas_call(kernel, out_shape=outs, in_specs=[SM] * scalars + [VM] * (...]
  transfers between devices with their start and end apart: 21 -> 21, of which waited for: 7 -> 6; matrix products, arithmetic and copies ran while one was open for 2% -> 2% of each run, Pallas kernels for 23% -> 24%
where the time goes in v11:
time: 85.3 us; the launch traced here: 85.1 us
  Pallas kernels  34.4 us (40%)
  starting transfers between devices  33.5 us (39%)
  waiting for transfers between devices  15.3 us (18%)
  other arithmetic  1.45 us (2%)
    pallas_call x10, Pallas kernels, call(): pl.pallas_call(kernel, out_shape=outs, in_specs=[SM] * scalars + [VM] * (...  31.3 us
    ppermute x7, starting transfers between devices, swap(): from_b = lax.ppermute(by_b, axis, pairs_b)  11.9 us
    ppermute x7, starting transfers between devices, body(): blocks[way] = lax.ppermute(blocks[way], 'gy', pairs)  11.5 us
    ppermute x7, starting transfers between devices, swap(): from_a = lax.ppermute(by_a, axis, pairs_a)  10.1 us
    ppermute x7, waiting for transfers between devices, swap(): from_a = lax.ppermute(by_a, axis, pairs_a)  6.73 us
    ppermute x7, waiting for transfers between devices, body(): blocks[way] = lax.ppermute(blocks[way], 'gy', pairs)  5.57 us
    ppermute x7, waiting for transfers between devices, swap(): from_b = lax.ppermute(by_b, axis, pairs_b)  2.96 us
    pallas_call x1, Pallas kernels, body(): pl.pallas_call(split, out_shape=[pltpu.VMEM((SIDE, kinds, parts), bf16)]...  1.71 us
  transfers between devices with their start and end apart: 21, of which 6 were waited for; matrix products, arithmetic and copies ran while one was open for 2% of the time, Pallas kernels for 24%

profile of v11, /device:TPU:0, one launch (start us, length us, event | category | flops | bytes accessed | tf_op | source)
XLA Modules:
  0.0 85.1 jit_solution(12316366079142080723)
XLA Ops:
  0.1 1.7 %split.1 = (bf16[8,64,256]{2,1,0:T(8,128)(2,1)S(1)}, bf16[8,64,256]{2,1,0:T(8,128)(2,1)S(1)}, f32[8,3,256]{2,1,0:T(4,128)S(1)}, f32[8,3,256]{2,1,0:T(4,128)S(1)}) custom-call(s32[6]{0:T(128)S(1)} %stack.19.meta_ref, bf16[16,64,256]{2,1,0:T(8,128)(2,1)} %x.1, f32[3,16,256]{2,1,0:T(8,128)} %bitcast.14), custom_call_target="tpu_custom_call" | custom-call | tf_op jit(solution)/shard_map/split/pallas_call | solution.py:397
  2.4 4.0 %collective-permute-start.1 = (f32[8,3,256]{2,1,0:T(4,128)S(1)}, f32[8,3,256]{2,1,0:T(4,128)S(1)}, u32[]{:S(2)}, u32[]{:S(2)}) collective-permute-start(f32[8,3,256]{2,1,0:T(4,128)S(1)} %get-tuple-element.40.refs_0_.o0), channel_id=1, source_target_pairs={{0,1},{1,0},{2,3},{3,2},{4,5},{5,4},{6,7},{7,6},{8,9},{9,8},{10,11... | collective-permute-start | bytes 73736 | tf_op jit(solution)/shard_map/ppermute | solution.py:123
  6.4 3.0 %collective-permute-start.5 = (bf16[8,64,256]{2,1,0:T(8,128)(2,1)S(1)}, bf16[8,64,256]{2,1,0:T(8,128)(2,1)S(1)}, u32[]{:S(2)}, u32[]{:S(2)}) collective-permute-start(bf16[8,64,256]{2,1,0:T(8,128)(2,1)S(1)} %get-tuple-element.49.refs_0_), channel_id=1, source_target_pairs={{0,1},{1,0},{2,3},{3,2},{4,5},{5,4},{6,7},{7,6},{8,9},{9,8},{10,11... | collective-permute-start | bytes 786440 | tf_op jit(solution)/shard_map/ppermute | solution.py:123
  9.4 3.8 %collective-permute-done.1.refs_3_.c1 = f32[8,3,256]{2,1,0:T(4,128)S(1)} collective-permute-done((f32[8,3,256]{2,1,0:T(4,128)S(1)}, f32[8,3,256]{2,1,0:T(4,128)S(1)}, u32[]{:S(2)}, u32[]{:S(2)}) %collective-permute-start.1) | collective-permute-done | bytes 24608 | tf_op jit(solution)/shard_map/ppermute | solution.py:123
  13.9 1.6 %collective-permute-start.3 = (f32[16,3,256]{2,1,0:T(4,128)S(1)}, f32[16,3,256]{2,1,0:T(4,128)S(1)}, u32[]{:S(2)}, u32[]{:S(2)}) collective-permute-start(f32[16,3,256]{2,1,0:T(4,128)S(1)} %get-tuple-element.47), channel_id=1, source_target_pairs={{0,2},{1,3},{2,0},{3,1},{4,6},{5,7},{6,4},{7,5},{8,16},{9,17},{10,... | collective-permute-start | bytes 147464 | tf_op jit(solution)/shard_map/ppermute | solution.py:122
  17.1 1.2 %shard_map.74 = (bf16[64,256,48]{2,1,0:T(8,128)(2,1)S(1)}, bf16[16,48,256]{2,1,0:T(8,128)(2,1)S(1)}) custom-call(s32[6]{0:T(128)S(1)} %stack.19.meta_ref, f32[8,3,256]{2,1,0:T(4,128)S(1)} %get-tuple-element.40.refs_0_.o0, f32[8,3,256]{2,1,0:T(4,128)S(1)} %get-tuple-element.41.refs_1_.o1, f32[8,3,256]{2,1,0:T(4,128)S(1)} %collective-permute-done.refs_2_.c0, ...), custom_call_target="tpu_custom_call" | custom-call | flops 1048576 | bytes 1048576 | tf_op jit(solution)/shard_map/pallas_call | solution.py:356
  19.5 3.3 %collective-permute-start.7 = (bf16[16,64,256]{2,1,0:T(8,128)(2,1)S(1)}, bf16[16,64,256]{2,1,0:T(8,128)(2,1)S(1)}, u32[]{:S(2)}, u32[]{:S(2)}) collective-permute-start(bf16[16,64,256]{2,1,0:T(8,128)(2,1)S(1)} %get-tuple-element.52), channel_id=1, source_target_pairs={{0,2},{1,3},{2,0},{3,1},{4,6},{5,7},{6,4},{7,5},{8,16},{9,17},{10,... | collective-permute-start | bytes 1572872 | tf_op jit(solution)/shard_map/ppermute | solution.py:122
  22.7 4.6 %shard_map.75 = (bf16[4,4096,256]{2,1,0:T(8,128)(2,1)S(1)}, bf16[64,256,48]{2,1,0:T(8,128)(2,1)S(1)}, s32[16]{0:T(128)S(1)}) custom-call(s32[272]{0:T(512)S(1)} %pad_add_fusion.near_ref, s32[6]{0:T(128)S(1)} %stack.19.meta_ref, bf16[64,256,48]{2,1,0:T(8,128)(2,1)S(1)} %get-tuple-element.44._, ...), custom_call_target="tpu_custom_call", output_to_operand_aliasing={{1}: (2, {})} | custom-call | flops 4294967296 | bytes 1048576 | tf_op jit(solution)/shard_map/pallas_call | solution.py:356
  27.4 8.9 %shard_map.77 = (bf16[4,4096,256]{2,1,0:T(8,128)(2,1)S(1)}, bf16[4,4096,256]{2,1,0:T(8,128)(2,1)S(1)}, bf16[4,4096,256]{2,1,0:T(8,128)(2,1)S(1)}) custom-call(s32[272]{0:T(512)S(1)} %pad_add_fusion.near_ref, bf16[64,256,48]{2,1,0:T(8,128)(2,1)S(1)} %get-tuple-element.54.source, bf16[16,48,256]{2,1,0:T(8,128)(2,1)S(1)} %get-tuple-element.45.target), custom_call_target="tpu_custom_call" | custom-call | flops 4294967296 | bytes 1048576 | tf_op jit(solution)/shard_map/pallas_call | solution.py:356
  36.4 3.7 %shard_map.78 = (bf16[8,64,256]{2,1,0:T(8,128)(2,1)S(1)}, f32[8,256]{1,0:T(8,128)S(1)}, bf16[64,64,256]{2,1,0:T(8,128)(2,1)S(1)}) custom-call(s32[272]{0:T(512)S(1)} %pad_add_fusion.near_ref, s32[6]{0:T(128)S(1)} %stack.19.meta_ref, bf16[8,64,256]{2,1,0:T(8,128)(2,1)S(1)} %get-tuple-element.49.refs_0_, bf16[8,64,256]{2,1,0:T(8,128)(2,1)S(1)} %get-tuple-element.50.refs_1_, ...), custom_call_target="tpu_custom_call" | custom-call | flops 2147483648 | bytes 1048576 | tf_op jit(solution)/shard_map/pallas_call | solution.py:356
  40.2 3.6 %shard_map.79 = (bf16[8,64,256]{2,1,0:T(8,128)(2,1)S(1)}, f32[8,256]{1,0:T(8,128)S(1)}) custom-call(s32[272]{0:T(512)S(1)} %pad_add_fusion.near_ref, s32[6]{0:T(128)S(1)} %stack.19.meta_ref, bf16[64,64,256]{2,1,0:T(8,128)(2,1)S(1)} %get-tuple-element.58.species, bf16[4,4096,256]{2,1,0:T(8,128)(2,1)S(1)} %get-tuple-element.53.refs_6_.refs_0_.refs_8_, ...), custom_call_target="tpu_custom_call" | custom-call | flops 2147483648 | bytes 1048576 | tf_op jit(solution)/shard_map/pallas_call | solution.py:356
  43.8 1.6 %collective-permute-start.9 = (bf16[8,64,256]{2,1,0:T(8,128)(2,1)S(1)}, bf16[8,64,256]{2,1,0:T(8,128)(2,1)S(1)}, u32[]{:S(2)}, u32[]{:S(2)}) collective-permute-start(bf16[8,64,256]{2,1,0:T(8,128)(2,1)S(1)} %get-tuple-element.59.refs_0_), channel_id=1, source_target_pairs={{0,1},{1,0},{2,3},{3,2},{4,5},{5,4},{6,7},{7,6},{8,9},{9,8},{10,11... | collective-permute-start | bytes 786440 | tf_op jit(solution)/shard_map/ppermute | solution.py:123
  47.1 3.8 %collective-permute-start.12 = (bf16[12,64,256]{2,1,0:T(8,128)(2,1)S(1)}, bf16[12,64,256]{2,1,0:T(8,128)(2,1)S(1)}, u32[]{:S(2)}, u32[]{:S(2)}) collective-permute-start(bf16[12,64,256]{2,1,0:T(8,128)(2,1)S(1)} %get-tuple-element.63), channel_id=1, source_target_pairs={{0,2},{1,3},{2,0},{3,1},{4,6},{5,7},{6,4},{7,5},{8,16},{9,17},{10,... | collective-permute-start | bytes 1179656 | tf_op jit(solution)/shard_map/ppermute | solution.py:122
  50.9 2.4 %collective-permute-done.9.refs_0_.refs_3_ = bf16[8,64,256]{2,1,0:T(8,128)(2,1)S(1)} collective-permute-done((bf16[8,64,256]{2,1,0:T(8,128)(2,1)S(1)}, bf16[8,64,256]{2,1,0:T(8,128)(2,1)S(1)}, u32[]{:S(2)}, u32[]{:S(2)}) %collective-permute-start.9) | collective-permute-done | bytes 262176 | tf_op jit(solution)/shard_map/ppermute | solution.py:123
  54.1 2.5 %collective-permute-start.13 = (bf16[4,64,256]{2,1,0:T(8,128)(2,1)S(1)}, bf16[4,64,256]{2,1,0:T(8,128)(2,1)S(1)}, u32[]{:S(2)}, u32[]{:S(2)}) collective-permute-start(bf16[4,64,256]{2,1,0:T(8,128)(2,1)S(1)} %get-tuple-element.64), channel_id=1, source_target_pairs={{0,2},{1,3},{2,0},{3,1},{4,6},{5,7},{6,4},{7,5},{8,16},{9,17},{10,... | collective-permute-start | bytes 393224 | tf_op jit(solution)/shard_map/ppermute | solution.py:122
  56.6 2.9 %collective-permute-done.13.refs_7_ = bf16[4,64,256]{2,1,0:T(8,128)(2,1)S(1)} collective-permute-done((bf16[4,64,256]{2,1,0:T(8,128)(2,1)S(1)}, bf16[4,64,256]{2,1,0:T(8,128)(2,1)S(1)}, u32[]{:S(2)}, u32[]{:S(2)}) %collective-permute-start.13) | collective-permute-done | bytes 131104 | tf_op jit(solution)/shard_map/ppermute | solution.py:122
  59.6 6.9 %shard_map.82 = (bf16[2,64,256]{2,1,0:T(8,128)(2,1)S(1)}, bf16[2,64,256]{2,1,0:T(8,128)(2,1)S(1)}, bf16[2,64,256]{2,1,0:T(8,128)(2,1)S(1)}, bf16[2,64,256]{2,1,0...) custom-call(s32[272]{0:T(512)S(1)} %pad_add_fusion.near_ref, ...), custom_call_target="tpu_custom_call" | custom-call | flops 4294967296 | bytes 1048576 | tf_op jit(solution)/shard_map/pallas_call | solution.py:356
  66.5 2.0 %collective-permute-start.14 = (bf16[2,64,256]{2,1,0:T(8,128)(2,1)S(1)}, bf16[2,64,256]{2,1,0:T(8,128)(2,1)S(1)}, u32[]{:S(2)}, u32[]{:S(2)}) collective-permute-start(bf16[2,64,256]{2,1,0:T(8,128)(2,1)S(1)} %get-tuple-element.68), channel_id=1, source_target_pairs={{0,1},{1,0},{2,3},{3,2},{4,5},{5,4},{6,7},{7,6},{8,9},{9,8},{10,11... | collective-permute-start | bytes 196616 | tf_op jit(solution)/shard_map/ppermute | solution.py:505
  68.5 1.3 %collective-permute-start.15 = (bf16[2,64,256]{2,1,0:T(8,128)(2,1)S(1)}, bf16[2,64,256]{2,1,0:T(8,128)(2,1)S(1)}, u32[]{:S(2)}, u32[]{:S(2)}) collective-permute-start(bf16[2,64,256]{2,1,0:T(8,128)(2,1)S(1)} %get-tuple-element.69), channel_id=1, source_target_pairs={{0,2},{1,3},{2,0},{3,1},{4,6},{5,7},{6,4},{7,5},{8,10},{9,11},{10,... | collective-permute-start | bytes 196616 | tf_op jit(solution)/shard_map/ppermute | solution.py:505
  70.1 3.2 %collective-permute-start.17 = (bf16[2,64,256]{2,1,0:T(8,128)(2,1)S(1)}, bf16[2,64,256]{2,1,0:T(8,128)(2,1)S(1)}, u32[]{:S(2)}, u32[]{:S(2)}) collective-permute-start(bf16[2,64,256]{2,1,0:T(8,128)(2,1)S(1)} %get-tuple-element.71), channel_id=1, source_target_pairs={{0,4},{1,5},{2,6},{3,7},{4,0},{5,1},{6,2},{7,3},{8,12},{9,13},{10,... | collective-permute-start | bytes 196616 | tf_op jit(solution)/shard_map/ppermute | solution.py:505
  74.4 2.1 %collective-permute-start.19 = (bf16[2,64,256]{2,1,0:T(8,128)(2,1)S(1)}, bf16[2,64,256]{2,1,0:T(8,128)(2,1)S(1)}, u32[]{:S(2)}, u32[]{:S(2)}) collective-permute-start(bf16[2,64,256]{2,1,0:T(8,128)(2,1)S(1)} %get-tuple-element.73), channel_id=1, source_target_pairs={{0,6},{1,7},{2,4},{3,5},{4,2},{5,3},{6,0},{7,1},{8,14},{9,15},{10,... | collective-permute-start | bytes 196616 | tf_op jit(solution)/shard_map/ppermute | solution.py:505
  76.5 1.5 %collective-permute-start.20 = (bf16[2,64,256]{2,1,0:T(8,128)(2,1)S(1)}, bf16[2,64,256]{2,1,0:T(8,128)(2,1)S(1)}, u32[]{:S(2)}, u32[]{:S(2)}) collective-permute-start(bf16[2,64,256]{2,1,0:T(8,128)(2,1)S(1)} %get-tuple-element.74), channel_id=1, source_target_pairs={{0,7},{1,6},{2,5},{3,4},{4,3},{5,2},{6,1},{7,0},{8,15},{9,14},{10,... | collective-permute-start | bytes 196616 | tf_op jit(solution)/shard_map/ppermute | solution.py:505
  78.0 4.8 %collective-permute-done.18.refs_5_ = bf16[2,64,256]{2,1,0:T(8,128)(2,1)S(1)} collective-permute-done((bf16[2,64,256]{2,1,0:T(8,128)(2,1)S(1)}, bf16[2,64,256]{2,1,0:T(8,128)(2,1)S(1)}, u32[]{:S(2)}, u32[]{:S(2)}) %collective-permute-start.18) | collective-permute-done | bytes 65568 | tf_op jit(solution)/shard_map/ppermute | solution.py:505
  83.6 1.4 %place.1 = bf16[16,64,256]{2,1,0:T(8,128)(2,1)} custom-call(s32[6]{0:T(128)S(1)} %stack.19.meta_ref, bf16[2,64,256]{2,1,0:T(8,128)(2,1)S(1)} %get-tuple-element.67.refs_0_, bf16[2,64,256]{2,1,0:T(8,128)(2,1)S(1)} %collective-permute-done.14.refs_1_, bf16[2,64,256]{2,1,0:T(8,128)(2,1)S(1)} %collective-permute-done.15.refs_2_, ...), custom_call_target="tpu_custom_call" | custom-call | tf_op jit(solution)/shard_map/place/pallas_call | solution.py:506
  (41 shorter events, 8.7 us)
Async XLA Ops:
  1.8 7.6 %collective-permute-start = (f32[8,3,256]{2,1,0:T(4,128)S(1)}, f32[8,3,256]{2,1,0:T(4,128)S(1)}, u32[]{:S(2)}, u32[]{:S(2)}) collective-permute-start(f32[8,3,256]{2,1,0:T(4,128)S(1)} %get-tuple-element.41.refs_1_.o1), channel_id=1, source_target_pairs={{0,8},{1,2},{2,1},{3,4},{4,3},{5,6},{6,5},{7,15},{8,0},{9,10},{10,... | collective-permute-start | bytes 73736 | tf_op jit(solution)/shard_map/ppermute | solution.py:122
  2.4 10.9 %collective-permute-start.1 = (f32[8,3,256]{2,1,0:T(4,128)S(1)}, f32[8,3,256]{2,1,0:T(4,128)S(1)}, u32[]{:S(2)}, u32[]{:S(2)}) collective-permute-start(f32[8,3,256]{2,1,0:T(4,128)S(1)} %get-tuple-element.40.refs_0_.o0), channel_id=1, source_target_pairs={{0,1},{1,0},{2,3},{3,2},{4,5},{5,4},{6,7},{7,6},{8,9},{9,8},{10,11... | collective-permute-start | bytes 73736 | tf_op jit(solution)/shard_map/ppermute | solution.py:123
  6.4 11.9 %collective-permute-start.4 = (bf16[8,64,256]{2,1,0:T(8,128)(2,1)S(1)}, bf16[8,64,256]{2,1,0:T(8,128)(2,1)S(1)}, u32[]{:S(2)}, u32[]{:S(2)}) collective-permute-start(bf16[8,64,256]{2,1,0:T(8,128)(2,1)S(1)} %get-tuple-element.50.refs_1_), channel_id=1, source_target_pairs={{0,8},{1,2},{2,1},{3,4},{4,3},{5,6},{6,5},{7,15},{8,0},{9,10},{10,... | collective-permute-start | bytes 786440 | tf_op jit(solution)/shard_map/ppermute | solution.py:122
  6.4 12.4 %collective-permute-start.5 = (bf16[8,64,256]{2,1,0:T(8,128)(2,1)S(1)}, bf16[8,64,256]{2,1,0:T(8,128)(2,1)S(1)}, u32[]{:S(2)}, u32[]{:S(2)}) collective-permute-start(bf16[8,64,256]{2,1,0:T(8,128)(2,1)S(1)} %get-tuple-element.49.refs_0_), channel_id=1, source_target_pairs={{0,1},{1,0},{2,3},{3,2},{4,5},{5,4},{6,7},{7,6},{8,9},{9,8},{10,11... | collective-permute-start | bytes 786440 | tf_op jit(solution)/shard_map/ppermute | solution.py:123
  13.8 8.9 %collective-permute-start.2 = (f32[16,3,256]{2,1,0:T(4,128)S(1)}, f32[16,3,256]{2,1,0:T(4,128)S(1)}, u32[]{:S(2)}, u32[]{:S(2)}) collective-permute-start(f32[16,3,256]{2,1,0:T(4,128)S(1)} %get-tuple-element.46), channel_id=1, source_target_pairs={{0,8},{1,9},{2,10},{3,11},{4,12},{5,13},{6,14},{7,15},{8,0},{9,1},... | collective-permute-start | bytes 147464 | tf_op jit(solution)/shard_map/ppermute | solution.py:123
  13.9 8.8 %collective-permute-start.3 = (f32[16,3,256]{2,1,0:T(4,128)S(1)}, f32[16,3,256]{2,1,0:T(4,128)S(1)}, u32[]{:S(2)}, u32[]{:S(2)}) collective-permute-start(f32[16,3,256]{2,1,0:T(4,128)S(1)} %get-tuple-element.47), channel_id=1, source_target_pairs={{0,2},{1,3},{2,0},{3,1},{4,6},{5,7},{6,4},{7,5},{8,16},{9,17},{10,... | collective-permute-start | bytes 147464 | tf_op jit(solution)/shard_map/ppermute | solution.py:122
  19.4 17.0 %collective-permute-start.6 = (bf16[16,64,256]{2,1,0:T(8,128)(2,1)S(1)}, bf16[16,64,256]{2,1,0:T(8,128)(2,1)S(1)}, u32[]{:S(2)}, u32[]{:S(2)}) collective-permute-start(bf16[16,64,256]{2,1,0:T(8,128)(2,1)S(1)} %get-tuple-element.51), channel_id=1, source_target_pairs={{0,8},{1,9},{2,10},{3,11},{4,12},{5,13},{6,14},{7,15},{8,0},{9,1},... | collective-permute-start | bytes 1572872 | tf_op jit(solution)/shard_map/ppermute | solution.py:123
  19.5 16.9 %collective-permute-start.7 = (bf16[16,64,256]{2,1,0:T(8,128)(2,1)S(1)}, bf16[16,64,256]{2,1,0:T(8,128)(2,1)S(1)}, u32[]{:S(2)}, u32[]{:S(2)}) collective-permute-start(bf16[16,64,256]{2,1,0:T(8,128)(2,1)S(1)} %get-tuple-element.52), channel_id=1, source_target_pairs={{0,2},{1,3},{2,0},{3,1},{4,6},{5,7},{6,4},{7,5},{8,16},{9,17},{10,... | collective-permute-start | bytes 1572872 | tf_op jit(solution)/shard_map/ppermute | solution.py:122
  27.3 9.0 %copy-start = (f32[16,256]{1,0:T(8,128)S(1)}, f32[16,256]{1,0:T(8,128)}, u32[]{:S(2)}) copy-start(f32[16,256]{1,0:T(8,128)} %refs_14_.1) | copy-start | bytes 49156
  27.3 9.0 %copy-start.1 = (f32[32]{0:T(128)S(1)}, f32[32]{0:T(128)}, u32[]{:S(2)}) copy-start(f32[32]{0:T(128)} %param.10) | copy-start | bytes 388
  27.4 9.0 %copy-start.2 = (f32[32]{0:T(128)S(1)}, f32[32]{0:T(128)}, u32[]{:S(2)}) copy-start(f32[32]{0:T(128)} %param.11) | copy-start | bytes 388
  40.1 5.3 %collective-permute-start.8 = (bf16[8,64,256]{2,1,0:T(8,128)(2,1)S(1)}, bf16[8,64,256]{2,1,0:T(8,128)(2,1)S(1)}, u32[]{:S(2)}, u32[]{:S(2)}) collective-permute-start(bf16[8,64,256]{2,1,0:T(8,128)(2,1)S(1)} %get-tuple-element.60.refs_1_), channel_id=1, source_target_pairs={{0,8},{1,2},{2,1},{3,4},{4,3},{5,6},{6,5},{7,15},{8,0},{9,10},{10,... | collective-permute-start | bytes 786440 | tf_op jit(solution)/shard_map/ppermute | solution.py:122
  43.8 9.5 %collective-permute-start.9 = (bf16[8,64,256]{2,1,0:T(8,128)(2,1)S(1)}, bf16[8,64,256]{2,1,0:T(8,128)(2,1)S(1)}, u32[]{:S(2)}, u32[]{:S(2)}) collective-permute-start(bf16[8,64,256]{2,1,0:T(8,128)(2,1)S(1)} %get-tuple-element.59.refs_0_), channel_id=1, source_target_pairs={{0,1},{1,0},{2,3},{3,2},{4,5},{5,4},{6,7},{7,6},{8,9},{9,8},{10,11... | collective-permute-start | bytes 786440 | tf_op jit(solution)/shard_map/ppermute | solution.py:123
  46.0 13.6 %collective-permute-start.10 = (bf16[12,64,256]{2,1,0:T(8,128)(2,1)S(1)}, bf16[12,64,256]{2,1,0:T(8,128)(2,1)S(1)}, u32[]{:S(2)}, u32[]{:S(2)}) collective-permute-start(bf16[12,64,256]{2,1,0:T(8,128)(2,1)S(1)} %get-tuple-element.61), channel_id=1, source_target_pairs={{0,8},{1,9},{2,10},{3,11},{4,12},{5,13},{6,14},{7,15},{8,0},{9,1},... | collective-permute-start | bytes 1179656 | tf_op jit(solution)/shard_map/ppermute | solution.py:123
  47.1 12.5 %collective-permute-start.12 = (bf16[12,64,256]{2,1,0:T(8,128)(2,1)S(1)}, bf16[12,64,256]{2,1,0:T(8,128)(2,1)S(1)}, u32[]{:S(2)}, u32[]{:S(2)}) collective-permute-start(bf16[12,64,256]{2,1,0:T(8,128)(2,1)S(1)} %get-tuple-element.63), channel_id=1, source_target_pairs={{0,2},{1,3},{2,0},{3,1},{4,6},{5,7},{6,4},{7,5},{8,16},{9,17},{10,... | collective-permute-start | bytes 1179656 | tf_op jit(solution)/shard_map/ppermute | solution.py:122
  53.9 2.8 %collective-permute-start.11 = (bf16[4,64,256]{2,1,0:T(8,128)(2,1)S(1)}, bf16[4,64,256]{2,1,0:T(8,128)(2,1)S(1)}, u32[]{:S(2)}, u32[]{:S(2)}) collective-permute-start(bf16[4,64,256]{2,1,0:T(8,128)(2,1)S(1)} %get-tuple-element.62), channel_id=1, source_target_pairs={{0,8},{1,9},{2,10},{3,11},{4,12},{5,13},{6,14},{7,15},{8,0},{9,1},... | collective-permute-start | bytes 393224 | tf_op jit(solution)/shard_map/ppermute | solution.py:123
  54.1 5.5 %collective-permute-start.13 = (bf16[4,64,256]{2,1,0:T(8,128)(2,1)S(1)}, bf16[4,64,256]{2,1,0:T(8,128)(2,1)S(1)}, u32[]{:S(2)}, u32[]{:S(2)}) collective-permute-start(bf16[4,64,256]{2,1,0:T(8,128)(2,1)S(1)} %get-tuple-element.64), channel_id=1, source_target_pairs={{0,2},{1,3},{2,0},{3,1},{4,6},{5,7},{6,4},{7,5},{8,16},{9,17},{10,... | collective-permute-start | bytes 393224 | tf_op jit(solution)/shard_map/ppermute | solution.py:122
  66.5 7.9 %collective-permute-start.14 = (bf16[2,64,256]{2,1,0:T(8,128)(2,1)S(1)}, bf16[2,64,256]{2,1,0:T(8,128)(2,1)S(1)}, u32[]{:S(2)}, u32[]{:S(2)}) collective-permute-start(bf16[2,64,256]{2,1,0:T(8,128)(2,1)S(1)} %get-tuple-element.68), channel_id=1, source_target_pairs={{0,1},{1,0},{2,3},{3,2},{4,5},{5,4},{6,7},{7,6},{8,9},{9,8},{10,11... | collective-permute-start | bytes 196616 | tf_op jit(solution)/shard_map/ppermute | solution.py:505
  68.5 8.0 %collective-permute-start.15 = (bf16[2,64,256]{2,1,0:T(8,128)(2,1)S(1)}, bf16[2,64,256]{2,1,0:T(8,128)(2,1)S(1)}, u32[]{:S(2)}, u32[]{:S(2)}) collective-permute-start(bf16[2,64,256]{2,1,0:T(8,128)(2,1)S(1)} %get-tuple-element.69), channel_id=1, source_target_pairs={{0,2},{1,3},{2,0},{3,1},{4,6},{5,7},{6,4},{7,5},{8,10},{9,11},{10,... | collective-permute-start | bytes 196616 | tf_op jit(solution)/shard_map/ppermute | solution.py:505
  69.8 8.2 %collective-permute-start.16 = (bf16[2,64,256]{2,1,0:T(8,128)(2,1)S(1)}, bf16[2,64,256]{2,1,0:T(8,128)(2,1)S(1)}, u32[]{:S(2)}, u32[]{:S(2)}) collective-permute-start(bf16[2,64,256]{2,1,0:T(8,128)(2,1)S(1)} %get-tuple-element.70), channel_id=1, source_target_pairs={{0,3},{1,2},{2,1},{3,0},{4,7},{5,6},{6,5},{7,4},{8,11},{9,10},{10,... | collective-permute-start | bytes 196616 | tf_op jit(solution)/shard_map/ppermute | solution.py:505
  70.1 7.9 %collective-permute-start.17 = (bf16[2,64,256]{2,1,0:T(8,128)(2,1)S(1)}, bf16[2,64,256]{2,1,0:T(8,128)(2,1)S(1)}, u32[]{:S(2)}, u32[]{:S(2)}) collective-permute-start(bf16[2,64,256]{2,1,0:T(8,128)(2,1)S(1)} %get-tuple-element.71), channel_id=1, source_target_pairs={{0,4},{1,5},{2,6},{3,7},{4,0},{5,1},{6,2},{7,3},{8,12},{9,13},{10,... | collective-permute-start | bytes 196616 | tf_op jit(solution)/shard_map/ppermute | solution.py:505
  73.3 9.5 %collective-permute-start.18 = (bf16[2,64,256]{2,1,0:T(8,128)(2,1)S(1)}, bf16[2,64,256]{2,1,0:T(8,128)(2,1)S(1)}, u32[]{:S(2)}, u32[]{:S(2)}) collective-permute-start(bf16[2,64,256]{2,1,0:T(8,128)(2,1)S(1)} %get-tuple-element.72), channel_id=1, source_target_pairs={{0,5},{1,4},{2,7},{3,6},{4,1},{5,0},{6,3},{7,2},{8,13},{9,12},{10,... | collective-permute-start | bytes 196616 | tf_op jit(solution)/shard_map/ppermute | solution.py:505
  74.4 8.4 %collective-permute-start.19 = (bf16[2,64,256]{2,1,0:T(8,128)(2,1)S(1)}, bf16[2,64,256]{2,1,0:T(8,128)(2,1)S(1)}, u32[]{:S(2)}, u32[]{:S(2)}) collective-permute-start(bf16[2,64,256]{2,1,0:T(8,128)(2,1)S(1)} %get-tuple-element.73), channel_id=1, source_target_pairs={{0,6},{1,7},{2,4},{3,5},{4,2},{5,3},{6,0},{7,1},{8,14},{9,15},{10,... | collective-permute-start | bytes 196616 | tf_op jit(solution)/shard_map/ppermute | solution.py:505
  76.5 7.1 %collective-permute-start.20 = (bf16[2,64,256]{2,1,0:T(8,128)(2,1)S(1)}, bf16[2,64,256]{2,1,0:T(8,128)(2,1)S(1)}, u32[]{:S(2)}, u32[]{:S(2)}) collective-permute-start(bf16[2,64,256]{2,1,0:T(8,128)(2,1)S(1)} %get-tuple-element.74), channel_id=1, source_target_pairs={{0,7},{1,6},{2,5},{3,4},{4,3},{5,2},{6,1},{7,0},{8,15},{9,14},{10,... | collective-permute-start | bytes 196616 | tf_op jit(solution)/shard_map/ppermute | solution.py:505
